TPU v7x, 32 devices: a whole 2x2x4 slice. The times are simulated.
32 devices in a mesh: grp: 4 (over z), shard: 8 (over y, x, core).
Axes of the slice: x: 2, y: 2, z: 4, core: 2. Of those that a mesh axis runs over, the one named last changes fastest.
Arguments:
- frames_in: float32 [128, 256, 768], P(('grp', 'shard')), may hold values from -6 to 6
- cotangent: float32 [128, 256, 768], P(('grp', 'shard')), may hold values from -6 to 6
- time_table: bfloat16 [1000, 768], P(None, 'shard'), may hold values from -6 to 6
- ada_weight: bfloat16 [768, 6912], P('shard'), may hold values from -0.21875 to 0.21875
- ada_bias: bfloat16 [6912], P('shard'), may hold values from -4 to 4
- space_qkv: bfloat16 [768, 2304], P('shard'), may hold values from -0.21875 to 0.21875
- space_out: bfloat16 [768, 768], P('shard'), may hold values from -2.5 to 2.5
- time_qkv: bfloat16 [768, 2304], P('shard'), may hold values from -0.21875 to 0.21875
- time_out: bfloat16 [768, 768], P('shard'), may hold values from -0.875 to 0.875
- up_weight: bfloat16 [768, 3072], P('shard'), may hold values from -0.21875 to 0.21875
- up_bias: bfloat16 [3072], P('shard'), may hold values from -6 to 6
- down_weight: bfloat16 [3072, 768], P('shard'), may hold values from -0.109375 to 0.109375
- down_bias: bfloat16 [768], P('shard'), may hold values from -4 to 4
- timesteps: int32 [8], P('grp'), may hold values from 0 to 999
- task_mask: int32 [8, 16], P('grp'), may hold values 0 or 1
- clip_weight: float32 [8], P('grp'), may hold values from 0.5 to 2
- frame_table: int32 [4, 32], P('grp'), may hold values from 0 to 31, each once within a row
Outputs:
- frames_out: float32 [128, 256, 768], P(('grp', 'shard'))
- grad_frames_in: float32 [128, 256, 768], P(('grp', 'shard'))
- grad_time_table: float32 [1000, 768], P(None, 'shard')
- grad_ada_weight: float32 [768, 6912], P('shard')
- grad_ada_bias: float32 [6912], P('shard')
- grad_space_qkv: float32 [768, 2304], P('shard')
- grad_space_out: float32 [768, 768], P('shard')
- grad_time_qkv: float32 [768, 2304], P('shard')
- grad_time_out: float32 [768, 768], P('shard')
- grad_up_weight: float32 [768, 3072], P('shard')
- grad_up_bias: float32 [3072], P('shard')
- grad_down_weight: float32 [3072, 768], P('shard')
- grad_down_bias: float32 [768], P('shard')
Inputs may be any that keep to these rules, and one draw needn't show every extreme that they name: `frame_table`: each row lists every frame of its group once.
All inputs are finite; a program needn't handle non-finite values. No bound on the sum of `task_mask` on one device may be relied on, other than what follows from the above.
Results may differ from a plain program's by a relative error of at most 0.014.
Values may be sent and summed in bfloat16 or wider, within the bound.
No kernel may reach another device: no remote copies, remote signals or barrier semaphores. Data moves between devices by JAX's collectives and lax.ppermute only.
A program may use at most 256 MiB of HBM per device.

v0:
```python
from functools import partial

import jax
import jax.numpy as jnp
from jax import lax
from jax.sharding import PartitionSpec as P

HEADS = 12
HEAD_DIM = 64


HIGH = lax.Precision.HIGHEST
EPSILON = 1e-06


def layer_norm(values):
    center = values - jnp.mean(values, axis=-1, keepdims=True)
    spread = jnp.mean(center * center, axis=-1, keepdims=True)
    inverse = lax.rsqrt(spread + EPSILON)
    return (center * inverse, inverse)


def norm_back(grad_normed, normed, inverse):
    first = jnp.mean(grad_normed, axis=-1, keepdims=True)
    second = jnp.mean(grad_normed * normed, axis=-1, keepdims=True)
    return inverse * (grad_normed - first - normed * second)


def split_heads(packed, width):
    shape = packed.shape[:-1] + (HEADS, HEAD_DIM)
    return (
        packed[..., :width].reshape(shape),
        packed[..., width : 2 * width].reshape(shape),
        packed[..., 2 * width :].reshape(shape),
    )


def attend_forward(packed):
    width = packed.shape[-1] // 3
    query, keys, values = split_heads(packed, width)
    scores = jnp.einsum(
        "blmhe,bkmhe->bmhlk", query, keys, preferred_element_type=jnp.float32
    ) * HEAD_DIM ** (-0.5)
    highest = jnp.max(scores, axis=-1, keepdims=True)
    logsum = highest + jnp.log(jnp.sum(jnp.exp(scores - highest), axis=-1, keepdims=True))
    probs = jnp.exp(scores - logsum).astype(jnp.bfloat16)
    mixed = jnp.einsum("bmhlk,bkmhe->blmhe", probs, values, preferred_element_type=jnp.float32)
    return (mixed.reshape(packed.shape[:-1] + (width,)).astype(jnp.bfloat16), logsum)


def attend_backward(packed, logsum, grad_mixed):
    width = packed.shape[-1] // 3
    query, keys, values = split_heads(packed, width)
    factor = HEAD_DIM ** (-0.5)
    scores = (
        jnp.einsum("blmhe,bkmhe->bmhlk", query, keys, preferred_element_type=jnp.float32) * factor
    )
    probs = jnp.exp(scores - logsum)
    grad_heads = grad_mixed.reshape(query.shape)
    grad_probs = jnp.einsum(
        "blmhe,bkmhe->bmhlk", grad_heads, values, preferred_element_type=jnp.float32
    )
    grad_values = jnp.einsum(
        "bmhlk,blmhe->bkmhe",
        probs.astype(jnp.bfloat16),
        grad_heads,
        preferred_element_type=jnp.float32,
    )
    grad_scores = (
        probs * (grad_probs - jnp.sum(probs * grad_probs, axis=-1, keepdims=True))
    ).astype(jnp.bfloat16)
    grad_query = (
        jnp.einsum("bmhlk,bkmhe->blmhe", grad_scores, keys, preferred_element_type=jnp.float32)
        * factor
    )
    grad_keys = (
        jnp.einsum("bmhlk,blmhe->bkmhe", grad_scores, query, preferred_element_type=jnp.float32)
        * factor
    )
    shape = packed.shape[:-1] + (width,)
    joined = jnp.concatenate(
        [grad_query.reshape(shape), grad_keys.reshape(shape), grad_values.reshape(shape)], axis=-1
    )
    return joined.astype(jnp.bfloat16)


def mixer_forward(resid, shift, scale, gate, qkv_weight, out_weight):
    normed, inverse = layer_norm(resid)
    entry = (normed * (1.0 + scale) + shift).astype(jnp.bfloat16)
    packed = jnp.einsum(
        "blmd,de->blme", entry, qkv_weight, preferred_element_type=jnp.float32
    ).astype(jnp.bfloat16)
    mixed, logsum = attend_forward(packed)
    branch = jnp.einsum("blmd,de->blme", mixed, out_weight, preferred_element_type=jnp.float32)
    return (resid + gate * branch, (normed, inverse, entry, packed, logsum, mixed, branch))


def mixer_backward(grad_out, scale, gate, qkv_weight, out_weight, kept, per_clip):
    normed, inverse, entry, packed, logsum, mixed, branch = kept
    grad_gate = per_clip(grad_out * branch)
    grad_branch = (gate * grad_out).astype(jnp.bfloat16)
    grad_outw = jnp.einsum("blmd,blme->de", mixed, grad_branch, preferred_element_type=jnp.float32)
    grad_mixed = jnp.einsum(
        "blme,de->blmd", grad_branch, out_weight, preferred_element_type=jnp.float32
    ).astype(jnp.bfloat16)
    grad_packed = attend_backward(packed, logsum, grad_mixed)
    grad_qkvw = jnp.einsum("blmd,blme->de", entry, grad_packed, preferred_element_type=jnp.float32)
    grad_entry = jnp.einsum(
        "blme,de->blmd", grad_packed, qkv_weight, preferred_element_type=jnp.float32
    )
    grad_shift = per_clip(grad_entry)
    grad_scale = per_clip(grad_entry * normed)
    grad_in = grad_out + norm_back(grad_entry * (1.0 + scale), normed, inverse)
    return (grad_in, (grad_shift, grad_scale, grad_gate), grad_qkvw, grad_outw)


def feed_forward(resid, shift, scale, gate, up_full, up_bias_full, down_full, down_bias_full):
    normed, inverse = layer_norm(resid)
    entry = (normed * (1.0 + scale) + shift).astype(jnp.bfloat16)
    upward = jnp.einsum(
        "blmd,df->blmf", entry, up_full, preferred_element_type=jnp.float32
    ) + up_bias_full.astype(jnp.float32)
    active = jax.nn.gelu(upward, approximate=False).astype(jnp.bfloat16)
    downward = jnp.einsum(
        "blmf,fd->blmd", active, down_full, preferred_element_type=jnp.float32
    ) + down_bias_full.astype(jnp.float32)
    return (resid + gate * downward, (normed, inverse, entry, upward, active, downward))


def feed_backward(grad_out, scale, gate, up_full, down_full, kept, per_clip):
    normed, inverse, entry, upward, active, downward = kept
    grad_gate = per_clip(grad_out * downward)
    grad_down_in = (gate * grad_out).astype(jnp.bfloat16)
    grad_down = jnp.einsum(
        "blmf,blmd->fd", active, grad_down_in, preferred_element_type=jnp.float32
    )
    grad_down_bias = jnp.sum(grad_down_in.astype(jnp.float32), axis=(0, 1, 2))
    grad_active = jnp.einsum(
        "blmd,fd->blmf", grad_down_in, down_full, preferred_element_type=jnp.float32
    )
    _, gelu_back = jax.vjp(partial(jax.nn.gelu, approximate=False), upward)
    grad_up_in = gelu_back(grad_active)[0].astype(jnp.bfloat16)
    grad_up = jnp.einsum("blmd,blmf->df", entry, grad_up_in, preferred_element_type=jnp.float32)
    grad_up_bias = jnp.sum(grad_up_in.astype(jnp.float32), axis=(0, 1, 2))
    grad_entry = jnp.einsum(
        "blmf,df->blmd", grad_up_in, up_full, preferred_element_type=jnp.float32
    )
    grad_shift = per_clip(grad_entry)
    grad_scale = per_clip(grad_entry * normed)
    grad_in = grad_out + norm_back(grad_entry * (1.0 + scale), normed, inverse)
    return (
        grad_in,
        (grad_shift, grad_scale, grad_gate),
        grad_up,
        grad_up_bias,
        grad_down,
        grad_down_bias,
    )


def body(
    frames_in,
    cotangent,
    time_table,
    ada_weight,
    ada_bias,
    space_qkv,
    space_out,
    time_qkv,
    time_out,
    up_weight,
    up_bias,
    down_weight,
    down_bias,
    timesteps,
    task_mask,
    clip_weight,
    frame_table,
):
    gathered = (
        lax.all_gather(time_table, "shard", axis=1, tiled=True),
        lax.all_gather(ada_weight, "shard", axis=0, tiled=True),
        lax.all_gather(ada_bias, "shard", axis=0, tiled=True),
        lax.all_gather(space_qkv, "shard", axis=0, tiled=True),
        lax.all_gather(space_out, "shard", axis=0, tiled=True),
        lax.all_gather(time_qkv, "shard", axis=0, tiled=True),
        lax.all_gather(time_out, "shard", axis=0, tiled=True),
        lax.all_gather(up_weight, "shard", axis=0, tiled=True),
        lax.all_gather(up_bias, "shard", axis=0, tiled=True),
        lax.all_gather(down_weight, "shard", axis=0, tiled=True),
        lax.all_gather(down_bias, "shard", axis=0, tiled=True),
    )
    (
        table_full,
        ada_full,
        ada_bias_full,
        space_qkv_full,
        space_out_full,
        time_qkv_full,
        time_out_full,
        up_full,
        up_bias_full,
        down_full,
        down_bias_full,
    ) = gathered
    shards = lax.axis_size("shard")
    shard_at = lax.axis_index("shard")
    frame_count, patches, width = frames_in.shape
    clips = timesteps.shape[0]
    frames = task_mask.shape[1]
    table = frame_table[0]
    group_frames = table.shape[0]
    columns = patches // shards
    vocab = table_full.shape[0]
    onehot = (timesteps[:, None] == jnp.arange(vocab, dtype=jnp.int32)[None, :]).astype(jnp.float32)
    embed = jnp.dot(onehot, table_full.astype(jnp.float32), precision=HIGH)
    cond = jax.nn.silu(embed).astype(jnp.bfloat16)
    modul = jnp.dot(cond, ada_full, preferred_element_type=jnp.float32) + ada_bias_full.astype(
        jnp.float32
    )
    slot_ids = shard_at * frame_count + jnp.arange(frame_count, dtype=jnp.int32)
    frame_ids = jnp.take(table, slot_ids)
    clip_of = frame_ids // frames
    frame_of = frame_ids % frames
    clip_hot = (clip_of[:, None] == jnp.arange(clips, dtype=jnp.int32)[None, :]).astype(jnp.float32)
    frame_mod = jnp.take(modul, clip_of, axis=0)
    own_parts = [
        frame_mod[:, part_at * width : (part_at + 1) * width][:, None, None, :]
        for part_at in range(9)
    ]
    all_parts = [
        modul[:, part_at * width : (part_at + 1) * width][:, None, None, :] for part_at in range(9)
    ]
    inverse = (
        jnp.zeros((group_frames,), jnp.int32)
        .at[table]
        .set(jnp.arange(group_frames, dtype=jnp.int32))
    )

    def frame_sums(values):
        return jnp.dot(clip_hot.T, jnp.sum(values, axis=(1, 2)), precision=HIGH)

    def column_sums(values):
        return jnp.sum(values, axis=(1, 2))

    space_rows = frames_in.reshape(frame_count, patches, 1, width)
    after_space, space_kept = mixer_forward(
        space_rows, own_parts[0], own_parts[1], own_parts[2], space_qkv_full, space_out_full
    )
    received = lax.all_to_all(
        after_space.reshape(frame_count, patches, width),
        "shard",
        split_axis=1,
        concat_axis=0,
        tiled=True,
    )
    columned = jnp.take(received, inverse, axis=0).reshape(clips, frames, columns, width)
    after_time, time_kept = mixer_forward(
        columned, all_parts[3], all_parts[4], all_parts[5], time_qkv_full, time_out_full
    )
    result, mlp_kept = feed_forward(
        after_time,
        all_parts[6],
        all_parts[7],
        all_parts[8],
        up_full,
        up_bias_full,
        down_full,
        down_bias_full,
    )
    leaving = jnp.take(result.reshape(group_frames, columns, width), table, axis=0)
    frames_out = lax.all_to_all(leaving, "shard", split_axis=0, concat_axis=1, tiled=True)
    row_weights = task_mask[clip_of, frame_of].astype(jnp.float32) * clip_weight[clip_of]
    weighted = cotangent * row_weights[:, None, None]
    arriving = lax.all_to_all(weighted, "shard", split_axis=1, concat_axis=0, tiled=True)
    grad_result = jnp.take(arriving, inverse, axis=0).reshape(clips, frames, columns, width)
    grad_after_time, mlp_mods, grad_up, grad_up_bias, grad_down, grad_down_bias = feed_backward(
        grad_result, all_parts[7], all_parts[8], up_full, down_full, mlp_kept, column_sums
    )
    grad_columned, time_mods, grad_time_qkv, grad_time_out = mixer_backward(
        grad_after_time,
        all_parts[4],
        all_parts[5],
        time_qkv_full,
        time_out_full,
        time_kept,
        column_sums,
    )
    going = jnp.take(grad_columned.reshape(group_frames, columns, width), table, axis=0)
    grad_space = lax.all_to_all(going, "shard", split_axis=0, concat_axis=1, tiled=True)
    grad_rows, space_mods, grad_space_qkv, grad_space_out = mixer_backward(
        grad_space.reshape(frame_count, patches, 1, width),
        own_parts[1],
        own_parts[2],
        space_qkv_full,
        space_out_full,
        space_kept,
        frame_sums,
    )
    mod_part = jnp.concatenate(space_mods + time_mods + mlp_mods, axis=1)
    grad_modul = lax.psum(mod_part, "shard").astype(jnp.bfloat16)
    rows_dev = width // shards
    cond_share = lax.dynamic_slice_in_dim(cond, shard_at * rows_dev, rows_dev, 1)
    grad_ada = jnp.einsum("cd,cj->dj", cond_share, grad_modul, preferred_element_type=jnp.float32)
    bias_dev = ada_bias.shape[0]
    grad_ada_bias = lax.dynamic_slice_in_dim(
        jnp.sum(grad_modul.astype(jnp.float32), axis=0), shard_at * bias_dev, bias_dev, 0
    )
    grad_cond = jnp.einsum("cj,dj->cd", grad_modul, ada_full, preferred_element_type=jnp.float32)
    _, silu_back = jax.vjp(jax.nn.silu, embed)
    grad_embed = silu_back(grad_cond)[0]
    grad_table = jnp.dot(
        onehot.T,
        lax.dynamic_slice_in_dim(grad_embed, shard_at * rows_dev, rows_dev, 1),
        precision=HIGH,
    )
    shares = (
        lax.psum_scatter(grad_space_qkv, "shard", scatter_dimension=0, tiled=True),
        lax.psum_scatter(grad_space_out, "shard", scatter_dimension=0, tiled=True),
        lax.psum_scatter(grad_time_qkv, "shard", scatter_dimension=0, tiled=True),
        lax.psum_scatter(grad_time_out, "shard", scatter_dimension=0, tiled=True),
        lax.psum_scatter(grad_up, "shard", scatter_dimension=0, tiled=True),
        lax.psum_scatter(grad_up_bias, "shard", scatter_dimension=0, tiled=True),
        lax.psum_scatter(grad_down, "shard", scatter_dimension=0, tiled=True),
        lax.psum_scatter(grad_down_bias, "shard", scatter_dimension=0, tiled=True),
    )
    totals = lax.psum(
        (
            grad_table,
            grad_ada,
            grad_ada_bias,
            shares[0],
            shares[1],
            shares[2],
            shares[3],
            shares[4],
            shares[5],
            shares[6],
            shares[7],
        ),
        "grp",
    )
    return (
        frames_out,
        grad_rows.reshape(frame_count, patches, width),
        totals[0],
        totals[1],
        totals[2],
        totals[3],
        totals[4],
        totals[5],
        totals[6],
        totals[7],
        totals[8],
        totals[9],
        totals[10],
    )


def solution(mesh):
    placed = (
        P(("grp", "shard"), None, None),
        P(("grp", "shard"), None, None),
        P(None, "shard"),
        P("shard", None),
        P("shard"),
        P("shard", None),
        P("shard", None),
        P("shard", None),
        P("shard", None),
        P("shard", None),
        P("shard"),
        P("shard", None),
        P("shard"),
        P("grp"),
        P("grp", None),
        P("grp"),
        P("grp", None),
    )
    return jax.shard_map(
        body,
        mesh=mesh,
        in_specs=placed,
        out_specs=(
            P(("grp", "shard"), None, None),
            P(("grp", "shard"), None, None),
            P(None, "shard"),
            P("shard", None),
            P("shard"),
            P("shard", None),
            P("shard", None),
            P("shard", None),
            P("shard", None),
            P("shard", None),
            P("shard"),
            P("shard", None),
            P("shard"),
        ),
        check_vma=False,
    )
```

profile of v0, /device:TPU:0, one launch (start us, length us, event | category | flops | bytes accessed | tf_op | source)
XLA Modules:
  0.0 1203.2 jit_solution(18428693430552086320)
XLA Ops:
  14.2 3.7 copy.204
  17.9 5.5 all-to-all-start.2
  27.0 59.0 %all-reduce.7 = (bf16[6912]{0:T(1024)(128)(2,1)S(1)}, bf16[768]{0:T(1024)(128)(2,1)S(1)}) all-reduce(bf16[6912]{0:T(1024)(128)(2,1)S(1)} %dynamic-update-slice, bf16[768]{0:T(1024)(128)(2,1)S(1)} %dynamic-update-slice.1), channel_id=1, replica_groups=mesh['grp'=4,'shard'=8] {'shard'}, use_global_device_ids=true, to_apply=%add | all-reduce | flops 7680 | bytes 30720
  89.3 28.9 %all-gather.12.cloned.1.call-done = bf16[768,6912]{1,0:T(8,128)(2,1)} async-done(((bf16[96,6912]{1,0:T(8,128)(2,1)}), bf16[768,6912]{1,0:T(8,128)(2,1)}) %all-gather.12.cloned.1.call-update) | async-done | bytes 10616848 | tf_op jit(solution)/shard_map/all_gather | solution.py:182
  118.2 5.5 convolution_add_fusion
  124.5 29.5 %all-gather.14.cloned.1.call-done = bf16[768,2304]{1,0:T(8,128)(2,1)} async-done(((bf16[96,2304]{1,0:T(8,128)(2,1)}), bf16[768,2304]{1,0:T(8,128)(2,1)}) %all-gather.14.cloned.1.call-update) | async-done | bytes 3538960 | tf_op jit(solution)/shard_map/all_gather | solution.py:184
  154.0 6.3 fusion.9
  170.6 3.7 multiply_reduce_fusion.1
  179.2 3.4 convolution_convert_fusion.3
  182.6 4.9 multiply_add_fusion.4
  187.5 3.7 copy.195
  191.2 3.8 all-to-all-start
  195.8 49.5 %all-gather = bf16[8,1,384]{2,1,0:T(2,128)(2,1)S(1)} all-gather(bf16[1,1,384]{2,1,0:T(2,128)(2,1)S(1)} %reshape.651), channel_id=1, replica_groups=mesh['grp'=4,'shard'=8] {'shard'}, dimensions={0}, use_global_device_ids=true | all-gather | bytes 6912 | tf_op jit(solution)/shard_map/all_gather | solution.py:189
  251.7 4.3 gather_fusion.6
  259.4 6.2 convert_reduce_fusion.1
  266.2 6.8 convolution_convert_fusion
  275.3 5.9 reshape.560
  281.2 6.0 reshape.561
  287.2 8.0 multiply_reduce_fusion.3
  298.8 6.0 reshape.559
  304.8 6.8 convert_bitcast_fusion.1
  311.6 3.1 copy.202
  314.7 6.1 convert_element_type.153
  320.8 5.9 multiply_add_fusion.3
  330.2 10.1 fusion.8
  340.3 4.6 copy-done.23
  344.9 29.8 %multiply_convert_fusion.1 = (bf16[2,16,32,3072]{3,2,1,0:T(8,128)(2,1)}, f32[2,16,32,3072]{3,2,1,0:T(8,128)}) fusion(f32[2,16,32,3072]{3,2,1,0:T(8,128)S(1)} %get-tuple-element.93, f32[3072]{0:T(1024)S(1)} %bitcast.260, u16[2,32,3072]{2,1,0:T(8,128)(2,1)S(1)} %get-tuple-element.15, u16[2,32,3072]{2,1,0:T(8,128)(2,1)S(1)} %get-tuple-element.14), kind=kLoop, calls=%fused_computation.20 | loop fusion | flops 223346688 | bytes 32256000 | tf_op jit(solution)/shard_map/convert_element_type | solution.py:123
  374.7 19.6 %convert_reduce_fusion = (f32[3072]{0:T(1024)}, bf16[2,16,32,3072]{3,2,1,0:T(8,128)(2,1)}) fusion(f32[2,16,32,3072]{3,2,1,0:T(8,128)} %get-tuple-element.47, bf16[3072,768]{1,0:T(8,128)(2,1)} %all-gather.24.cloned.1.call-done, f32[2,16,32,768]{3,2,1,0:T(8,128)} %bitcast.246, f32[2,768]{1,0:T(2,128)S(1)} %get-tuple-element.70, ...), kind=kOutput, calls=%fused_computation.16 | convolution fusion | flops 4886885376 | bytes 39352320 | tf_op jit(solution)/shard_map/blmd,fd->blmf/dot_general | solution.py:138
  394.4 11.1 multiply_reduce_fusion.5
  405.5 9.3 multiply_reduce_fusion.4
  419.0 6.2 reshape.564
  425.2 8.5 convert_bitcast_fusion
  433.8 11.5 multiply_reduce_fusion.2
  445.2 4.2 multiply_convert_fusion.4
  449.5 4.0 fusion.25
  453.5 3.8 fusion.24
  460.2 3.0 copy.215
  463.2 6.2 reshape.567
  472.5 6.2 reshape.566
  481.8 5.2 reshape.565
  490.4 8.2 multiply_reduce_fusion.7
  501.8 4.4 gather_fusion.7
  506.2 4.6 gather_fusion.5
  510.9 5.4 broadcast_select_fusion
  516.3 48.0 %all_to_all.69 = f32[32,32,768]{2,1,0:T(8,128)S(1)} all-to-all(f32[32,32,768]{2,1,0:T(8,128)S(1)} %get-tuple-element.78), channel_id=1, replica_groups=mesh['grp'=4,'shard'=8] {'shard'}, dimensions={0} | all-to-all | bytes 6291456 | tf_op jit(solution)/shard_map/all_to_all | solution.py:290
  569.7 8.5 convolution_bitcast_fusion.2
  588.2 12.0 multiply_reduce_fusion
  601.2 7.2 multiply_convert_fusion
  614.3 5.9 multiply_convert_fusion.7
  622.8 10.1 convolution_convert_fusion.2
  636.0 9.5 convolution_bitcast_fusion.3
  646.1 11.0 convolution_bitcast_fusion.1
  657.2 10.5 convolution_bitcast_fusion
  667.9 8.6 multiply_reduce_fusion.8
  680.3 23.2 %all-reduce.4 = (bf16[2,6912]{1,0:T(2,128)(2,1)S(1)}, f32[3072]{0:T(1024)S(1)}, f32[768]{0:T(1024)S(1)}) all-reduce(f32[2,6912]{1,0:T(2,128)S(1)} %constant_dynamic-update-slice_fusion.3, f32[3072]{0:T(1024)S(1)} %copy-done.68, f32[768]{0:T(1024)S(1)} %copy-done.63), channel_id=1, replica_groups=mesh['grp'=4,'shard'=8] {'shard'}, use_global_device_ids=true, to_apply=%region_28.30 | all-reduce | flops 17664 | bytes 113664 | tf_op jit(solution)/shard_map/psum | solution.py:301
  703.5 6.9 fusion.90
  715.1 35.5 %reduce-scatter.7.cloned.1.call-done = f32[96,2304]{1,0:T(8,128)} async-done(((f32[768,2304]{1,0:T(8,128)}), f32[96,2304]{1,0:T(8,128)}) %reduce-scatter.7.cloned.1.call-update) | async-done | bytes 884752 | tf_op jit(solution)/shard_map/reduce_scatter | solution.py:318
  750.6 80.3 %reduce-scatter.15.cloned.1.call-done = f32[96,3072]{1,0:T(8,128)} async-done(((f32[768,3072]{1,0:T(8,128)}), f32[96,3072]{1,0:T(8,128)}) %reduce-scatter.15.cloned.1.call-update) | async-done | bytes 1179664 | tf_op jit(solution)/shard_map/reduce_scatter | solution.py:322
  830.9 80.2 %reduce-scatter.17.cloned.1.call-done = f32[384,768]{1,0:T(8,128)} async-done(((f32[3072,768]{1,0:T(8,128)}), f32[384,768]{1,0:T(8,128)}) %reduce-scatter.17.cloned.1.call-update) | async-done | bytes 1179664 | tf_op jit(solution)/shard_map/reduce_scatter | solution.py:324
  911.1 3.7 all-to-all-start.1
  916.1 36.5 %all-to-all-done.1 = f32[32,32,768]{2,1,0:T(8,128)S(1)} async-done(((f32[32,32,768]{2,1,0:T(8,128)}), f32[32,32,768]{2,1,0:T(8,128)S(1)}, u32[]{:S(2)}, u32[]{:S(2)}) %all-to-all-start.1) | async-done | bytes 3145760 | tf_op jit(solution)/shard_map/all_to_all | solution.py:272
  954.8 14.5 %all-reduce.5 = (f32[864]{0:T(1024)}, f32[384]{0:T(512)}, f32[96]{0:T(128)}) all-reduce(f32[864]{0:T(1024)S(1)} %dynamic_slice.11, f32[384]{0:T(512)S(1)} %dynamic-slice.3, f32[96]{0:T(128)S(1)} %dynamic-slice.5), channel_id=1, replica_groups=mesh['grp'=4,'shard'=8] {'grp'}, use_global_device_ids=true, to_apply=%region_32.34 | all-reduce | flops 1344 | bytes 10752 | tf_op jit(solution)/shard_map/psum | solution.py:327
  969.3 216.5 %all-reduce.10.cloned.1.call-done = (f32[1000,96]{0,1:T(8,128)}, f32[96,6912]{1,0:T(8,128)}, f32[96,2304]{1,0:T(8,128)}, f32[96,768]{1,0:T(8,128)}, f32[96,2304]...) async-done(((f32[1000,96]{0,1:T(8,128)}, f32[96,6912]{1,0:T(8,128)}, f32[96,2304]{1,0:T(8,128)}, f32[96,768]{1,0:T(8,128)}, ...) | async-done | bytes 7756816 | tf_op jit(solution)/shard_map/psum | solution.py:327
  1187.6 3.5 copy.287
  (328 shorter events, 114.8 us)
Async XLA Ops:
  7.2 6.0 copy-start
  7.2 5.3 copy-start.3
  7.2 6.6 copy-start.34
  7.2 79.6 %all-gather.10.cloned.1.call-start = ((), (), s32[]{:S(2)}) async-start(), calls=%async_computation.10 | async-start | bytes 1769472 | tf_op jit(solution)/shard_map/all_gather | solution.py:181
  7.9 110.3 %all-gather.12.cloned.1.call-start = ((), (), s32[]{:S(2)}) async-start(), calls=%async_computation.11 | async-start | bytes 11943936 | tf_op jit(solution)/shard_map/all_gather | solution.py:182
  8.7 145.3 %all-gather.14.cloned.1.call-start = ((), (), s32[]{:S(2)}) async-start(), calls=%async_computation.12 | async-start | bytes 3981312 | tf_op jit(solution)/shard_map/all_gather | solution.py:184
  9.4 173.2 %all-gather.16.cloned.1.call-start = ((), (), s32[]{:S(2)}) async-start(), calls=%async_computation.13 | async-start | bytes 1327104 | tf_op jit(solution)/shard_map/all_gather | solution.py:185
  10.0 256.1 %all-gather.18.cloned.1.call-start = ((), (), s32[]{:S(2)}) async-start(), calls=%async_computation.14 | async-start | bytes 3981312 | tf_op jit(solution)/shard_map/all_gather | solution.py:186
  10.6 310.2 %all-gather.20.cloned.1.call-start = ((), (), s32[]{:S(2)}) async-start(), calls=%async_computation.15 | async-start | bytes 1327104 | tf_op jit(solution)/shard_map/all_gather | solution.py:187
  17.9 6.8 copy-start.79
  17.9 8.7 copy-start.80
  17.9 8.9 copy-start.84
  17.9 68.1 %copy-start.7 = (f32[4,256,768]{2,1,0:T(8,128)S(1)}, f32[4,256,768]{2,1,0:T(8,128)}, u32[]{:S(2)}) copy-start(f32[4,256,768]{2,1,0:T(8,128)} %param.19) | copy-start | bytes 9437188
  17.9 173.3 %all-to-all-start.2 = ((f32[4,256,768]{2,0,1:T(4,128)}), f32[4,256,768]{2,0,1:T(4,128)}, u32[]{:S(2)}, u32[]{:S(2)}) async-start(f32[4,256,768]{2,0,1:T(4,128)} %copy.204), calls=%async_computation.2 | async-start | bytes 6291456 | tf_op jit(solution)/shard_map/all_to_all | solution.py:275
  23.3 306.8 %all-gather.22.cloned.1.call-start = ((), (), s32[]{:S(2)}) async-start(), calls=%async_computation.16 | async-start | bytes 5308416 | tf_op jit(solution)/shard_map/all_gather | solution.py:188
  86.2 67.7 %copy-start.58 = (f32[4,256]{1,0:T(4,128)}, f32[4,256]{1,0:T(4,128)S(1)}, u32[]{:S(2)}) copy-start(f32[4,256]{1,0:T(4,128)S(1)} %broadcast_multiply_fusion.9) | copy-start | bytes 12292
  86.7 67.2 %copy-start.64 = (f32[4,256]{1,0:T(4,128)}, f32[4,256]{1,0:T(4,128)S(1)}, u32[]{:S(2)}) copy-start(f32[4,256]{1,0:T(4,128)S(1)} %add_rsqrt_fusion.2) | copy-start | bytes 12292
  89.3 28.9 %copy-start.60 = (bf16[2,768]{1,0:T(2,128)(2,1)}, bf16[2,768]{1,0:T(2,128)(2,1)S(1)}, u32[]{:S(2)}) copy-start(bf16[2,768]{1,0:T(2,128)(2,1)S(1)} %get-tuple-element.52) | copy-start | bytes 9220
  124.4 35.9 %copy-start.56 = (f32[4,768]{1,0:T(4,128)}, f32[4,768]{1,0:T(4,128)S(1)}, u32[]{:S(2)}) copy-start(f32[4,768]{1,0:T(4,128)S(1)} %get-tuple-element.69) | copy-start | bytes 36868
  124.5 35.9 %copy-start.66 = (f32[4,768]{1,0:T(4,128)}, f32[4,768]{1,0:T(4,128)S(1)}, u32[]{:S(2)}) copy-start(f32[4,768]{1,0:T(4,128)S(1)} %get-tuple-element.68) | copy-start | bytes 36868
  124.5 58.2 %copy-start.50 = (f32[4,768]{1,0:T(4,128)}, f32[4,768]{1,0:T(4,128)S(1)}, u32[]{:S(2)}) copy-start(f32[4,768]{1,0:T(4,128)S(1)} %get-tuple-element.67) | copy-start | bytes 36868
  191.2 54.1 %copy-start.2 = (s32[1,32]{1,0:T(1,128)S(1)}, s32[1,32]{1,0:T(1,128)}, u32[]{:S(2)}) copy-start(s32[1,32]{1,0:T(1,128)} %param.35) | copy-start | bytes 388
  191.2 64.8 %all-to-all-start = ((f32[4,256,768]{2,0,1:T(4,128)}), f32[4,256,768]{2,0,1:T(4,128)S(1)}, u32[]{:S(2)}, u32[]{:S(2)}) async-start(f32[4,256,768]{2,0,1:T(4,128)} %copy.195), calls=%async_computation | async-start | bytes 6291456 | tf_op jit(solution)/shard_map/all_to_all | solution.py:250
  195.0 179.7 %all-gather.24.cloned.1.call-start = ((), (), s32[]{:S(2)}) async-start(), calls=%async_computation.17 | async-start | bytes 5308416 | tf_op jit(solution)/shard_map/all_gather | solution.py:190
  195.7 519.4 %reduce-scatter.13.cloned.1.call-start = ((), (), s32[]{:S(2)}) async-start(), calls=%async_computation.21 | async-start | bytes 2654208 | tf_op jit(solution)/shard_map/reduce_scatter | solution.py:321
  256.0 10.1 copy-start.61
  256.0 10.1 copy-start.71
  256.0 74.1 %copy-start.69 = (f32[2,768]{1,0:T(2,128)}, f32[2,768]{1,0:T(2,128)S(1)}, u32[]{:S(2)}) copy-start(f32[2,768]{1,0:T(2,128)S(1)} %get-tuple-element.71) | copy-start | bytes 18436
  265.6 55.2 %copy-start.9 = (f32[32,32,768]{2,1,0:T(8,128)}, f32[32,32,768]{2,1,0:T(8,128)S(1)}, u32[]{:S(2)}) copy-start(f32[32,32,768]{2,1,0:T(8,128)S(1)} %get-tuple-element.81) | copy-start | bytes 9437188
  265.6 7.4 copy-start.52
  266.1 6.9 copy-start.54
  394.3 11.1 copy-start.32
  394.3 11.1 copy-start.35
  394.3 11.1 copy-start.83
  405.4 11.0 copy-start.42
  419.0 6.2 copy-start.22
  419.0 14.8 %slice-start.3 = ((s8[6291456]{0:T(1024)(128)(4,1)}), s8[2097152]{0:T(1024)(128)(4,1)S(1)}, s32[]{:S(2)}) async-start(s8[6291456]{0:T(1024)(128)(4,1)} %bitcast.218), calls=%async_computation.28 | async-start | bytes 4194304
  425.2 8.6 slice-start.4
  463.2 6.2 copy-start.27
  472.5 6.2 copy-start.26
  490.4 8.3 copy-start.47
  490.4 8.3 copy-start.28
  490.4 8.3 copy-start.38
  510.8 204.3 %reduce-scatter.9.cloned.1.call-start = ((), (), s32[]{:S(2)}) async-start(), calls=%async_computation.19 | async-start | bytes 2654208 | tf_op jit(solution)/shard_map/reduce_scatter | solution.py:319
  516.3 48.0 %copy-start.51 = (f32[4,768]{1,0:T(4,128)S(1)}, f32[4,768]{1,0:T(4,128)}, u32[]{:S(2)}) copy-start(f32[4,768]{1,0:T(4,128)} %copy-done.50) | copy-start | bytes 36868
  569.7 145.4 %reduce-scatter.11.cloned.1.call-start = ((), (), s32[]{:S(2)}) async-start(), calls=%async_computation.20 | async-start | bytes 7962624 | tf_op jit(solution)/shard_map/reduce_scatter | solution.py:320
  578.2 172.3 %reduce-scatter.7.cloned.1.call-start = ((), (), s32[]{:S(2)}) async-start(), calls=%async_computation.18 | async-start | bytes 7962624 | tf_op jit(solution)/shard_map/reduce_scatter | solution.py:318
  588.1 12.0 slice-start
  588.2 12.0 slice-start.1
  588.2 13.0 %slice-start.2 = ((s8[12582912]{0:T(1024)(128)(4,1)}), s8[4194304]{0:T(1024)(128)(4,1)S(1)}, s32[]{:S(2)}) async-start(s8[12582912]{0:T(1024)(128)(4,1)} %bitcast.216), calls=%async_computation.27 | async-start | bytes 8388608
  601.2 7.2 copy-start.19
  622.8 13.1 %copy-start.57 = (f32[4,768]{1,0:T(4,128)S(1)}, f32[4,768]{1,0:T(4,128)}, u32[]{:S(2)}) copy-start(f32[4,768]{1,0:T(4,128)} %copy-done.56) | copy-start | bytes 36868
  622.8 13.1 %copy-start.59 = (f32[4,256]{1,0:T(4,128)S(1)}, f32[4,256]{1,0:T(4,128)}, u32[]{:S(2)}) copy-start(f32[4,256]{1,0:T(4,128)} %copy-done.58) | copy-start | bytes 12292
  622.8 13.1 %copy-start.65 = (f32[4,256]{1,0:T(4,128)S(1)}, f32[4,256]{1,0:T(4,128)}, u32[]{:S(2)}) copy-start(f32[4,256]{1,0:T(4,128)} %copy-done.64) | copy-start | bytes 12292
  622.8 13.1 %copy-start.67 = (f32[4,768]{1,0:T(4,128)S(1)}, f32[4,768]{1,0:T(4,128)}, u32[]{:S(2)}) copy-start(f32[4,768]{1,0:T(4,128)} %copy-done.66) | copy-start | bytes 36868
  645.5 185.4 %reduce-scatter.15.cloned.1.call-start = ((), (), s32[]{:S(2)}) async-start(), calls=%async_computation.22 | async-start | bytes 10616832 | tf_op jit(solution)/shard_map/reduce_scatter | solution.py:322
  657.2 253.9 %reduce-scatter.17.cloned.1.call-start = ((), (), s32[]{:S(2)}) async-start(), calls=%async_computation.23 | async-start | bytes 10616832 | tf_op jit(solution)/shard_map/reduce_scatter | solution.py:324
  667.8 518.0 %all-reduce.10.cloned.1.call-start = ((), (), s32[]{:S(2)}) async-start(), calls=%async_computation.24 | async-start | bytes 15532032 | tf_op jit(solution)/shard_map/psum | solution.py:327
  667.8 8.7 copy-start.82
  667.8 9.2 copy-start.12
  667.9 9.2 copy-start.24
  703.5 6.9 copy-start.77
  911.1 41.5 %all-to-all-start.1 = ((f32[32,32,768]{2,1,0:T(8,128)}), f32[32,32,768]{2,1,0:T(8,128)S(1)}, u32[]{:S(2)}, u32[]{:S(2)}) async-start(f32[32,32,768]{2,1,0:T(8,128)} %get-tuple-element.79), calls=%async_computation.1 | async-start | bytes 6291456 | tf_op jit(solution)/shard_map/all_to_all | solution.py:272
  1185.8 5.4 copy-start.46
  (44 other events, 129.7 us)
Sparse Core Ops, SparseCore 0:
  9.9 41.0 all-gather.9
  52.9 65.3 all-gather.11
  120.1 33.8 all-gather.13
  155.7 23.9 all-gather.15
  181.4 51.8 all-gather.17
  235.0 26.3 all-gather.19
  263.3 38.7 all-gather.21
  304.0 38.7 all-gather.23
  510.9 56.5 reduce-scatter.12
  570.7 41.8 reduce-scatter.8
  616.1 65.4 reduce-scatter.10
  685.0 65.4 reduce-scatter.6
  754.1 76.8 reduce-scatter.14
  834.3 76.8 reduce-scatter.16
  914.5 271.2 all-reduce.9
where the time goes:
time: 1210 us; the launch traced here: 1200 us
  waiting for transfers between devices  513 us (42%)
  matrix products  242 us (20%)
  blocking collectives  194 us (16%)
  local copies, waits for them, and re-layouts  152 us (13%)
  other arithmetic  71.4 us (6%)
  between operations  18 us (1%)
  starting transfers between devices  13.5 us (1%)
    psum x1, waiting for transfers between devices, body(): lax.psum((grad_table, grad_ada, grad_ada_bias, shares[0], shares[1], shar...  216 us
    reduce_scatter x1, waiting for transfers between devices, body(): lax.psum_scatter(grad_up, 'shard', scatter_dimension=0, tiled=True)  80.3 us
    reduce_scatter x1, waiting for transfers between devices, body(): lax.psum_scatter(grad_down, 'shard', scatter_dimension=0, tiled=True)  80.2 us
    unnamed x1, blocking collectives  59 us
    all_gather x1, blocking collectives, body(): lax.all_gather(up_bias, 'shard', axis=0, tiled=True)  49.5 us
    all_to_all x1, blocking collectives, body(): lax.all_to_all(going, 'shard', split_axis=0, concat_axis=1, tiled=True)  48 us
    all_to_all x1, waiting for transfers between devices, body(): lax.all_to_all(leaving, 'shard', split_axis=0, concat_axis=1, tiled=True)  36.5 us
    reduce_scatter x1, waiting for transfers between devices, body(): lax.psum_scatter(grad_space_qkv, 'shard', scatter_dimension=0, tiled=True)  35.5 us
  transfers between devices with their start and end apart: 18, of which 7 were waited for; matrix products, arithmetic and copies ran while one was open for 25% of the time, Pallas kernels for 0%

commit v1 on v0

--- a/solution.py
+++ b/solution.py
@@ -177,32 +177,6 @@
     clip_weight,
     frame_table,
 ):
-    gathered = (
-        lax.all_gather(time_table, "shard", axis=1, tiled=True),
-        lax.all_gather(ada_weight, "shard", axis=0, tiled=True),
-        lax.all_gather(ada_bias, "shard", axis=0, tiled=True),
-        lax.all_gather(space_qkv, "shard", axis=0, tiled=True),
-        lax.all_gather(space_out, "shard", axis=0, tiled=True),
-        lax.all_gather(time_qkv, "shard", axis=0, tiled=True),
-        lax.all_gather(time_out, "shard", axis=0, tiled=True),
-        lax.all_gather(up_weight, "shard", axis=0, tiled=True),
-        lax.all_gather(up_bias, "shard", axis=0, tiled=True),
-        lax.all_gather(down_weight, "shard", axis=0, tiled=True),
-        lax.all_gather(down_bias, "shard", axis=0, tiled=True),
-    )
-    (
-        table_full,
-        ada_full,
-        ada_bias_full,
-        space_qkv_full,
-        space_out_full,
-        time_qkv_full,
-        time_out_full,
-        up_full,
-        up_bias_full,
-        down_full,
-        down_bias_full,
-    ) = gathered
     shards = lax.axis_size("shard")
     shard_at = lax.axis_index("shard")
     frame_count, patches, width = frames_in.shape
@@ -211,13 +185,33 @@
     table = frame_table[0]
     group_frames = table.shape[0]
     columns = patches // shards
-    vocab = table_full.shape[0]
-    onehot = (timesteps[:, None] == jnp.arange(vocab, dtype=jnp.int32)[None, :]).astype(jnp.float32)
-    embed = jnp.dot(onehot, table_full.astype(jnp.float32), precision=HIGH)
+    space_qkv_full = lax.all_gather(space_qkv, "shard", axis=0, tiled=True)
+    space_out_full = lax.all_gather(space_out, "shard", axis=0, tiled=True)
+    time_qkv_full = lax.all_gather(time_qkv, "shard", axis=0, tiled=True)
+    time_out_full = lax.all_gather(time_out, "shard", axis=0, tiled=True)
+    up_full = lax.all_gather(up_weight, "shard", axis=0, tiled=True)
+    down_full = lax.all_gather(down_weight, "shard", axis=0, tiled=True)
+    embed = jnp.take(time_table, timesteps, axis=0).astype(jnp.float32)
     cond = jax.nn.silu(embed).astype(jnp.bfloat16)
-    modul = jnp.dot(cond, ada_full, preferred_element_type=jnp.float32) + ada_bias_full.astype(
-        jnp.float32
-    )
+    mod_local = jnp.dot(cond, ada_weight, preferred_element_type=jnp.float32)
+
+    def spread(local):
+        full = jnp.zeros((shards, local.shape[0]), jnp.float32)
+        return lax.dynamic_update_slice_in_dim(
+            full, local.astype(jnp.float32)[None], shard_at, 0
+        ).reshape(-1)
+
+    small = jnp.concatenate(
+        [
+            (mod_local + spread(ada_bias)[None]).reshape(-1),
+            spread(up_bias),
+            spread(down_bias),
+        ]
+    )
+    small = lax.psum(small, "shard")
+    modul = small[: clips * 9 * width].reshape(clips, 9 * width)
+    up_bias_full = small[clips * 9 * width : -width]
+    down_bias_full = small[-width:]
     slot_ids = shard_at * frame_count + jnp.arange(frame_count, dtype=jnp.int32)
     frame_ids = jnp.take(table, slot_ids)
     clip_of = frame_ids // frames
@@ -243,18 +237,25 @@
     def column_sums(values):
         return jnp.sum(values, axis=(1, 2))
 
+    def to_columns(rows):
+        parts = rows.astype(jnp.bfloat16).reshape(frame_count, shards, columns, width)
+        parts = jnp.swapaxes(parts, 0, 1)
+        moved = lax.all_to_all(parts, "shard", split_axis=0, concat_axis=0, tiled=True)
+        return moved.reshape(group_frames, columns, width)
+
+    def to_frames(cols):
+        parts = cols.astype(jnp.bfloat16).reshape(shards, frame_count, columns, width)
+        moved = lax.all_to_all(parts, "shard", split_axis=0, concat_axis=0, tiled=True)
+        moved = jnp.swapaxes(moved, 0, 1)
+        return moved.reshape(frame_count, patches, width).astype(jnp.float32)
+
     space_rows = frames_in.reshape(frame_count, patches, 1, width)
     after_space, space_kept = mixer_forward(
         space_rows, own_parts[0], own_parts[1], own_parts[2], space_qkv_full, space_out_full
     )
-    received = lax.all_to_all(
-        after_space.reshape(frame_count, patches, width),
-        "shard",
-        split_axis=1,
-        concat_axis=0,
-        tiled=True,
-    )
+    received = to_columns(after_space.reshape(frame_count, patches, width))
     columned = jnp.take(received, inverse, axis=0).reshape(clips, frames, columns, width)
+    columned = columned.astype(jnp.float32)
     after_time, time_kept = mixer_forward(
         columned, all_parts[3], all_parts[4], all_parts[5], time_qkv_full, time_out_full
     )
@@ -269,11 +270,12 @@
         down_bias_full,
     )
     leaving = jnp.take(result.reshape(group_frames, columns, width), table, axis=0)
-    frames_out = lax.all_to_all(leaving, "shard", split_axis=0, concat_axis=1, tiled=True)
+    frames_out = to_frames(leaving)
     row_weights = task_mask[clip_of, frame_of].astype(jnp.float32) * clip_weight[clip_of]
     weighted = cotangent * row_weights[:, None, None]
-    arriving = lax.all_to_all(weighted, "shard", split_axis=1, concat_axis=0, tiled=True)
+    arriving = to_columns(weighted)
     grad_result = jnp.take(arriving, inverse, axis=0).reshape(clips, frames, columns, width)
+    grad_result = grad_result.astype(jnp.float32)
     grad_after_time, mlp_mods, grad_up, grad_up_bias, grad_down, grad_down_bias = feed_backward(
         grad_result, all_parts[7], all_parts[8], up_full, down_full, mlp_kept, column_sums
     )
@@ -287,7 +289,7 @@
         column_sums,
     )
     going = jnp.take(grad_columned.reshape(group_frames, columns, width), table, axis=0)
-    grad_space = lax.all_to_all(going, "shard", split_axis=0, concat_axis=1, tiled=True)
+    grad_space = to_frames(going)
     grad_rows, space_mods, grad_space_qkv, grad_space_out = mixer_backward(
         grad_space.reshape(frame_count, patches, 1, width),
         own_parts[1],
@@ -298,62 +300,79 @@
         frame_sums,
     )
     mod_part = jnp.concatenate(space_mods + time_mods + mlp_mods, axis=1)
-    grad_modul = lax.psum(mod_part, "shard").astype(jnp.bfloat16)
-    rows_dev = width // shards
-    cond_share = lax.dynamic_slice_in_dim(cond, shard_at * rows_dev, rows_dev, 1)
-    grad_ada = jnp.einsum("cd,cj->dj", cond_share, grad_modul, preferred_element_type=jnp.float32)
+    small_grads = jnp.concatenate([mod_part.reshape(-1), grad_up_bias, grad_down_bias])
+    small_grads = lax.psum(small_grads, "shard")
+    mod_size = clips * 9 * width
+    grad_modul = small_grads[:mod_size].reshape(clips, 9 * width).astype(jnp.bfloat16)
+    up_dev = up_bias.shape[0]
+    down_dev = down_bias.shape[0]
     bias_dev = ada_bias.shape[0]
-    grad_ada_bias = lax.dynamic_slice_in_dim(
-        jnp.sum(grad_modul.astype(jnp.float32), axis=0), shard_at * bias_dev, bias_dev, 0
-    )
-    grad_cond = jnp.einsum("cj,dj->cd", grad_modul, ada_full, preferred_element_type=jnp.float32)
-    _, silu_back = jax.vjp(jax.nn.silu, embed)
-    grad_embed = silu_back(grad_cond)[0]
-    grad_table = jnp.dot(
-        onehot.T,
-        lax.dynamic_slice_in_dim(grad_embed, shard_at * rows_dev, rows_dev, 1),
-        precision=HIGH,
-    )
-    shares = (
-        lax.psum_scatter(grad_space_qkv, "shard", scatter_dimension=0, tiled=True),
-        lax.psum_scatter(grad_space_out, "shard", scatter_dimension=0, tiled=True),
-        lax.psum_scatter(grad_time_qkv, "shard", scatter_dimension=0, tiled=True),
-        lax.psum_scatter(grad_time_out, "shard", scatter_dimension=0, tiled=True),
-        lax.psum_scatter(grad_up, "shard", scatter_dimension=0, tiled=True),
-        lax.psum_scatter(grad_up_bias, "shard", scatter_dimension=0, tiled=True),
-        lax.psum_scatter(grad_down, "shard", scatter_dimension=0, tiled=True),
-        lax.psum_scatter(grad_down_bias, "shard", scatter_dimension=0, tiled=True),
-    )
-    totals = lax.psum(
-        (
-            grad_table,
-            grad_ada,
-            grad_ada_bias,
-            shares[0],
-            shares[1],
-            shares[2],
-            shares[3],
-            shares[4],
-            shares[5],
-            shares[6],
-            shares[7],
+    every_modul = lax.all_gather(grad_modul, "grp", axis=0, tiled=True)
+    bias_sums = lax.psum(
+        jnp.concatenate(
+            [
+                lax.dynamic_slice_in_dim(small_grads, mod_size + shard_at * up_dev, up_dev, 0),
+                lax.dynamic_slice_in_dim(
+                    small_grads, mod_size + shards * up_dev + shard_at * down_dev, down_dev, 0
+                ),
+            ]
         ),
         "grp",
     )
+    every_embed = lax.all_gather(embed.astype(jnp.bfloat16), "grp", axis=0, tiled=True)
+    every_embed = every_embed.astype(jnp.float32)
+    groups = lax.axis_size("grp")
+    step_slots = jnp.zeros((groups, clips), jnp.float32)
+    step_slots = lax.dynamic_update_slice_in_dim(
+        step_slots, timesteps.astype(jnp.float32)[None], lax.axis_index("grp"), 0
+    )
+    every_steps = lax.psum(step_slots.reshape(-1), "grp").astype(jnp.int32)
+    every_cond = jax.nn.silu(every_embed).astype(jnp.bfloat16)
+    grad_ada = jnp.einsum("cd,cj->dj", every_cond, every_modul, preferred_element_type=jnp.float32)
+    grad_ada_bias = lax.dynamic_slice_in_dim(
+        jnp.sum(every_modul.astype(jnp.float32), axis=0), shard_at * bias_dev, bias_dev, 0
+    )
+    grad_cond = jnp.einsum(
+        "cj,dj->cd", every_modul, ada_weight, preferred_element_type=jnp.float32
+    )
+    _, silu_back = jax.vjp(jax.nn.silu, every_embed)
+    grad_embed = silu_back(grad_cond)[0]
+    vocab = time_table.shape[0]
+    onehot = (jnp.arange(vocab, dtype=jnp.int32)[:, None] == every_steps[None, :]).astype(
+        jnp.float32
+    )
+    grad_table = jnp.dot(onehot, grad_embed, precision=HIGH)
+
+    def total(parts):
+        flat = [part.astype(jnp.bfloat16).reshape(shards, -1, width) for part in parts]
+        rows = [part.shape[1] for part in flat]
+        packed = jnp.concatenate(flat, axis=1)
+        share = lax.psum_scatter(packed, "shard", scatter_dimension=0, tiled=True)[0]
+        share = lax.psum(share, "grp").astype(jnp.float32)
+        out, at = [], 0
+        for part, count in zip(parts, rows):
+            piece = share[at : at + count].reshape(part.shape[0] // shards, part.shape[1])
+            out.append(piece)
+            at += count
+        return out
+
+    grad_up, grad_down = total([grad_up, grad_down])
+    grad_time_qkv, grad_time_out = total([grad_time_qkv, grad_time_out])
+    grad_space_qkv, grad_space_out = total([grad_space_qkv, grad_space_out])
     return (
         frames_out,
         grad_rows.reshape(frame_count, patches, width),
-        totals[0],
-        totals[1],
-        totals[2],
-        totals[3],
-        totals[4],
-        totals[5],
-        totals[6],
-        totals[7],
-        totals[8],
-        totals[9],
-        totals[10],
+        grad_table,
+        grad_ada,
+        grad_ada_bias,
+        grad_space_qkv,
+        grad_space_out,
+        grad_time_qkv,
+        grad_time_out,
+        grad_up,
+        bias_sums[:up_dev],
+        grad_down,
+        bias_sums[up_dev:],
     )
 
 

time: 1210 us -> 898 us (0.74)
  waiting for transfers between devices: 513 us -> 321 us
  blocking collectives: 194 us -> 37.5 us
  other arithmetic: 71.4 us -> 103 us
  matrix products: 242 us -> 219 us
  local copies, waits for them, and re-layouts: 152 us -> 173 us
    reduce_scatter x6 -> x3, waiting for transfers between devices: 196 us -> 109 us  [total(): lax.psum_scatter(packed, 'shard', scatter_dimension=0, tiled=True)[0]]
    psum x1 -> x3, waiting for transfers between devices: 216 us -> 142 us  [the longest x1 64 us: total(): share = lax.psum(share, 'grp').astype(jnp.float32)]
    unnamed x1 -> x0, blocking collectives: 59 us -> none
    all_to_all x1 -> x0, blocking collectives: 48 us -> none  [body(): lax.all_to_all(going, 'shard', split_axis=0, concat_axis=1, tiled=True)]
    reshape x0 -> x12, local copies, waits for them, and re-layouts: none -> 28.5 us  [the longest x3 22.2 us: total(): part.astype(jnp.bfloat16).reshape(shards, -1, width)]
    psum x2 -> x1, blocking collectives: 37.7 us -> 12.1 us  [body(): every_steps = lax.psum(step_slots.reshape(-1), 'grp').astype(jnp.int32)]
    all_gather x1 -> x2, blocking collectives: 49.5 us -> 25.4 us  [the longest x1 14.5 us: body(): every_modul = lax.all_gather(grad_modul, 'grp', axis=0, tiled=True)]
    all_gather x8 -> x6, waiting for transfers between devices: 58.4 us -> 35.4 us  [the longest x1 35.3 us: body(): space_qkv_full = lax.all_gather(space_qkv, 'shard', axis=0, tiled=True)]
  transfers between devices with their start and end apart: 18 -> 16, of which waited for: 7 -> 8; matrix products, arithmetic and copies ran while one was open for 25% -> 37% of each run, Pallas kernels for 0% -> 0%
where the time goes in v1:
time: 898 us; the launch traced here: 887 us
  waiting for transfers between devices  321 us (36%)
  matrix products  219 us (24%)
  local copies, waits for them, and re-layouts  173 us (19%)
  other arithmetic  103 us (11%)
  blocking collectives  37.5 us (4%)
  starting transfers between devices  16.8 us (2%)
  between operations  16 us (2%)
    reduce_scatter x3, waiting for transfers between devices, total(): lax.psum_scatter(packed, 'shard', scatter_dimension=0, tiled=True)[0]  109 us
    psum x1, waiting for transfers between devices, total(): share = lax.psum(share, 'grp').astype(jnp.float32)  64 us
    psum x1, waiting for transfers between devices, body(): small_grads = lax.psum(small_grads, 'shard')  42.6 us
    all_gather x1, waiting for transfers between devices, body(): space_qkv_full = lax.all_gather(space_qkv, 'shard', axis=0, tiled=True)  35.3 us
    psum x1, waiting for transfers between devices, body(): small = lax.psum(small, 'shard')  35.1 us
    convert_element_type x1, other arithmetic, feed_forward(): active = jax.nn.gelu(upward, approximate=False).astype(jnp.bfloat16)  29.8 us
    unnamed x176, local copies, waits for them, and re-layouts  23.9 us
    all_to_all x2, waiting for transfers between devices, to_columns(): lax.all_to_all(parts, 'shard', split_axis=0, concat_axis=0, tiled=True)  23 us
  transfers between devices with their start and end apart: 16, of which 8 were waited for; matrix products, arithmetic and copies ran while one was open for 37% of the time, Pallas kernels for 0%

profile of v1, /device:TPU:0, one launch (start us, length us, event | category | flops | bytes accessed | tf_op | source)
XLA Modules:
  0.0 886.7 jit_solution(1337077079453278443)
XLA Ops:
  24.4 5.2 all-to-all-start.2
  34.7 35.1 %all-reduce.6.cloned.1.call-done = f32[17664]{0:T(1024)} async-done(((f32[17664]{0:T(1024)}), f32[17664]{0:T(1024)}) %all-reduce.6.cloned.1.call-update) | async-done | bytes 70672 | tf_op jit(solution)/shard_map/psum | solution.py:211
  71.3 35.3 %all-gather.9.cloned.1.call-done = bf16[768,2304]{1,0:T(8,128)(2,1)} async-done(((bf16[96,2304]{1,0:T(8,128)(2,1)}), bf16[768,2304]{1,0:T(8,128)(2,1)}) %all-gather.9.cloned.1.call-update) | async-done | bytes 3538960 | tf_op jit(solution)/shard_map/all_gather | solution.py:188
  106.7 7.0 fusion.9
  119.1 3.8 multiply_reduce_fusion.1
  129.7 8.7 convolution_convert_fusion.3
  138.3 5.9 add_convert_fusion.3
  145.5 3.6 all-to-all-start
  156.5 23.0 %all-to-all-done = bf16[8,4,32,768]{3,2,1,0:T(8,128)(2,1)S(1)} async-done(((bf16[8,4,32,768]{3,2,1,0:T(8,128)(2,1)}), bf16[8,4,32,768]{3,2,1,0:T(8,128)(2,1)S(1)}, u32[]{:S(2)}, u32[]{:S(2)}) %all-to-all-start) | async-done | bytes 1572896 | tf_op jit(solution)/shard_map/all_to_all | solution.py:243
  182.7 5.2 select_convert_fusion.2
  190.2 7.0 convolution_convert_fusion
  199.5 6.0 reshape.639
  205.5 5.9 reshape.640
  211.4 5.9 reshape.638
  217.3 8.0 multiply_reduce_fusion.3
  229.8 3.9 convert_bitcast_fusion.2
  233.7 5.0 copy.166
  238.7 6.3 convert_element_type.258
  245.0 5.9 multiply_add_fusion.3
  255.5 11.7 %fusion.8 = (u16[2,32,3072]{2,1,0:T(8,128)(2,1)S(1)}, u16[2,32,3072]{2,1,0:T(8,128)(2,1)S(1)}, f32[2,16,32,3072]{3,2,1,0:T(8,128)S(1)}) fusion(f32[3072]{0:T(1024)S(1)} %slice.149, bf16[768,3072]{1,0:T(8,128)(2,1)} %all-gather.17.cloned.1.call-done, f32[2,16,32,768]{3,2,1,0:T(8,128)} %get-tuple-element.73, f32[2,768]{1,0:T(2,128)S(1)} %get-tuple-element.54, ...), kind=kOutput, calls=%fused_computation.51 | convolution fusion | flops 4879417344 | bytes 21266432 | tf_op jit(solution)/shard_map/blmd,df->blmf/dot_general | solution.py:120
  267.2 4.9 copy-done.30
  272.1 29.8 %multiply_convert_fusion.1 = (bf16[2,16,32,3072]{3,2,1,0:T(8,128)(2,1)}, f32[2,16,32,3072]{3,2,1,0:T(8,128)}) fusion(f32[2,16,32,3072]{3,2,1,0:T(8,128)S(1)} %get-tuple-element.75, f32[3072]{0:T(1024)S(1)} %slice.149, u16[2,32,3072]{2,1,0:T(8,128)(2,1)S(1)} %get-tuple-element.16, u16[2,32,3072]{2,1,0:T(8,128)(2,1)S(1)} %get-tuple-element.15), kind=kLoop, calls=%fused_computation.21 | loop fusion | flops 223346688 | bytes 32256000 | tf_op jit(solution)/shard_map/convert_element_type | solution.py:123
  301.9 20.0 %convert_reduce_fusion = (f32[3072]{0:T(1024)}, bf16[2,16,32,3072]{3,2,1,0:T(8,128)(2,1)}) fusion(f32[2,16,32,3072]{3,2,1,0:T(8,128)} %get-tuple-element.37, bf16[3072,768]{1,0:T(8,128)(2,1)} %all-gather.19.cloned.1.call-done, f32[2,16,32,768]{3,2,1,0:T(8,128)} %bitcast.240, f32[2,768]{1,0:T(2,128)S(1)} %get-tuple-element.55, ...), kind=kOutput, calls=%fused_computation.17 | convolution fusion | flops 4886885376 | bytes 39352320 | tf_op jit(solution)/shard_map/blmd,fd->blmf/dot_general | solution.py:138
  321.9 10.0 %multiply_reduce_fusion.5 = (f32[2,768]{1,0:T(2,128)}, f32[2,16,32]{2,1,0:T(8,128)S(1)}, f32[2,16,32]{2,1,0:T(8,128)S(1)}, f32[2,768]{1,0:T(2,128)}, f32[2,16,32,768]{3,2,1,0:T(8,128)S(1)}) fusion(f32[2,16,32,768]{3,2,1,0:T(8,128)S(1)} %copy-done.10, f32[2,16,32]{2,1,0:T(8,128)S(1)} %add_rsqrt_fusion, f32[2,16,32]{2,1,0:T(8,128)S(1)} %broadcast_multiply_fusion.4, ...), kind=kOutput, calls=%fused_computation.88 | convolution fusion | flops 4838910976 | bytes 17336320 | tf_op jit(solution)/shard_map/blmf,df->blmd/dot_general | solution.py:145
  338.4 6.2 reshape.645
  344.6 13.1 %multiply_reduce_fusion.2 = (f32[2,32,12,16]{3,2,1,0:T(8,128)S(1)}, f32[2,32,12,16,16]{3,4,2,1,0:T(8,128)}) fusion(f32[2,32,12,16,16]{3,4,2,1,0:T(8,128)} %copy-done.5, f32[2,32,12,16]{3,2,1,0:T(8,128)} %copy-done.28, bf16[2,16,32,12,64]{4,3,2,1,0:T(8,128)(2,1)} %reshape.638, bf16[2,16,32,12,64]{4,3,2,1,0:T(8,128)(2,1)} %reshape.645), kind=kOutput, calls=%fused_computation.47 | convolution fusion | flops 25939968 | bytes 4816896 | tf_op jit(solution)/shard_map/blmhe,bkmhe->bmhlk/dot_general | solution.py:60
  357.8 6.7 convert_bitcast_fusion.1
  366.8 4.0 fusion.26
  376.6 5.2 reshape.646
  381.9 5.0 copy.175
  386.9 6.1 reshape.647
  393.0 5.0 copy.177
  398.0 6.1 reshape.648
  408.4 5.8 bitcast_convert_fusion.2
  414.2 7.0 reshape.657
  421.3 4.5 pad_maximum_fusion.3
  425.8 10.9 %multiply_reduce_fusion.7 = (f32[2,768]{1,0:T(2,128)}, f32[2,16,32]{2,1,0:T(8,128)S(1)}, f32[2,16,32]{2,1,0:T(8,128)S(1)}, f32[2,768]{1,0:T(2,128)}, f32[2,16,32,768]{3,2,1,0:T(8,128)}) fusion(f32[2,16,32,768]{3,2,1,0:T(8,128)} %bitcast.258, f32[2,16,32]{2,1,0:T(8,128)S(1)} %bitcast.274, f32[2,16,32]{2,1,0:T(8,128)S(1)} %bitcast.270, ...), kind=kOutput, calls=%fused_computation.90 | convolution fusion | flops 3630951424 | bytes 14583808 | tf_op jit(solution)/shard_map/blme,de->blmd/dot_general | solution.py:108
  436.8 9.3 %multiply_add_fusion.2 = (bf16[2,16,32,768]{3,2,1,0:T(8,128)(2,1)}, f32[2,16,32,768]{3,2,1,0:T(8,128)}) fusion(f32[2,16,32,768]{3,2,1,0:T(8,128)S(1)} %copy-done.11, f32[768]{0:T(1024)S(1)} %copy-done.61, f32[2,768]{1,0:T(2,128)S(1)} %get-tuple-element.55, bf16[2,16,32,3072]{3,2,1,0:T(8,128)(2,1)S(1)} %bitcast.250, ...), kind=kOutput, calls=%fused_computation.103 | convolution fusion | flops 4834983936 | bytes 18883584 | tf_op jit(solution)/shard_map/blmf,fd->blmd/dot_general | solution.py:124
  446.1 3.5 gather_fusion.6
  449.6 4.4 multiply_add_fusion
  454.1 3.5 gather_fusion.8
  457.6 4.1 select_convert_fusion
  461.7 3.7 all-to-all-start.3
  465.5 10.6 %bitcast_convert_fusion.1 = bf16[768,3072]{1,0:T(8,128)(2,1)} fusion(bf16[2,16,32,3072]{3,2,1,0:T(8,128)(2,1)} %get-tuple-element.86, f32[2,16,32,768]{3,2,1,0:T(8,128)} %get-tuple-element.73, f32[2,768]{1,0:T(2,128)S(1)} %copy-done.66, f32[2,768]{1,0:T(2,128)S(1)} %get-tuple-element.53, f32[2,16,32]{2,1,0:T(8,128)S(1)} %add_rsqrt_fusion, ...), kind=kOutput, calls=%fused_computation.39 | convolution fusion | flops 4838129664 | bytes 14176256 | tf_op jit(solution)/shard_map/blmd,blmf->df/dot_general | solution.py:143
  476.0 8.5 reshape.660
  484.5 8.1 all-to-all-done.3
  503.3 8.1 convolution_convert_fusion.2
  514.1 6.9 multiply_reduce_fusion
  521.1 7.4 multiply_convert_fusion
  534.3 6.0 multiply_convert_fusion.6
  543.1 8.8 bitcast_convert_fusion.3
  551.9 6.7 reshape.654
  564.1 8.2 bitcast_convert_fusion
  572.4 6.9 pad_maximum_fusion
  579.3 3.6 all-to-all-start.1
  583.2 3.5 multiply_reduce_fusion.6
  591.5 7.0 multiply_reduce_fusion.8
  603.0 29.1 %reduce-scatter.4.cloned.1.call-done = bf16[1,384,768]{2,1,0:T(8,128)(2,1)} async-done(((bf16[8,384,768]{2,1,0:T(8,128)(2,1)}), bf16[1,384,768]{2,1,0:T(8,128)(2,1)}) %reduce-scatter.4.cloned.1.call-update) | async-done | bytes 589840 | tf_op jit(solution)/shard_map/reduce_scatter | solution.py:350
  632.1 80.2 %reduce-scatter.8.cloned.1.call-done = bf16[1,768,768]{2,1,0:T(8,128)(2,1)} async-done(((bf16[8,768,768]{2,1,0:T(8,128)(2,1)}), bf16[1,768,768]{2,1,0:T(8,128)(2,1)}) %reduce-scatter.8.cloned.1.call-update) | async-done | bytes 1179664 | tf_op jit(solution)/shard_map/reduce_scatter | solution.py:350
  712.5 10.9 %all-gather.1 = bf16[4,2,96]{2,1,0:T(2,128)(2,1)S(1)} all-gather(bf16[1,2,96]{2,1,0:T(2,128)(2,1)S(1)} %fusion.91), channel_id=1, replica_groups=mesh['grp'=4,'shard'=8] {'grp'}, dimensions={0}, use_global_device_ids=true | all-gather | bytes 1920 | tf_op jit(solution)/shard_map/all_gather | solution.py:322
  723.4 42.6 %all-reduce.8.cloned.1.call-done = f32[17664]{0:T(1024)} async-done(((f32[17664]{0:T(1024)}), f32[17664]{0:T(1024)}) %all-reduce.8.cloned.1.call-update) | async-done | bytes 70672 | tf_op jit(solution)/shard_map/psum | solution.py:304
  769.7 12.1 %all-reduce = (f32[8]{0:T(128)S(1)}, f32[480]{0:T(512)S(1)}) all-reduce(f32[8]{0:T(128)S(1)} %reshape.652, f32[480]{0:T(512)S(1)} %pad_maximum_fusion.8), channel_id=1, replica_groups=mesh['grp'=4,'shard'=8] {'grp'}, use_global_device_ids=true, to_apply=%region_20.23 | all-reduce | flops 488 | bytes 3904 | tf_op jit(solution)/shard_map/psum | solution.py:329
  783.1 14.5 %all-gather = bf16[4,2,6912]{2,1,0:T(2,128)(2,1)S(1)} all-gather(bf16[1,2,6912]{2,1,0:T(2,128)(2,1)S(1)} %reshape.753), channel_id=1, replica_groups=mesh['grp'=4,'shard'=8] {'grp'}, dimensions={0}, use_global_device_ids=true | all-gather | bytes 138240 | tf_op jit(solution)/shard_map/all_gather | solution.py:310
  802.2 64.0 %all-reduce.10.cloned.1.call-done = (bf16[384,768]{1,0:T(8,128)(2,1)}, bf16[384,768]{1,0:T(8,128)(2,1)}, bf16[768,768]{1,0:T(8,128)(2,1)}) async-done(((bf16[384,768]{1,0:T(8,128)(2,1)}, bf16[384,768]{1,0:T(8,128)(2,1)}, bf16[768,768]{1,0:T(8,128)(2,1)}), (bf16[384,768]{1,0:T(8,128)(2,1)}, bf16[384,768]{1,0:T(8,128)(2,1)}, bf16[768,768]{1,0:T(8,128)(2,1)})) %all-reduce.10.cloned.1.call-update) | async-done | bytes 2359312 | tf_op jit(solution)/shard_map/psum | solution.py:351
  (338 shorter events, 139.7 us)
Async XLA Ops:
  7.2 7.4 copy-start
  7.2 11.8 %copy-start.2 = (s32[1,32]{1,0:T(1,128)S(1)}, s32[1,32]{1,0:T(1,128)}, u32[]{:S(2)}) copy-start(s32[1,32]{1,0:T(1,128)} %param.37) | copy-start | bytes 388
  7.2 12.4 %copy-start.4 = (s32[2,16]{1,0:T(2,128)S(1)}, s32[2,16]{1,0:T(2,128)}, u32[]{:S(2)}) copy-start(s32[2,16]{1,0:T(2,128)} %param.35) | copy-start | bytes 388
  7.2 13.1 %copy-start.1 = (f32[2]{0:T(128)S(1)}, f32[2]{0:T(128)}, u32[]{:S(2)}) copy-start(f32[2]{0:T(128)} %param.36) | copy-start | bytes 28
  7.2 62.5 %all-reduce.6.cloned.1.call-start = ((), (), s32[]{:S(2)}) async-start(), calls=%async_computation.7 | async-start | bytes 147456 | tf_op jit(solution)/shard_map/psum | solution.py:211
  8.0 15.1 %copy-start.73 = (pred[2]{0:T(512)(128)(4,1)}, pred[2]{0:T(512)(128)(4,1)S(1)}, u32[]{:S(2)}) copy-start(pred[2]{0:T(512)(128)(4,1)S(1)} %compare_and_fusion.2) | copy-start | bytes 10
  14.6 8.6 copy-start.71
  15.7 91.0 %all-gather.9.cloned.1.call-start = ((), (), s32[]{:S(2)}) async-start(), calls=%async_computation.8 | async-start | bytes 3981312 | tf_op jit(solution)/shard_map/all_gather | solution.py:188
  16.5 121.9 %all-gather.11.cloned.1.call-start = ((), (), s32[]{:S(2)}) async-start(), calls=%async_computation.9 | async-start | bytes 1327104 | tf_op jit(solution)/shard_map/all_gather | solution.py:189
  17.2 173.0 %all-gather.13.cloned.1.call-start = ((), (), s32[]{:S(2)}) async-start(), calls=%async_computation.10 | async-start | bytes 3981312 | tf_op jit(solution)/shard_map/all_gather | solution.py:190
  17.8 227.3 %all-gather.15.cloned.1.call-start = ((), (), s32[]{:S(2)}) async-start(), calls=%async_computation.11 | async-start | bytes 1327104 | tf_op jit(solution)/shard_map/all_gather | solution.py:191
  18.4 237.1 %all-gather.17.cloned.1.call-start = ((), (), s32[]{:S(2)}) async-start(), calls=%async_computation.12 | async-start | bytes 5308416 | tf_op jit(solution)/shard_map/all_gather | solution.py:192
  24.4 121.1 %all-to-all-start.2 = ((bf16[8,4,32,768]{3,2,1,0:T(8,128)(2,1)}), bf16[8,4,32,768]{3,2,1,0:T(8,128)(2,1)}, u32[]{:S(2)}, u32[]{:S(2)}) async-start(bf16[8,4,32,768]{3,2,1,0:T(8,128)(2,1)} %copy.168), calls=%async_computation.2 | async-start | bytes 3145728 | tf_op jit(solution)/shard_map/all_to_all | solution.py:243
  32.3 81.4 %copy-start.56 = (f32[4,256]{1,0:T(4,128)}, f32[4,256]{1,0:T(4,128)S(1)}, u32[]{:S(2)}) copy-start(f32[4,256]{1,0:T(4,128)S(1)} %broadcast_multiply_fusion.8) | copy-start | bytes 12292
  34.7 79.1 %copy-start.59 = (f32[4,256]{1,0:T(4,128)}, f32[4,256]{1,0:T(4,128)S(1)}, u32[]{:S(2)}) copy-start(f32[4,256]{1,0:T(4,128)S(1)} %add_rsqrt_fusion.2) | copy-start | bytes 12292
  71.3 42.4 %copy-start.54 = (f32[4,768]{1,0:T(4,128)}, f32[4,768]{1,0:T(4,128)S(1)}, u32[]{:S(2)}) copy-start(f32[4,768]{1,0:T(4,128)S(1)} %get-tuple-element.52) | copy-start | bytes 36868
  71.3 42.4 %copy-start.62 = (f32[4,768]{1,0:T(4,128)}, f32[4,768]{1,0:T(4,128)S(1)}, u32[]{:S(2)}) copy-start(f32[4,768]{1,0:T(4,128)S(1)} %get-tuple-element.51) | copy-start | bytes 36868
  71.3 67.0 %copy-start.52 = (f32[4,768]{1,0:T(4,128)}, f32[4,768]{1,0:T(4,128)S(1)}, u32[]{:S(2)}) copy-start(f32[4,768]{1,0:T(4,128)S(1)} %get-tuple-element.50) | copy-start | bytes 36868
  119.0 3.8 copy-start.21
  122.9 4.5 copy-start.3
  127.4 10.9 %copy-start.43 = (f32[4,12,256]{2,1,0:T(8,128)}, f32[4,12,256]{2,1,0:T(8,128)S(1)}, u32[]{:S(2)}) copy-start(f32[4,12,256]{2,1,0:T(8,128)S(1)} %log_add_fusion.1) | copy-start | bytes 147460
  129.6 8.7 copy-start.25
  145.5 34.0 %all-to-all-start = ((bf16[8,4,32,768]{3,2,1,0:T(8,128)(2,1)}), bf16[8,4,32,768]{3,2,1,0:T(8,128)(2,1)S(1)}, u32[]{:S(2)}, u32[]{:S(2)}) async-start(bf16[8,4,32,768]{3,2,1,0:T(8,128)(2,1)} %bitcast.226), calls=%async_computation | async-start | bytes 3145728 | tf_op jit(solution)/shard_map/all_to_all | solution.py:243
  149.1 152.8 %all-gather.19.cloned.1.call-start = ((), (), s32[]{:S(2)}) async-start(), calls=%async_computation.13 | async-start | bytes 5308416 | tf_op jit(solution)/shard_map/all_gather | solution.py:193
  149.9 453.2 %reduce-scatter.6.cloned.1.call-start = ((), (), s32[]{:S(2)}) async-start(), calls=%async_computation.16 | async-start | bytes 5308416 | tf_op jit(solution)/shard_map/reduce_scatter | solution.py:350
  153.3 102.2 %copy-start.65 = (f32[2,768]{1,0:T(2,128)}, f32[2,768]{1,0:T(2,128)S(1)}, u32[]{:S(2)}) copy-start(f32[2,768]{1,0:T(2,128)S(1)} %get-tuple-element.54) | copy-start | bytes 18436
  182.7 62.4 %copy-start.6 = (bf16[32,32,768]{2,1,0:T(8,128)(2,1)}, bf16[32,32,768]{2,1,0:T(8,128)(2,1)S(1)}, u32[]{:S(2)}) copy-start(bf16[32,32,768]{2,1,0:T(8,128)(2,1)S(1)} %gather_fusion.5) | copy-start | bytes 4718596
  182.7 5.2 copy-start.19
  225.4 4.5 copy-start.15
  229.8 3.9 copy-start.28
  267.2 4.9 copy-start.30
  301.9 20.0 %copy-start.10 = (f32[2,16,32,768]{3,2,1,0:T(8,128)S(1)}, f32[2,16,32,768]{3,2,1,0:T(8,128)}, u32[]{:S(2)}) copy-start(f32[2,16,32,768]{3,2,1,0:T(8,128)} %get-tuple-element.73) | copy-start | bytes 9437188
  321.9 10.0 %copy-start.20 = (bf16[32,32,768]{2,1,0:T(8,128)(2,1)S(1)}, bf16[32,32,768]{2,1,0:T(8,128)(2,1)}, u32[]{:S(2)}) copy-start(bf16[32,32,768]{2,1,0:T(8,128)(2,1)} %gather_fusion.7) | copy-start | bytes 4718596
  338.4 19.3 %slice-start = ((s8[6291456]{0:T(1024)(128)(4,1)}), s8[2097152]{0:T(1024)(128)(4,1)S(1)}, s32[]{:S(2)}) async-start(s8[6291456]{0:T(1024)(128)(4,1)} %bitcast.230), calls=%async_computation.19 | async-start | bytes 4194304
  344.6 13.1 %slice-start.1 = ((s8[6291456]{0:T(1024)(128)(4,1)}), s8[4194304]{0:T(1024)(128)(4,1)S(1)}, s32[]{:S(2)}) async-start(s8[6291456]{0:T(1024)(128)(4,1)} %bitcast.230), calls=%async_computation.20 | async-start | bytes 8388608
  344.6 13.1 %copy-start.29 = (f32[2,32,12,16]{3,2,1,0:T(8,128)S(1)}, f32[2,32,12,16]{3,2,1,0:T(8,128)}, u32[]{:S(2)}) copy-start(f32[2,32,12,16]{3,2,1,0:T(8,128)} %copy-done.28) | copy-start | bytes 147460
  357.8 6.8 copy-start.18
  366.8 4.0 copy-start.17
  414.2 7.1 copy-start.48
  425.8 11.0 %slice-start.2 = ((s8[6291456]{0:T(1024)(128)(4,1)}), s8[2097152]{0:T(1024)(128)(4,1)S(1)}, s32[]{:S(2)}) async-start(s8[6291456]{0:T(1024)(128)(4,1)} %bitcast.249), calls=%async_computation.21 | async-start | bytes 4194304
  425.8 11.0 %copy-start.11 = (f32[2,16,32,768]{3,2,1,0:T(8,128)S(1)}, f32[2,16,32,768]{3,2,1,0:T(8,128)}, u32[]{:S(2)}) copy-start(f32[2,16,32,768]{3,2,1,0:T(8,128)} %get-tuple-element.73) | copy-start | bytes 9437188
  425.8 11.0 %slice-start.3 = ((s8[6291456]{0:T(1024)(128)(4,1)}), s8[4194304]{0:T(1024)(128)(4,1)S(1)}, s32[]{:S(2)}) async-start(s8[6291456]{0:T(1024)(128)(4,1)} %bitcast.249), calls=%async_computation.22 | async-start | bytes 8388608
  425.8 11.0 %copy-start.61 = (f32[768]{0:T(1024)S(1)}, f32[768]{0:T(1024)}, u32[]{:S(2)}) copy-start(f32[768]{0:T(1024)} %slice.150) | copy-start | bytes 9220
  461.7 3.8 copy-start.66
  461.7 30.9 %all-to-all-start.3 = ((bf16[8,4,32,768]{3,2,1,0:T(8,128)(2,1)}), bf16[8,4,32,768]{3,2,1,0:T(8,128)(2,1)S(1)}, u32[]{:S(2)}, u32[]{:S(2)}) async-start(bf16[8,4,32,768]{3,2,1,0:T(8,128)(2,1)} %bitcast.248), calls=%async_computation.3 | async-start | bytes 3145728 | tf_op jit(solution)/shard_map/all_to_all | solution.py:248
  465.4 166.7 %reduce-scatter.4.cloned.1.call-start = ((), (), s32[]{:S(2)}) async-start(), calls=%async_computation.15 | async-start | bytes 5308416 | tf_op jit(solution)/shard_map/reduce_scatter | solution.py:350
  476.0 16.6 %copy-start.53 = (f32[4,768]{1,0:T(4,128)S(1)}, f32[4,768]{1,0:T(4,128)}, u32[]{:S(2)}) copy-start(f32[4,768]{1,0:T(4,128)} %copy-done.52) | copy-start | bytes 36868
  521.1 7.4 copy-start.23
  551.9 6.7 copy-start.38
  564.1 148.2 %reduce-scatter.8.cloned.1.call-start = ((), (), s32[]{:S(2)}) async-start(), calls=%async_computation.17 | async-start | bytes 10616832 | tf_op jit(solution)/shard_map/reduce_scatter | solution.py:350
  579.3 188.3 %all-to-all-start.1 = ((bf16[8,4,32,768]{3,2,1,0:T(8,128)(2,1)}), bf16[8,4,32,768]{3,2,1,0:T(8,128)(2,1)S(1)}, u32[]{:S(2)}, u32[]{:S(2)}) async-start(bf16[8,4,32,768]{3,2,1,0:T(8,128)(2,1)} %bitcast.32), calls=%async_computation.1 | async-start | bytes 3145728 | tf_op jit(solution)/shard_map/all_to_all | solution.py:248
  582.9 183.2 %all-reduce.8.cloned.1.call-start = ((), (), s32[]{:S(2)}) async-start(), calls=%async_computation.14 | async-start | bytes 147456 | tf_op jit(solution)/shard_map/psum | solution.py:304
  583.2 4.5 copy-start.32
  583.2 5.5 copy-start.40
  591.5 7.1 copy-start.77
  591.5 7.6 copy-start.14
  591.5 7.6 copy-start.31
  599.2 113.1 %copy-start.76 = (f32[1,2]{1,0:T(1,128)S(1)}, f32[1,2]{1,0:T(1,128)}, u32[]{:S(2)}) copy-start(f32[1,2]{1,0:T(1,128)} %get-tuple-element.59) | copy-start | bytes 28
  599.2 113.2 %copy-start.72 = (bf16[2,96]{1,0:T(2,128)(2,1)S(1)}, bf16[2,96]{1,0:T(2,128)(2,1)}, u32[]{:S(2)}) copy-start(bf16[2,96]{1,0:T(2,128)(2,1)} %copy-done.71) | copy-start | bytes 1156
  599.2 113.2 %copy-start.74 = (pred[2]{0:T(512)(128)(4,1)S(1)}, pred[2]{0:T(512)(128)(4,1)}, u32[]{:S(2)}) copy-start(pred[2]{0:T(512)(128)(4,1)} %copy-done.73) | copy-start | bytes 10
  603.0 263.3 %all-reduce.10.cloned.1.call-start = ((), (), s32[]{:S(2)}) async-start(), calls=%async_computation.18 | async-start | bytes 4718592 | tf_op jit(solution)/shard_map/psum | solution.py:351
  781.7 87.3 %copy-start.78 = (f32[480]{0:T(512)}, f32[480]{0:T(512)S(1)}, u32[]{:S(2)}) copy-start(f32[480]{0:T(512)S(1)} %get-tuple-element.32) | copy-start | bytes 5764
  866.3 4.5 copy-start.42
  869.1 6.2 copy-start.39
  (35 other events, 89.2 us)
Sparse Core Ops, SparseCore 0:
  15.8 53.8 all-reduce.5
  71.6 35.0 all-gather.8
  108.6 23.9 all-gather.10
  134.3 43.2 all-gather.12
  179.3 26.4 all-gather.14
  207.6 38.7 all-gather.16
  248.3 38.7 all-gather.18
  425.9 62.7 reduce-scatter.5
  564.2 67.8 reduce-scatter.3
  635.4 76.8 reduce-scatter.7
  715.9 50.0 all-reduce.7
  768.5 97.7 all-reduce.9

commit v2 on v1

v2 whole, which is shorter than its diff:
```python
from functools import partial

import jax
import jax.numpy as jnp
from jax import lax
from jax.experimental import pallas as pl
from jax.experimental.pallas import tpu as pltpu
from jax.sharding import PartitionSpec as P

HEADS = 12
HEAD_DIM = 64
PAIR = 2 * HEAD_DIM
ROWS = 256
NEAR = 16
HIGH = lax.Precision.HIGHEST
EPSILON = 1e-06
BF = jnp.bfloat16
F32 = jnp.float32
VMEM_LIMIT = 60 * 1024 * 1024


def layer_norm(values):
    center = values - jnp.mean(values, axis=-1, keepdims=True)
    spread = jnp.mean(center * center, axis=-1, keepdims=True)
    inverse = lax.rsqrt(spread + EPSILON)
    return (center * inverse, inverse)


def norm_back(grad_normed, normed, inverse):
    first = jnp.mean(grad_normed, axis=-1, keepdims=True)
    second = jnp.mean(grad_normed * normed, axis=-1, keepdims=True)
    return inverse * (grad_normed - first - normed * second)


def mul(left, right):
    return jnp.dot(left, right, preferred_element_type=F32)


def mul_rt(left, right):
    return lax.dot_general(left, right, (((1,), (1,)), ((), ())), preferred_element_type=F32)


def mul_lt(left, right):
    return lax.dot_general(left, right, (((0,), (0,)), ((), ())), preferred_element_type=F32)


def half_masks(value):
    lane = lax.broadcasted_iota(jnp.int32, (1, PAIR), 1)
    low = jnp.where(lane < HEAD_DIM, value, 0.0)
    return (low.astype(BF), (value - low).astype(BF))


def same_patch():
    rows = lax.broadcasted_iota(jnp.int32, (ROWS, ROWS), 0)
    cols = lax.broadcasted_iota(jnp.int32, (ROWS, ROWS), 1)
    return jnp.bitwise_and(rows, NEAR - 1) == jnp.bitwise_and(cols, NEAR - 1)


def mixer_forward(resid, mods, at, width, weight, out_weight, keep, near):
    packed_ref, mixed_ref, lse_ref, branch_ref = keep
    shift, scale, gate = mods[at : at + 1], mods[at + 1 : at + 2], mods[at + 2 : at + 3]
    normed, _ = layer_norm(resid)
    entry = (normed * (1.0 + scale) + shift).astype(BF)
    for part in range(3):
        packed_ref[0, :, part * width : (part + 1) * width] = mul(
            entry, weight[:, part * width : (part + 1) * width]
        ).astype(BF)
    same = same_patch() if near else None
    lane = lax.broadcasted_iota(jnp.int32, (ROWS, PAIR), 1)
    scaled = half_masks(HEAD_DIM ** (-0.5))
    for pair in range(HEADS // 2):
        at_q = pair * PAIR
        query = packed_ref[0, :, at_q : at_q + PAIR]
        keys = packed_ref[0, :, width + at_q : width + at_q + PAIR]
        values = packed_ref[0, :, 2 * width + at_q : 2 * width + at_q + PAIR]
        halves = []
        for half in range(2):
            scores = mul_rt(keys, query * scaled[half])
            if near:
                scores = jnp.where(same, scores, -jnp.inf)
            highest = jnp.max(scores, axis=0, keepdims=True)
            weights = jnp.exp(scores - highest)
            total = jnp.sum(weights, axis=0, keepdims=True)
            head = 2 * pair + half
            lse_ref[0, head : head + 1, :] = highest + jnp.log(total)
            probs = (weights * (1.0 / total)).astype(BF)
            halves.append(mul_lt(probs, values))
        mixed_ref[0, :, at_q : at_q + PAIR] = jnp.where(
            lane < HEAD_DIM, halves[0], halves[1]
        ).astype(BF)
    branch = mul(mixed_ref[0], out_weight[...])
    branch_ref[0] = branch.astype(BF)
    return resid + gate * branch


def mixer_backward(grad_out, resid, mods, at, width, weight, out_weight, kept, work, near):
    packed_ref, mixed_ref, lse_ref, branch_ref = kept
    entry_ref, packed_grad_ref, branch_grad_ref = work
    shift, scale, gate = mods[at : at + 1], mods[at + 1 : at + 2], mods[at + 2 : at + 3]
    grad_gate = jnp.sum(grad_out * branch_ref[0].astype(F32), axis=0, keepdims=True)
    grad_branch = (gate * grad_out).astype(BF)
    branch_grad_ref[...] = grad_branch
    grad_mixed = mul_rt(grad_branch, out_weight[...]).astype(BF)
    same = same_patch() if near else None
    lane = lax.broadcasted_iota(jnp.int32, (ROWS, PAIR), 1)
    scaled = half_masks(HEAD_DIM ** (-0.5))
    ones = half_masks(1.0)
    for pair in range(HEADS // 2):
        at_q = pair * PAIR
        query = packed_ref[0, :, at_q : at_q + PAIR]
        keys = packed_ref[0, :, width + at_q : width + at_q + PAIR]
        values = packed_ref[0, :, 2 * width + at_q : 2 * width + at_q + PAIR]
        grads = grad_mixed[:, at_q : at_q + PAIR]
        grad_query = []
        grad_keys = None
        grad_values = None
        for half in range(2):
            head = 2 * pair + half
            own_query = query * scaled[half]
            own_grads = grads * ones[half]
            scores = mul_rt(keys, own_query)
            if near:
                scores = jnp.where(same, scores, -jnp.inf)
            probs = jnp.exp(scores - lse_ref[0, head : head + 1, :])
            grad_probs = mul_rt(values, own_grads)
            inner = jnp.sum(probs * grad_probs, axis=0, keepdims=True)
            grad_scores = (probs * (grad_probs - inner)).astype(BF)
            part_values = mul(probs.astype(BF), own_grads)
            part_keys = mul(grad_scores, own_query)
            grad_query.append(mul_lt(grad_scores, keys))
            grad_keys = part_keys if half == 0 else grad_keys + part_keys
            grad_values = part_values if half == 0 else grad_values + part_values
        joined = jnp.where(lane < HEAD_DIM, grad_query[0], grad_query[1])
        packed_grad_ref[:, at_q : at_q + PAIR] = (joined * HEAD_DIM ** (-0.5)).astype(BF)
        packed_grad_ref[:, width + at_q : width + at_q + PAIR] = grad_keys.astype(BF)
        packed_grad_ref[:, 2 * width + at_q : 2 * width + at_q + PAIR] = (
            grad_values.astype(BF)
        )
    grad_entry = mul_rt(packed_grad_ref[...], weight[...])
    normed, inverse = layer_norm(resid)
    entry_ref[...] = (normed * (1.0 + scale) + shift).astype(BF)
    grad_shift = jnp.sum(grad_entry, axis=0, keepdims=True)
    grad_scale = jnp.sum(grad_entry * normed, axis=0, keepdims=True)
    grad_in = grad_out + norm_back(grad_entry * (1.0 + scale), normed, inverse)
    return grad_in, (grad_shift, grad_scale, grad_gate)


def fetch_weights(packed, places, sem):
    copies = []
    for shard in range(packed.shape[0]):
        for block in range(packed.shape[1]):
            copies.append(
                pltpu.make_async_copy(packed.at[shard, block], places(shard, block), sem)
            )
    for copy in copies:
        copy.start()
    for copy in copies:
        copy.wait()


def fetch_pieces(me, pieces, weight, out_weight, sem):
    _, rows, width = pieces[0].shape
    copies = []
    for distance, piece in enumerate(pieces):
        first = pl.multiple_of(jnp.bitwise_xor(me, distance) * rows, rows)
        for block in range(3):
            target = weight.at[pl.ds(first, rows), block * width : (block + 1) * width]
            copies.append(pltpu.make_async_copy(piece.at[block], target, sem))
        copies.append(
            pltpu.make_async_copy(piece.at[3], out_weight.at[pl.ds(first, rows), :], sem)
        )
    for copy in copies:
        copy.start()
    for copy in copies:
        copy.wait()


def mixer_places(weight, out_weight, rows, width):
    def places(shard, block):
        if block < 3:
            return weight.at[
                shard * rows : (shard + 1) * rows, block * width : (block + 1) * width
            ]
        return out_weight.at[shard * rows : (shard + 1) * rows, :]

    return places


def mixer_weight_grads(entry, packed_grad, mixed, branch_grad, out, shards, width):
    rows = width // shards
    entry_t = entry[...].T
    for block in range(3):
        grad = mul(entry_t, packed_grad[:, block * width : (block + 1) * width]).astype(BF)
        out[:, block] = grad.reshape(shards, rows, width)
    grad = mul(mixed.T, branch_grad[...]).astype(BF)
    out[:, 3] = grad.reshape(shards, rows, width)


def add_mods(mods_out, clip, grads):
    for at, grad in enumerate(grads):
        mods_out[clip, at : at + 1, :] += grad


def space_forward_kernel(shards, where, frames_ref, mods_ref, *refs):
    pieces = refs[:shards]
    after_ref, packed_ref, mixed_ref, lse_ref, branch_ref = refs[shards : shards + 5]
    weight, out_weight, sem = refs[shards + 5 :]
    step = pl.program_id(0)
    width = frames_ref.shape[-1]

    @pl.when(step == 0)
    def _():
        fetch_pieces(where[pl.num_programs(0)], pieces, weight, out_weight, sem)

    mods = mods_ref[where[step]]
    after = mixer_forward(
        frames_ref[0], mods, 0, width, weight, out_weight,
        (packed_ref, mixed_ref, lse_ref, branch_ref), False,
    )
    after_ref[...] = after.astype(BF).reshape(after_ref.shape)


def space_backward_kernel(
    shards, where, grad_ref, frames_ref, mods_ref, packed_ref, mixed_ref, lse_ref, branch_ref, *refs
):
    pieces = refs[:shards]
    rows_out, mods_out, grads_out = refs[shards : shards + 3]
    weight, out_weight, entry, packed_grad, mixed, branch_grad, sem = refs[shards + 3 :]
    step = pl.program_id(0)
    width = frames_ref.shape[-1]

    @pl.when(step == 0)
    def _():
        fetch_pieces(where[pl.num_programs(0)], pieces, weight, out_weight, sem)
        mods_out[...] = jnp.zeros_like(mods_out)

    clip = where[step]
    own = pl.ds(pl.multiple_of(step * ROWS, ROWS), ROWS)
    grad_out = grad_ref[...].reshape(ROWS, width).astype(F32)
    grad_in, grads = mixer_backward(
        grad_out, frames_ref[0], mods_ref[clip], 0, width, weight, out_weight,
        (packed_ref, mixed_ref, lse_ref, branch_ref),
        (entry.at[own], packed_grad.at[own], branch_grad.at[own]), False,
    )
    rows_out[0] = grad_in
    mixed[own] = mixed_ref[0]
    add_mods(mods_out, clip, grads)

    @pl.when(step == pl.num_programs(0) - 1)
    def _():
        mixer_weight_grads(entry, packed_grad, mixed[...], branch_grad, grads_out, shards, width)


def load_near(source, inverse, resid, clip, first, frames):
    for frame in range(frames):
        values = source[inverse[clip * frames + frame], pl.ds(first, NEAR), :]
        resid[frame * NEAR : (frame + 1) * NEAR, :] = values.astype(F32)


def store_near(target, inverse, values, clip, first, frames):
    for frame in range(frames):
        own = values[frame * NEAR : (frame + 1) * NEAR]
        target[inverse[clip * frames + frame], pl.ds(first, NEAR), :] = own.astype(BF)


def block_place(columns):
    step = pl.program_id(0)
    per_clip = columns // NEAR
    clip = step // per_clip
    first = pl.multiple_of((step - clip * per_clip) * NEAR, NEAR)
    return step, clip, first


def time_forward_kernel(
    frames, inverse, source, mods_ref, packed_w, resid_ref, after_ref, packed_ref, mixed_ref,
    lse_ref, branch_ref, weight, out_weight, resid, sem,
):
    step, clip, first = block_place(source.shape[1])
    shards, _, rows, width = packed_w.shape

    @pl.when(step == 0)
    def _():
        fetch_weights(packed_w, mixer_places(weight, out_weight, rows, width), sem)

    load_near(source, inverse, resid, clip, first, frames)
    resid_ref[0] = resid[...].astype(BF)
    after_ref[0] = mixer_forward(
        resid[...], mods_ref[clip], 3, width, weight, out_weight,
        (packed_ref, mixed_ref, lse_ref, branch_ref), True,
    )


def time_backward_kernel(
    frames, inverse, grad_ref, resid_ref, mods_ref, packed_ref, mixed_ref, lse_ref, branch_ref,
    packed_w, going, mods_out, grads_out, weight, out_weight, entry, packed_grad, mixed,
    branch_grad, sem,
):
    step, clip, first = block_place(going.shape[1])
    shards, _, rows, width = packed_w.shape

    @pl.when(step == 0)
    def _():
        fetch_weights(packed_w, mixer_places(weight, out_weight, rows, width), sem)
        mods_out[...] = jnp.zeros_like(mods_out)

    own = pl.ds(pl.multiple_of(step * ROWS, ROWS), ROWS)
    grad_in, grads = mixer_backward(
        grad_ref[0], resid_ref[0].astype(F32), mods_ref[clip], 3, width, weight, out_weight,
        (packed_ref, mixed_ref, lse_ref, branch_ref),
        (entry.at[own], packed_grad.at[own], branch_grad.at[own]), True,
    )
    store_near(going, inverse, grad_in, clip, first, frames)
    mixed[own] = mixed_ref[0]
    add_mods(mods_out, clip, grads)

    @pl.when(step == pl.num_programs(0) - 1)
    def _():
        mixer_weight_grads(entry, packed_grad, mixed[...], branch_grad, grads_out, shards, width)


def feed_kernel(
    frames, inverse, after_ref, source, mods_ref, up_bias, down_bias, packed_w, result, grad_ref,
    mods_out, up_bias_out, down_bias_out, grads_out, up, down, entry, active, grad_up_in,
    grad_down_in, grad_result, staged, sem, out_sem,
):
    step, clip, first = block_place(source.shape[1])
    shards, _, rows, width = packed_w.shape
    hidden = up.shape[1]
    chunks = hidden // width

    @pl.when(step == 0)
    def _():
        def places(shard, block):
            if block < chunks:
                return up.at[
                    shard * rows : (shard + 1) * rows, block * width : (block + 1) * width
                ]
            start = (shard * chunks + block - chunks) * rows
            return down.at[start : start + rows, :]

        fetch_weights(packed_w, places, sem)
        mods_out[...] = jnp.zeros_like(mods_out)
        up_bias_out[...] = jnp.zeros_like(up_bias_out)
        down_bias_out[...] = jnp.zeros_like(down_bias_out)

    own = pl.ds(pl.multiple_of(step * ROWS, ROWS), ROWS)
    mods = mods_ref[clip]
    shift, scale, gate = mods[6:7], mods[7:8], mods[8:9]
    load_near(source, inverse, grad_result, clip, first, frames)
    grad_out = grad_result[...]
    down_in = (gate * grad_out).astype(BF)
    grad_down_in[own] = down_in
    down_bias_out[...] += jnp.sum(down_in.astype(F32), axis=0, keepdims=True)
    resid = after_ref[0]
    normed, inverse_std = layer_norm(resid)
    entered = (normed * (1.0 + scale) + shift).astype(BF)
    entry[own] = entered
    downward = jnp.broadcast_to(down_bias[...], (ROWS, width))
    grad_entry = jnp.zeros((ROWS, width), F32)
    for chunk in range(chunks):
        cols = slice(chunk * width, (chunk + 1) * width)
        upward = mul(entered, up[:, cols]) + up_bias[:, cols]
        below = 0.5 + 0.5 * lax.erf(upward * 2.0 ** (-0.5))
        density = jnp.exp(-0.5 * upward * upward) * 0.3989422804014327
        acted = (upward * below).astype(BF)
        active[own, cols] = acted
        downward = downward + mul(acted, down[cols, :])
        grad_active = mul_rt(down_in, down[cols, :])
        up_in = (grad_active * (below + upward * density)).astype(BF)
        grad_up_in[own, cols] = up_in
        up_bias_out[:, cols] += jnp.sum(up_in.astype(F32), axis=0, keepdims=True)
        grad_entry = grad_entry + mul_rt(up_in, up[:, cols])
    store_near(result, inverse, resid + gate * downward, clip, first, frames)
    grad_gate = jnp.sum(grad_out * downward, axis=0, keepdims=True)
    grad_shift = jnp.sum(grad_entry, axis=0, keepdims=True)
    grad_scale = jnp.sum(grad_entry * normed, axis=0, keepdims=True)
    add_mods(mods_out, clip, (grad_shift, grad_scale, grad_gate))
    grad_ref[0] = grad_out + norm_back(grad_entry * (1.0 + scale), normed, inverse_std)

    @pl.when(step == pl.num_programs(0) - 1)
    def _():
        entry_t = entry[...].T
        copies = []
        for chunk in range(chunks):
            grad = mul(entry_t, grad_up_in[:, chunk * width : (chunk + 1) * width]).astype(BF)
            staged[chunk] = grad.reshape(shards, rows, width)
            copies.append(
                pltpu.make_async_copy(staged.at[chunk], grads_out.at[:, chunk], out_sem.at[chunk])
            )
            copies[-1].start()
        group = shards // chunks
        for chunk in range(chunks):
            grad = mul_lt(active[:, chunk * width : (chunk + 1) * width], grad_down_in[...])
            slot = chunks + chunk
            staged[slot] = grad.astype(BF).reshape(shards, rows, width)
            copies.append(
                pltpu.make_async_copy(
                    staged.at[slot].reshape(group, chunks, rows, width),
                    grads_out.at[chunk * group : (chunk + 1) * group, chunks:],
                    out_sem.at[slot],
                )
            )
            copies[-1].start()
        for copy in copies:
            copy.wait()


def whole(shape):
    return pl.BlockSpec(shape, lambda *_: (0,) * len(shape))


def per_step(shape):
    return pl.BlockSpec((1,) + tuple(shape[1:]), lambda step, *_: (step,) + (0,) * (len(shape) - 1))


ANY = pl.BlockSpec(memory_space=pl.ANY)


def run(kernel, steps, table, ins, in_specs, outs, out_specs, scratch, flops, name):
    size = lambda shaped: shaped.size * shaped.dtype.itemsize
    moved = sum(size(a) for a in ins) + sum(size(a) for a in outs)
    return pl.pallas_call(
        kernel,
        grid_spec=pltpu.PrefetchScalarGridSpec(
            num_scalar_prefetch=1, grid=(steps,), in_specs=in_specs, out_specs=out_specs,
            scratch_shapes=scratch,
        ),
        out_shape=outs,
        compiler_params=pltpu.CompilerParams(
            dimension_semantics=("arbitrary",), vmem_limit_bytes=VMEM_LIMIT
        ),
        cost_estimate=pl.CostEstimate(flops=flops, bytes_accessed=moved, transcendentals=0),
        name=name,
    )(table, *ins)


def body(
    frames_in,
    cotangent,
    time_table,
    ada_weight,
    ada_bias,
    space_qkv,
    space_out,
    time_qkv,
    time_out,
    up_weight,
    up_bias,
    down_weight,
    down_bias,
    timesteps,
    task_mask,
    clip_weight,
    frame_table,
):
    shards = lax.axis_size("shard")
    shard_at = lax.axis_index("shard")
    frame_count, patches, width = frames_in.shape
    clips = timesteps.shape[0]
    frames = task_mask.shape[1]
    table = frame_table[0]
    group_frames = table.shape[0]
    columns = patches // shards
    rows = width // shards
    hidden = up_weight.shape[1]
    chunks = hidden // width
    tokens = group_frames * columns
    steps = tokens // ROWS
    shaped = jax.ShapeDtypeStruct

    def column_blocks(weight):
        return jnp.swapaxes(weight.reshape(rows, -1, width), 0, 1)

    def swap(values, distance):
        pairs = [(at, at ^ distance) for at in range(shards)]
        return lax.ppermute(values, "shard", pairs)

    def gather(packed):
        return lax.all_gather(packed[None], "shard", axis=0, tiled=True)

    def shard_sum(values):
        distance = 1
        while distance < shards:
            values = values + swap(values, distance)
            distance *= 2
        return values

    own_space = jnp.concatenate([column_blocks(space_qkv), space_out[None]], axis=0)
    even = [own_space] + [swap(own_space, distance) for distance in range(2, shards, 2)]

    embed = jnp.take(time_table, timesteps, axis=0).astype(F32)
    cond = jax.nn.silu(embed).astype(BF)
    mod_local = jnp.dot(cond, ada_weight, preferred_element_type=F32)

    def spread(local):
        full = jnp.zeros((shards, local.shape[0]), F32)
        return lax.dynamic_update_slice_in_dim(
            full, local.astype(F32)[None], shard_at, 0
        ).reshape(-1)

    small = jnp.concatenate(
        [
            (mod_local + spread(ada_bias)[None]).reshape(-1),
            spread(up_bias),
            spread(down_bias),
        ]
    )
    small = lax.all_gather(small.reshape(1, -1, 128), "shard", axis=0, tiled=True)
    small, even[1] = lax.optimization_barrier((small, even[1]))
    small = jnp.sum(small, axis=0).reshape(-1)
    space_w = []
    for piece in even:
        space_w += [piece, swap(piece, 1)]
    own_time = jnp.concatenate([column_blocks(time_qkv), time_out[None]], axis=0)
    own_feed = jnp.concatenate(
        [column_blocks(up_weight), down_weight.reshape(chunks, rows, width)], axis=0
    )
    own_time, own_feed, *_ = lax.optimization_barrier((own_time, own_feed, *even[1:]))
    time_w = gather(own_time)
    feed_w = gather(own_feed)
    mod_size = clips * 9 * width
    modul = small[:mod_size].reshape(clips, 9, width)
    up_bias_full = small[mod_size:-width].reshape(1, hidden)
    down_bias_full = small[-width:].reshape(1, width)

    slot_ids = shard_at * frame_count + jnp.arange(frame_count, dtype=jnp.int32)
    frame_ids = jnp.take(table, slot_ids)
    clip_of = frame_ids // frames
    frame_of = frame_ids % frames
    where = jnp.concatenate([clip_of, shard_at[None].astype(jnp.int32)])
    slots = jnp.arange(group_frames, dtype=jnp.int32)
    inverse = jnp.sum(jnp.where(table[None, :] == slots[:, None], slots[None, :], 0), axis=1)

    def exchange(parts):
        return lax.all_to_all(parts, "shard", split_axis=0, concat_axis=0, tiled=True)

    row_weights = task_mask[clip_of, frame_of].astype(F32) * clip_weight[clip_of]
    weighted = (cotangent * row_weights[:, None, None]).astype(BF)
    weighted = jnp.swapaxes(weighted.reshape(frame_count, shards, columns, width), 0, 1)
    arriving = exchange(weighted).reshape(group_frames, columns, width)

    own_shape = (shards, frame_count, columns, width)
    own_spec = pl.BlockSpec((shards, 1, columns, width), lambda step, *_: (0, step, 0, 0))
    mods_spec = whole((clips, 9, width))
    mods_out = shaped((clips, 3, width), F32)
    mods_out_spec = whole((clips, 3, width))
    grads_shape = (shards, 4, rows, width)
    weight_scratch = [
        pltpu.VMEM((width, 3 * width), BF),
        pltpu.VMEM((width, width), BF),
    ]
    dma = pltpu.SemaphoreType.DMA

    def kept(count):
        shapes = [
            shaped((count, ROWS, 3 * width), BF),
            shaped((count, ROWS, width), BF),
            shaped((count, 16, ROWS), F32),
            shaped((count, ROWS, width), BF),
        ]
        return shapes, [per_step(one.shape) for one in shapes]

    def back_scratch(count):
        return [
            pltpu.VMEM((count * ROWS, width), BF),
            pltpu.VMEM((count * ROWS, 3 * width), BF),
            pltpu.VMEM((count * ROWS, width), BF),
            pltpu.VMEM((count * ROWS, width), BF),
        ]

    mixer_flops = 2 * tokens * width * 4 * width + 4 * tokens * ROWS * width * 2
    space_keep, space_keep_specs = kept(frame_count)
    after_space, *space_kept = run(
        partial(space_forward_kernel, shards), frame_count, where,
        [frames_in, modul] + space_w,
        [per_step(frames_in.shape), mods_spec] + [ANY] * shards,
        [shaped(own_shape, BF)] + space_keep,
        [own_spec] + space_keep_specs,
        weight_scratch + [dma(())],
        mixer_flops, "space_forward",
    )
    received = exchange(after_space).reshape(group_frames, columns, width)
    own_ids = jnp.concatenate([embed, timesteps.astype(F32)[:, None]], axis=1)
    own_ids, _ = lax.optimization_barrier((own_ids, after_space))
    every_ids = lax.all_gather(own_ids, "grp", axis=0, tiled=True)
    received, every_ids = lax.optimization_barrier((received, every_ids))

    cols_spec = whole((group_frames, columns, width))
    cols_shape = shaped((group_frames, columns, width), BF)
    block_shape = (steps, ROWS, width)
    time_keep, time_keep_specs = kept(steps)
    time_resid, after_time, *time_kept = run(
        partial(time_forward_kernel, frames), steps, inverse,
        [received, modul, time_w],
        [cols_spec, mods_spec, ANY],
        [shaped(block_shape, BF), shaped(block_shape, F32)] + time_keep,
        [per_step(block_shape)] * 2 + time_keep_specs,
        weight_scratch + [pltpu.VMEM((ROWS, width), F32), dma(())],
        mixer_flops, "time_forward",
    )

    result, grad_after_time, mlp_mods, grad_up_bias, grad_down_bias, feed_grads = run(
        partial(feed_kernel, frames), steps, inverse,
        [after_time, arriving, modul, up_bias_full, down_bias_full, feed_w],
        [per_step(block_shape), cols_spec, mods_spec, whole((1, hidden)), whole((1, width)), ANY],
        [
            cols_shape,
            shaped(block_shape, F32),
            mods_out,
            shaped((1, hidden), F32),
            shaped((1, width), F32),
            shaped((shards, 2 * chunks, rows, width), BF),
        ],
        [
            cols_spec, per_step(block_shape), mods_out_spec, whole((1, hidden)),
            whole((1, width)), ANY,
        ],
        [
            pltpu.VMEM((width, hidden), BF),
            pltpu.VMEM((hidden, width), BF),
            pltpu.VMEM((tokens, width), BF),
            pltpu.VMEM((tokens, hidden), BF),
            pltpu.VMEM((tokens, hidden), BF),
            pltpu.VMEM((tokens, width), BF),
            pltpu.VMEM((ROWS, width), F32),
            pltpu.VMEM((2 * chunks, shards, rows, width), BF),
            dma(()),
            dma((2 * chunks,)),
        ],
        6 * 2 * tokens * width * hidden, "feed",
    )

    def to_rows(moved):
        moved = jnp.swapaxes(moved.reshape(own_shape), 0, 1)
        return moved.reshape(frame_count, patches, width).astype(F32)

    def shard_total(packed):
        return lax.psum_scatter(packed, "shard", scatter_dimension=0, tiled=True)[0]

    groups = lax.axis_size("grp")
    group_at = lax.axis_index("grp")

    def swap_group(values, distance):
        pairs = [(at, at ^ distance) for at in range(groups)]
        return lax.ppermute(values, "grp", pairs)

    def total(share):
        parts = share.reshape(groups, -1, width)

        def part(values, at):
            return lax.dynamic_index_in_dim(values, at, 0, keepdims=False)

        own = part(parts, group_at).astype(F32)
        for distance in range(1, groups):
            own = own + swap_group(part(parts, group_at ^ distance), distance).astype(F32)
        own = own.astype(BF)
        near = jnp.stack([own] + [swap_group(own, distance) for distance in range(1, groups)])
        step = 1
        while step < groups:
            flipped = near.reshape(-1, 2, step, *own.shape)[:, ::-1].reshape(near.shape)
            near = jnp.where(jnp.bitwise_and(group_at, step) > 0, flipped, near)
            step *= 2
        return near.reshape(share.shape).astype(F32)

    feed_share = shard_total(feed_grads)

    going, time_mods, time_grads = run(
        partial(time_backward_kernel, frames), steps, inverse,
        [grad_after_time, time_resid, modul] + time_kept + [time_w],
        [per_step(block_shape)] * 2 + [mods_spec] + time_keep_specs + [ANY],
        [cols_shape, mods_out, shaped(grads_shape, BF)],
        [cols_spec, mods_out_spec, whole(grads_shape)],
        weight_scratch + back_scratch(steps) + [dma(())],
        3 * mixer_flops, "time_backward",
    )
    grad_space = exchange(going.reshape(own_shape))
    time_grads, feed_share, grad_space, result = lax.optimization_barrier(
        (time_grads, feed_share, grad_space, result)
    )
    time_share = shard_total(time_grads)
    arrived = exchange(result.reshape(own_shape))
    grad_rows, space_mods, space_grads = run(
        partial(space_backward_kernel, shards), frame_count, where,
        [grad_space, frames_in, modul] + space_kept + space_w,
        [own_spec, per_step(frames_in.shape), mods_spec] + space_keep_specs + [ANY] * shards,
        [shaped(frames_in.shape, F32), mods_out, shaped(grads_shape, BF)],
        [per_step(frames_in.shape), mods_out_spec, whole(grads_shape)],
        weight_scratch + back_scratch(frame_count) + [dma(())],
        3 * mixer_flops, "space_backward",
    )
    space_grads, arrived = lax.optimization_barrier((space_grads, arrived))
    space_share = shard_total(space_grads)
    frames_out = to_rows(arrived)
    feed_share, space_mods = lax.optimization_barrier((feed_share, space_mods))
    feed_share = total(feed_share)
    time_share = total(time_share)
    space_share = total(space_share)

    mod_part = jnp.concatenate([space_mods, time_mods, mlp_mods], axis=1)
    small_grads = jnp.concatenate(
        [mod_part.reshape(-1), grad_up_bias.reshape(-1), grad_down_bias.reshape(-1)]
    )
    small_grads = shard_sum(small_grads.reshape(-1, 128)).reshape(-1)
    up_dev = up_bias.shape[0]
    down_dev = down_bias.shape[0]
    bias_dev = ada_bias.shape[0]
    small_grads = jnp.concatenate(
        [
            small_grads[:mod_size],
            lax.dynamic_slice_in_dim(small_grads, mod_size + shard_at * up_dev, up_dev, 0),
            lax.dynamic_slice_in_dim(
                small_grads, mod_size + shards * up_dev + shard_at * down_dev, down_dev, 0
            ),
        ]
    )
    small_size = small_grads.shape[0]
    small_grads = jnp.pad(small_grads, (0, -small_size % 1024)).reshape(1, -1, 128)
    every_small = lax.all_gather(small_grads, "grp", axis=0, tiled=True).reshape(groups, -1)
    every_modul = every_small[:, :mod_size].reshape(groups * clips, 9 * width).astype(BF)
    bias_sums = jnp.sum(every_small[:, mod_size:small_size], axis=0)
    every_embed = every_ids[:, :-1]
    every_steps = every_ids[:, -1].astype(jnp.int32)
    every_cond = jax.nn.silu(every_embed).astype(BF)
    grad_ada = jnp.einsum("cd,cj->dj", every_cond, every_modul, preferred_element_type=F32)
    grad_ada_bias = lax.dynamic_slice_in_dim(
        jnp.sum(every_modul.astype(F32), axis=0), shard_at * bias_dev, bias_dev, 0
    )
    grad_cond = jnp.einsum("cj,dj->cd", every_modul, ada_weight, preferred_element_type=F32)
    _, silu_back = jax.vjp(jax.nn.silu, every_embed)
    grad_embed = silu_back(grad_cond)[0]
    vocab = time_table.shape[0]
    onehot = (jnp.arange(vocab, dtype=jnp.int32)[:, None] == every_steps[None, :]).astype(F32)
    grad_table = jnp.dot(onehot, grad_embed, precision=HIGH)

    def rows_of(blocks):
        return jnp.swapaxes(blocks, 0, 1).reshape(rows, -1)

    return (
        frames_out,
        grad_rows,
        grad_table,
        grad_ada,
        grad_ada_bias,
        rows_of(space_share[:3]),
        space_share[3],
        rows_of(time_share[:3]),
        time_share[3],
        rows_of(feed_share[:chunks]),
        bias_sums[:up_dev],
        feed_share[chunks:].reshape(chunks * rows, width),
        bias_sums[up_dev:],
    )


def solution(mesh):
    placed = (
        P(("grp", "shard"), None, None),
        P(("grp", "shard"), None, None),
        P(None, "shard"),
        P("shard", None),
        P("shard"),
        P("shard", None),
        P("shard", None),
        P("shard", None),
        P("shard", None),
        P("shard", None),
        P("shard"),
        P("shard", None),
        P("shard"),
        P("grp"),
        P("grp", None),
        P("grp"),
        P("grp", None),
    )
    return jax.shard_map(
        body,
        mesh=mesh,
        in_specs=placed,
        out_specs=(
            P(("grp", "shard"), None, None),
            P(("grp", "shard"), None, None),
            P(None, "shard"),
            P("shard", None),
            P("shard"),
            P("shard", None),
            P("shard", None),
            P("shard", None),
            P("shard", None),
            P("shard", None),
            P("shard"),
            P("shard", None),
            P("shard"),
        ),
        check_vma=False,
    )
```

time: 898 us -> 525 us (0.58)
  matrix products: 219 us -> 4.08 us
  waiting for transfers between devices: 321 us -> 131 us
  Pallas kernels: 0 us -> 159 us
  local copies, waits for them, and re-layouts: 173 us -> 34.7 us
  other arithmetic: 103 us -> 16.5 us
  blocking collectives: 37.5 us -> 105 us
  starting transfers between devices: 16.8 us -> 52.2 us
    dot_general x36 -> x3, matrix products: 217 us -> 2.84 us  [the longest x1 2.07 us: body(): jnp.einsum('cd,cj->dj', every_cond, every_modul, preferred_element_type=F32)]
    pallas_call x0 -> x5, Pallas kernels: none -> 159 us  [run(): pl.pallas_call(kernel, grid_spec=pltpu.PrefetchScalarGridSpec(num_scalar_...]
    psum x3 -> x0, waiting for transfers between devices: 142 us -> none  [the longest x1 64 us: total(): share = lax.psum(share, 'grp').astype(jnp.float32)]
    reduce_scatter x3, waiting for transfers between devices: 109 us -> 20.6 us  [shard_total(): return lax.psum_scatter(packed, 'shard', scatter_dimension=0, tiled=True)[0]]
    reshape x17 -> x11, local copies, waits for them, and re-layouts: 69.8 us -> 8.87 us  [the longest x3 3.06 us: rows_of(): return jnp.swapaxes(blocks, 0, 1).reshape(rows, -1)]
    ppermute x0 -> x28, waiting for transfers between devices: none -> 52.7 us  [the longest x18 46.3 us: swap_group(): return lax.ppermute(values, 'grp', pairs)]
    all_gather x2 -> x3, blocking collectives: 25.4 us -> 71.8 us  [the longest x1 32.9 us: body(): lax.all_gather(small_grads, 'grp', axis=0, tiled=True).reshape(groups, -1)]
    convert_element_type x11 -> x10, other arithmetic: 53.9 us -> 9.96 us  [the longest x3 4 us: total(): return near.reshape(share.shape).astype(F32)]
  transfers between devices with their start and end apart: 16 -> 36, of which waited for: 8 -> 17; matrix products, arithmetic and copies ran while one was open for 37% -> 8% of each run, Pallas kernels for 0% -> 22%
where the time goes in v2:
time: 525 us; the launch traced here: 516 us
  Pallas kernels  159 us (30%)
  waiting for transfers between devices  131 us (25%)
  blocking collectives  105 us (20%)
  starting transfers between devices  52.2 us (10%)
  local copies, waits for them, and re-layouts  34.7 us (7%)
  other arithmetic  16.5 us (3%)
  between operations  14.8 us (3%)
    pallas_call x5, Pallas kernels, run(): pl.pallas_call(kernel, grid_spec=pltpu.PrefetchScalarGridSpec(num_scalar_...  159 us
    ppermute x18, waiting for transfers between devices, swap_group(): return lax.ppermute(values, 'grp', pairs)  46.3 us
    all_gather x2, waiting for transfers between devices, gather(): return lax.all_gather(packed[None], 'shard', axis=0, tiled=True)  33.9 us
    all_gather x1, blocking collectives, body(): lax.all_gather(small_grads, 'grp', axis=0, tiled=True).reshape(groups, -1)  32.9 us
    all_to_all x1, blocking collectives, exchange(): lax.all_to_all(parts, 'shard', split_axis=0, concat_axis=0, tiled=True)  32.7 us
    ppermute x18, starting transfers between devices, swap_group(): return lax.ppermute(values, 'grp', pairs)  30.7 us
    all_gather x1, blocking collectives, body(): lax.all_gather(small.reshape(1, -1, 128), 'shard', axis=0, tiled=True)  27.6 us
    all_to_all x3, waiting for transfers between devices, exchange(): lax.all_to_all(parts, 'shard', split_axis=0, concat_axis=0, tiled=True)  23.2 us
  transfers between devices with their start and end apart: 36, of which 17 were waited for; matrix products, arithmetic and copies ran while one was open for 8% of the time, Pallas kernels for 22%

profile of v2, /device:TPU:0, one launch (start us, length us, event | category | flops | bytes accessed | tf_op | source)
XLA Modules:
  0.0 516.2 jit_solution(2553870216565353870)
XLA Ops:
  7.3 1.1 copy.114
  8.4 1.8 pad_maximum_fusion.2.refs_0_
  10.2 3.0 collective-permute-start
  13.2 1.5 collective-permute-start.3
  16.4 1.2 reshape.387
  17.7 1.3 copy.95
  19.4 27.6 %all_gather.15 = f32[8,138,128]{2,1,0:T(8,128)S(1)} all-gather(f32[1,138,128]{2,1,0:T(8,128)S(1)} %maximum_bitcast_fusion), channel_id=1, replica_groups=mesh['grp'=4,'shard'=8] {'shard'}, dimensions={0}, use_global_device_ids=true | all-gather | bytes 635904 | tf_op jit(solution)/shard_map/all_gather | solution.py:508
  49.3 1.2 copy.98
  55.4 18.5 %space_forward.1 = (bf16[8,4,32,768]{3,2,1,0:T(8,128)(2,1)}, bf16[4,256,2304]{2,1,0:T(8,128)(2,1)}, bf16[4,256,768]{2,1,0:T(8,128)(2,1)}, f32[4,16,256]{2,1,0:T(8,128)}, bf16[4,256,768]{2,1,0:T(8,128)(2,1)}) custom-call(s32[5]{0:T(128)} %pad_add_fusion.where, f32[4,256,768]{2,1,0:T(8,128)} %frames_ref.3, f32[2,9,768]{2,1,0:T(8,128)} %reshape.384.mods_ref, ...), custom_call_target="tpu_custom_call" | custom-call | flops 6442450944 | bytes 17422336 | tf_op jit(solution)/shard_map/space_forward/pallas_call | solution.py:422
  74.0 3.6 all-to-all-start
  78.9 2.2 multiply_convert_fusion
  81.1 1.2 copy.113
  82.4 22.1 %all-to-all-done = bf16[8,4,32,768]{3,2,1,0:T(8,128)(2,1)S(1)} async-done(((bf16[8,4,32,768]{3,2,1,0:T(8,128)(2,1)}), bf16[8,4,32,768]{3,2,1,0:T(8,128)(2,1)S(1)}, u32[]{:S(2)}, u32[]{:S(2)}) %all-to-all-start) | async-done | bytes 1572896 | tf_op jit(solution)/shard_map/all_to_all | solution.py:535
  104.5 1.1 copy-done.8
  105.6 4.3 all-to-all-start.1
  112.0 11.4 %all-gather.2 = f32[4,2,97]{2,1,0:T(2,128)S(1)} all-gather(f32[1,2,97]{2,1,0:T(2,128)S(1)} %bitcast.237), channel_id=1, replica_groups=mesh['grp'=4,'shard'=8] {'grp'}, dimensions={0}, use_global_device_ids=true | all-gather | bytes 3880 | tf_op jit(solution)/shard_map/all_gather | solution.py:585
  123.4 19.0 %time_forward.1 = (bf16[4,256,768]{2,1,0:T(8,128)(2,1)}, f32[4,256,768]{2,1,0:T(8,128)}, bf16[4,256,2304]{2,1,0:T(8,128)(2,1)}, bf16[4,256,768]{2,1,0:T(8,128)(2...) custom-call(s32[32]{0:T(128)} %select_reduce_fusion.inverse, bf16[32,32,768]{2,1,0:T(8,128)(2,1)} %bitcast.193, ...), custom_call_target="tpu_custom_call" | custom-call | flops 6442450944 | bytes 18995200 | tf_op jit(solution)/shard_map/time_forward/pallas_call | solution.py:422
  142.4 1.1 all-to-all-done.1
  143.5 33.9 %all-gather.8.cloned.1.call-done = bf16[64,96,768]{2,1,0:T(8,128)(2,1)} async-done(((bf16[8,96,768]{2,1,0:T(8,128)(2,1)}), bf16[64,96,768]{2,1,0:T(8,128)(2,1)}) %all-gather.8.cloned.1.call-update) | async-done | bytes 9437200 | tf_op jit(solution)/shard_map/all_gather | solution.py:479
  177.4 43.5 %feed.1 = (bf16[32,32,768]{2,1,0:T(8,128)(2,1)}, f32[4,256,768]{2,1,0:T(8,128)}, f32[2,3,768]{2,1,0:T(4,128)}, f32[1,3072]{1,0:T(1,128)}, f32[1,768]{1,0:T(1,128)}, /*index=5*/bf16[8,8,96,768]{3,2,1,0:T(8,128)(2,1)}) custom-call(s32[32]{0:T(128)} %select_reduce_fusion.inverse, f32[4,256,768]{2,1,0:T(8,128)} %get-tuple-element.57.after_ref, ...), custom_call_target="tpu_custom_call" | custom-call | flops 28991029248 | bytes 28416000 | tf_op jit(solution)/shard_map/feed/pallas_call | solution.py:422
  221.0 38.9 %time_backward.1 = (bf16[32,32,768]{2,1,0:T(8,128)(2,1)}, f32[2,3,768]{2,1,0:T(4,128)}, bf16[8,4,96,768]{3,2,1,0:T(8,128)(2,1)}) custom-call(s32[32]{0:T(128)} %select_reduce_fusion.inverse, f32[4,256,768]{2,1,0:T(8,128)} %get-tuple-element.59.grad_ref, bf16[4,256,768]{2,1,0:T(8,128)(2,1)} %get-tuple-element.60.resid_ref, f32[2,9,768]{2,1,0:T(8,128)} %reshape.384.mods_ref, ...), custom_call_target="tpu_custom_call" | custom-call | flops 19327352832 | bytes 23732224 | tf_op jit(solution)/shard_map/time_backward/pallas_call | solution.py:422
  260.0 32.7 %all_to_all.20.grad_ref = bf16[8,4,32,768]{3,2,1,0:T(8,128)(2,1)} all-to-all(bf16[8,4,32,768]{3,2,1,0:T(8,128)(2,1)} %bitcast.194), channel_id=1, replica_groups=mesh['grp'=4,'shard'=8] {'shard'}, dimensions={0} | all-to-all | bytes 3145728 | tf_op jit(solution)/shard_map/all_to_all | solution.py:535
  292.6 20.6 %reduce-scatter.4.cloned.1.call-done = bf16[1,8,96,768]{3,2,1,0:T(8,128)(2,1)} async-done(((bf16[8,8,96,768]{3,2,1,0:T(8,128)(2,1)}), bf16[1,8,96,768]{3,2,1,0:T(8,128)(2,1)}) %reduce-scatter.4.cloned.1.call-update) | async-done | bytes 1179664 | tf_op jit(solution)/shard_map/reduce_scatter | solution.py:638
  313.3 3.6 all-to-all-start.3
  316.9 39.0 %space_backward.1 = (f32[4,256,768]{2,1,0:T(8,128)}, f32[2,3,768]{2,1,0:T(4,128)}, bf16[8,4,96,768]{3,2,1,0:T(8,128)(2,1)}) custom-call(s32[5]{0:T(128)} %pad_add_fusion.where, bf16[8,4,32,768]{3,2,1,0:T(8,128)(2,1)} %all_to_all.20.grad_ref, f32[4,256,768]{2,1,0:T(8,128)} %frames_ref.3, f32[2,9,768]{2,1,0:T(8,128)} %reshape.384.mods_ref, ...), custom_call_target="tpu_custom_call" | custom-call | flops 19327352832 | bytes 25305088 | tf_op jit(solution)/shard_map/space_backward/pallas_call | solution.py:422
  358.6 1.9 collective-permute-start.8
  360.7 3.6 collective-permute-done.8
  364.4 1.8 collective-permute-start.9
  366.2 1.2 dynamic-slice_bitcast_fusion.2
  367.4 1.6 collective-permute-start.22
  369.0 2.4 collective-permute-start.23
  372.0 32.9 %all_gather.19 = f32[4,112,128]{2,1,0:T(8,128)S(1)} all-gather(f32[1,112,128]{2,1,0:T(8,128)S(1)} %fusion.15), channel_id=1, replica_groups=mesh['grp'=4,'shard'=8] {'grp'}, dimensions={0}, use_global_device_ids=true | all-gather | bytes 286720 | tf_op jit(solution)/shard_map/all_gather | solution.py:718
  405.6 1.2 fusion.7
  406.9 1.1 fusion.2
  408.1 2.0 collective-permute-start.26
  410.0 2.4 collective-permute-start.27
  413.7 2.1 fusion.22
  415.7 4.2 collective-permute-done.25
  419.9 9.2 %collective-permute-done.26 = bf16[192,768]{1,0:T(8,128)(2,1)S(1)} collective-permute-done((bf16[192,768]{1,0:T(8,128)(2,1)S(1)}, bf16[192,768]{1,0:T(8,128)(2,1)S(1)}, u32[]{:S(2)}, u32[]{:S(2)}) %collective-permute-start.26) | collective-permute-done | bytes 294944 | tf_op jit(solution)/shard_map/ppermute | solution.py:645
  429.3 1.1 rev.22
  430.4 1.3 bitcast_select_fusion
  431.7 2.4 rev.23
  434.1 1.6 select_convert_fusion
  436.8 5.2 %collective-permute-start.16 = (bf16[96,768]{1,0:T(8,128)(2,1)S(1)}, bf16[96,768]{1,0:T(8,128)(2,1)S(1)}, u32[]{:S(2)}, u32[]{:S(2)}) collective-permute-start(bf16[96,768]{1,0:T(8,128)(2,1)S(1)} %get-tuple-element.94), channel_id=1, source_target_pairs={{0,8},{8,0},{16,24},{24,16},{1,9},{9,1},{17,25},{25,17},{2,10},{10... | collective-permute-start | bytes 442376 | tf_op jit(solution)/shard_map/ppermute | solution.py:645
  442.6 1.8 collective-permute-start.18
  444.4 2.8 fusion.40
  447.2 1.1 copy.106
  448.3 5.0 collective-permute-done.17
  454.4 2.2 collective-permute-start.19
  457.4 1.6 collective-permute-start.21
  459.4 2.0 copy.99
  461.4 7.9 %collective-permute-done.20 = bf16[96,768]{1,0:T(8,128)(2,1)S(1)} collective-permute-done((bf16[96,768]{1,0:T(8,128)(2,1)S(1)}, bf16[96,768]{1,0:T(8,128)(2,1)S(1)}, u32[]{:S(2)}, u32[]{:S(2)}) %collective-permute-start.20) | collective-permute-done | bytes 147488 | tf_op jit(solution)/shard_map/ppermute | solution.py:645
  471.0 1.3 fusion.4
  473.4 2.2 collective-permute-start.10
  475.6 1.2 collective-permute-start.11
  476.7 1.4 collective-permute-start.12
  479.2 1.2 collective-permute-done.10
  480.4 8.7 %collective-permute-done.11 = bf16[96,768]{1,0:T(8,128)(2,1)S(1)} collective-permute-done((bf16[96,768]{1,0:T(8,128)(2,1)S(1)}, bf16[96,768]{1,0:T(8,128)(2,1)S(1)}, u32[]{:S(2)}, u32[]{:S(2)}) %collective-permute-start.11) | collective-permute-done | bytes 147488 | tf_op jit(solution)/shard_map/ppermute | solution.py:645
  490.1 2.2 collective-permute-start.13
  492.3 1.2 collective-permute-start.14
  493.4 1.4 collective-permute-start.15
  495.6 1.5 collective-permute-done.13
  497.1 8.6 %collective-permute-done.14 = bf16[96,768]{1,0:T(8,128)(2,1)S(1)} collective-permute-done((bf16[96,768]{1,0:T(8,128)(2,1)S(1)}, bf16[96,768]{1,0:T(8,128)(2,1)S(1)}, u32[]{:S(2)}, u32[]{:S(2)}) %collective-permute-start.14) | collective-permute-done | bytes 147488 | tf_op jit(solution)/shard_map/ppermute | solution.py:645
  506.5 1.1 fusion.6
  (181 shorter events, 30.3 us)
Async XLA Ops:
  7.2 8.6 %copy-start = (bf16[96,6912]{1,0:T(8,128)(2,1)S(1)}, bf16[96,6912]{1,0:T(8,128)(2,1)}, u32[]{:S(2)}) copy-start(bf16[96,6912]{1,0:T(8,128)(2,1)} %param.20) | copy-start | bytes 3981316
  7.2 7.5 %copy-start.25 = (s32[2]{0:T(128)S(1)}, s32[2]{0:T(128)}, u32[]{:S(2)}) copy-start(s32[2]{0:T(128)} %param.30) | copy-start | bytes 28
  7.2 7.5 %copy-start.22 = (bf16[864]{0:T(1024)(128)(2,1)S(1)}, bf16[864]{0:T(1024)(128)(2,1)}, u32[]{:S(2)}) copy-start(bf16[864]{0:T(1024)(128)(2,1)} %param.21) | copy-start | bytes 5188
  7.2 7.8 %copy-start.14 = (bf16[1000,96]{0,1:T(8,128)(2,1)S(1)}, bf16[1000,96]{0,1:T(8,128)(2,1)}, u32[]{:S(2)}) copy-start(bf16[1000,96]{0,1:T(8,128)(2,1)} %param.19) | copy-start | bytes 576004
  7.2 116.2 %all-gather.6.cloned.1.call-start = ((), (), s32[]{:S(2)}) async-start(), calls=%async_computation.10 | async-start | bytes 5308416 | tf_op jit(solution)/shard_map/all_gather | solution.py:479
  8.4 7.7 %copy-start.26 = (bf16[96]{0:T(256)(128)(2,1)S(1)}, bf16[96]{0:T(256)(128)(2,1)}, u32[]{:S(2)}) copy-start(bf16[96]{0:T(256)(128)(2,1)} %param.29) | copy-start | bytes 580
  10.2 6.0 %copy-start.23 = (bf16[384]{0:T(512)(128)(2,1)S(1)}, bf16[384]{0:T(512)(128)(2,1)}, u32[]{:S(2)}) copy-start(bf16[384]{0:T(512)(128)(2,1)} %param.27) | copy-start | bytes 2308
  10.2 6.2 %copy-start.9 = (bf16[96,3072]{1,0:T(8,128)(2,1)S(1)}, bf16[96,3072]{1,0:T(8,128)(2,1)}, u32[]{:S(2)}) copy-start(bf16[96,3072]{1,0:T(8,128)(2,1)} %param.26) | copy-start | bytes 1769476
  10.2 38.0 %collective-permute-start = (bf16[4,96,768]{2,1,0:T(8,128)(2,1)}, bf16[4,96,768]{2,1,0:T(8,128)(2,1)}, u32[]{:S(2)}, u32[]{:S(2)}) collective-permute-start(bf16[4,96,768]{2,1,0:T(8,128)(2,1)} %pad_maximum_fusion.2.refs_0_), channel_id=1, source_target_pairs={{0,2},{1,3},{2,0},{3,1},{4,6},{5,7},{6,4},{7,5},{8,10},{9,11},{10,... | collective-permute-start | bytes 1769480 | tf_op jit(solution)/shard_map/ppermute | solution.py:476
  13.2 35.1 %collective-permute-start.3 = (bf16[4,96,768]{2,1,0:T(8,128)(2,1)}, bf16[4,96,768]{2,1,0:T(8,128)(2,1)}, u32[]{:S(2)}, u32[]{:S(2)}) collective-permute-start(bf16[4,96,768]{2,1,0:T(8,128)(2,1)} %pad_maximum_fusion.2.refs_0_), channel_id=1, source_target_pairs={{0,4},{1,5},{2,6},{3,7},{4,0},{5,1},{6,2},{7,3},{8,12},{9,13},{10,... | collective-permute-start | bytes 1769480 | tf_op jit(solution)/shard_map/ppermute | solution.py:476
  14.7 33.6 %collective-permute-start.5 = (bf16[4,96,768]{2,1,0:T(8,128)(2,1)}, bf16[4,96,768]{2,1,0:T(8,128)(2,1)}, u32[]{:S(2)}, u32[]{:S(2)}) collective-permute-start(bf16[4,96,768]{2,1,0:T(8,128)(2,1)} %pad_maximum_fusion.2.refs_0_), channel_id=1, source_target_pairs={{0,6},{1,7},{2,4},{3,5},{4,2},{5,3},{6,0},{7,1},{8,14},{9,15},{10,... | collective-permute-start | bytes 1769480 | tf_op jit(solution)/shard_map/ppermute | solution.py:476
  15.8 1.9 copy-start.10
  16.1 2.8 copy-start.13
  17.7 1.5 copy-start.15
  19.1 28.5 %copy-start.6 = (bf16[96,4,768]{2,1,0:T(4,128)(2,1)S(1)}, bf16[96,4,768]{2,1,0:T(4,128)(2,1)}, u32[]{:S(2)}) copy-start(bf16[96,4,768]{2,1,0:T(4,128)(2,1)} %reshape.387) | copy-start | bytes 1769476
  19.2 28.5 %copy-start.7 = (bf16[4,96,768]{2,0,1:T(4,128)(2,1)S(1)}, bf16[4,96,768]{2,0,1:T(4,128)(2,1)}, u32[]{:S(2)}) copy-start(bf16[4,96,768]{2,0,1:T(4,128)(2,1)} %copy.95) | copy-start | bytes 1769476
  49.2 2.4 copy-start.2
  49.2 128.2 %all-gather.8.cloned.1.call-start = ((), (), s32[]{:S(2)}) async-start(), calls=%async_computation.11 | async-start | bytes 10616832 | tf_op jit(solution)/shard_map/all_gather | solution.py:479
  50.5 3.1 collective-permute-start.1
  50.9 2.8 collective-permute-start.2
  51.1 3.5 collective-permute-start.4
  51.4 4.0 collective-permute-start.6
  53.6 1.9 copy-start.24
  73.9 3.7 copy-start.1
  74.0 4.3 copy-start.3
  74.0 30.5 %all-to-all-start = ((bf16[8,4,32,768]{3,2,1,0:T(8,128)(2,1)}), bf16[8,4,32,768]{3,2,1,0:T(8,128)(2,1)S(1)}, u32[]{:S(2)}, u32[]{:S(2)}) async-start(bf16[8,4,32,768]{3,2,1,0:T(8,128)(2,1)} %get-tuple-element.53), calls=%async_computation | async-start | bytes 3145728 | tf_op jit(solution)/shard_map/all_to_all | solution.py:535
  104.5 1.1 copy-start.8
  105.6 37.9 %all-to-all-start.1 = ((bf16[8,4,32,768]{3,2,1,0:T(8,128)(2,1)}), bf16[8,4,32,768]{3,2,1,0:T(8,128)(2,1)}, u32[]{:S(2)}, u32[]{:S(2)}) async-start(bf16[8,4,32,768]{3,2,1,0:T(8,128)(2,1)} %bitcast.167), calls=%async_computation.1 | async-start | bytes 3145728 | tf_op jit(solution)/shard_map/all_to_all | solution.py:535
  109.9 203.3 %reduce-scatter.4.cloned.1.call-start = ((), (), s32[]{:S(2)}) async-start(), calls=%async_computation.7 | async-start | bytes 10616832 | tf_op jit(solution)/shard_map/reduce_scatter | solution.py:638
  221.0 214.7 %reduce-scatter.8.cloned.1.call-start = ((), (), s32[]{:S(2)}) async-start(), calls=%async_computation.9 | async-start | bytes 5308416 | tf_op jit(solution)/shard_map/reduce_scatter | solution.py:638
  313.3 42.7 %all-to-all-start.3 = ((bf16[8,4,32,768]{3,2,1,0:T(8,128)(2,1)}), bf16[8,4,32,768]{3,2,1,0:T(8,128)(2,1)S(1)}, u32[]{:S(2)}, u32[]{:S(2)}) async-start(bf16[8,4,32,768]{3,2,1,0:T(8,128)(2,1)} %bitcast.192), calls=%async_computation.4 | async-start | bytes 3145728 | tf_op jit(solution)/shard_map/all_to_all | solution.py:535
  316.9 155.4 %reduce-scatter.6.cloned.1.call-start = ((), (), s32[]{:S(2)}) async-start(), calls=%async_computation.8 | async-start | bytes 5308416 | tf_op jit(solution)/shard_map/reduce_scatter | solution.py:638
  355.9 1.1 copy-start.4
  355.9 1.1 copy-start.20
  356.0 1.1 copy-start.17
  356.0 1.1 copy-start.18
  356.0 1.1 copy-start.19
  356.0 1.2 copy-start.16
  357.2 1.3 collective-permute-start.7
  358.6 5.8 %collective-permute-start.8 = (f32[138,128]{1,0:T(8,128)S(1)}, f32[138,128]{1,0:T(8,128)S(1)}, u32[]{:S(2)}, u32[]{:S(2)}) collective-permute-start(f32[138,128]{1,0:T(8,128)S(1)} %fusion.39), channel_id=1, source_target_pairs={{0,2},{1,3},{2,0},{3,1},{4,6},{5,7},{6,4},{7,5},{8,10},{9,11},{10,... | collective-permute-start | bytes 211976 | tf_op jit(solution)/shard_map/ppermute | solution.py:476
  364.4 7.5 %collective-permute-start.9 = (f32[138,128]{1,0:T(8,128)S(1)}, f32[138,128]{1,0:T(8,128)S(1)}, u32[]{:S(2)}, u32[]{:S(2)}) collective-permute-start(f32[138,128]{1,0:T(8,128)S(1)} %fusion.46), channel_id=1, source_target_pairs={{0,4},{1,5},{2,6},{3,7},{4,0},{5,1},{6,2},{7,3},{8,12},{9,13},{10,... | collective-permute-start | bytes 211976 | tf_op jit(solution)/shard_map/ppermute | solution.py:476
  367.4 39.5 %collective-permute-start.22 = (bf16[192,768]{1,0:T(8,128)(2,1)S(1)}, bf16[192,768]{1,0:T(8,128)(2,1)S(1)}, u32[]{:S(2)}, u32[]{:S(2)}) collective-permute-start(bf16[192,768]{1,0:T(8,128)(2,1)S(1)} %get-tuple-element.91), channel_id=1, source_target_pairs={{0,8},{8,0},{16,24},{24,16},{1,9},{9,1},{17,25},{25,17},{2,10},{10... | collective-permute-start | bytes 884744 | tf_op jit(solution)/shard_map/ppermute | solution.py:645
  369.0 37.9 %collective-permute-start.23 = (bf16[192,768]{1,0:T(8,128)(2,1)S(1)}, bf16[192,768]{1,0:T(8,128)(2,1)S(1)}, u32[]{:S(2)}, u32[]{:S(2)}) collective-permute-start(bf16[192,768]{1,0:T(8,128)(2,1)S(1)} %get-tuple-element.93), channel_id=1, source_target_pairs={{0,16},{8,24},{16,0},{24,8},{1,17},{9,25},{17,1},{25,9},{2,18},{10... | collective-permute-start | bytes 884744 | tf_op jit(solution)/shard_map/ppermute | solution.py:645
  371.4 35.5 %collective-permute-start.24 = (bf16[192,768]{1,0:T(8,128)(2,1)S(1)}, bf16[192,768]{1,0:T(8,128)(2,1)S(1)}, u32[]{:S(2)}, u32[]{:S(2)}) collective-permute-start(bf16[192,768]{1,0:T(8,128)(2,1)S(1)} %get-tuple-element.92), channel_id=1, source_target_pairs={{0,24},{8,16},{16,8},{24,0},{1,25},{9,17},{17,9},{25,1},{2,26},{10... | collective-permute-start | bytes 884744 | tf_op jit(solution)/shard_map/ppermute | solution.py:645
  408.0 11.9 %collective-permute-start.25 = (bf16[192,768]{1,0:T(8,128)(2,1)S(1)}, bf16[192,768]{1,0:T(8,128)(2,1)S(1)}, u32[]{:S(2)}, u32[]{:S(2)}) collective-permute-start(bf16[192,768]{1,0:T(8,128)(2,1)S(1)} %fusion.2), channel_id=1, source_target_pairs={{0,8},{8,0},{16,24},{24,16},{1,9},{9,1},{17,25},{25,17},{2,10},{10... | collective-permute-start | bytes 884744 | tf_op jit(solution)/shard_map/ppermute | solution.py:645
  408.1 21.0 %collective-permute-start.26 = (bf16[192,768]{1,0:T(8,128)(2,1)S(1)}, bf16[192,768]{1,0:T(8,128)(2,1)S(1)}, u32[]{:S(2)}, u32[]{:S(2)}) collective-permute-start(bf16[192,768]{1,0:T(8,128)(2,1)S(1)} %fusion.2), channel_id=1, source_target_pairs={{0,16},{8,24},{16,0},{24,8},{1,17},{9,25},{17,1},{25,9},{2,18},{10... | collective-permute-start | bytes 884744 | tf_op jit(solution)/shard_map/ppermute | solution.py:645
  410.0 19.1 %collective-permute-start.27 = (bf16[192,768]{1,0:T(8,128)(2,1)S(1)}, bf16[192,768]{1,0:T(8,128)(2,1)S(1)}, u32[]{:S(2)}, u32[]{:S(2)}) collective-permute-start(bf16[192,768]{1,0:T(8,128)(2,1)S(1)} %fusion.2), channel_id=1, source_target_pairs={{0,24},{8,16},{16,8},{24,0},{1,25},{9,17},{17,9},{25,1},{2,26},{10... | collective-permute-start | bytes 884744 | tf_op jit(solution)/shard_map/ppermute | solution.py:645
  412.5 3.3 copy-start.21
  436.8 11.6 %collective-permute-start.16 = (bf16[96,768]{1,0:T(8,128)(2,1)S(1)}, bf16[96,768]{1,0:T(8,128)(2,1)S(1)}, u32[]{:S(2)}, u32[]{:S(2)}) collective-permute-start(bf16[96,768]{1,0:T(8,128)(2,1)S(1)} %get-tuple-element.94), channel_id=1, source_target_pairs={{0,8},{8,0},{16,24},{24,16},{1,9},{9,1},{17,25},{25,17},{2,10},{10... | collective-permute-start | bytes 442376 | tf_op jit(solution)/shard_map/ppermute | solution.py:645
  442.0 11.4 %collective-permute-start.17 = (bf16[96,768]{1,0:T(8,128)(2,1)S(1)}, bf16[96,768]{1,0:T(8,128)(2,1)S(1)}, u32[]{:S(2)}, u32[]{:S(2)}) collective-permute-start(bf16[96,768]{1,0:T(8,128)(2,1)S(1)} %get-tuple-element.96), channel_id=1, source_target_pairs={{0,16},{8,24},{16,0},{24,8},{1,17},{9,25},{17,1},{25,9},{2,18},{10... | collective-permute-start | bytes 442376 | tf_op jit(solution)/shard_map/ppermute | solution.py:645
  442.6 10.7 %collective-permute-start.18 = (bf16[96,768]{1,0:T(8,128)(2,1)S(1)}, bf16[96,768]{1,0:T(8,128)(2,1)S(1)}, u32[]{:S(2)}, u32[]{:S(2)}) collective-permute-start(bf16[96,768]{1,0:T(8,128)(2,1)S(1)} %get-tuple-element.95), channel_id=1, source_target_pairs={{0,24},{8,16},{16,8},{24,0},{1,25},{9,17},{17,9},{25,1},{2,26},{10... | collective-permute-start | bytes 442376 | tf_op jit(solution)/shard_map/ppermute | solution.py:645
  447.2 11.8 %copy-start.5 = (bf16[8,4,32,768]{3,2,1,0:T(8,128)(2,1)S(1)}, bf16[8,4,32,768]{3,2,1,0:T(8,128)(2,1)}, u32[]{:S(2)}) copy-start(bf16[8,4,32,768]{3,2,1,0:T(8,128)(2,1)} %copy-done.4) | copy-start | bytes 4718596
  454.4 7.1 %collective-permute-start.19 = (bf16[96,768]{1,0:T(8,128)(2,1)S(1)}, bf16[96,768]{1,0:T(8,128)(2,1)S(1)}, u32[]{:S(2)}, u32[]{:S(2)}) collective-permute-start(bf16[96,768]{1,0:T(8,128)(2,1)S(1)} %fusion.10), channel_id=1, source_target_pairs={{0,8},{8,0},{16,24},{24,16},{1,9},{9,1},{17,25},{25,17},{2,10},{10... | collective-permute-start | bytes 442376 | tf_op jit(solution)/shard_map/ppermute | solution.py:645
  456.6 12.8 %collective-permute-start.20 = (bf16[96,768]{1,0:T(8,128)(2,1)S(1)}, bf16[96,768]{1,0:T(8,128)(2,1)S(1)}, u32[]{:S(2)}, u32[]{:S(2)}) collective-permute-start(bf16[96,768]{1,0:T(8,128)(2,1)S(1)} %fusion.10), channel_id=1, source_target_pairs={{0,16},{8,24},{16,0},{24,8},{1,17},{9,25},{17,1},{25,9},{2,18},{10... | collective-permute-start | bytes 442376 | tf_op jit(solution)/shard_map/ppermute | solution.py:645
  457.4 11.9 %collective-permute-start.21 = (bf16[96,768]{1,0:T(8,128)(2,1)S(1)}, bf16[96,768]{1,0:T(8,128)(2,1)S(1)}, u32[]{:S(2)}, u32[]{:S(2)}) collective-permute-start(bf16[96,768]{1,0:T(8,128)(2,1)S(1)} %fusion.10), channel_id=1, source_target_pairs={{0,24},{8,16},{16,8},{24,0},{1,25},{9,17},{17,9},{25,1},{2,26},{10... | collective-permute-start | bytes 442376 | tf_op jit(solution)/shard_map/ppermute | solution.py:645
  469.3 0.7 copy-start.11
  473.4 7.0 %collective-permute-start.10 = (bf16[96,768]{1,0:T(8,128)(2,1)S(1)}, bf16[96,768]{1,0:T(8,128)(2,1)S(1)}, u32[]{:S(2)}, u32[]{:S(2)}) collective-permute-start(bf16[96,768]{1,0:T(8,128)(2,1)S(1)} %get-tuple-element.97), channel_id=1, source_target_pairs={{0,8},{8,0},{16,24},{24,16},{1,9},{9,1},{17,25},{25,17},{2,10},{10... | collective-permute-start | bytes 442376 | tf_op jit(solution)/shard_map/ppermute | solution.py:645
  475.6 13.5 %collective-permute-start.11 = (bf16[96,768]{1,0:T(8,128)(2,1)S(1)}, bf16[96,768]{1,0:T(8,128)(2,1)S(1)}, u32[]{:S(2)}, u32[]{:S(2)}) collective-permute-start(bf16[96,768]{1,0:T(8,128)(2,1)S(1)} %get-tuple-element.99), channel_id=1, source_target_pairs={{0,16},{8,24},{16,0},{24,8},{1,17},{9,25},{17,1},{25,9},{2,18},{10... | collective-permute-start | bytes 442376 | tf_op jit(solution)/shard_map/ppermute | solution.py:645
  476.7 12.3 %collective-permute-start.12 = (bf16[96,768]{1,0:T(8,128)(2,1)S(1)}, bf16[96,768]{1,0:T(8,128)(2,1)S(1)}, u32[]{:S(2)}, u32[]{:S(2)}) collective-permute-start(bf16[96,768]{1,0:T(8,128)(2,1)S(1)} %get-tuple-element.98), channel_id=1, source_target_pairs={{0,24},{8,16},{16,8},{24,0},{1,25},{9,17},{17,9},{25,1},{2,26},{10... | collective-permute-start | bytes 442376 | tf_op jit(solution)/shard_map/ppermute | solution.py:645
  490.1 7.0 %collective-permute-start.13 = (bf16[96,768]{1,0:T(8,128)(2,1)S(1)}, bf16[96,768]{1,0:T(8,128)(2,1)S(1)}, u32[]{:S(2)}, u32[]{:S(2)}) collective-permute-start(bf16[96,768]{1,0:T(8,128)(2,1)S(1)} %fusion.13), channel_id=1, source_target_pairs={{0,8},{8,0},{16,24},{24,16},{1,9},{9,1},{17,25},{25,17},{2,10},{10... | collective-permute-start | bytes 442376 | tf_op jit(solution)/shard_map/ppermute | solution.py:645
  492.3 13.4 %collective-permute-start.14 = (bf16[96,768]{1,0:T(8,128)(2,1)S(1)}, bf16[96,768]{1,0:T(8,128)(2,1)S(1)}, u32[]{:S(2)}, u32[]{:S(2)}) collective-permute-start(bf16[96,768]{1,0:T(8,128)(2,1)S(1)} %fusion.13), channel_id=1, source_target_pairs={{0,16},{8,24},{16,0},{24,8},{1,17},{9,25},{17,1},{25,9},{2,18},{10... | collective-permute-start | bytes 442376 | tf_op jit(solution)/shard_map/ppermute | solution.py:645
  493.4 12.2 %collective-permute-start.15 = (bf16[96,768]{1,0:T(8,128)(2,1)S(1)}, bf16[96,768]{1,0:T(8,128)(2,1)S(1)}, u32[]{:S(2)}, u32[]{:S(2)}) collective-permute-start(bf16[96,768]{1,0:T(8,128)(2,1)S(1)} %fusion.13), channel_id=1, source_target_pairs={{0,24},{8,16},{16,8},{24,0},{1,25},{9,17},{17,9},{25,1},{2,26},{10... | collective-permute-start | bytes 442376 | tf_op jit(solution)/shard_map/ppermute | solution.py:645
  505.6 0.7 copy-start.12
Sparse Core Ops, SparseCore 0:
  49.3 49.3 all-gather.5
  101.1 76.2 all-gather.7
  221.1 92.0 reduce-scatter.3
  316.5 55.3 reduce-scatter.7
  375.2 53.7 reduce-scatter.5

commit v3 on v2

--- a/solution.py
+++ b/solution.py
@@ -145,6 +145,15 @@
     return grad_in, (grad_shift, grad_scale, grad_gate)
 
 
+def by_distance(me, grad, out, block, shards):
+    rows = grad.shape[0] // shards
+    for shard in range(shards):
+        distance = jnp.bitwise_xor(me, shard)
+        out[jnp.bitwise_and(distance, 1), lax.shift_right_logical(distance, 1), block] = grad[
+            shard * rows : (shard + 1) * rows
+        ]
+
+
 def fetch_weights(packed, places, sem):
     copies = []
     for shard in range(packed.shape[0]):
@@ -175,25 +184,11 @@
         copy.wait()
 
 
-def mixer_places(weight, out_weight, rows, width):
-    def places(shard, block):
-        if block < 3:
-            return weight.at[
-                shard * rows : (shard + 1) * rows, block * width : (block + 1) * width
-            ]
-        return out_weight.at[shard * rows : (shard + 1) * rows, :]
-
-    return places
-
-
-def mixer_weight_grads(entry, packed_grad, mixed, branch_grad, out, shards, width):
-    rows = width // shards
+def mixer_weight_grads(entry, packed_grad, mixed, branch_grad, put, width):
     entry_t = entry[...].T
     for block in range(3):
-        grad = mul(entry_t, packed_grad[:, block * width : (block + 1) * width]).astype(BF)
-        out[:, block] = grad.reshape(shards, rows, width)
-    grad = mul(mixed.T, branch_grad[...]).astype(BF)
-    out[:, 3] = grad.reshape(shards, rows, width)
+        put(block, mul(entry_t, packed_grad[:, block * width : (block + 1) * width]).astype(BF))
+    put(3, mul(mixed.T, branch_grad[...]).astype(BF))
 
 
 def add_mods(mods_out, clip, grads):
@@ -235,6 +230,7 @@
         mods_out[...] = jnp.zeros_like(mods_out)
 
     clip = where[step]
+    me = where[pl.num_programs(0)]
     own = pl.ds(pl.multiple_of(step * ROWS, ROWS), ROWS)
     grad_out = grad_ref[...].reshape(ROWS, width).astype(F32)
     grad_in, grads = mixer_backward(
@@ -248,7 +244,10 @@
 
     @pl.when(step == pl.num_programs(0) - 1)
     def _():
-        mixer_weight_grads(entry, packed_grad, mixed[...], branch_grad, grads_out, shards, width)
+        def put(block, grad):
+            by_distance(me, grad, grads_out, block, shards)
+
+        mixer_weight_grads(entry, packed_grad, mixed[...], branch_grad, put, width)
 
 
 def load_near(source, inverse, resid, clip, first, frames):
@@ -271,16 +270,16 @@
     return step, clip, first
 
 
-def time_forward_kernel(
-    frames, inverse, source, mods_ref, packed_w, resid_ref, after_ref, packed_ref, mixed_ref,
-    lse_ref, branch_ref, weight, out_weight, resid, sem,
-):
+def time_forward_kernel(frames, shards, inverse, source, mods_ref, *refs):
+    pieces = refs[:shards]
+    resid_ref, after_ref, packed_ref, mixed_ref, lse_ref, branch_ref = refs[shards : shards + 6]
+    weight, out_weight, resid, sem = refs[shards + 6 :]
     step, clip, first = block_place(source.shape[1])
-    shards, _, rows, width = packed_w.shape
+    width = source.shape[-1]
 
     @pl.when(step == 0)
     def _():
-        fetch_weights(packed_w, mixer_places(weight, out_weight, rows, width), sem)
+        fetch_pieces(inverse[source.shape[0]], pieces, weight, out_weight, sem)
 
     load_near(source, inverse, resid, clip, first, frames)
     resid_ref[0] = resid[...].astype(BF)
@@ -291,16 +290,18 @@
 
 
 def time_backward_kernel(
-    frames, inverse, grad_ref, resid_ref, mods_ref, packed_ref, mixed_ref, lse_ref, branch_ref,
-    packed_w, going, mods_out, grads_out, weight, out_weight, entry, packed_grad, mixed,
-    branch_grad, sem,
+    frames, shards, inverse, grad_ref, resid_ref, mods_ref, packed_ref, mixed_ref, lse_ref,
+    branch_ref, *refs
 ):
+    pieces = refs[:shards]
+    going, mods_out, grads_out = refs[shards : shards + 3]
+    weight, out_weight, entry, packed_grad, mixed, branch_grad, sem = refs[shards + 3 :]
     step, clip, first = block_place(going.shape[1])
-    shards, _, rows, width = packed_w.shape
+    width = going.shape[-1]
 
     @pl.when(step == 0)
     def _():
-        fetch_weights(packed_w, mixer_places(weight, out_weight, rows, width), sem)
+        fetch_pieces(inverse[going.shape[0]], pieces, weight, out_weight, sem)
         mods_out[...] = jnp.zeros_like(mods_out)
 
     own = pl.ds(pl.multiple_of(step * ROWS, ROWS), ROWS)
@@ -315,7 +316,10 @@
 
     @pl.when(step == pl.num_programs(0) - 1)
     def _():
-        mixer_weight_grads(entry, packed_grad, mixed[...], branch_grad, grads_out, shards, width)
+        def put(block, grad):
+            grads_out[:, block] = grad.reshape(shards, width // shards, width)
+
+        mixer_weight_grads(entry, packed_grad, mixed[...], branch_grad, put, width)
 
 
 def feed_kernel(
@@ -478,6 +482,20 @@
     def gather(packed):
         return lax.all_gather(packed[None], "shard", axis=0, tiled=True)
 
+    groups = lax.axis_size("grp")
+    group_at = lax.axis_index("grp")
+
+    def swap_group(values, distance):
+        pairs = [(at, at ^ distance) for at in range(groups)]
+        return lax.ppermute(values, "grp", pairs)
+
+    def every(values):
+        stacked = jnp.zeros((groups,) + values.shape, values.dtype)
+        for distance in range(groups):
+            piece = swap_group(values, distance) if distance else values
+            stacked = lax.dynamic_update_index_in_dim(stacked, piece, group_at ^ distance, 0)
+        return stacked
+
     def shard_sum(values):
         distance = 1
         while distance < shards:
@@ -485,8 +503,17 @@
             distance *= 2
         return values
 
+    def even_pieces(own):
+        return [own] + [swap(own, distance) for distance in range(2, shards, 2)]
+
+    def all_pieces(even):
+        pieces = []
+        for piece in even:
+            pieces += [piece, swap(piece, 1)]
+        return pieces
+
     own_space = jnp.concatenate([column_blocks(space_qkv), space_out[None]], axis=0)
-    even = [own_space] + [swap(own_space, distance) for distance in range(2, shards, 2)]
+    even = even_pieces(own_space)
 
     embed = jnp.take(time_table, timesteps, axis=0).astype(F32)
     cond = jax.nn.silu(embed).astype(BF)
@@ -508,15 +535,13 @@
     small = lax.all_gather(small.reshape(1, -1, 128), "shard", axis=0, tiled=True)
     small, even[1] = lax.optimization_barrier((small, even[1]))
     small = jnp.sum(small, axis=0).reshape(-1)
-    space_w = []
-    for piece in even:
-        space_w += [piece, swap(piece, 1)]
+    space_w = all_pieces(even)
     own_time = jnp.concatenate([column_blocks(time_qkv), time_out[None]], axis=0)
     own_feed = jnp.concatenate(
         [column_blocks(up_weight), down_weight.reshape(chunks, rows, width)], axis=0
     )
     own_time, own_feed, *_ = lax.optimization_barrier((own_time, own_feed, *even[1:]))
-    time_w = gather(own_time)
+    time_w = all_pieces(even_pieces(own_time))
     feed_w = gather(own_feed)
     mod_size = clips * 9 * width
     modul = small[:mod_size].reshape(clips, 9, width)
@@ -530,6 +555,7 @@
     where = jnp.concatenate([clip_of, shard_at[None].astype(jnp.int32)])
     slots = jnp.arange(group_frames, dtype=jnp.int32)
     inverse = jnp.sum(jnp.where(table[None, :] == slots[:, None], slots[None, :], 0), axis=1)
+    inverse = jnp.concatenate([inverse, shard_at[None].astype(jnp.int32)])
 
     def exchange(parts):
         return lax.all_to_all(parts, "shard", split_axis=0, concat_axis=0, tiled=True)
@@ -545,6 +571,7 @@
     mods_out = shaped((clips, 3, width), F32)
     mods_out_spec = whole((clips, 3, width))
     grads_shape = (shards, 4, rows, width)
+    split_shape = (2, shards // 2, 4, rows, width)
     weight_scratch = [
         pltpu.VMEM((width, 3 * width), BF),
         pltpu.VMEM((width, width), BF),
@@ -582,17 +609,16 @@
     received = exchange(after_space).reshape(group_frames, columns, width)
     own_ids = jnp.concatenate([embed, timesteps.astype(F32)[:, None]], axis=1)
     own_ids, _ = lax.optimization_barrier((own_ids, after_space))
-    every_ids = lax.all_gather(own_ids, "grp", axis=0, tiled=True)
-    received, every_ids = lax.optimization_barrier((received, every_ids))
+    every_ids = every(own_ids).reshape(-1, own_ids.shape[1])
 
     cols_spec = whole((group_frames, columns, width))
     cols_shape = shaped((group_frames, columns, width), BF)
     block_shape = (steps, ROWS, width)
     time_keep, time_keep_specs = kept(steps)
     time_resid, after_time, *time_kept = run(
-        partial(time_forward_kernel, frames), steps, inverse,
-        [received, modul, time_w],
-        [cols_spec, mods_spec, ANY],
+        partial(time_forward_kernel, frames, shards), steps, inverse,
+        [received, modul] + time_w,
+        [cols_spec, mods_spec] + [ANY] * shards,
         [shaped(block_shape, BF), shaped(block_shape, F32)] + time_keep,
         [per_step(block_shape)] * 2 + time_keep_specs,
         weight_scratch + [pltpu.VMEM((ROWS, width), F32), dma(())],
@@ -637,37 +663,59 @@
     def shard_total(packed):
         return lax.psum_scatter(packed, "shard", scatter_dimension=0, tiled=True)[0]
 
-    groups = lax.axis_size("grp")
-    group_at = lax.axis_index("grp")
-
-    def swap_group(values, distance):
-        pairs = [(at, at ^ distance) for at in range(groups)]
-        return lax.ppermute(values, "grp", pairs)
-
-    def total(share):
+    def parts_of(share):
         parts = share.reshape(groups, -1, width)
 
-        def part(values, at):
-            return lax.dynamic_index_in_dim(values, at, 0, keepdims=False)
-
-        own = part(parts, group_at).astype(F32)
-        for distance in range(1, groups):
-            own = own + swap_group(part(parts, group_at ^ distance), distance).astype(F32)
+        def part(at):
+            return lax.dynamic_index_in_dim(parts, at, 0, keepdims=False)
+
+        return [part(group_at)] + [
+            swap_group(part(group_at ^ distance), distance) for distance in range(1, groups)
+        ]
+
+    def spread_parts(parts, share):
+        own = parts[0].astype(F32)
+        for piece in parts[1:]:
+            own = own + piece.astype(F32)
         own = own.astype(BF)
-        near = jnp.stack([own] + [swap_group(own, distance) for distance in range(1, groups)])
+        near = [own] + [swap_group(own, distance) for distance in range(1, groups)]
         step = 1
         while step < groups:
-            flipped = near.reshape(-1, 2, step, *own.shape)[:, ::-1].reshape(near.shape)
-            near = jnp.where(jnp.bitwise_and(group_at, step) > 0, flipped, near)
+            odd = jnp.bitwise_and(group_at, step) > 0
+            near = [jnp.where(odd, near[at ^ step], near[at]) for at in range(groups)]
             step *= 2
-        return near.reshape(share.shape).astype(F32)
+        return jnp.concatenate(near).reshape(share.shape).astype(F32)
+
+    def total(share):
+        return spread_parts(parts_of(share), share)
+
+    def halving(values, bits):
+        left = [bit for bit in range(shards.bit_length() - 2)]
+        blocks = values.shape[1:]
+        values = values.reshape((2,) * len(left) + blocks)
+        for bit in bits:
+            axis = len(left) - 1 - left.index(bit)
+            kept, sent = (lax.index_in_dim(values, side, axis, keepdims=False) for side in (0, 1))
+            values = (kept.astype(F32) + swap(sent, 2 << bit).astype(F32)).astype(BF)
+            left.remove(bit)
+        return values
+
+    def near_total(grads):
+        return (grads[0].astype(F32) + swap(grads[1], 1).astype(F32)).astype(BF)
+
+    def far_total(kept):
+        bits = list(range(shards.bit_length() - 2))
+        half = kept.shape[1] // 2
+        return jnp.concatenate(
+            [halving(kept[:, :half], bits), halving(kept[:, half:], bits[::-1])], axis=0
+        )
 
     feed_share = shard_total(feed_grads)
 
     going, time_mods, time_grads = run(
-        partial(time_backward_kernel, frames), steps, inverse,
-        [grad_after_time, time_resid, modul] + time_kept + [time_w],
-        [per_step(block_shape)] * 2 + [mods_spec] + time_keep_specs + [ANY],
+        partial(time_backward_kernel, frames, shards), steps, inverse,
+        [grad_after_time, time_resid, modul] + time_kept + time_w,
+        [per_step(block_shape)] * 2 + [mods_spec] + time_keep_specs + [ANY] * shards,
         [cols_shape, mods_out, shaped(grads_shape, BF)],
         [cols_spec, mods_out_spec, whole(grads_shape)],
         weight_scratch + back_scratch(steps) + [dma(())],
@@ -678,21 +726,25 @@
         (time_grads, feed_share, grad_space, result)
     )
     time_share = shard_total(time_grads)
+    feed_parts = parts_of(feed_share)
     arrived = exchange(result.reshape(own_shape))
     grad_rows, space_mods, space_grads = run(
         partial(space_backward_kernel, shards), frame_count, where,
         [grad_space, frames_in, modul] + space_kept + space_w,
         [own_spec, per_step(frames_in.shape), mods_spec] + space_keep_specs + [ANY] * shards,
-        [shaped(frames_in.shape, F32), mods_out, shaped(grads_shape, BF)],
-        [per_step(frames_in.shape), mods_out_spec, whole(grads_shape)],
+        [shaped(frames_in.shape, F32), mods_out, shaped(split_shape, BF)],
+        [per_step(frames_in.shape), mods_out_spec, whole(split_shape)],
         weight_scratch + back_scratch(frame_count) + [dma(())],
         3 * mixer_flops, "space_backward",
     )
-    space_grads, arrived = lax.optimization_barrier((space_grads, arrived))
-    space_share = shard_total(space_grads)
+    space_grads, space_mods, arrived, *feed_parts = lax.optimization_barrier(
+        (space_grads, space_mods, arrived, *feed_parts)
+    )
+    space_near = near_total(space_grads)
+    feed_share = spread_parts(feed_parts, feed_share)
     frames_out = to_rows(arrived)
-    feed_share, space_mods = lax.optimization_barrier((feed_share, space_mods))
-    feed_share = total(feed_share)
+    space_near, time_share = lax.optimization_barrier((space_near, time_share))
+    space_share = far_total(space_near)
     time_share = total(time_share)
     space_share = total(space_share)
 
@@ -715,7 +767,7 @@
     )
     small_size = small_grads.shape[0]
     small_grads = jnp.pad(small_grads, (0, -small_size % 1024)).reshape(1, -1, 128)
-    every_small = lax.all_gather(small_grads, "grp", axis=0, tiled=True).reshape(groups, -1)
+    every_small = every(small_grads).reshape(groups, -1)
     every_modul = every_small[:, :mod_size].reshape(groups * clips, 9 * width).astype(BF)
     bias_sums = jnp.sum(every_small[:, mod_size:small_size], axis=0)
     every_embed = every_ids[:, :-1]

time: 525 us -> 495 us (0.943)
  blocking collectives: 105 us -> 26.2 us
  waiting for transfers between devices: 131 us -> 158 us
  starting transfers between devices: 52.2 us -> 68.2 us
    all_gather x2 -> x0, blocking collectives: 44.2 us -> none  [the longest x1 32.9 us: body(): lax.all_gather(small_grads, 'grp', axis=0, tiled=True).reshape(groups, -1)]
    ppermute x10 -> x22, waiting for transfers between devices: 6.42 us -> 40.7 us  [swap(): return lax.ppermute(values, 'shard', pairs)]
    all_gather x2 -> x1, waiting for transfers between devices: 33.9 us -> 0.02 us  [gather(): return lax.all_gather(packed[None], 'shard', axis=0, tiled=True)]
    all_to_all x1 -> x0, blocking collectives: 32.7 us -> none  [exchange(): lax.all_to_all(parts, 'shard', split_axis=0, concat_axis=0, tiled=True)]
    all_to_all x3 -> x4, waiting for transfers between devices: 23.2 us -> 50.4 us  [exchange(): lax.all_to_all(parts, 'shard', split_axis=0, concat_axis=0, tiled=True)]
    ppermute x10 -> x22, starting transfers between devices: 9.75 us -> 18.5 us  [swap(): return lax.ppermute(values, 'shard', pairs)]
    all_to_all x3 -> x4, starting transfers between devices: 11.5 us -> 15.4 us  [exchange(): lax.all_to_all(parts, 'shard', split_axis=0, concat_axis=0, tiled=True)]
    ppermute x18 -> x24, starting transfers between devices: 30.7 us -> 33.7 us  [swap_group(): return lax.ppermute(values, 'grp', pairs)]
  transfers between devices with their start and end apart: 36 -> 53, of which waited for: 17 -> 21; matrix products, arithmetic and copies ran while one was open for 8% -> 10% of each run, Pallas kernels for 22% -> 24%
where the time goes in v3:
time: 495 us; the launch traced here: 488 us
  Pallas kernels  160 us (32%)
  waiting for transfers between devices  158 us (32%)
  starting transfers between devices  68.2 us (14%)
  local copies, waits for them, and re-layouts  33.9 us (7%)
  blocking collectives  26.2 us (5%)
  other arithmetic  21.6 us (4%)
  between operations  15.1 us (3%)
    pallas_call x5, Pallas kernels, run(): pl.pallas_call(kernel, grid_spec=pltpu.PrefetchScalarGridSpec(num_scalar_...  160 us
    all_to_all x4, waiting for transfers between devices, exchange(): lax.all_to_all(parts, 'shard', split_axis=0, concat_axis=0, tiled=True)  50.4 us
    ppermute x24, waiting for transfers between devices, swap_group(): return lax.ppermute(values, 'grp', pairs)  44.8 us
    ppermute x22, waiting for transfers between devices, swap(): return lax.ppermute(values, 'shard', pairs)  40.7 us
    ppermute x24, starting transfers between devices, swap_group(): return lax.ppermute(values, 'grp', pairs)  33.7 us
    all_gather x1, blocking collectives, body(): lax.all_gather(small.reshape(1, -1, 128), 'shard', axis=0, tiled=True)  26.2 us
    reduce_scatter x2, waiting for transfers between devices, shard_total(): return lax.psum_scatter(packed, 'shard', scatter_dimension=0, tiled=True)[0]  22.3 us
    ppermute x22, starting transfers between devices, swap(): return lax.ppermute(values, 'shard', pairs)  18.5 us
  transfers between devices with their start and end apart: 53, of which 21 were waited for; matrix products, arithmetic and copies ran while one was open for 10% of the time, Pallas kernels for 24%

profile of v3, /device:TPU:0, one launch (start us, length us, event | category | flops | bytes accessed | tf_op | source)
XLA Modules:
  0.0 487.7 jit_solution(8372940213967458558)
XLA Ops:
  7.3 1.1 copy.117
  8.5 1.8 pad_maximum_fusion.1.refs_0_
  10.3 3.9 collective-permute-start.5
  20.0 26.2 %all_gather.6 = f32[8,138,128]{2,1,0:T(8,128)S(1)} all-gather(f32[1,138,128]{2,1,0:T(8,128)S(1)} %maximum_bitcast_fusion), channel_id=1, replica_groups=mesh['grp'=4,'shard'=8] {'shard'}, dimensions={0}, use_global_device_ids=true | all-gather | bytes 635904 | tf_op jit(solution)/shard_map/all_gather | solution.py:535
  46.9 1.2 copy.91
  53.1 18.8 %space_forward.1 = (bf16[8,4,32,768]{3,2,1,0:T(8,128)(2,1)}, bf16[4,256,2304]{2,1,0:T(8,128)(2,1)}, bf16[4,256,768]{2,1,0:T(8,128)(2,1)}, f32[4,16,256]{2,1,0:T(8,128)}, bf16[4,256,768]{2,1,0:T(8,128)(2,1)}) custom-call(s32[5]{0:T(128)} %pad_add_fusion.where, f32[4,256,768]{2,1,0:T(8,128)} %frames_ref.3, f32[2,9,768]{2,1,0:T(8,128)} %reshape.308.mods_ref, ...), custom_call_target="tpu_custom_call" | custom-call | flops 6442450944 | bytes 17422336 | tf_op jit(solution)/shard_map/space_forward/pallas_call | solution.py:426
  72.0 3.6 all-to-all-start
  76.9 2.8 collective-permute-start.12
  80.4 2.2 multiply_convert_fusion
  82.6 1.2 copy.115
  83.8 29.2 %all-to-all-done = bf16[8,4,32,768]{3,2,1,0:T(8,128)(2,1)S(1)} async-done(((bf16[8,4,32,768]{3,2,1,0:T(8,128)(2,1)}), bf16[8,4,32,768]{3,2,1,0:T(8,128)(2,1)S(1)}, u32[]{:S(2)}, u32[]{:S(2)}) %all-to-all-start) | async-done | bytes 1572896 | tf_op jit(solution)/shard_map/all_to_all | solution.py:561
  113.1 1.1 copy-done.6
  114.2 4.4 all-to-all-start.1
  119.6 15.5 %collective-permute-done.12.refs_6_ = bf16[4,96,768]{2,1,0:T(8,128)(2,1)} collective-permute-done((bf16[4,96,768]{2,1,0:T(8,128)(2,1)S(1)}, bf16[4,96,768]{2,1,0:T(8,128)(2,1)}, u32[]{:S(2)}, u32[]{:S(2)}) %collective-permute-start.12) | collective-permute-done | bytes 589856 | tf_op jit(solution)/shard_map/ppermute | solution.py:480
  135.1 6.7 %collective-permute-done.10.refs_4_ = bf16[4,96,768]{2,1,0:T(8,128)(2,1)} collective-permute-done((bf16[4,96,768]{2,1,0:T(8,128)(2,1)S(1)}, bf16[4,96,768]{2,1,0:T(8,128)(2,1)}, u32[]{:S(2)}, u32[]{:S(2)}) %collective-permute-start.10) | collective-permute-done | bytes 589856 | tf_op jit(solution)/shard_map/ppermute | solution.py:480
  141.8 5.0 %collective-permute-done.8.refs_2_ = bf16[4,96,768]{2,1,0:T(8,128)(2,1)} collective-permute-done((bf16[4,96,768]{2,1,0:T(8,128)(2,1)S(1)}, bf16[4,96,768]{2,1,0:T(8,128)(2,1)}, u32[]{:S(2)}, u32[]{:S(2)}) %collective-permute-start.8) | collective-permute-done | bytes 589856 | tf_op jit(solution)/shard_map/ppermute | solution.py:480
  147.5 1.3 slice.145
  151.1 19.0 %time_forward.1 = (bf16[4,256,768]{2,1,0:T(8,128)(2,1)}, f32[4,256,768]{2,1,0:T(8,128)}, bf16[4,256,2304]{2,1,0:T(8,128)(2,1)}, bf16[4,256,768]{2,1,0:T(8,128)(2...) custom-call(s32[33]{0:T(128)} %pad_add_fusion.1.inverse, bf16[32,32,768]{2,1,0:T(8,128)(2,1)} %bitcast.203, ...), custom_call_target="tpu_custom_call" | custom-call | flops 6442450944 | bytes 18995200 | tf_op jit(solution)/shard_map/time_forward/pallas_call | solution.py:426
  170.1 43.5 %feed.1 = (bf16[32,32,768]{2,1,0:T(8,128)(2,1)}, f32[4,256,768]{2,1,0:T(8,128)}, f32[2,3,768]{2,1,0:T(4,128)}, f32[1,3072]{1,0:T(1,128)}, f32[1,768]{1,0:T(1,128)}, /*index=5*/bf16[8,8,96,768]{3,2,1,0:T(8,128)(2,1)}) custom-call(s32[33]{0:T(128)} %pad_add_fusion.1.inverse, f32[4,256,768]{2,1,0:T(8,128)} %get-tuple-element.58.after_ref, ...), custom_call_target="tpu_custom_call" | custom-call | flops 28991029248 | bytes 28416000 | tf_op jit(solution)/shard_map/feed/pallas_call | solution.py:426
  213.7 39.0 %time_backward.1 = (bf16[32,32,768]{2,1,0:T(8,128)(2,1)}, f32[2,3,768]{2,1,0:T(4,128)}, bf16[8,4,96,768]{3,2,1,0:T(8,128)(2,1)}) custom-call(s32[33]{0:T(128)} %pad_add_fusion.1.inverse, f32[4,256,768]{2,1,0:T(8,128)} %get-tuple-element.60.grad_ref, bf16[4,256,768]{2,1,0:T(8,128)(2,1)} %get-tuple-element.61.resid_ref, f32[2,9,768]{2,1,0:T(8,128)} %reshape.308.mods_ref, ...), custom_call_target="tpu_custom_call" | custom-call | flops 19327352832 | bytes 23732224 | tf_op jit(solution)/shard_map/time_backward/pallas_call | solution.py:426
  252.7 3.6 all-to-all-start.2
  256.6 3.6 collective-permute-start.19
  261.0 2.8 collective-permute-done.17
  264.7 21.1 %all-to-all-done.2.grad_ref = bf16[8,4,32,768]{3,2,1,0:T(8,128)(2,1)S(1)} async-done(((bf16[8,4,32,768]{3,2,1,0:T(8,128)(2,1)}), bf16[8,4,32,768]{3,2,1,0:T(8,128)(2,1)S(1)}, u32[]{:S(2)}, u32[]{:S(2)}) %all-to-all-start.2) | async-done | bytes 1572896 | tf_op jit(solution)/shard_map/all_to_all | solution.py:561
  285.8 22.3 %reduce-scatter.3.cloned.1.call-done = bf16[1,8,96,768]{3,2,1,0:T(8,128)(2,1)} async-done(((bf16[8,8,96,768]{3,2,1,0:T(8,128)(2,1)}), bf16[1,8,96,768]{3,2,1,0:T(8,128)(2,1)}) %reduce-scatter.3.cloned.1.call-update) | async-done | bytes 1179664 | tf_op jit(solution)/shard_map/reduce_scatter | solution.py:664
  308.9 3.8 all-to-all-start.3
  312.7 2.2 dynamic-slice_bitcast_fusion
  314.9 3.3 collective-permute-start.16
  319.3 40.1 %space_backward.1 = (f32[4,256,768]{2,1,0:T(8,128)}, f32[2,3,768]{2,1,0:T(4,128)}, bf16[2,4,4,96,768]{4,3,2,1,0:T(8,128)(2,1)}) custom-call(s32[5]{0:T(128)} %pad_add_fusion.where, bf16[8,4,32,768]{3,2,1,0:T(8,128)(2,1)} %copy-done.5, f32[4,256,768]{2,1,0:T(8,128)} %frames_ref.3, f32[2,9,768]{2,1,0:T(8,128)} %reshape.308.mods_ref, ...), custom_call_target="tpu_custom_call" | custom-call | flops 19327352832 | bytes 25305088 | tf_op jit(solution)/shard_map/space_backward/pallas_call | solution.py:426
  361.8 1.3 add_convert_fusion.1
  363.1 1.1 collective-permute-start.45
  364.2 2.9 collective-permute-start.44
  368.3 2.0 collective-permute-start.21
  370.3 3.2 slice_bitcast_fusion
  373.5 1.6 collective-permute-start.22
  375.4 2.0 copy.92
  378.4 10.1 %collective-permute-done.23 = f32[1,112,128]{2,1,0:T(8,128)S(1)} collective-permute-done((f32[1,112,128]{2,1,0:T(8,128)S(1)}, f32[1,112,128]{2,1,0:T(8,128)S(1)}, u32[]{:S(2)}, u32[]{:S(2)}) %collective-permute-start.23) | collective-permute-done | bytes 57376 | tf_op jit(solution)/shard_map/ppermute | solution.py:490
  388.9 7.1 %collective-permute-done.24 = f32[1,112,128]{2,1,0:T(8,128)S(1)} collective-permute-done((f32[1,112,128]{2,1,0:T(8,128)S(1)}, f32[1,112,128]{2,1,0:T(8,128)S(1)}, u32[]{:S(2)}, u32[]{:S(2)}) %collective-permute-start.24) | collective-permute-done | bytes 57376 | tf_op jit(solution)/shard_map/ppermute | solution.py:490
  396.0 2.4 collective-permute-start.25
  398.4 3.5 collective-permute-done.25
  402.6 1.3 fusion.4
  405.2 2.1 fusion.27
  407.2 1.4 broadcast_select_fusion.7
  408.6 1.5 maximum_convert_fusion
  410.2 3.7 fusion
  413.9 1.1 slice.121
  415.0 2.0 collective-permute-start.29
  417.0 2.8 fusion.45
  419.8 1.1 copy.105
  422.0 1.5 collective-permute-start.27
  423.7 2.5 collective-permute-start.39
  427.1 1.8 collective-permute-done.29
  429.1 1.8 collective-permute-start.30
  430.9 7.4 %collective-permute-done.27 = bf16[2,2,96,768]{3,2,1,0:T(8,128)(2,1)S(1)} collective-permute-done((bf16[2,2,96,768]{3,2,1,0:T(8,128)(2,1)S(1)}, bf16[2,2,96,768]{3,2,1,0:T(8,128)(2,1)S(1)}, u32[]{:S(2)}, u32[]{:S(2)}) %collective-permute-start.27) | collective-permute-done | bytes 589856 | tf_op jit(solution)/shard_map/ppermute | solution.py:480
  438.8 3.0 collective-permute-start.41
  441.8 1.4 collective-permute-start.40
  443.3 2.0 collective-permute-done.28
  445.6 3.0 collective-permute-start.32
  448.6 1.8 collective-permute-start.33
  450.4 2.5 collective-permute-done.41
  452.9 10.6 %collective-permute-done.32 = bf16[96,768]{1,0:T(8,128)(2,1)S(1)} collective-permute-done((bf16[96,768]{1,0:T(8,128)(2,1)S(1)}, bf16[96,768]{1,0:T(8,128)(2,1)S(1)}, u32[]{:S(2)}, u32[]{:S(2)}) %collective-permute-start.32) | collective-permute-done | bytes 147488 | tf_op jit(solution)/shard_map/ppermute | solution.py:490
  463.6 2.2 collective-permute-start.36
  466.9 1.4 collective-permute-start.34
  470.9 7.3 %collective-permute-done.35 = bf16[96,768]{1,0:T(8,128)(2,1)S(1)} collective-permute-done((bf16[96,768]{1,0:T(8,128)(2,1)S(1)}, bf16[96,768]{1,0:T(8,128)(2,1)S(1)}, u32[]{:S(2)}, u32[]{:S(2)}) %collective-permute-start.35) | collective-permute-done | bytes 147488 | tf_op jit(solution)/shard_map/ppermute | solution.py:490
  (246 shorter events, 37.7 us)
Async XLA Ops:
  7.2 9.2 %copy-start = (bf16[96,6912]{1,0:T(8,128)(2,1)S(1)}, bf16[96,6912]{1,0:T(8,128)(2,1)}, u32[]{:S(2)}) copy-start(bf16[96,6912]{1,0:T(8,128)(2,1)} %param.20) | copy-start | bytes 3981316
  7.2 8.4 %copy-start.15 = (bf16[1000,96]{0,1:T(8,128)(2,1)S(1)}, bf16[1000,96]{0,1:T(8,128)(2,1)}, u32[]{:S(2)}) copy-start(bf16[1000,96]{0,1:T(8,128)(2,1)} %param.19) | copy-start | bytes 576004
  7.2 162.9 %all-gather.3.cloned.1.call-start = ((), (), s32[]{:S(2)}) async-start(), calls=%async_computation.8 | async-start | bytes 10616832 | tf_op jit(solution)/shard_map/all_gather | solution.py:483
  8.4 9.8 %copy-start.11 = (bf16[96,2304]{1,0:T(8,128)(2,1)S(1)}, bf16[96,2304]{1,0:T(8,128)(2,1)}, u32[]{:S(2)}) copy-start(bf16[96,2304]{1,0:T(8,128)(2,1)} %param.24) | copy-start | bytes 1327108
  10.3 36.6 %collective-permute-start.5 = (bf16[4,96,768]{2,1,0:T(8,128)(2,1)}, bf16[4,96,768]{2,1,0:T(8,128)(2,1)}, u32[]{:S(2)}, u32[]{:S(2)}) collective-permute-start(bf16[4,96,768]{2,1,0:T(8,128)(2,1)} %pad_maximum_fusion.1.refs_0_), channel_id=1, source_target_pairs={{0,6},{1,7},{2,4},{3,5},{4,2},{5,3},{6,0},{7,1},{8,14},{9,15},{10,... | collective-permute-start | bytes 1769480 | tf_op jit(solution)/shard_map/ppermute | solution.py:480
  14.2 32.7 %collective-permute-start.3 = (bf16[4,96,768]{2,1,0:T(8,128)(2,1)}, bf16[4,96,768]{2,1,0:T(8,128)(2,1)}, u32[]{:S(2)}, u32[]{:S(2)}) collective-permute-start(bf16[4,96,768]{2,1,0:T(8,128)(2,1)} %pad_maximum_fusion.1.refs_0_), channel_id=1, source_target_pairs={{0,4},{1,5},{2,6},{3,7},{4,0},{5,1},{6,2},{7,3},{8,12},{9,13},{10,... | collective-permute-start | bytes 1769480 | tf_op jit(solution)/shard_map/ppermute | solution.py:480
  14.7 32.2 %collective-permute-start = (bf16[4,96,768]{2,1,0:T(8,128)(2,1)}, bf16[4,96,768]{2,1,0:T(8,128)(2,1)}, u32[]{:S(2)}, u32[]{:S(2)}) collective-permute-start(bf16[4,96,768]{2,1,0:T(8,128)(2,1)} %pad_maximum_fusion.1.refs_0_), channel_id=1, source_target_pairs={{0,2},{1,3},{2,0},{3,1},{4,6},{5,7},{6,4},{7,5},{8,10},{9,11},{10,... | collective-permute-start | bytes 1769480 | tf_op jit(solution)/shard_map/ppermute | solution.py:480
  18.7 27.5 %copy-start.16 = (bf16[96,768]{1,0:T(8,128)(2,1)S(1)}, bf16[96,768]{1,0:T(8,128)(2,1)}, u32[]{:S(2)}) copy-start(bf16[96,768]{1,0:T(8,128)(2,1)} %param.25) | copy-start | bytes 442372
  46.3 72.9 %copy-start.10 = (bf16[4,96,768]{2,1,0:T(8,128)(2,1)}, bf16[4,96,768]{2,1,0:T(8,128)(2,1)S(1)}, u32[]{:S(2)}) copy-start(bf16[4,96,768]{2,1,0:T(8,128)(2,1)S(1)} %pad_maximum_fusion.2.refs_0_) | copy-start | bytes 1769476
  48.2 3.1 collective-permute-start.1
  48.6 2.8 collective-permute-start.6
  48.7 3.5 collective-permute-start.4
  49.1 4.0 collective-permute-start.2
  50.6 21.4 %copy-start.12 = (f32[138,128]{1,0:T(8,128)}, f32[138,128]{1,0:T(8,128)S(1)}, u32[]{:S(2)}) copy-start(f32[138,128]{1,0:T(8,128)S(1)} %reduce_sum.37) | copy-start | bytes 211972
  72.0 41.1 %all-to-all-start = ((bf16[8,4,32,768]{3,2,1,0:T(8,128)(2,1)}), bf16[8,4,32,768]{3,2,1,0:T(8,128)(2,1)S(1)}, u32[]{:S(2)}, u32[]{:S(2)}) async-start(bf16[8,4,32,768]{3,2,1,0:T(8,128)(2,1)} %get-tuple-element.56), calls=%async_computation | async-start | bytes 3145728 | tf_op jit(solution)/shard_map/all_to_all | solution.py:561
  76.9 58.1 %collective-permute-start.12 = (bf16[4,96,768]{2,1,0:T(8,128)(2,1)S(1)}, bf16[4,96,768]{2,1,0:T(8,128)(2,1)}, u32[]{:S(2)}, u32[]{:S(2)}) collective-permute-start(bf16[4,96,768]{2,1,0:T(8,128)(2,1)S(1)} %pad_maximum_fusion.2.refs_0_), channel_id=1, source_target_pairs={{0,6},{1,7},{2,4},{3,5},{4,2},{5,3},{6,0},{7,1},{8,14},{9,15},{10,... | collective-permute-start | bytes 1769480 | tf_op jit(solution)/shard_map/ppermute | solution.py:480
  79.8 62.0 %collective-permute-start.10 = (bf16[4,96,768]{2,1,0:T(8,128)(2,1)S(1)}, bf16[4,96,768]{2,1,0:T(8,128)(2,1)}, u32[]{:S(2)}, u32[]{:S(2)}) collective-permute-start(bf16[4,96,768]{2,1,0:T(8,128)(2,1)S(1)} %pad_maximum_fusion.2.refs_0_), channel_id=1, source_target_pairs={{0,4},{1,5},{2,6},{3,7},{4,0},{5,1},{6,2},{7,3},{8,12},{9,13},{10,... | collective-permute-start | bytes 1769480 | tf_op jit(solution)/shard_map/ppermute | solution.py:480
  80.3 66.5 %collective-permute-start.8 = (bf16[4,96,768]{2,1,0:T(8,128)(2,1)S(1)}, bf16[4,96,768]{2,1,0:T(8,128)(2,1)}, u32[]{:S(2)}, u32[]{:S(2)}) collective-permute-start(bf16[4,96,768]{2,1,0:T(8,128)(2,1)S(1)} %pad_maximum_fusion.2.refs_0_), channel_id=1, source_target_pairs={{0,2},{1,3},{2,0},{3,1},{4,6},{5,7},{6,4},{7,5},{8,10},{9,11},{10,... | collective-permute-start | bytes 1769480 | tf_op jit(solution)/shard_map/ppermute | solution.py:480
  114.2 55.9 %all-to-all-start.1 = ((bf16[8,4,32,768]{3,2,1,0:T(8,128)(2,1)}), bf16[8,4,32,768]{3,2,1,0:T(8,128)(2,1)}, u32[]{:S(2)}, u32[]{:S(2)}) async-start(bf16[8,4,32,768]{3,2,1,0:T(8,128)(2,1)} %bitcast.177), calls=%async_computation.1 | async-start | bytes 3145728 | tf_op jit(solution)/shard_map/all_to_all | solution.py:561
  118.6 189.5 %reduce-scatter.3.cloned.1.call-start = ((), (), s32[]{:S(2)}) async-start(), calls=%async_computation.6 | async-start | bytes 10616832 | tf_op jit(solution)/shard_map/reduce_scatter | solution.py:664
  119.2 30.9 %collective-permute-start.7 = (bf16[4,96,768]{2,1,0:T(8,128)(2,1)S(1)}, bf16[4,96,768]{2,1,0:T(8,128)(2,1)S(1)}, u32[]{:S(2)}, u32[]{:S(2)}) collective-permute-start(bf16[4,96,768]{2,1,0:T(8,128)(2,1)S(1)} %pad_maximum_fusion.2.refs_0_), channel_id=1, source_target_pairs={{0,1},{1,0},{2,3},{3,2},{4,5},{5,4},{6,7},{7,6},{8,9},{9,8},{10,11... | collective-permute-start | bytes 1769480 | tf_op jit(solution)/shard_map/ppermute | solution.py:480
  135.1 15.0 %collective-permute-start.13 = (bf16[4,96,768]{2,1,0:T(8,128)(2,1)}, bf16[4,96,768]{2,1,0:T(8,128)(2,1)S(1)}, u32[]{:S(2)}, u32[]{:S(2)}) collective-permute-start(bf16[4,96,768]{2,1,0:T(8,128)(2,1)} %collective-permute-done.12.refs_6_), channel_id=1, source_target_pairs={{0,1},{1,0},{2,3},{3,2},{4,5},{5,4},{6,7},{7,6},{8,9},{9,8},{10,11... | collective-permute-start | bytes 1769480 | tf_op jit(solution)/shard_map/ppermute | solution.py:480
  141.8 8.3 %collective-permute-start.11 = (bf16[4,96,768]{2,1,0:T(8,128)(2,1)}, bf16[4,96,768]{2,1,0:T(8,128)(2,1)}, u32[]{:S(2)}, u32[]{:S(2)}) collective-permute-start(bf16[4,96,768]{2,1,0:T(8,128)(2,1)} %collective-permute-done.10.refs_4_), channel_id=1, source_target_pairs={{0,1},{1,0},{2,3},{3,2},{4,5},{5,4},{6,7},{7,6},{8,9},{9,8},{10,11... | collective-permute-start | bytes 1769480 | tf_op jit(solution)/shard_map/ppermute | solution.py:480
  146.8 3.3 collective-permute-start.9
  252.7 33.1 %all-to-all-start.2 = ((bf16[8,4,32,768]{3,2,1,0:T(8,128)(2,1)}), bf16[8,4,32,768]{3,2,1,0:T(8,128)(2,1)S(1)}, u32[]{:S(2)}, u32[]{:S(2)}) async-start(bf16[8,4,32,768]{3,2,1,0:T(8,128)(2,1)} %bitcast.202), calls=%async_computation.3 | async-start | bytes 3145728 | tf_op jit(solution)/shard_map/all_to_all | solution.py:561
  256.3 157.6 %reduce-scatter.5.cloned.1.call-start = ((), (), s32[]{:S(2)}) async-start(), calls=%async_computation.7 | async-start | bytes 5308416 | tf_op jit(solution)/shard_map/reduce_scatter | solution.py:664
  256.6 51.5 %collective-permute-start.19 = (f32[2,97]{1,0:T(2,128)S(1)}, f32[2,97]{1,0:T(2,128)S(1)}, u32[]{:S(2)}, u32[]{:S(2)}) collective-permute-start(f32[2,97]{1,0:T(2,128)S(1)} %pad_maximum_fusion.4), channel_id=1, source_target_pairs={{0,24},{8,16},{16,8},{24,0},{1,25},{9,17},{17,9},{25,1},{2,26},{10... | collective-permute-start | bytes 2336 | tf_op jit(solution)/shard_map/ppermute | solution.py:490
  260.2 4.5 collective-permute-start.18
  260.2 3.6 collective-permute-start.17
  285.8 22.3 %copy-start.5 = (bf16[8,4,32,768]{3,2,1,0:T(8,128)(2,1)}, bf16[8,4,32,768]{3,2,1,0:T(8,128)(2,1)S(1)}, u32[]{:S(2)}) copy-start(bf16[8,4,32,768]{3,2,1,0:T(8,128)(2,1)S(1)} %all-to-all-done.2.grad_ref) | copy-start | bytes 4718596
  308.9 51.3 %all-to-all-start.3 = ((bf16[8,4,32,768]{3,2,1,0:T(8,128)(2,1)}), bf16[8,4,32,768]{3,2,1,0:T(8,128)(2,1)S(1)}, u32[]{:S(2)}, u32[]{:S(2)}) async-start(bf16[8,4,32,768]{3,2,1,0:T(8,128)(2,1)} %bitcast.201), calls=%async_computation.4 | async-start | bytes 3145728 | tf_op jit(solution)/shard_map/all_to_all | solution.py:561
  314.9 44.5 %collective-permute-start.16 = (bf16[192,768]{1,0:T(8,128)(2,1)}, bf16[192,768]{1,0:T(8,128)(2,1)S(1)}, u32[]{:S(2)}, u32[]{:S(2)}) collective-permute-start(bf16[192,768]{1,0:T(8,128)(2,1)} %get-tuple-element.101), channel_id=1, source_target_pairs={{0,24},{8,16},{16,8},{24,0},{1,25},{9,17},{17,9},{25,1},{2,26},{10... | collective-permute-start | bytes 884744 | tf_op jit(solution)/shard_map/ppermute | solution.py:490
  318.2 41.2 %collective-permute-start.15 = (bf16[192,768]{1,0:T(8,128)(2,1)}, bf16[192,768]{1,0:T(8,128)(2,1)S(1)}, u32[]{:S(2)}, u32[]{:S(2)}) collective-permute-start(bf16[192,768]{1,0:T(8,128)(2,1)} %get-tuple-element.102), channel_id=1, source_target_pairs={{0,16},{8,24},{16,0},{24,8},{1,17},{9,25},{17,1},{25,9},{2,18},{10... | collective-permute-start | bytes 884744 | tf_op jit(solution)/shard_map/ppermute | solution.py:490
  318.2 42.0 %collective-permute-start.14 = (bf16[192,768]{1,0:T(8,128)(2,1)}, bf16[192,768]{1,0:T(8,128)(2,1)}, u32[]{:S(2)}, u32[]{:S(2)}) collective-permute-start(bf16[192,768]{1,0:T(8,128)(2,1)} %get-tuple-element.103), channel_id=1, source_target_pairs={{0,8},{8,0},{16,24},{24,16},{1,9},{9,1},{17,25},{25,17},{2,10},{10... | collective-permute-start | bytes 884744 | tf_op jit(solution)/shard_map/ppermute | solution.py:490
  319.2 41.0 %copy-start.18 = (f32[2,3,768]{2,1,0:T(4,128)S(1)}, f32[2,3,768]{2,1,0:T(4,128)}, u32[]{:S(2)}) copy-start(f32[2,3,768]{2,1,0:T(4,128)} %get-tuple-element.84) | copy-start | bytes 55300
  319.3 41.0 %copy-start.19 = (f32[2,3,768]{2,1,0:T(4,128)S(1)}, f32[2,3,768]{2,1,0:T(4,128)}, u32[]{:S(2)}) copy-start(f32[2,3,768]{2,1,0:T(4,128)} %get-tuple-element.83) | copy-start | bytes 55300
  361.8 5.8 %collective-permute-start.20 = (f32[138,128]{1,0:T(8,128)S(1)}, f32[138,128]{1,0:T(8,128)S(1)}, u32[]{:S(2)}, u32[]{:S(2)}) collective-permute-start(f32[138,128]{1,0:T(8,128)S(1)} %maximum_bitcast_fusion.1), channel_id=1, source_target_pairs={{0,1},{1,0},{2,3},{3,2},{4,5},{5,4},{6,7},{7,6},{8,9},{9,8},{10,11... | collective-permute-start | bytes 211976 | tf_op jit(solution)/shard_map/ppermute | solution.py:480
  363.1 44.1 %collective-permute-start.45 = (bf16[192,768]{1,0:T(8,128)(2,1)S(1)}, bf16[192,768]{1,0:T(8,128)(2,1)}, u32[]{:S(2)}, u32[]{:S(2)}) collective-permute-start(bf16[192,768]{1,0:T(8,128)(2,1)S(1)} %add_convert_fusion.1), channel_id=1, source_target_pairs={{0,8},{8,0},{16,24},{24,16},{1,9},{9,1},{17,25},{25,17},{2,10},{10... | collective-permute-start | bytes 884744 | tf_op jit(solution)/shard_map/ppermute | solution.py:490
  364.2 43.0 %collective-permute-start.44 = (bf16[192,768]{1,0:T(8,128)(2,1)S(1)}, bf16[192,768]{1,0:T(8,128)(2,1)}, u32[]{:S(2)}, u32[]{:S(2)}) collective-permute-start(bf16[192,768]{1,0:T(8,128)(2,1)S(1)} %add_convert_fusion.1), channel_id=1, source_target_pairs={{0,16},{8,24},{16,0},{24,8},{1,17},{9,25},{17,1},{25,9},{2,18},{10... | collective-permute-start | bytes 884744 | tf_op jit(solution)/shard_map/ppermute | solution.py:490
  367.1 40.1 %collective-permute-start.43 = (bf16[192,768]{1,0:T(8,128)(2,1)S(1)}, bf16[192,768]{1,0:T(8,128)(2,1)}, u32[]{:S(2)}, u32[]{:S(2)}) collective-permute-start(bf16[192,768]{1,0:T(8,128)(2,1)S(1)} %add_convert_fusion.1), channel_id=1, source_target_pairs={{0,24},{8,16},{16,8},{24,0},{1,25},{9,17},{17,9},{25,1},{2,26},{10... | collective-permute-start | bytes 884744 | tf_op jit(solution)/shard_map/ppermute | solution.py:490
  368.3 5.2 %collective-permute-start.21 = (f32[138,128]{1,0:T(8,128)S(1)}, f32[138,128]{1,0:T(8,128)S(1)}, u32[]{:S(2)}, u32[]{:S(2)}) collective-permute-start(f32[138,128]{1,0:T(8,128)S(1)} %fusion.44), channel_id=1, source_target_pairs={{0,2},{1,3},{2,0},{3,1},{4,6},{5,7},{6,4},{7,5},{8,10},{9,11},{10,... | collective-permute-start | bytes 211976 | tf_op jit(solution)/shard_map/ppermute | solution.py:480
  373.5 4.4 collective-permute-start.22
  377.5 32.7 %collective-permute-start.26 = (bf16[4,4,96,768]{3,2,1,0:T(8,128)(2,1)}, bf16[4,4,96,768]{3,2,1,0:T(8,128)(2,1)}, u32[]{:S(2)}, u32[]{:S(2)}) collective-permute-start(bf16[4,4,96,768]{3,2,1,0:T(8,128)(2,1)} %slice_bitcast_fusion), channel_id=1, source_target_pairs={{0,1},{1,0},{2,3},{3,2},{4,5},{5,4},{6,7},{7,6},{8,9},{9,8},{10,11... | collective-permute-start | bytes 7077896 | tf_op jit(solution)/shard_map/ppermute | solution.py:480
  378.1 24.5 %copy-start.24 = (s32[8]{0:T(128)S(1)}, s32[8]{0:T(128)}, u32[]{:S(2)}) copy-start(s32[8]{0:T(128)} %convert_reduce_fusion.1) | copy-start | bytes 100
  378.1 10.4 %collective-permute-start.23 = (f32[1,112,128]{2,1,0:T(8,128)S(1)}, f32[1,112,128]{2,1,0:T(8,128)S(1)}, u32[]{:S(2)}, u32[]{:S(2)}) collective-permute-start(f32[1,112,128]{2,1,0:T(8,128)S(1)} %fusion.20), channel_id=1, source_target_pairs={{0,8},{8,0},{16,24},{24,16},{1,9},{9,1},{17,25},{25,17},{2,10},{10... | collective-permute-start | bytes 172040 | tf_op jit(solution)/shard_map/ppermute | solution.py:490
  388.5 7.5 %collective-permute-start.24 = (f32[1,112,128]{2,1,0:T(8,128)S(1)}, f32[1,112,128]{2,1,0:T(8,128)S(1)}, u32[]{:S(2)}, u32[]{:S(2)}) collective-permute-start(f32[1,112,128]{2,1,0:T(8,128)S(1)} %fusion.20), channel_id=1, source_target_pairs={{0,16},{8,24},{16,0},{24,8},{1,17},{9,25},{17,1},{25,9},{2,18},{10... | collective-permute-start | bytes 172040 | tf_op jit(solution)/shard_map/ppermute | solution.py:490
  388.9 21.2 %slice-start = ((s8[4718592]{0:T(1024)(128)(4,1)}), s8[524288]{0:T(1024)(128)(4,1)S(1)}, s32[]{:S(2)}) async-start(s8[4718592]{0:T(1024)(128)(4,1)} %bitcast.188), calls=%async_computation.9 | async-start | bytes 1048576
  396.0 6.0 %collective-permute-start.25 = (f32[1,112,128]{2,1,0:T(8,128)S(1)}, f32[1,112,128]{2,1,0:T(8,128)S(1)}, u32[]{:S(2)}, u32[]{:S(2)}) collective-permute-start(f32[1,112,128]{2,1,0:T(8,128)S(1)} %fusion.20), channel_id=1, source_target_pairs={{0,24},{8,16},{16,8},{24,0},{1,25},{9,17},{17,9},{25,1},{2,26},{10... | collective-permute-start | bytes 172040 | tf_op jit(solution)/shard_map/ppermute | solution.py:490
  415.0 13.9 %collective-permute-start.29 = (bf16[2,2,96,768]{3,2,1,0:T(8,128)(2,1)S(1)}, bf16[2,2,96,768]{3,2,1,0:T(8,128)(2,1)S(1)}, u32[]{:S(2)}, u32[]{:S(2)}) collective-permute-start(bf16[2,2,96,768]{3,2,1,0:T(8,128)(2,1)S(1)} %slice.121), channel_id=1, source_target_pairs={{0,4},{1,5},{2,6},{3,7},{4,0},{5,1},{6,2},{7,3},{8,12},{9,13},{10,... | collective-permute-start | bytes 1769480 | tf_op jit(solution)/shard_map/ppermute | solution.py:480
  422.0 16.3 %collective-permute-start.27 = (bf16[2,2,96,768]{3,2,1,0:T(8,128)(2,1)S(1)}, bf16[2,2,96,768]{3,2,1,0:T(8,128)(2,1)S(1)}, u32[]{:S(2)}, u32[]{:S(2)}) collective-permute-start(bf16[2,2,96,768]{3,2,1,0:T(8,128)(2,1)S(1)} %slice_bitcast_fusion.1), channel_id=1, source_target_pairs={{0,2},{1,3},{2,0},{3,1},{4,6},{5,7},{6,4},{7,5},{8,10},{9,11},{10,... | collective-permute-start | bytes 1769480 | tf_op jit(solution)/shard_map/ppermute | solution.py:480
  423.6 15.1 %collective-permute-start.37 = (bf16[96,768]{1,0:T(8,128)(2,1)S(1)}, bf16[96,768]{1,0:T(8,128)(2,1)S(1)}, u32[]{:S(2)}, u32[]{:S(2)}) collective-permute-start(bf16[96,768]{1,0:T(8,128)(2,1)S(1)} %get-tuple-element.109), channel_id=1, source_target_pairs={{0,8},{8,0},{16,24},{24,16},{1,9},{9,1},{17,25},{25,17},{2,10},{10... | collective-permute-start | bytes 442376 | tf_op jit(solution)/shard_map/ppermute | solution.py:490
  423.7 15.0 %collective-permute-start.39 = (bf16[96,768]{1,0:T(8,128)(2,1)S(1)}, bf16[96,768]{1,0:T(8,128)(2,1)S(1)}, u32[]{:S(2)}, u32[]{:S(2)}) collective-permute-start(bf16[96,768]{1,0:T(8,128)(2,1)S(1)} %get-tuple-element.110), channel_id=1, source_target_pairs={{0,24},{8,16},{16,8},{24,0},{1,25},{9,17},{17,9},{25,1},{2,26},{10... | collective-permute-start | bytes 442376 | tf_op jit(solution)/shard_map/ppermute | solution.py:490
  426.2 12.5 %collective-permute-start.38 = (bf16[96,768]{1,0:T(8,128)(2,1)S(1)}, bf16[96,768]{1,0:T(8,128)(2,1)S(1)}, u32[]{:S(2)}, u32[]{:S(2)}) collective-permute-start(bf16[96,768]{1,0:T(8,128)(2,1)S(1)} %get-tuple-element.111), channel_id=1, source_target_pairs={{0,16},{8,24},{16,0},{24,8},{1,17},{9,25},{17,1},{25,9},{2,18},{10... | collective-permute-start | bytes 442376 | tf_op jit(solution)/shard_map/ppermute | solution.py:490
  429.1 14.1 %collective-permute-start.30 = (bf16[2,96,768]{2,1,0:T(8,128)(2,1)S(1)}, bf16[2,96,768]{2,1,0:T(8,128)(2,1)S(1)}, u32[]{:S(2)}, u32[]{:S(2)}) collective-permute-start(bf16[2,96,768]{2,1,0:T(8,128)(2,1)S(1)} %slice_bitcast_fusion.3), channel_id=1, source_target_pairs={{0,2},{1,3},{2,0},{3,1},{4,6},{5,7},{6,4},{7,5},{8,10},{9,11},{10,... | collective-permute-start | bytes 884744 | tf_op jit(solution)/shard_map/ppermute | solution.py:480
  438.5 6.8 %collective-permute-start.28 = (bf16[2,96,768]{2,1,0:T(8,128)(2,1)S(1)}, bf16[2,96,768]{2,1,0:T(8,128)(2,1)S(1)}, u32[]{:S(2)}, u32[]{:S(2)}) collective-permute-start(bf16[2,96,768]{2,1,0:T(8,128)(2,1)S(1)} %slice_bitcast_fusion.5), channel_id=1, source_target_pairs={{0,4},{1,5},{2,6},{3,7},{4,0},{5,1},{6,2},{7,3},{8,12},{9,13},{10,... | collective-permute-start | bytes 884744 | tf_op jit(solution)/shard_map/ppermute | solution.py:480
  438.7 9.8 %collective-permute-start.42 = (bf16[96,768]{1,0:T(8,128)(2,1)S(1)}, bf16[96,768]{1,0:T(8,128)(2,1)S(1)}, u32[]{:S(2)}, u32[]{:S(2)}) collective-permute-start(bf16[96,768]{1,0:T(8,128)(2,1)S(1)} %fusion.7), channel_id=1, source_target_pairs={{0,8},{8,0},{16,24},{24,16},{1,9},{9,1},{17,25},{25,17},{2,10},{10... | collective-permute-start | bytes 442376 | tf_op jit(solution)/shard_map/ppermute | solution.py:490
  438.8 14.0 %collective-permute-start.41 = (bf16[96,768]{1,0:T(8,128)(2,1)S(1)}, bf16[96,768]{1,0:T(8,128)(2,1)S(1)}, u32[]{:S(2)}, u32[]{:S(2)}) collective-permute-start(bf16[96,768]{1,0:T(8,128)(2,1)S(1)} %fusion.7), channel_id=1, source_target_pairs={{0,16},{8,24},{16,0},{24,8},{1,17},{9,25},{17,1},{25,9},{2,18},{10... | collective-permute-start | bytes 442376 | tf_op jit(solution)/shard_map/ppermute | solution.py:490
  441.8 11.0 %collective-permute-start.40 = (bf16[96,768]{1,0:T(8,128)(2,1)S(1)}, bf16[96,768]{1,0:T(8,128)(2,1)S(1)}, u32[]{:S(2)}, u32[]{:S(2)}) collective-permute-start(bf16[96,768]{1,0:T(8,128)(2,1)S(1)} %fusion.7), channel_id=1, source_target_pairs={{0,24},{8,16},{16,8},{24,0},{1,25},{9,17},{17,9},{25,1},{2,26},{10... | collective-permute-start | bytes 442376 | tf_op jit(solution)/shard_map/ppermute | solution.py:490
  445.5 7.4 %collective-permute-start.31 = (bf16[96,768]{1,0:T(8,128)(2,1)S(1)}, bf16[96,768]{1,0:T(8,128)(2,1)S(1)}, u32[]{:S(2)}, u32[]{:S(2)}) collective-permute-start(bf16[96,768]{1,0:T(8,128)(2,1)S(1)} %get-tuple-element.116), channel_id=1, source_target_pairs={{0,8},{8,0},{16,24},{24,16},{1,9},{9,1},{17,25},{25,17},{2,10},{10... | collective-permute-start | bytes 442376 | tf_op jit(solution)/shard_map/ppermute | solution.py:490
  445.6 17.9 %collective-permute-start.32 = (bf16[96,768]{1,0:T(8,128)(2,1)S(1)}, bf16[96,768]{1,0:T(8,128)(2,1)S(1)}, u32[]{:S(2)}, u32[]{:S(2)}) collective-permute-start(bf16[96,768]{1,0:T(8,128)(2,1)S(1)} %get-tuple-element.117), channel_id=1, source_target_pairs={{0,16},{8,24},{16,0},{24,8},{1,17},{9,25},{17,1},{25,9},{2,18},{10... | collective-permute-start | bytes 442376 | tf_op jit(solution)/shard_map/ppermute | solution.py:490
  448.6 14.9 %collective-permute-start.33 = (bf16[96,768]{1,0:T(8,128)(2,1)S(1)}, bf16[96,768]{1,0:T(8,128)(2,1)S(1)}, u32[]{:S(2)}, u32[]{:S(2)}) collective-permute-start(bf16[96,768]{1,0:T(8,128)(2,1)S(1)} %get-tuple-element.118), channel_id=1, source_target_pairs={{0,24},{8,16},{16,8},{24,0},{1,25},{9,17},{17,9},{25,1},{2,26},{10... | collective-permute-start | bytes 442376 | tf_op jit(solution)/shard_map/ppermute | solution.py:490
  463.6 7.2 %collective-permute-start.36 = (bf16[96,768]{1,0:T(8,128)(2,1)S(1)}, bf16[96,768]{1,0:T(8,128)(2,1)S(1)}, u32[]{:S(2)}, u32[]{:S(2)}) collective-permute-start(bf16[96,768]{1,0:T(8,128)(2,1)S(1)} %fusion.10), channel_id=1, source_target_pairs={{0,8},{8,0},{16,24},{24,16},{1,9},{9,1},{17,25},{25,17},{2,10},{10... | collective-permute-start | bytes 442376 | tf_op jit(solution)/shard_map/ppermute | solution.py:490
  465.9 12.3 %collective-permute-start.35 = (bf16[96,768]{1,0:T(8,128)(2,1)S(1)}, bf16[96,768]{1,0:T(8,128)(2,1)S(1)}, u32[]{:S(2)}, u32[]{:S(2)}) collective-permute-start(bf16[96,768]{1,0:T(8,128)(2,1)S(1)} %fusion.10), channel_id=1, source_target_pairs={{0,16},{8,24},{16,0},{24,8},{1,17},{9,25},{17,1},{25,9},{2,18},{10... | collective-permute-start | bytes 442376 | tf_op jit(solution)/shard_map/ppermute | solution.py:490
  466.9 11.2 %collective-permute-start.34 = (bf16[96,768]{1,0:T(8,128)(2,1)S(1)}, bf16[96,768]{1,0:T(8,128)(2,1)S(1)}, u32[]{:S(2)}, u32[]{:S(2)}) collective-permute-start(bf16[96,768]{1,0:T(8,128)(2,1)S(1)} %fusion.10), channel_id=1, source_target_pairs={{0,24},{8,16},{16,8},{24,0},{1,25},{9,17},{17,9},{25,1},{2,26},{10... | collective-permute-start | bytes 442376 | tf_op jit(solution)/shard_map/ppermute | solution.py:490
  (27 other events, 96.4 us)
Sparse Core Ops, SparseCore 0:
  48.3 109.5 all-gather.2
  213.8 94.2 reduce-scatter.2
  311.6 53.7 reduce-scatter.4

commit v4 on v3

--- a/solution.py
+++ b/solution.py
@@ -324,7 +324,7 @@
 
 def feed_kernel(
     frames, inverse, after_ref, source, mods_ref, up_bias, down_bias, packed_w, result, grad_ref,
-    mods_out, up_bias_out, down_bias_out, grads_out, up, down, entry, active, grad_up_in,
+    mods_out, up_bias_out, down_bias_out, up_out, down_out, up, down, entry, active, grad_up_in,
     grad_down_in, grad_result, staged, sem, out_sem,
 ):
     step, clip, first = block_place(source.shape[1])
@@ -389,22 +389,27 @@
             grad = mul(entry_t, grad_up_in[:, chunk * width : (chunk + 1) * width]).astype(BF)
             staged[chunk] = grad.reshape(shards, rows, width)
             copies.append(
-                pltpu.make_async_copy(staged.at[chunk], grads_out.at[:, chunk], out_sem.at[chunk])
+                pltpu.make_async_copy(staged.at[chunk], up_out.at[:, chunk], out_sem.at[chunk])
             )
             copies[-1].start()
         group = shards // chunks
+        me = inverse[source.shape[0]]
         for chunk in range(chunks):
             grad = mul_lt(active[:, chunk * width : (chunk + 1) * width], grad_down_in[...])
             slot = chunks + chunk
             staged[slot] = grad.astype(BF).reshape(shards, rows, width)
-            copies.append(
-                pltpu.make_async_copy(
-                    staged.at[slot].reshape(group, chunks, rows, width),
-                    grads_out.at[chunk * group : (chunk + 1) * group, chunks:],
-                    out_sem.at[slot],
+            for part in range(group):
+                shard = chunk * group + part
+                distance = jnp.bitwise_xor(me, shard)
+                place = jnp.bitwise_and(distance, 1), lax.shift_right_logical(distance, 1)
+                copies.append(
+                    pltpu.make_async_copy(
+                        staged.at[slot, part * chunks : (part + 1) * chunks],
+                        down_out.at[place],
+                        out_sem.at[chunks + shard],
+                    )
                 )
-            )
-            copies[-1].start()
+                copies[-1].start()
         for copy in copies:
             copy.wait()
 
@@ -625,7 +630,7 @@
         mixer_flops, "time_forward",
     )
 
-    result, grad_after_time, mlp_mods, grad_up_bias, grad_down_bias, feed_grads = run(
+    result, grad_after_time, mlp_mods, grad_up_bias, grad_down_bias, up_grads, down_grads = run(
         partial(feed_kernel, frames), steps, inverse,
         [after_time, arriving, modul, up_bias_full, down_bias_full, feed_w],
         [per_step(block_shape), cols_spec, mods_spec, whole((1, hidden)), whole((1, width)), ANY],
@@ -635,11 +640,12 @@
             mods_out,
             shaped((1, hidden), F32),
             shaped((1, width), F32),
-            shaped((shards, 2 * chunks, rows, width), BF),
+            shaped((shards, chunks, rows, width), BF),
+            shaped((2, shards // 2, chunks, rows, width), BF),
         ],
         [
             cols_spec, per_step(block_shape), mods_out_spec, whole((1, hidden)),
-            whole((1, width)), ANY,
+            whole((1, width)), ANY, ANY,
         ],
         [
             pltpu.VMEM((width, hidden), BF),
@@ -651,7 +657,7 @@
             pltpu.VMEM((ROWS, width), F32),
             pltpu.VMEM((2 * chunks, shards, rows, width), BF),
             dma(()),
-            dma((2 * chunks,)),
+            dma((chunks + shards,)),
         ],
         6 * 2 * tokens * width * hidden, "feed",
     )
@@ -689,28 +695,36 @@
     def total(share):
         return spread_parts(parts_of(share), share)
 
-    def halving(values, bits):
-        left = [bit for bit in range(shards.bit_length() - 2)]
-        blocks = values.shape[1:]
-        values = values.reshape((2,) * len(left) + blocks)
-        for bit in bits:
-            axis = len(left) - 1 - left.index(bit)
-            kept, sent = (lax.index_in_dim(values, side, axis, keepdims=False) for side in (0, 1))
-            values = (kept.astype(F32) + swap(sent, 2 << bit).astype(F32)).astype(BF)
-            left.remove(bit)
-        return values
+    far_bits = list(range(shards.bit_length() - 2))
+
+    def halve(values, left, bit):
+        axis = len(left) - 1 - left.index(bit)
+        kept, sent = (lax.index_in_dim(values, side, axis, keepdims=False) for side in (0, 1))
+        return (kept.astype(F32) + swap(sent, 2 << bit).astype(F32)).astype(BF)
 
     def near_total(grads):
         return (grads[0].astype(F32) + swap(grads[1], 1).astype(F32)).astype(BF)
 
-    def far_total(kept):
-        bits = list(range(shards.bit_length() - 2))
+    def far_start(kept):
         half = kept.shape[1] // 2
-        return jnp.concatenate(
-            [halving(kept[:, :half], bits), halving(kept[:, half:], bits[::-1])], axis=0
-        )
-
-    feed_share = shard_total(feed_grads)
+        folded = (2,) * len(far_bits)
+        return [
+            halve(part.reshape(folded + part.shape[1:]), far_bits, bit)
+            for part, bit in ((kept[:, :half], far_bits[0]), (kept[:, half:], far_bits[-1]))
+        ]
+
+    def far_finish(parts):
+        done = []
+        for values, order in zip(parts, (far_bits, far_bits[::-1])):
+            left = [bit for bit in far_bits if bit != order[0]]
+            for bit in order[1:]:
+                values = halve(values, left, bit)
+                left = [other for other in left if other != bit]
+            done.append(values)
+        return jnp.concatenate(done, axis=0)
+
+    up_share = shard_total(up_grads)
+    down_far = far_start(near_total(down_grads))
 
     going, time_mods, time_grads = run(
         partial(time_backward_kernel, frames, shards), steps, inverse,
@@ -722,11 +736,12 @@
         3 * mixer_flops, "time_backward",
     )
     grad_space = exchange(going.reshape(own_shape))
-    time_grads, feed_share, grad_space, result = lax.optimization_barrier(
-        (time_grads, feed_share, grad_space, result)
+    time_grads, up_share, grad_space, result, *down_far = lax.optimization_barrier(
+        (time_grads, up_share, grad_space, result, *down_far)
     )
     time_share = shard_total(time_grads)
-    feed_parts = parts_of(feed_share)
+    up_parts = parts_of(up_share)
+    down_share = far_finish(down_far)
     arrived = exchange(result.reshape(own_shape))
     grad_rows, space_mods, space_grads = run(
         partial(space_backward_kernel, shards), frame_count, where,
@@ -737,16 +752,16 @@
         weight_scratch + back_scratch(frame_count) + [dma(())],
         3 * mixer_flops, "space_backward",
     )
-    space_grads, space_mods, arrived, *feed_parts = lax.optimization_barrier(
-        (space_grads, space_mods, arrived, *feed_parts)
+    space_grads, space_mods, arrived, down_share, *up_parts = lax.optimization_barrier(
+        (space_grads, space_mods, arrived, down_share, *up_parts)
     )
     space_near = near_total(space_grads)
-    feed_share = spread_parts(feed_parts, feed_share)
+    up_share = spread_parts(up_parts, up_share)
     frames_out = to_rows(arrived)
     space_near, time_share = lax.optimization_barrier((space_near, time_share))
-    space_share = far_total(space_near)
-    time_share = total(time_share)
-    space_share = total(space_share)
+    space_share = far_finish(far_start(space_near))
+    pair = total(jnp.stack([down_share, time_share], axis=1))
+    down_share, time_share = pair[:, 0], pair[:, 1]
 
     mod_part = jnp.concatenate([space_mods, time_mods, mlp_mods], axis=1)
     small_grads = jnp.concatenate(
@@ -767,6 +782,8 @@
     )
     small_size = small_grads.shape[0]
     small_grads = jnp.pad(small_grads, (0, -small_size % 1024)).reshape(1, -1, 128)
+    small_grads, space_share = lax.optimization_barrier((small_grads, space_share))
+    space_share = total(space_share)
     every_small = every(small_grads).reshape(groups, -1)
     every_modul = every_small[:, :mod_size].reshape(groups * clips, 9 * width).astype(BF)
     bias_sums = jnp.sum(every_small[:, mod_size:small_size], axis=0)
@@ -797,9 +814,9 @@
         space_share[3],
         rows_of(time_share[:3]),
         time_share[3],
-        rows_of(feed_share[:chunks]),
+        rows_of(up_share),
         bias_sums[:up_dev],
-        feed_share[chunks:].reshape(chunks * rows, width),
+        down_share.reshape(chunks * rows, width),
         bias_sums[up_dev:],
     )
 

time: 495 us -> 494 us (level)
  waiting for transfers between devices: 158 us -> 140 us
  starting transfers between devices: 68.2 us -> 77 us
    reduce_scatter x2, waiting for transfers between devices: 22.3 us -> 0.01 us  [shard_total(): return lax.psum_scatter(packed, 'shard', scatter_dimension=0, tiled=True)[0]]
    all_to_all x4, waiting for transfers between devices: 50.4 us -> 29.3 us  [exchange(): lax.all_to_all(parts, 'shard', split_axis=0, concat_axis=0, tiled=True)]
    ppermute x22 -> x27, waiting for transfers between devices: 40.7 us -> 54.7 us  [swap(): return lax.ppermute(values, 'shard', pairs)]
    ppermute x24, waiting for transfers between devices: 44.8 us -> 56.3 us  [swap_group(): return lax.ppermute(values, 'grp', pairs)]
    ppermute x24, starting transfers between devices: 33.7 us -> 39.9 us  [swap_group(): return lax.ppermute(values, 'grp', pairs)]
    ppermute x22 -> x27, starting transfers between devices: 18.5 us -> 21.5 us  [swap(): return lax.ppermute(values, 'shard', pairs)]
  transfers between devices with their start and end apart: 53 -> 58, of which waited for: 21 -> 19; matrix products, arithmetic and copies ran while one was open for 10% -> 11% of each run, Pallas kernels for 24% -> 24%
where the time goes in v4:
time: 494 us; the launch traced here: 486 us
  Pallas kernels  160 us (32%)
  waiting for transfers between devices  140 us (28%)
  starting transfers between devices  77 us (16%)
  local copies, waits for them, and re-layouts  37.6 us (8%)
  blocking collectives  26.2 us (5%)
  other arithmetic  25.6 us (5%)
  between operations  15 us (3%)
    pallas_call x5, Pallas kernels, run(): pl.pallas_call(kernel, grid_spec=pltpu.PrefetchScalarGridSpec(num_scalar_...  160 us
    ppermute x24, waiting for transfers between devices, swap_group(): return lax.ppermute(values, 'grp', pairs)  56.3 us
    ppermute x27, waiting for transfers between devices, swap(): return lax.ppermute(values, 'shard', pairs)  54.7 us
    ppermute x24, starting transfers between devices, swap_group(): return lax.ppermute(values, 'grp', pairs)  39.9 us
    all_to_all x4, waiting for transfers between devices, exchange(): lax.all_to_all(parts, 'shard', split_axis=0, concat_axis=0, tiled=True)  29.3 us
    all_gather x1, blocking collectives, body(): lax.all_gather(small.reshape(1, -1, 128), 'shard', axis=0, tiled=True)  26.2 us
    ppermute x27, starting transfers between devices, swap(): return lax.ppermute(values, 'shard', pairs)  21.5 us
    all_to_all x4, starting transfers between devices, exchange(): lax.all_to_all(parts, 'shard', split_axis=0, concat_axis=0, tiled=True)  15.3 us
  transfers between devices with their start and end apart: 58, of which 19 were waited for; matrix products, arithmetic and copies ran while one was open for 11% of the time, Pallas kernels for 24%

profile of v4, /device:TPU:0, one launch (start us, length us, event | category | flops | bytes accessed | tf_op | source)
XLA Modules:
  0.0 486.4 jit_solution(12287971000427727143)
XLA Ops:
  7.3 1.1 copy.136
  8.5 1.8 pad_maximum_fusion.3.refs_0_
  10.3 3.9 collective-permute-start.5
  20.0 26.2 %all_gather.6 = f32[8,138,128]{2,1,0:T(8,128)S(1)} all-gather(f32[1,138,128]{2,1,0:T(8,128)S(1)} %maximum_bitcast_fusion), channel_id=1, replica_groups=mesh['grp'=4,'shard'=8] {'shard'}, dimensions={0}, use_global_device_ids=true | all-gather | bytes 635904 | tf_op jit(solution)/shard_map/all_gather | solution.py:540
  46.9 1.2 copy.104
  53.1 18.8 %space_forward.1 = (bf16[8,4,32,768]{3,2,1,0:T(8,128)(2,1)}, bf16[4,256,2304]{2,1,0:T(8,128)(2,1)}, bf16[4,256,768]{2,1,0:T(8,128)(2,1)}, f32[4,16,256]{2,1,0:T(8,128)}, bf16[4,256,768]{2,1,0:T(8,128)(2,1)}) custom-call(s32[5]{0:T(128)} %pad_add_fusion.where, f32[4,256,768]{2,1,0:T(8,128)} %frames_ref.3, f32[2,9,768]{2,1,0:T(8,128)} %reshape.324.mods_ref, ...), custom_call_target="tpu_custom_call" | custom-call | flops 6442450944 | bytes 17422336 | tf_op jit(solution)/shard_map/space_forward/pallas_call | solution.py:431
  72.0 3.6 all-to-all-start
  76.9 2.8 collective-permute-start.12
  80.4 2.2 multiply_convert_fusion
  82.6 1.2 copy.134
  83.8 29.2 %all-to-all-done = bf16[8,4,32,768]{3,2,1,0:T(8,128)(2,1)S(1)} async-done(((bf16[8,4,32,768]{3,2,1,0:T(8,128)(2,1)}), bf16[8,4,32,768]{3,2,1,0:T(8,128)(2,1)S(1)}, u32[]{:S(2)}, u32[]{:S(2)}) %all-to-all-start) | async-done | bytes 1572896 | tf_op jit(solution)/shard_map/all_to_all | solution.py:566
  113.1 1.1 copy-done.6
  114.2 4.4 all-to-all-start.1
  119.3 15.8 %collective-permute-done.12.refs_6_ = bf16[4,96,768]{2,1,0:T(8,128)(2,1)} collective-permute-done((bf16[4,96,768]{2,1,0:T(8,128)(2,1)S(1)}, bf16[4,96,768]{2,1,0:T(8,128)(2,1)}, u32[]{:S(2)}, u32[]{:S(2)}) %collective-permute-start.12) | collective-permute-done | bytes 589856 | tf_op jit(solution)/shard_map/ppermute | solution.py:485
  135.1 6.7 %collective-permute-done.10.refs_4_ = bf16[4,96,768]{2,1,0:T(8,128)(2,1)} collective-permute-done((bf16[4,96,768]{2,1,0:T(8,128)(2,1)S(1)}, bf16[4,96,768]{2,1,0:T(8,128)(2,1)}, u32[]{:S(2)}, u32[]{:S(2)}) %collective-permute-start.10) | collective-permute-done | bytes 589856 | tf_op jit(solution)/shard_map/ppermute | solution.py:485
  141.8 5.0 %collective-permute-done.8.refs_2_ = bf16[4,96,768]{2,1,0:T(8,128)(2,1)} collective-permute-done((bf16[4,96,768]{2,1,0:T(8,128)(2,1)S(1)}, bf16[4,96,768]{2,1,0:T(8,128)(2,1)}, u32[]{:S(2)}, u32[]{:S(2)}) %collective-permute-start.8) | collective-permute-done | bytes 589856 | tf_op jit(solution)/shard_map/ppermute | solution.py:485
  147.5 1.3 slice.188
  151.1 19.0 %time_forward.1 = (bf16[4,256,768]{2,1,0:T(8,128)(2,1)}, f32[4,256,768]{2,1,0:T(8,128)}, bf16[4,256,2304]{2,1,0:T(8,128)(2,1)}, bf16[4,256,768]{2,1,0:T(8,128)(2...) custom-call(s32[33]{0:T(128)} %pad_add_fusion.1.inverse, bf16[32,32,768]{2,1,0:T(8,128)(2,1)} %bitcast.244, ...), custom_call_target="tpu_custom_call" | custom-call | flops 6442450944 | bytes 18995200 | tf_op jit(solution)/shard_map/time_forward/pallas_call | solution.py:431
  170.1 43.9 %feed.1 = (bf16[32,32,768]{2,1,0:T(8,128)(2,1)}, f32[4,256,768]{2,1,0:T(8,128)}, f32[2,3,768]{2,1,0:T(4,128)}, f32[1,3072]{1,0:T(1,128)}, f32[1,768]{1,0:T(1,128...) custom-call(s32[33]{0:T(128)} %pad_add_fusion.1.inverse, ...), custom_call_target="tpu_custom_call" | custom-call | flops 28991029248 | bytes 28416000 | tf_op jit(solution)/shard_map/feed/pallas_call | solution.py:431
  214.0 3.2 slice_bitcast_fusion.1
  217.9 39.9 %time_backward.1 = (bf16[32,32,768]{2,1,0:T(8,128)(2,1)}, f32[2,3,768]{2,1,0:T(4,128)}, bf16[8,4,96,768]{3,2,1,0:T(8,128)(2,1)}) custom-call(s32[33]{0:T(128)} %pad_add_fusion.1.inverse, f32[4,256,768]{2,1,0:T(8,128)} %get-tuple-element.66.grad_ref, bf16[4,256,768]{2,1,0:T(8,128)(2,1)} %get-tuple-element.67.resid_ref, f32[2,9,768]{2,1,0:T(8,128)} %reshape.324.mods_ref, ...), custom_call_target="tpu_custom_call" | custom-call | flops 19327352832 | bytes 23732224 | tf_op jit(solution)/shard_map/time_backward/pallas_call | solution.py:431
  257.8 3.6 all-to-all-start.2
  261.5 3.1 fusion.1
  264.7 2.0 collective-permute-start.16
  266.7 1.6 collective-permute-start.15
  268.4 3.7 collective-permute-start.24
  272.8 23.9 %collective-permute-done.16 = bf16[2,2,96,768]{3,2,1,0:T(8,128)(2,1)S(1)} collective-permute-done((bf16[2,2,96,768]{3,2,1,0:T(8,128)(2,1)S(1)}, bf16[2,2,96,768]{3,2,1,0:T(8,128)(2,1)S(1)}, u32[]{:S(2)}, u32[]{:S(2)}) %collective-permute-start.16) | collective-permute-done | bytes 589856 | tf_op jit(solution)/shard_map/ppermute | solution.py:485
  299.8 3.8 all-to-all-start.3
  304.3 2.0 collective-permute-start.18
  306.2 1.7 slice_bitcast_fusion.13
  308.0 1.5 collective-permute-start.17
  310.2 3.3 collective-permute-start.21
  314.6 38.9 %space_backward.1 = (f32[4,256,768]{2,1,0:T(8,128)}, f32[2,3,768]{2,1,0:T(4,128)}, bf16[2,4,4,96,768]{4,3,2,1,0:T(8,128)(2,1)}) custom-call(s32[5]{0:T(128)} %pad_add_fusion.where, bf16[8,4,32,768]{3,2,1,0:T(8,128)(2,1)} %copy-done.5, f32[4,256,768]{2,1,0:T(8,128)} %frames_ref.3, f32[2,9,768]{2,1,0:T(8,128)} %reshape.324.mods_ref, ...), custom_call_target="tpu_custom_call" | custom-call | flops 19327352832 | bytes 25305088 | tf_op jit(solution)/shard_map/space_backward/pallas_call | solution.py:431
  355.8 3.3 slice_bitcast_fusion
  361.8 1.2 add_convert_fusion.2
  364.1 2.9 collective-permute-start.49
  369.2 2.0 copy.107
  371.2 1.4 collective-permute-done.26
  373.2 4.8 collective-permute-done.49
  379.6 3.8 fusion
  383.4 1.2 pad_maximum_fusion.1
  384.7 1.6 copy-done.4
  386.9 2.8 collective-permute-start.42
  389.8 2.4 collective-permute-start.44
  392.5 4.9 %collective-permute-done.42 = bf16[192,768]{1,0:T(8,128)(2,1)S(1)} collective-permute-done((bf16[192,768]{1,0:T(8,128)(2,1)S(1)}, bf16[192,768]{1,0:T(8,128)(2,1)S(1)}, u32[]{:S(2)}, u32[]{:S(2)}) %collective-permute-start.42) | collective-permute-done | bytes 294944 | tf_op jit(solution)/shard_map/ppermute | solution.py:495
  397.4 9.1 %collective-permute-done.44 = bf16[192,768]{1,0:T(8,128)(2,1)S(1)} collective-permute-done((bf16[192,768]{1,0:T(8,128)(2,1)S(1)}, bf16[192,768]{1,0:T(8,128)(2,1)S(1)}, u32[]{:S(2)}, u32[]{:S(2)}) %collective-permute-start.44) | collective-permute-done | bytes 294944 | tf_op jit(solution)/shard_map/ppermute | solution.py:495
  406.5 9.6 %collective-permute-done.43 = bf16[192,768]{1,0:T(8,128)(2,1)S(1)} collective-permute-done((bf16[192,768]{1,0:T(8,128)(2,1)S(1)}, bf16[192,768]{1,0:T(8,128)(2,1)S(1)}, u32[]{:S(2)}, u32[]{:S(2)}) %collective-permute-start.43) | collective-permute-done | bytes 294944 | tf_op jit(solution)/shard_map/ppermute | solution.py:495
  416.3 3.0 collective-permute-start.46
  419.3 1.4 collective-permute-start.45
  421.4 1.8 collective-permute-start.30
  423.2 5.1 %collective-permute-done.47 = bf16[192,768]{1,0:T(8,128)(2,1)S(1)} collective-permute-done((bf16[192,768]{1,0:T(8,128)(2,1)S(1)}, bf16[192,768]{1,0:T(8,128)(2,1)S(1)}, u32[]{:S(2)}, u32[]{:S(2)}) %collective-permute-start.47) | collective-permute-done | bytes 294944 | tf_op jit(solution)/shard_map/ppermute | solution.py:495
  428.2 11.5 %collective-permute-done.46 = bf16[192,768]{1,0:T(8,128)(2,1)S(1)} collective-permute-done((bf16[192,768]{1,0:T(8,128)(2,1)S(1)}, bf16[192,768]{1,0:T(8,128)(2,1)S(1)}, u32[]{:S(2)}, u32[]{:S(2)}) %collective-permute-start.46) | collective-permute-done | bytes 294944 | tf_op jit(solution)/shard_map/ppermute | solution.py:495
  443.3 2.2 collective-permute-start.35
  445.5 3.9 collective-permute-start.34
  449.6 2.0 collective-permute-start.36
  451.6 2.4 collective-permute-start.38
  454.6 1.9 collective-permute-start.37
  456.8 2.1 fusion.23
  460.5 4.0 collective-permute-done.37
  464.6 2.8 collective-permute-start.40
  467.5 1.6 collective-permute-start.39
  469.0 1.2 fusion.11
  470.3 2.1 collective-permute-done.41
  472.4 4.6 collective-permute-done.40
  (270 shorter events, 45.2 us)
Async XLA Ops:
  7.2 162.9 %all-gather.3.cloned.1.call-start = ((), (), s32[]{:S(2)}) async-start(), calls=%async_computation.8 | async-start | bytes 10616832 | tf_op jit(solution)/shard_map/all_gather | solution.py:488
  10.3 36.6 %collective-permute-start.5 = (bf16[4,96,768]{2,1,0:T(8,128)(2,1)}, bf16[4,96,768]{2,1,0:T(8,128)(2,1)}, u32[]{:S(2)}, u32[]{:S(2)}) collective-permute-start(bf16[4,96,768]{2,1,0:T(8,128)(2,1)} %pad_maximum_fusion.3.refs_0_), channel_id=1, source_target_pairs={{0,6},{1,7},{2,4},{3,5},{4,2},{5,3},{6,0},{7,1},{8,14},{9,15},{10,... | collective-permute-start | bytes 1769480 | tf_op jit(solution)/shard_map/ppermute | solution.py:485
  14.2 32.7 %collective-permute-start.3 = (bf16[4,96,768]{2,1,0:T(8,128)(2,1)}, bf16[4,96,768]{2,1,0:T(8,128)(2,1)}, u32[]{:S(2)}, u32[]{:S(2)}) collective-permute-start(bf16[4,96,768]{2,1,0:T(8,128)(2,1)} %pad_maximum_fusion.3.refs_0_), channel_id=1, source_target_pairs={{0,4},{1,5},{2,6},{3,7},{4,0},{5,1},{6,2},{7,3},{8,12},{9,13},{10,... | collective-permute-start | bytes 1769480 | tf_op jit(solution)/shard_map/ppermute | solution.py:485
  14.7 32.2 %collective-permute-start = (bf16[4,96,768]{2,1,0:T(8,128)(2,1)}, bf16[4,96,768]{2,1,0:T(8,128)(2,1)}, u32[]{:S(2)}, u32[]{:S(2)}) collective-permute-start(bf16[4,96,768]{2,1,0:T(8,128)(2,1)} %pad_maximum_fusion.3.refs_0_), channel_id=1, source_target_pairs={{0,2},{1,3},{2,0},{3,1},{4,6},{5,7},{6,4},{7,5},{8,10},{9,11},{10,... | collective-permute-start | bytes 1769480 | tf_op jit(solution)/shard_map/ppermute | solution.py:485
  18.7 27.5 %copy-start.14 = (bf16[96,768]{1,0:T(8,128)(2,1)S(1)}, bf16[96,768]{1,0:T(8,128)(2,1)}, u32[]{:S(2)}) copy-start(bf16[96,768]{1,0:T(8,128)(2,1)} %param.25) | copy-start | bytes 442372
  46.3 72.6 %copy-start.9 = (bf16[4,96,768]{2,1,0:T(8,128)(2,1)}, bf16[4,96,768]{2,1,0:T(8,128)(2,1)S(1)}, u32[]{:S(2)}) copy-start(bf16[4,96,768]{2,1,0:T(8,128)(2,1)S(1)} %pad_maximum_fusion.4.refs_0_) | copy-start | bytes 1769476
  48.2 3.1 collective-permute-start.1
  48.6 2.8 collective-permute-start.6
  48.7 3.5 collective-permute-start.4
  49.1 4.0 collective-permute-start.2
  50.6 21.4 %copy-start.12 = (f32[138,128]{1,0:T(8,128)}, f32[138,128]{1,0:T(8,128)S(1)}, u32[]{:S(2)}) copy-start(f32[138,128]{1,0:T(8,128)S(1)} %reduce_sum.37) | copy-start | bytes 211972
  72.0 41.1 %all-to-all-start = ((bf16[8,4,32,768]{3,2,1,0:T(8,128)(2,1)}), bf16[8,4,32,768]{3,2,1,0:T(8,128)(2,1)S(1)}, u32[]{:S(2)}, u32[]{:S(2)}) async-start(bf16[8,4,32,768]{3,2,1,0:T(8,128)(2,1)} %get-tuple-element.62), calls=%async_computation | async-start | bytes 3145728 | tf_op jit(solution)/shard_map/all_to_all | solution.py:566
  76.9 58.1 %collective-permute-start.12 = (bf16[4,96,768]{2,1,0:T(8,128)(2,1)S(1)}, bf16[4,96,768]{2,1,0:T(8,128)(2,1)}, u32[]{:S(2)}, u32[]{:S(2)}) collective-permute-start(bf16[4,96,768]{2,1,0:T(8,128)(2,1)S(1)} %pad_maximum_fusion.4.refs_0_), channel_id=1, source_target_pairs={{0,6},{1,7},{2,4},{3,5},{4,2},{5,3},{6,0},{7,1},{8,14},{9,15},{10,... | collective-permute-start | bytes 1769480 | tf_op jit(solution)/shard_map/ppermute | solution.py:485
  79.8 62.0 %collective-permute-start.10 = (bf16[4,96,768]{2,1,0:T(8,128)(2,1)S(1)}, bf16[4,96,768]{2,1,0:T(8,128)(2,1)}, u32[]{:S(2)}, u32[]{:S(2)}) collective-permute-start(bf16[4,96,768]{2,1,0:T(8,128)(2,1)S(1)} %pad_maximum_fusion.4.refs_0_), channel_id=1, source_target_pairs={{0,4},{1,5},{2,6},{3,7},{4,0},{5,1},{6,2},{7,3},{8,12},{9,13},{10,... | collective-permute-start | bytes 1769480 | tf_op jit(solution)/shard_map/ppermute | solution.py:485
  80.3 66.5 %collective-permute-start.8 = (bf16[4,96,768]{2,1,0:T(8,128)(2,1)S(1)}, bf16[4,96,768]{2,1,0:T(8,128)(2,1)}, u32[]{:S(2)}, u32[]{:S(2)}) collective-permute-start(bf16[4,96,768]{2,1,0:T(8,128)(2,1)S(1)} %pad_maximum_fusion.4.refs_0_), channel_id=1, source_target_pairs={{0,2},{1,3},{2,0},{3,1},{4,6},{5,7},{6,4},{7,5},{8,10},{9,11},{10,... | collective-permute-start | bytes 1769480 | tf_op jit(solution)/shard_map/ppermute | solution.py:485
  114.2 55.9 %all-to-all-start.1 = ((bf16[8,4,32,768]{3,2,1,0:T(8,128)(2,1)}), bf16[8,4,32,768]{3,2,1,0:T(8,128)(2,1)}, u32[]{:S(2)}, u32[]{:S(2)}) async-start(bf16[8,4,32,768]{3,2,1,0:T(8,128)(2,1)} %bitcast.214), calls=%async_computation.1 | async-start | bytes 3145728 | tf_op jit(solution)/shard_map/all_to_all | solution.py:566
  118.6 179.2 %reduce-scatter.3.cloned.1.call-start = ((), (), s32[]{:S(2)}) async-start(), calls=%async_computation.6 | async-start | bytes 5308416 | tf_op jit(solution)/shard_map/reduce_scatter | solution.py:670
  118.9 31.2 %collective-permute-start.7 = (bf16[4,96,768]{2,1,0:T(8,128)(2,1)S(1)}, bf16[4,96,768]{2,1,0:T(8,128)(2,1)S(1)}, u32[]{:S(2)}, u32[]{:S(2)}) collective-permute-start(bf16[4,96,768]{2,1,0:T(8,128)(2,1)S(1)} %pad_maximum_fusion.4.refs_0_), channel_id=1, source_target_pairs={{0,1},{1,0},{2,3},{3,2},{4,5},{5,4},{6,7},{7,6},{8,9},{9,8},{10,11... | collective-permute-start | bytes 1769480 | tf_op jit(solution)/shard_map/ppermute | solution.py:485
  135.1 15.0 %collective-permute-start.13 = (bf16[4,96,768]{2,1,0:T(8,128)(2,1)}, bf16[4,96,768]{2,1,0:T(8,128)(2,1)S(1)}, u32[]{:S(2)}, u32[]{:S(2)}) collective-permute-start(bf16[4,96,768]{2,1,0:T(8,128)(2,1)} %collective-permute-done.12.refs_6_), channel_id=1, source_target_pairs={{0,1},{1,0},{2,3},{3,2},{4,5},{5,4},{6,7},{7,6},{8,9},{9,8},{10,11... | collective-permute-start | bytes 1769480 | tf_op jit(solution)/shard_map/ppermute | solution.py:485
  141.8 8.3 %collective-permute-start.11 = (bf16[4,96,768]{2,1,0:T(8,128)(2,1)}, bf16[4,96,768]{2,1,0:T(8,128)(2,1)}, u32[]{:S(2)}, u32[]{:S(2)}) collective-permute-start(bf16[4,96,768]{2,1,0:T(8,128)(2,1)} %collective-permute-done.10.refs_4_), channel_id=1, source_target_pairs={{0,1},{1,0},{2,3},{3,2},{4,5},{5,4},{6,7},{7,6},{8,9},{9,8},{10,11... | collective-permute-start | bytes 1769480 | tf_op jit(solution)/shard_map/ppermute | solution.py:485
  146.8 3.3 collective-permute-start.9
  217.3 44.2 %collective-permute-start.14 = (bf16[4,4,96,768]{3,2,1,0:T(8,128)(2,1)}, bf16[4,4,96,768]{3,2,1,0:T(8,128)(2,1)}, u32[]{:S(2)}, u32[]{:S(2)}) collective-permute-start(bf16[4,4,96,768]{3,2,1,0:T(8,128)(2,1)} %slice_bitcast_fusion.1), channel_id=1, source_target_pairs={{0,1},{1,0},{2,3},{3,2},{4,5},{5,4},{6,7},{7,6},{8,9},{9,8},{10,11... | collective-permute-start | bytes 7077896 | tf_op jit(solution)/shard_map/ppermute | solution.py:485
  257.8 40.1 %all-to-all-start.2 = ((bf16[8,4,32,768]{3,2,1,0:T(8,128)(2,1)}), bf16[8,4,32,768]{3,2,1,0:T(8,128)(2,1)S(1)}, u32[]{:S(2)}, u32[]{:S(2)}) async-start(bf16[8,4,32,768]{3,2,1,0:T(8,128)(2,1)} %bitcast.245), calls=%async_computation.3 | async-start | bytes 3145728 | tf_op jit(solution)/shard_map/all_to_all | solution.py:566
  261.4 122.0 %reduce-scatter.5.cloned.1.call-start = ((), (), s32[]{:S(2)}) async-start(), calls=%async_computation.7 | async-start | bytes 5308416 | tf_op jit(solution)/shard_map/reduce_scatter | solution.py:670
  264.7 32.0 %collective-permute-start.16 = (bf16[2,2,96,768]{3,2,1,0:T(8,128)(2,1)S(1)}, bf16[2,2,96,768]{3,2,1,0:T(8,128)(2,1)S(1)}, u32[]{:S(2)}, u32[]{:S(2)}) collective-permute-start(bf16[2,2,96,768]{3,2,1,0:T(8,128)(2,1)S(1)} %slice.194), channel_id=1, source_target_pairs={{0,4},{1,5},{2,6},{3,7},{4,0},{5,1},{6,2},{7,3},{8,12},{9,13},{10,... | collective-permute-start | bytes 1769480 | tf_op jit(solution)/shard_map/ppermute | solution.py:485
  266.7 30.2 %collective-permute-start.15 = (bf16[2,2,96,768]{3,2,1,0:T(8,128)(2,1)S(1)}, bf16[2,2,96,768]{3,2,1,0:T(8,128)(2,1)S(1)}, u32[]{:S(2)}, u32[]{:S(2)}) collective-permute-start(bf16[2,2,96,768]{3,2,1,0:T(8,128)(2,1)S(1)} %slice_bitcast_fusion.5), channel_id=1, source_target_pairs={{0,2},{1,3},{2,0},{3,1},{4,6},{5,7},{6,4},{7,5},{8,10},{9,11},{10,... | collective-permute-start | bytes 1769480 | tf_op jit(solution)/shard_map/ppermute | solution.py:485
  268.4 30.6 %collective-permute-start.24 = (f32[2,97]{1,0:T(2,128)S(1)}, f32[2,97]{1,0:T(2,128)S(1)}, u32[]{:S(2)}, u32[]{:S(2)}) collective-permute-start(f32[2,97]{1,0:T(2,128)S(1)} %pad_maximum_fusion.9), channel_id=1, source_target_pairs={{0,24},{8,16},{16,8},{24,0},{1,25},{9,17},{17,9},{25,1},{2,26},{10... | collective-permute-start | bytes 2336 | tf_op jit(solution)/shard_map/ppermute | solution.py:495
  272.1 26.9 %collective-permute-start.23 = (f32[2,97]{1,0:T(2,128)S(1)}, f32[2,97]{1,0:T(2,128)S(1)}, u32[]{:S(2)}, u32[]{:S(2)}) collective-permute-start(f32[2,97]{1,0:T(2,128)S(1)} %pad_maximum_fusion.9), channel_id=1, source_target_pairs={{0,16},{8,24},{16,0},{24,8},{1,17},{9,25},{17,1},{25,9},{2,18},{10... | collective-permute-start | bytes 2336 | tf_op jit(solution)/shard_map/ppermute | solution.py:495
  272.1 26.9 %collective-permute-start.22 = (f32[2,97]{1,0:T(2,128)S(1)}, f32[2,97]{1,0:T(2,128)S(1)}, u32[]{:S(2)}, u32[]{:S(2)}) collective-permute-start(f32[2,97]{1,0:T(2,128)S(1)} %pad_maximum_fusion.9), channel_id=1, source_target_pairs={{0,8},{8,0},{16,24},{24,16},{1,9},{9,1},{17,25},{25,17},{2,10},{10... | collective-permute-start | bytes 2336 | tf_op jit(solution)/shard_map/ppermute | solution.py:495
  299.8 56.0 %all-to-all-start.3 = ((bf16[8,4,32,768]{3,2,1,0:T(8,128)(2,1)}), bf16[8,4,32,768]{3,2,1,0:T(8,128)(2,1)S(1)}, u32[]{:S(2)}, u32[]{:S(2)}) async-start(bf16[8,4,32,768]{3,2,1,0:T(8,128)(2,1)} %bitcast.243), calls=%async_computation.4 | async-start | bytes 3145728 | tf_op jit(solution)/shard_map/all_to_all | solution.py:566
  304.3 49.3 %collective-permute-start.18 = (bf16[2,96,768]{2,1,0:T(8,128)(2,1)}, bf16[2,96,768]{2,1,0:T(8,128)(2,1)}, u32[]{:S(2)}, u32[]{:S(2)}) collective-permute-start(bf16[2,96,768]{2,1,0:T(8,128)(2,1)} %slice_bitcast_fusion.12), channel_id=1, source_target_pairs={{0,2},{1,3},{2,0},{3,1},{4,6},{5,7},{6,4},{7,5},{8,10},{9,11},{10,... | collective-permute-start | bytes 884744 | tf_op jit(solution)/shard_map/ppermute | solution.py:485
  308.0 46.6 %collective-permute-start.17 = (bf16[2,96,768]{2,1,0:T(8,128)(2,1)}, bf16[2,96,768]{2,1,0:T(8,128)(2,1)S(1)}, u32[]{:S(2)}, u32[]{:S(2)}) collective-permute-start(bf16[2,96,768]{2,1,0:T(8,128)(2,1)} %slice_bitcast_fusion.13), channel_id=1, source_target_pairs={{0,4},{1,5},{2,6},{3,7},{4,0},{5,1},{6,2},{7,3},{8,12},{9,13},{10,... | collective-permute-start | bytes 884744 | tf_op jit(solution)/shard_map/ppermute | solution.py:485
  310.2 45.5 %collective-permute-start.21 = (bf16[96,768]{1,0:T(8,128)(2,1)}, bf16[96,768]{1,0:T(8,128)(2,1)}, u32[]{:S(2)}, u32[]{:S(2)}) collective-permute-start(bf16[96,768]{1,0:T(8,128)(2,1)} %get-tuple-element.125), channel_id=1, source_target_pairs={{0,24},{8,16},{16,8},{24,0},{1,25},{9,17},{17,9},{25,1},{2,26},{10... | collective-permute-start | bytes 442376 | tf_op jit(solution)/shard_map/ppermute | solution.py:495
  313.6 42.1 %collective-permute-start.20 = (bf16[96,768]{1,0:T(8,128)(2,1)}, bf16[96,768]{1,0:T(8,128)(2,1)}, u32[]{:S(2)}, u32[]{:S(2)}) collective-permute-start(bf16[96,768]{1,0:T(8,128)(2,1)} %get-tuple-element.126), channel_id=1, source_target_pairs={{0,16},{8,24},{16,0},{24,8},{1,17},{9,25},{17,1},{25,9},{2,18},{10... | collective-permute-start | bytes 442376 | tf_op jit(solution)/shard_map/ppermute | solution.py:495
  313.6 42.1 %collective-permute-start.19 = (bf16[96,768]{1,0:T(8,128)(2,1)S(1)}, bf16[96,768]{1,0:T(8,128)(2,1)}, u32[]{:S(2)}, u32[]{:S(2)}) collective-permute-start(bf16[96,768]{1,0:T(8,128)(2,1)S(1)} %get-tuple-element.127), channel_id=1, source_target_pairs={{0,8},{8,0},{16,24},{24,16},{1,9},{9,1},{17,25},{25,17},{2,10},{10... | collective-permute-start | bytes 442376 | tf_op jit(solution)/shard_map/ppermute | solution.py:495
  359.0 20.6 %collective-permute-start.28 = (bf16[4,4,96,768]{3,2,1,0:T(8,128)(2,1)}, bf16[4,4,96,768]{3,2,1,0:T(8,128)(2,1)}, u32[]{:S(2)}, u32[]{:S(2)}) collective-permute-start(bf16[4,4,96,768]{3,2,1,0:T(8,128)(2,1)} %slice_bitcast_fusion), channel_id=1, source_target_pairs={{0,1},{1,0},{2,3},{3,2},{4,5},{5,4},{6,7},{7,6},{8,9},{9,8},{10,11... | collective-permute-start | bytes 7077896 | tf_op jit(solution)/shard_map/ppermute | solution.py:485
  361.3 6.2 %collective-permute-start.25 = (f32[138,128]{1,0:T(8,128)S(1)}, f32[138,128]{1,0:T(8,128)S(1)}, u32[]{:S(2)}, u32[]{:S(2)}) collective-permute-start(f32[138,128]{1,0:T(8,128)S(1)} %maximum_bitcast_fusion.1), channel_id=1, source_target_pairs={{0,1},{1,0},{2,3},{3,2},{4,5},{5,4},{6,7},{7,6},{8,9},{9,8},{10,11... | collective-permute-start | bytes 211976 | tf_op jit(solution)/shard_map/ppermute | solution.py:485
  363.0 10.2 %collective-permute-start.50 = (bf16[96,768]{1,0:T(8,128)(2,1)S(1)}, bf16[96,768]{1,0:T(8,128)(2,1)S(1)}, u32[]{:S(2)}, u32[]{:S(2)}) collective-permute-start(bf16[96,768]{1,0:T(8,128)(2,1)S(1)} %add_convert_fusion.2), channel_id=1, source_target_pairs={{0,8},{8,0},{16,24},{24,16},{1,9},{9,1},{17,25},{25,17},{2,10},{10... | collective-permute-start | bytes 442376 | tf_op jit(solution)/shard_map/ppermute | solution.py:495
  364.1 14.0 %collective-permute-start.49 = (bf16[96,768]{1,0:T(8,128)(2,1)S(1)}, bf16[96,768]{1,0:T(8,128)(2,1)S(1)}, u32[]{:S(2)}, u32[]{:S(2)}) collective-permute-start(bf16[96,768]{1,0:T(8,128)(2,1)S(1)} %add_convert_fusion.2), channel_id=1, source_target_pairs={{0,16},{8,24},{16,0},{24,8},{1,17},{9,25},{17,1},{25,9},{2,18},{10... | collective-permute-start | bytes 442376 | tf_op jit(solution)/shard_map/ppermute | solution.py:495
  367.0 11.1 %collective-permute-start.48 = (bf16[96,768]{1,0:T(8,128)(2,1)S(1)}, bf16[96,768]{1,0:T(8,128)(2,1)S(1)}, u32[]{:S(2)}, u32[]{:S(2)}) collective-permute-start(bf16[96,768]{1,0:T(8,128)(2,1)S(1)} %add_convert_fusion.2), channel_id=1, source_target_pairs={{0,24},{8,16},{16,8},{24,0},{1,25},{9,17},{17,9},{25,1},{2,26},{10... | collective-permute-start | bytes 442376 | tf_op jit(solution)/shard_map/ppermute | solution.py:495
  368.2 4.4 collective-permute-start.26
  368.8 10.8 %slice-start = ((s8[4718592]{0:T(1024)(128)(4,1)}), s8[4194304]{0:T(1024)(128)(4,1)S(1)}, s32[]{:S(2)}) async-start(s8[4718592]{0:T(1024)(128)(4,1)} %bitcast.227), calls=%async_computation.9 | async-start | bytes 8388608
  369.2 10.4 %slice-start.1 = ((s8[4718592]{0:T(1024)(128)(4,1)}), s8[524288]{0:T(1024)(128)(4,1)S(1)}, s32[]{:S(2)}) async-start(s8[4718592]{0:T(1024)(128)(4,1)} %bitcast.227), calls=%async_computation.10 | async-start | bytes 1048576
  372.7 6.8 %collective-permute-start.27 = (f32[138,128]{1,0:T(8,128)S(1)}, f32[138,128]{1,0:T(8,128)S(1)}, u32[]{:S(2)}, u32[]{:S(2)}) collective-permute-start(f32[138,128]{1,0:T(8,128)S(1)} %fusion.46), channel_id=1, source_target_pairs={{0,4},{1,5},{2,6},{3,7},{4,0},{5,1},{6,2},{7,3},{8,12},{9,13},{10,... | collective-permute-start | bytes 211976 | tf_op jit(solution)/shard_map/ppermute | solution.py:485
  386.3 34.4 %collective-permute-start.31 = (bf16[2,2,96,768]{3,2,1,0:T(8,128)(2,1)S(1)}, bf16[2,2,96,768]{3,2,1,0:T(8,128)(2,1)S(1)}, u32[]{:S(2)}, u32[]{:S(2)}) collective-permute-start(bf16[2,2,96,768]{3,2,1,0:T(8,128)(2,1)S(1)} %slice.164), channel_id=1, source_target_pairs={{0,4},{1,5},{2,6},{3,7},{4,0},{5,1},{6,2},{7,3},{8,12},{9,13},{10,... | collective-permute-start | bytes 1769480 | tf_op jit(solution)/shard_map/ppermute | solution.py:485
  386.9 10.5 %collective-permute-start.42 = (bf16[192,768]{1,0:T(8,128)(2,1)S(1)}, bf16[192,768]{1,0:T(8,128)(2,1)S(1)}, u32[]{:S(2)}, u32[]{:S(2)}) collective-permute-start(bf16[192,768]{1,0:T(8,128)(2,1)S(1)} %get-tuple-element.111), channel_id=1, source_target_pairs={{0,8},{8,0},{16,24},{24,16},{1,9},{9,1},{17,25},{25,17},{2,10},{10... | collective-permute-start | bytes 884744 | tf_op jit(solution)/shard_map/ppermute | solution.py:495
  389.8 16.7 %collective-permute-start.44 = (bf16[192,768]{1,0:T(8,128)(2,1)S(1)}, bf16[192,768]{1,0:T(8,128)(2,1)S(1)}, u32[]{:S(2)}, u32[]{:S(2)}) collective-permute-start(bf16[192,768]{1,0:T(8,128)(2,1)S(1)} %get-tuple-element.112), channel_id=1, source_target_pairs={{0,24},{8,16},{16,8},{24,0},{1,25},{9,17},{17,9},{25,1},{2,26},{10... | collective-permute-start | bytes 884744 | tf_op jit(solution)/shard_map/ppermute | solution.py:495
  392.2 23.8 %collective-permute-start.43 = (bf16[192,768]{1,0:T(8,128)(2,1)S(1)}, bf16[192,768]{1,0:T(8,128)(2,1)S(1)}, u32[]{:S(2)}, u32[]{:S(2)}) collective-permute-start(bf16[192,768]{1,0:T(8,128)(2,1)S(1)} %get-tuple-element.113), channel_id=1, source_target_pairs={{0,16},{8,24},{16,0},{24,8},{1,17},{9,25},{17,1},{25,9},{2,18},{10... | collective-permute-start | bytes 884744 | tf_op jit(solution)/shard_map/ppermute | solution.py:495
  392.4 28.8 %collective-permute-start.29 = (bf16[2,2,96,768]{3,2,1,0:T(8,128)(2,1)S(1)}, bf16[2,2,96,768]{3,2,1,0:T(8,128)(2,1)S(1)}, u32[]{:S(2)}, u32[]{:S(2)}) collective-permute-start(bf16[2,2,96,768]{3,2,1,0:T(8,128)(2,1)S(1)} %slice_bitcast_fusion.3), channel_id=1, source_target_pairs={{0,2},{1,3},{2,0},{3,1},{4,6},{5,7},{6,4},{7,5},{8,10},{9,11},{10,... | collective-permute-start | bytes 1769480 | tf_op jit(solution)/shard_map/ppermute | solution.py:485
  416.2 12.0 %collective-permute-start.47 = (bf16[192,768]{1,0:T(8,128)(2,1)S(1)}, bf16[192,768]{1,0:T(8,128)(2,1)S(1)}, u32[]{:S(2)}, u32[]{:S(2)}) collective-permute-start(bf16[192,768]{1,0:T(8,128)(2,1)S(1)} %fusion.6), channel_id=1, source_target_pairs={{0,8},{8,0},{16,24},{24,16},{1,9},{9,1},{17,25},{25,17},{2,10},{10... | collective-permute-start | bytes 884744 | tf_op jit(solution)/shard_map/ppermute | solution.py:495
  416.3 23.5 %collective-permute-start.46 = (bf16[192,768]{1,0:T(8,128)(2,1)S(1)}, bf16[192,768]{1,0:T(8,128)(2,1)S(1)}, u32[]{:S(2)}, u32[]{:S(2)}) collective-permute-start(bf16[192,768]{1,0:T(8,128)(2,1)S(1)} %fusion.6), channel_id=1, source_target_pairs={{0,16},{8,24},{16,0},{24,8},{1,17},{9,25},{17,1},{25,9},{2,18},{10... | collective-permute-start | bytes 884744 | tf_op jit(solution)/shard_map/ppermute | solution.py:495
  419.3 20.5 %collective-permute-start.45 = (bf16[192,768]{1,0:T(8,128)(2,1)S(1)}, bf16[192,768]{1,0:T(8,128)(2,1)S(1)}, u32[]{:S(2)}, u32[]{:S(2)}) collective-permute-start(bf16[192,768]{1,0:T(8,128)(2,1)S(1)} %fusion.6), channel_id=1, source_target_pairs={{0,24},{8,16},{16,8},{24,0},{1,25},{9,17},{17,9},{25,1},{2,26},{10... | collective-permute-start | bytes 884744 | tf_op jit(solution)/shard_map/ppermute | solution.py:495
  420.8 22.3 %collective-permute-start.32 = (bf16[2,96,768]{2,1,0:T(8,128)(2,1)S(1)}, bf16[2,96,768]{2,1,0:T(8,128)(2,1)S(1)}, u32[]{:S(2)}, u32[]{:S(2)}) collective-permute-start(bf16[2,96,768]{2,1,0:T(8,128)(2,1)S(1)} %slice_bitcast_fusion.8), channel_id=1, source_target_pairs={{0,2},{1,3},{2,0},{3,1},{4,6},{5,7},{6,4},{7,5},{8,10},{9,11},{10,... | collective-permute-start | bytes 884744 | tf_op jit(solution)/shard_map/ppermute | solution.py:485
  421.4 21.8 %collective-permute-start.30 = (bf16[2,96,768]{2,1,0:T(8,128)(2,1)S(1)}, bf16[2,96,768]{2,1,0:T(8,128)(2,1)S(1)}, u32[]{:S(2)}, u32[]{:S(2)}) collective-permute-start(bf16[2,96,768]{2,1,0:T(8,128)(2,1)S(1)} %slice_bitcast_fusion.10), channel_id=1, source_target_pairs={{0,4},{1,5},{2,6},{3,7},{4,0},{5,1},{6,2},{7,3},{8,12},{9,13},{10,... | collective-permute-start | bytes 884744 | tf_op jit(solution)/shard_map/ppermute | solution.py:485
  443.3 13.2 %collective-permute-start.35 = (f32[1,112,128]{2,1,0:T(8,128)S(1)}, f32[1,112,128]{2,1,0:T(8,128)S(1)}, u32[]{:S(2)}, u32[]{:S(2)}) collective-permute-start(f32[1,112,128]{2,1,0:T(8,128)S(1)} %fusion.16), channel_id=1, source_target_pairs={{0,24},{8,16},{16,8},{24,0},{1,25},{9,17},{17,9},{25,1},{2,26},{10... | collective-permute-start | bytes 172040 | tf_op jit(solution)/shard_map/ppermute | solution.py:495
  445.5 10.9 %collective-permute-start.34 = (f32[1,112,128]{2,1,0:T(8,128)S(1)}, f32[1,112,128]{2,1,0:T(8,128)S(1)}, u32[]{:S(2)}, u32[]{:S(2)}) collective-permute-start(f32[1,112,128]{2,1,0:T(8,128)S(1)} %fusion.16), channel_id=1, source_target_pairs={{0,16},{8,24},{16,0},{24,8},{1,17},{9,25},{17,1},{25,9},{2,18},{10... | collective-permute-start | bytes 172040 | tf_op jit(solution)/shard_map/ppermute | solution.py:495
  449.5 5.1 %collective-permute-start.33 = (f32[1,112,128]{2,1,0:T(8,128)S(1)}, f32[1,112,128]{2,1,0:T(8,128)S(1)}, u32[]{:S(2)}, u32[]{:S(2)}) collective-permute-start(f32[1,112,128]{2,1,0:T(8,128)S(1)} %fusion.16), channel_id=1, source_target_pairs={{0,8},{8,0},{16,24},{24,16},{1,9},{9,1},{17,25},{25,17},{2,10},{10... | collective-permute-start | bytes 172040 | tf_op jit(solution)/shard_map/ppermute | solution.py:495
  449.6 10.9 %collective-permute-start.36 = (bf16[96,768]{1,0:T(8,128)(2,1)S(1)}, bf16[96,768]{1,0:T(8,128)(2,1)S(1)}, u32[]{:S(2)}, u32[]{:S(2)}) collective-permute-start(bf16[96,768]{1,0:T(8,128)(2,1)S(1)} %get-tuple-element.122), channel_id=1, source_target_pairs={{0,8},{8,0},{16,24},{24,16},{1,9},{9,1},{17,25},{25,17},{2,10},{10... | collective-permute-start | bytes 442376 | tf_op jit(solution)/shard_map/ppermute | solution.py:495
  451.6 8.8 %collective-permute-start.38 = (bf16[96,768]{1,0:T(8,128)(2,1)S(1)}, bf16[96,768]{1,0:T(8,128)(2,1)S(1)}, u32[]{:S(2)}, u32[]{:S(2)}) collective-permute-start(bf16[96,768]{1,0:T(8,128)(2,1)S(1)} %get-tuple-element.123), channel_id=1, source_target_pairs={{0,24},{8,16},{16,8},{24,0},{1,25},{9,17},{17,9},{25,1},{2,26},{10... | collective-permute-start | bytes 442376 | tf_op jit(solution)/shard_map/ppermute | solution.py:495
  454.6 9.9 %collective-permute-start.37 = (bf16[96,768]{1,0:T(8,128)(2,1)S(1)}, bf16[96,768]{1,0:T(8,128)(2,1)S(1)}, u32[]{:S(2)}, u32[]{:S(2)}) collective-permute-start(bf16[96,768]{1,0:T(8,128)(2,1)S(1)} %get-tuple-element.124), channel_id=1, source_target_pairs={{0,16},{8,24},{16,0},{24,8},{1,17},{9,25},{17,1},{25,9},{2,18},{10... | collective-permute-start | bytes 442376 | tf_op jit(solution)/shard_map/ppermute | solution.py:495
  458.9 10.1 %copy-start.23 = (s32[8]{0:T(128)S(1)}, s32[8]{0:T(128)}, u32[]{:S(2)}) copy-start(s32[8]{0:T(128)} %convert_reduce_fusion.1) | copy-start | bytes 100
  464.6 7.8 %collective-permute-start.41 = (bf16[96,768]{1,0:T(8,128)(2,1)S(1)}, bf16[96,768]{1,0:T(8,128)(2,1)S(1)}, u32[]{:S(2)}, u32[]{:S(2)}) collective-permute-start(bf16[96,768]{1,0:T(8,128)(2,1)S(1)} %fusion.14), channel_id=1, source_target_pairs={{0,8},{8,0},{16,24},{24,16},{1,9},{9,1},{17,25},{25,17},{2,10},{10... | collective-permute-start | bytes 442376 | tf_op jit(solution)/shard_map/ppermute | solution.py:495
  464.6 12.4 %collective-permute-start.40 = (bf16[96,768]{1,0:T(8,128)(2,1)S(1)}, bf16[96,768]{1,0:T(8,128)(2,1)S(1)}, u32[]{:S(2)}, u32[]{:S(2)}) collective-permute-start(bf16[96,768]{1,0:T(8,128)(2,1)S(1)} %fusion.14), channel_id=1, source_target_pairs={{0,16},{8,24},{16,0},{24,8},{1,17},{9,25},{17,1},{25,9},{2,18},{10... | collective-permute-start | bytes 442376 | tf_op jit(solution)/shard_map/ppermute | solution.py:495
  467.5 9.6 %collective-permute-start.39 = (bf16[96,768]{1,0:T(8,128)(2,1)S(1)}, bf16[96,768]{1,0:T(8,128)(2,1)S(1)}, u32[]{:S(2)}, u32[]{:S(2)}) collective-permute-start(bf16[96,768]{1,0:T(8,128)(2,1)S(1)} %fusion.14), channel_id=1, source_target_pairs={{0,24},{8,16},{16,8},{24,0},{1,25},{9,17},{17,9},{25,1},{2,26},{10... | collective-permute-start | bytes 442376 | tf_op jit(solution)/shard_map/ppermute | solution.py:495
  (31 other events, 128.9 us)
Sparse Core Ops, SparseCore 0:
  48.3 109.5 all-gather.2
  214.1 57.1 reduce-scatter.2
  298.0 61.0 reduce-scatter.4

commit v5 on v4

--- a/solution.py
+++ b/solution.py
@@ -184,6 +184,21 @@
         copy.wait()
 
 
+def fetch_spread(me, group, pieces, both, sem):
+    count, rows, cols = pieces[0].shape
+    copies = []
+    for at, piece in enumerate(pieces):
+        left = pl.multiple_of(jnp.bitwise_xor(group, at // 2) * cols, cols)
+        for k in range(count):
+            first = pl.multiple_of(jnp.bitwise_xor(me, 2 * k + at % 2) * rows, rows)
+            target = both.at[pl.ds(first, rows), pl.ds(left, cols)]
+            copies.append(pltpu.make_async_copy(piece.at[k], target, sem))
+    for copy in copies:
+        copy.start()
+    for copy in copies:
+        copy.wait()
+
+
 def mixer_weight_grads(entry, packed_grad, mixed, branch_grad, put, width):
     entry_t = entry[...].T
     for block in range(3):
@@ -270,17 +285,19 @@
     return step, clip, first
 
 
-def time_forward_kernel(frames, shards, inverse, source, mods_ref, *refs):
-    pieces = refs[:shards]
-    resid_ref, after_ref, packed_ref, mixed_ref, lse_ref, branch_ref = refs[shards : shards + 6]
-    weight, out_weight, resid, sem = refs[shards + 6 :]
+def time_forward_kernel(frames, count, inverse, source, mods_ref, *refs):
+    pieces = refs[:count]
+    resid_ref, after_ref, packed_ref, mixed_ref, lse_ref, branch_ref = refs[count : count + 6]
+    both, resid, sem = refs[count + 6 :]
     step, clip, first = block_place(source.shape[1])
     width = source.shape[-1]
 
     @pl.when(step == 0)
     def _():
-        fetch_pieces(inverse[source.shape[0]], pieces, weight, out_weight, sem)
-
+        slots = source.shape[0]
+        fetch_spread(inverse[slots], inverse[slots + 1], pieces, both, sem)
+
+    weight, out_weight = both.at[:, : 3 * width], both.at[:, 3 * width :]
     load_near(source, inverse, resid, clip, first, frames)
     resid_ref[0] = resid[...].astype(BF)
     after_ref[0] = mixer_forward(
@@ -290,18 +307,20 @@
 
 
 def time_backward_kernel(
-    frames, shards, inverse, grad_ref, resid_ref, mods_ref, packed_ref, mixed_ref, lse_ref,
+    frames, shards, count, inverse, grad_ref, resid_ref, mods_ref, packed_ref, mixed_ref, lse_ref,
     branch_ref, *refs
 ):
-    pieces = refs[:shards]
-    going, mods_out, grads_out = refs[shards : shards + 3]
-    weight, out_weight, entry, packed_grad, mixed, branch_grad, sem = refs[shards + 3 :]
+    pieces = refs[:count]
+    going, mods_out, grads_out = refs[count : count + 3]
+    both, entry, packed_grad, mixed, branch_grad, sem = refs[count + 3 :]
     step, clip, first = block_place(going.shape[1])
     width = going.shape[-1]
+    weight, out_weight = both.at[:, : 3 * width], both.at[:, 3 * width :]
 
     @pl.when(step == 0)
     def _():
-        fetch_pieces(inverse[going.shape[0]], pieces, weight, out_weight, sem)
+        slots = going.shape[0]
+        fetch_spread(inverse[slots], inverse[slots + 1], pieces, both, sem)
         mods_out[...] = jnp.zeros_like(mods_out)
 
     own = pl.ds(pl.multiple_of(step * ROWS, ROWS), ROWS)
@@ -517,7 +536,13 @@
             pieces += [piece, swap(piece, 1)]
         return pieces
 
+    own_time = jnp.concatenate([time_qkv, time_out], axis=1)
+    part_cols = own_time.shape[1] // groups
+    own_time = lax.dynamic_slice_in_dim(own_time, group_at * part_cols, part_cols, 1)
     own_space = jnp.concatenate([column_blocks(space_qkv), space_out[None]], axis=0)
+    even_time, own_space = lax.optimization_barrier((even_pieces(own_time), own_space))
+    even_time = jnp.stack(even_time)
+    even_time = [even_time] + [swap_group(even_time, distance) for distance in range(1, groups)]
     even = even_pieces(own_space)
 
     embed = jnp.take(time_table, timesteps, axis=0).astype(F32)
@@ -538,15 +563,13 @@
         ]
     )
     small = lax.all_gather(small.reshape(1, -1, 128), "shard", axis=0, tiled=True)
-    small, even[1] = lax.optimization_barrier((small, even[1]))
+    small, even[1:], even_time[2:3] = lax.optimization_barrier((small, even[1:], even_time[2:3]))
     small = jnp.sum(small, axis=0).reshape(-1)
     space_w = all_pieces(even)
-    own_time = jnp.concatenate([column_blocks(time_qkv), time_out[None]], axis=0)
     own_feed = jnp.concatenate(
         [column_blocks(up_weight), down_weight.reshape(chunks, rows, width)], axis=0
     )
-    own_time, own_feed, *_ = lax.optimization_barrier((own_time, own_feed, *even[1:]))
-    time_w = all_pieces(even_pieces(own_time))
+    own_feed, *_ = lax.optimization_barrier((own_feed, *even[1:]))
     feed_w = gather(own_feed)
     mod_size = clips * 9 * width
     modul = small[:mod_size].reshape(clips, 9, width)
@@ -560,7 +583,7 @@
     where = jnp.concatenate([clip_of, shard_at[None].astype(jnp.int32)])
     slots = jnp.arange(group_frames, dtype=jnp.int32)
     inverse = jnp.sum(jnp.where(table[None, :] == slots[:, None], slots[None, :], 0), axis=1)
-    inverse = jnp.concatenate([inverse, shard_at[None].astype(jnp.int32)])
+    inverse = jnp.concatenate([inverse, jnp.stack([shard_at, group_at]).astype(jnp.int32)])
 
     def exchange(parts):
         return lax.all_to_all(parts, "shard", split_axis=0, concat_axis=0, tiled=True)
@@ -581,6 +604,7 @@
         pltpu.VMEM((width, 3 * width), BF),
         pltpu.VMEM((width, width), BF),
     ]
+    both_scratch = pltpu.VMEM((width, 4 * width), BF)
     dma = pltpu.SemaphoreType.DMA
 
     def kept(count):
@@ -611,6 +635,8 @@
         weight_scratch + [dma(())],
         mixer_flops, "space_forward",
     )
+    after_space, even_time = lax.optimization_barrier((after_space, even_time))
+    time_w = all_pieces(even_time)
     received = exchange(after_space).reshape(group_frames, columns, width)
     own_ids = jnp.concatenate([embed, timesteps.astype(F32)[:, None]], axis=1)
     own_ids, _ = lax.optimization_barrier((own_ids, after_space))
@@ -621,12 +647,12 @@
     block_shape = (steps, ROWS, width)
     time_keep, time_keep_specs = kept(steps)
     time_resid, after_time, *time_kept = run(
-        partial(time_forward_kernel, frames, shards), steps, inverse,
+        partial(time_forward_kernel, frames, 2 * groups), steps, inverse,
         [received, modul] + time_w,
-        [cols_spec, mods_spec] + [ANY] * shards,
+        [cols_spec, mods_spec] + [ANY] * (2 * groups),
         [shaped(block_shape, BF), shaped(block_shape, F32)] + time_keep,
         [per_step(block_shape)] * 2 + time_keep_specs,
-        weight_scratch + [pltpu.VMEM((ROWS, width), F32), dma(())],
+        [both_scratch, pltpu.VMEM((ROWS, width), F32), dma(())],
         mixer_flops, "time_forward",
     )
 
@@ -727,12 +753,12 @@
     down_far = far_start(near_total(down_grads))
 
     going, time_mods, time_grads = run(
-        partial(time_backward_kernel, frames, shards), steps, inverse,
+        partial(time_backward_kernel, frames, shards, 2 * groups), steps, inverse,
         [grad_after_time, time_resid, modul] + time_kept + time_w,
-        [per_step(block_shape)] * 2 + [mods_spec] + time_keep_specs + [ANY] * shards,
+        [per_step(block_shape)] * 2 + [mods_spec] + time_keep_specs + [ANY] * (2 * groups),
         [cols_shape, mods_out, shaped(grads_shape, BF)],
         [cols_spec, mods_out_spec, whole(grads_shape)],
-        weight_scratch + back_scratch(steps) + [dma(())],
+        [both_scratch] + back_scratch(steps) + [dma(())],
         3 * mixer_flops, "time_backward",
     )
     grad_space = exchange(going.reshape(own_shape))
@@ -760,7 +786,7 @@
     frames_out = to_rows(arrived)
     space_near, time_share = lax.optimization_barrier((space_near, time_share))
     space_share = far_finish(far_start(space_near))
-    pair = total(jnp.stack([down_share, time_share], axis=1))
+    pair = lax.psum(jnp.stack([down_share, time_share], axis=1), "grp").astype(F32)
     down_share, time_share = pair[:, 0], pair[:, 1]
 
     mod_part = jnp.concatenate([space_mods, time_mods, mlp_mods], axis=1)

time: 494 us -> 512 us (1.036)
  waiting for transfers between devices: 140 us -> 151 us
  Pallas kernels: 160 us -> 168 us
    psum x0 -> x1, waiting for transfers between devices: none -> 27.2 us  [body(): lax.psum(jnp.stack([down_share, time_share], axis=1), 'grp').astype(F32)]
    ppermute x24 -> x21, waiting for transfers between devices: 56.3 us -> 41.1 us  [swap_group(): return lax.ppermute(values, 'grp', pairs)]
    pallas_call x5, Pallas kernels: 160 us -> 168 us  [run(): pl.pallas_call(kernel, grid_spec=pltpu.PrefetchScalarGridSpec(num_scalar_...]
    ppermute x24 -> x21, starting transfers between devices: 39.9 us -> 35 us  [swap_group(): return lax.ppermute(values, 'grp', pairs)]
  transfers between devices with their start and end apart: 58 -> 56, of which waited for: 19 -> 20; matrix products, arithmetic and copies ran while one was open for 11% -> 12% of each run, Pallas kernels for 24% -> 23%
where the time goes in v5:
time: 512 us; the launch traced here: 504 us
  Pallas kernels  168 us (33%)
  waiting for transfers between devices  151 us (29%)
  starting transfers between devices  72.9 us (14%)
  local copies, waits for them, and re-layouts  39.6 us (8%)
  other arithmetic  27.6 us (5%)
  blocking collectives  25.4 us (5%)
  between operations  15.2 us (3%)
    pallas_call x5, Pallas kernels, run(): pl.pallas_call(kernel, grid_spec=pltpu.PrefetchScalarGridSpec(num_scalar_...  168 us
    ppermute x27, waiting for transfers between devices, swap(): return lax.ppermute(values, 'shard', pairs)  49.8 us
    ppermute x21, waiting for transfers between devices, swap_group(): return lax.ppermute(values, 'grp', pairs)  41.1 us
    ppermute x21, starting transfers between devices, swap_group(): return lax.ppermute(values, 'grp', pairs)  35 us
    all_to_all x4, waiting for transfers between devices, exchange(): lax.all_to_all(parts, 'shard', split_axis=0, concat_axis=0, tiled=True)  32.6 us
    psum x1, waiting for transfers between devices, body(): lax.psum(jnp.stack([down_share, time_share], axis=1), 'grp').astype(F32)  27.2 us
    all_gather x1, blocking collectives, body(): lax.all_gather(small.reshape(1, -1, 128), 'shard', axis=0, tiled=True)  25.4 us
    ppermute x27, starting transfers between devices, swap(): return lax.ppermute(values, 'shard', pairs)  21.9 us
  transfers between devices with their start and end apart: 56, of which 20 were waited for; matrix products, arithmetic and copies ran while one was open for 12% of the time, Pallas kernels for 23%

profile of v5, /device:TPU:0, one launch (start us, length us, event | category | flops | bytes accessed | tf_op | source)
XLA Modules:
  0.0 504.0 jit_solution(4958889345114585943)
XLA Ops:
  8.4 4.0 collective-permute-start.2
  13.0 1.2 compare_and_fusion
  14.2 1.3 convert_bitcast_fusion.2
  21.7 2.9 collective-permute-start.5
  26.2 3.0 collective-permute-start.6
  30.6 25.4 %all_gather.6 = f32[8,138,128]{2,1,0:T(8,128)S(1)} all-gather(f32[1,138,128]{2,1,0:T(8,128)S(1)} %maximum_bitcast_fusion), channel_id=1, replica_groups=mesh['grp'=4,'shard'=8] {'shard'}, dimensions={0}, use_global_device_ids=true | all-gather | bytes 635904 | tf_op jit(solution)/shard_map/all_gather | solution.py:565
  56.6 1.2 copy.95
  60.1 3.6 collective-permute-start.12
  65.3 18.6 %space_forward.1 = (bf16[8,4,32,768]{3,2,1,0:T(8,128)(2,1)}, bf16[4,256,2304]{2,1,0:T(8,128)(2,1)}, bf16[4,256,768]{2,1,0:T(8,128)(2,1)}, f32[4,16,256]{2,1,0:T(8,128)}, bf16[4,256,768]{2,1,0:T(8,128)(2,1)}) custom-call(s32[5]{0:T(128)} %pad_add_fusion.where, f32[4,256,768]{2,1,0:T(8,128)} %frames_ref.3, f32[2,9,768]{2,1,0:T(8,128)} %reshape.313.mods_ref, ...), custom_call_target="tpu_custom_call" | custom-call | flops 6442450944 | bytes 17422336 | tf_op jit(solution)/shard_map/space_forward/pallas_call | solution.py:450
  83.9 6.7 %collective-permute-done.11.refs_2_ = bf16[4,96,768]{2,1,0:T(8,128)(2,1)S(1)} collective-permute-done((bf16[4,96,768]{2,1,0:T(8,128)(2,1)}, bf16[4,96,768]{2,1,0:T(8,128)(2,1)S(1)}, u32[]{:S(2)}, u32[]{:S(2)}) %collective-permute-start.11) | collective-permute-done | bytes 589856 | tf_op jit(solution)/shard_map/ppermute | solution.py:514
  91.4 3.7 all-to-all-start
  96.4 2.3 multiply_convert_fusion
  98.8 1.2 copy.122
  100.0 32.6 %all-to-all-done = bf16[8,4,32,768]{3,2,1,0:T(8,128)(2,1)S(1)} async-done(((bf16[8,4,32,768]{3,2,1,0:T(8,128)(2,1)}), bf16[8,4,32,768]{3,2,1,0:T(8,128)(2,1)S(1)}, u32[]{:S(2)}, u32[]{:S(2)}) %all-to-all-start) | async-done | bytes 1572896 | tf_op jit(solution)/shard_map/all_to_all | solution.py:589
  132.7 1.1 copy-done.7
  133.8 4.3 all-to-all-start.1
  143.4 19.0 %time_forward.1 = (bf16[4,256,768]{2,1,0:T(8,128)(2,1)}, f32[4,256,768]{2,1,0:T(8,128)}, bf16[4,256,2304]{2,1,0:T(8,128)(2,1)}, bf16[4,256,768]{2,1,0:T(8,128)(2...) custom-call(s32[34]{0:T(128)} %pad_add_fusion.1.inverse, bf16[32,32,768]{2,1,0:T(8,128)(2,1)} %bitcast.224, ...), custom_call_target="tpu_custom_call" | custom-call | flops 6442450944 | bytes 18995200 | tf_op jit(solution)/shard_map/time_forward/pallas_call | solution.py:450
  162.4 51.6 %feed.1 = (bf16[32,32,768]{2,1,0:T(8,128)(2,1)}, f32[4,256,768]{2,1,0:T(8,128)}, f32[2,3,768]{2,1,0:T(4,128)}, f32[1,3072]{1,0:T(1,128)}, f32[1,768]{1,0:T(1,128...) custom-call(s32[34]{0:T(128)} %pad_add_fusion.1.inverse, ...), custom_call_target="tpu_custom_call" | custom-call | flops 28991029248 | bytes 28416000 | tf_op jit(solution)/shard_map/feed/pallas_call | solution.py:450
  214.0 3.2 slice_bitcast_fusion.1
  217.6 39.4 %time_backward.1 = (bf16[32,32,768]{2,1,0:T(8,128)(2,1)}, f32[2,3,768]{2,1,0:T(4,128)}, bf16[8,4,96,768]{3,2,1,0:T(8,128)(2,1)}) custom-call(s32[34]{0:T(128)} %pad_add_fusion.1.inverse, f32[4,256,768]{2,1,0:T(8,128)} %get-tuple-element.90.grad_ref, bf16[4,256,768]{2,1,0:T(8,128)(2,1)} %get-tuple-element.91.resid_ref, f32[2,9,768]{2,1,0:T(8,128)} %reshape.313.mods_ref, ...), custom_call_target="tpu_custom_call" | custom-call | flops 19327352832 | bytes 23732224 | tf_op jit(solution)/shard_map/time_backward/pallas_call | solution.py:450
  257.0 4.0 all-to-all-start.2
  261.0 3.1 fusion.1
  264.1 2.0 collective-permute-start.19
  266.3 1.5 collective-permute-start.18
  267.8 29.3 %collective-permute-done.19 = bf16[2,2,96,768]{3,2,1,0:T(8,128)(2,1)S(1)} collective-permute-done((bf16[2,2,96,768]{3,2,1,0:T(8,128)(2,1)S(1)}, bf16[2,2,96,768]{3,2,1,0:T(8,128)(2,1)S(1)}, u32[]{:S(2)}, u32[]{:S(2)}) %collective-permute-start.19) | collective-permute-done | bytes 589856 | tf_op jit(solution)/shard_map/ppermute | solution.py:504
  299.6 3.3 collective-permute-start.27
  304.0 2.5 collective-permute-done.25
  306.6 3.6 all-to-all-start.3
  310.3 1.8 slice_bitcast_fusion.12
  312.0 1.9 collective-permute-start.21
  314.6 1.5 collective-permute-start.20
  316.9 2.3 collective-permute-start.24
  319.2 39.9 %space_backward.1 = (f32[4,256,768]{2,1,0:T(8,128)}, f32[2,3,768]{2,1,0:T(4,128)}, bf16[2,4,4,96,768]{4,3,2,1,0:T(8,128)(2,1)}) custom-call(s32[5]{0:T(128)} %pad_add_fusion.where, bf16[8,4,32,768]{3,2,1,0:T(8,128)(2,1)} %copy-done.6, f32[4,256,768]{2,1,0:T(8,128)} %frames_ref.3, f32[2,9,768]{2,1,0:T(8,128)} %reshape.313.mods_ref, ...), custom_call_target="tpu_custom_call" | custom-call | flops 19327352832 | bytes 25305088 | tf_op jit(solution)/shard_map/space_backward/pallas_call | solution.py:450
  361.0 1.5 collective-permute-start.22
  363.5 5.1 %collective-permute-done.23 = bf16[96,768]{1,0:T(8,128)(2,1)S(1)} collective-permute-done((bf16[96,768]{1,0:T(8,128)(2,1)}, bf16[96,768]{1,0:T(8,128)(2,1)S(1)}, u32[]{:S(2)}, u32[]{:S(2)}) %collective-permute-start.23) | collective-permute-done | bytes 147488 | tf_op jit(solution)/shard_map/ppermute | solution.py:514
  369.3 3.3 slice_bitcast_fusion
  374.7 2.5 collective-permute-start.46
  377.2 1.9 collective-permute-start.45
  380.1 2.0 copy.98
  382.1 1.4 collective-permute-done.29
  384.1 4.6 collective-permute-done.46
  388.9 1.1 copy.114
  390.1 3.8 fusion
  395.7 1.3 slice.158
  397.3 10.7 %collective-permute-done.34 = bf16[2,2,96,768]{3,2,1,0:T(8,128)(2,1)S(1)} collective-permute-done((bf16[2,2,96,768]{3,2,1,0:T(8,128)(2,1)S(1)}, bf16[2,2,96,768]{3,2,1,0:T(8,128)(2,1)S(1)}, u32[]{:S(2)}, u32[]{:S(2)}) %collective-permute-start.34) | collective-permute-done | bytes 589856 | tf_op jit(solution)/shard_map/ppermute | solution.py:504
  407.9 1.2 add_convert_fusion
  410.2 1.6 collective-permute-done.32
  414.6 1.9 collective-permute-done.35
  416.6 3.0 collective-permute-done.33
  419.7 2.7 collective-permute-start.38
  422.4 1.4 collective-permute-start.37
  424.3 1.7 collective-permute-start.39
  426.0 2.3 collective-permute-start.41
  428.3 2.7 collective-permute-done.36
  431.0 2.1 collective-permute-start.40
  435.1 2.1 fusion.21
  437.3 1.2 fusion.8
  438.5 4.4 collective-permute-done.39
  442.9 2.3 collective-permute-done.41
  445.2 12.6 %collective-permute-done.40 = bf16[96,768]{1,0:T(8,128)(2,1)S(1)} collective-permute-done((bf16[96,768]{1,0:T(8,128)(2,1)S(1)}, bf16[96,768]{1,0:T(8,128)(2,1)S(1)}, u32[]{:S(2)}, u32[]{:S(2)}) %collective-permute-start.40) | collective-permute-done | bytes 147488 | tf_op jit(solution)/shard_map/ppermute | solution.py:514
  457.9 2.6 collective-permute-start.43
  460.5 1.8 collective-permute-start.42
  462.3 27.2 %all-reduce.3.cloned.1.call-done = bf16[4,2,96,768]{3,2,0,1:T(8,128)(2,1)} async-done(((bf16[4,2,96,768]{3,2,0,1:T(8,128)(2,1)}), bf16[4,2,96,768]{3,2,0,1:T(8,128)(2,1)}) %all-reduce.3.cloned.1.call-update) | async-done | bytes 1179664 | tf_op jit(solution)/shard_map/psum | solution.py:789
  489.5 1.5 convert_element_type.270
  (260 shorter events, 50.1 us)
Async XLA Ops:
  7.2 22.0 %copy-start = (bf16[96,6912]{1,0:T(8,128)(2,1)S(1)}, bf16[96,6912]{1,0:T(8,128)(2,1)}, u32[]{:S(2)}) copy-start(bf16[96,6912]{1,0:T(8,128)(2,1)} %param.20) | copy-start | bytes 3981316
  7.2 13.0 %copy-start.13 = (bf16[96,2304]{1,0:T(8,128)(2,1)S(1)}, bf16[96,2304]{1,0:T(8,128)(2,1)}, u32[]{:S(2)}) copy-start(bf16[96,2304]{1,0:T(8,128)(2,1)} %param.22) | copy-start | bytes 1327108
  7.2 13.6 %copy-start.14 = (bf16[96,768]{1,0:T(8,128)(2,1)S(1)}, bf16[96,768]{1,0:T(8,128)(2,1)}, u32[]{:S(2)}) copy-start(bf16[96,768]{1,0:T(8,128)(2,1)} %param.23) | copy-start | bytes 442372
  7.2 155.1 %all-gather.3.cloned.1.call-start = ((), (), s32[]{:S(2)}) async-start(), calls=%async_computation.9 | async-start | bytes 10616832 | tf_op jit(solution)/shard_map/all_gather | solution.py:507
  8.4 13.4 %collective-permute-start.2 = (bf16[96,768]{1,0:T(8,128)(2,1)S(1)}, bf16[96,768]{1,0:T(8,128)(2,1)S(1)}, u32[]{:S(2)}, u32[]{:S(2)}) collective-permute-start(bf16[96,768]{1,0:T(8,128)(2,1)S(1)} %fusion.13), channel_id=1, source_target_pairs={{0,6},{1,7},{2,4},{3,5},{4,2},{5,3},{6,0},{7,1},{8,14},{9,15},{10,... | collective-permute-start | bytes 442376 | tf_op jit(solution)/shard_map/ppermute | solution.py:504
  12.4 9.4 %collective-permute-start.1 = (bf16[96,768]{1,0:T(8,128)(2,1)S(1)}, bf16[96,768]{1,0:T(8,128)(2,1)S(1)}, u32[]{:S(2)}, u32[]{:S(2)}) collective-permute-start(bf16[96,768]{1,0:T(8,128)(2,1)S(1)} %fusion.13), channel_id=1, source_target_pairs={{0,4},{1,5},{2,6},{3,7},{4,0},{5,1},{6,2},{7,3},{8,12},{9,13},{10,... | collective-permute-start | bytes 442376 | tf_op jit(solution)/shard_map/ppermute | solution.py:504
  12.9 8.9 %collective-permute-start = (bf16[96,768]{1,0:T(8,128)(2,1)S(1)}, bf16[96,768]{1,0:T(8,128)(2,1)S(1)}, u32[]{:S(2)}, u32[]{:S(2)}) collective-permute-start(bf16[96,768]{1,0:T(8,128)(2,1)S(1)} %fusion.13), channel_id=1, source_target_pairs={{0,2},{1,3},{2,0},{3,1},{4,6},{5,7},{6,4},{7,5},{8,10},{9,11},{10,... | collective-permute-start | bytes 442376 | tf_op jit(solution)/shard_map/ppermute | solution.py:504
  20.3 8.9 %copy-start.17 = (f32[6912]{0:T(1024)S(1)}, f32[6912]{0:T(1024)}, u32[]{:S(2)}) copy-start(f32[6912]{0:T(1024)} %add.238) | copy-start | bytes 82948
  20.3 8.9 %copy-start.26 = (pred[2]{0:T(512)(128)(4,1)S(1)}, pred[2]{0:T(512)(128)(4,1)}, u32[]{:S(2)}) copy-start(pred[2]{0:T(512)(128)(4,1)} %compare_and_fusion) | copy-start | bytes 10
  20.8 8.7 %copy-start.23 = (bf16[2,96]{1,0:T(2,128)(2,1)}, bf16[2,96]{1,0:T(2,128)(2,1)S(1)}, u32[]{:S(2)}) copy-start(bf16[2,96]{1,0:T(2,128)(2,1)S(1)} %gather_fusion.1) | copy-start | bytes 1156
  21.7 34.8 %collective-permute-start.5 = (bf16[4,96,768]{2,1,0:T(8,128)(2,1)}, bf16[4,96,768]{2,1,0:T(8,128)(2,1)}, u32[]{:S(2)}, u32[]{:S(2)}) collective-permute-start(bf16[4,96,768]{2,1,0:T(8,128)(2,1)} %pad_maximum_fusion.2.refs_0_), channel_id=1, source_target_pairs={{0,6},{1,7},{2,4},{3,5},{4,2},{5,3},{6,0},{7,1},{8,14},{9,15},{10,... | collective-permute-start | bytes 1769480 | tf_op jit(solution)/shard_map/ppermute | solution.py:504
  24.7 31.9 %collective-permute-start.4 = (bf16[4,96,768]{2,1,0:T(8,128)(2,1)}, bf16[4,96,768]{2,1,0:T(8,128)(2,1)}, u32[]{:S(2)}, u32[]{:S(2)}) collective-permute-start(bf16[4,96,768]{2,1,0:T(8,128)(2,1)} %pad_maximum_fusion.2.refs_0_), channel_id=1, source_target_pairs={{0,4},{1,5},{2,6},{3,7},{4,0},{5,1},{6,2},{7,3},{8,12},{9,13},{10,... | collective-permute-start | bytes 1769480 | tf_op jit(solution)/shard_map/ppermute | solution.py:504
  25.2 31.4 %collective-permute-start.3 = (bf16[4,96,768]{2,1,0:T(8,128)(2,1)}, bf16[4,96,768]{2,1,0:T(8,128)(2,1)}, u32[]{:S(2)}, u32[]{:S(2)}) collective-permute-start(bf16[4,96,768]{2,1,0:T(8,128)(2,1)} %pad_maximum_fusion.2.refs_0_), channel_id=1, source_target_pairs={{0,2},{1,3},{2,0},{3,1},{4,6},{5,7},{6,4},{7,5},{8,10},{9,11},{10,... | collective-permute-start | bytes 1769480 | tf_op jit(solution)/shard_map/ppermute | solution.py:504
  26.2 30.3 %collective-permute-start.6 = (bf16[4,96,768]{2,1,0:T(8,128)(2,1)}, bf16[4,96,768]{2,1,0:T(8,128)(2,1)}, u32[]{:S(2)}, u32[]{:S(2)}) collective-permute-start(bf16[4,96,768]{2,1,0:T(8,128)(2,1)} %pad_maximum_fusion.3.refs_0_), channel_id=1, source_target_pairs={{0,16},{8,24},{16,0},{24,8},{1,17},{9,25},{17,1},{25,9},{2,18},{10... | collective-permute-start | bytes 1769480 | tf_op jit(solution)/shard_map/ppermute | solution.py:514
  57.8 6.6 %collective-permute-start.7 = (bf16[4,96,768]{2,1,0:T(8,128)(2,1)}, bf16[4,96,768]{2,1,0:T(8,128)(2,1)S(1)}, u32[]{:S(2)}, u32[]{:S(2)}) collective-permute-start(bf16[4,96,768]{2,1,0:T(8,128)(2,1)} %pad_maximum_fusion.2.refs_0_), channel_id=1, source_target_pairs={{0,1},{1,0},{2,3},{3,2},{4,5},{5,4},{6,7},{7,6},{8,9},{9,8},{10,11... | collective-permute-start | bytes 1769480 | tf_op jit(solution)/shard_map/ppermute | solution.py:504
  58.2 6.2 %collective-permute-start.8 = (bf16[4,96,768]{2,1,0:T(8,128)(2,1)}, bf16[4,96,768]{2,1,0:T(8,128)(2,1)}, u32[]{:S(2)}, u32[]{:S(2)}) collective-permute-start(bf16[4,96,768]{2,1,0:T(8,128)(2,1)} %collective-permute-done.3.refs_2_), channel_id=1, source_target_pairs={{0,1},{1,0},{2,3},{3,2},{4,5},{5,4},{6,7},{7,6},{8,9},{9,8},{10,11... | collective-permute-start | bytes 1769480 | tf_op jit(solution)/shard_map/ppermute | solution.py:504
  58.4 6.1 %collective-permute-start.9 = (bf16[4,96,768]{2,1,0:T(8,128)(2,1)}, bf16[4,96,768]{2,1,0:T(8,128)(2,1)}, u32[]{:S(2)}, u32[]{:S(2)}) collective-permute-start(bf16[4,96,768]{2,1,0:T(8,128)(2,1)} %collective-permute-done.4.refs_4_), channel_id=1, source_target_pairs={{0,1},{1,0},{2,3},{3,2},{4,5},{5,4},{6,7},{7,6},{8,9},{9,8},{10,11... | collective-permute-start | bytes 1769480 | tf_op jit(solution)/shard_map/ppermute | solution.py:504
  58.8 5.7 %collective-permute-start.10 = (bf16[4,96,768]{2,1,0:T(8,128)(2,1)}, bf16[4,96,768]{2,1,0:T(8,128)(2,1)}, u32[]{:S(2)}, u32[]{:S(2)}) collective-permute-start(bf16[4,96,768]{2,1,0:T(8,128)(2,1)} %collective-permute-done.5.refs_6_), channel_id=1, source_target_pairs={{0,1},{1,0},{2,3},{3,2},{4,5},{5,4},{6,7},{7,6},{8,9},{9,8},{10,11... | collective-permute-start | bytes 1769480 | tf_op jit(solution)/shard_map/ppermute | solution.py:504
  60.1 23.7 %collective-permute-start.12 = (bf16[4,96,768]{2,1,0:T(8,128)(2,1)}, bf16[4,96,768]{2,1,0:T(8,128)(2,1)}, u32[]{:S(2)}, u32[]{:S(2)}) collective-permute-start(bf16[4,96,768]{2,1,0:T(8,128)(2,1)} %pad_maximum_fusion.3.refs_0_), channel_id=1, source_target_pairs={{0,24},{8,16},{16,8},{24,0},{1,25},{9,17},{17,9},{25,1},{2,26},{10... | collective-permute-start | bytes 1769480 | tf_op jit(solution)/shard_map/ppermute | solution.py:514
  64.5 26.1 %collective-permute-start.11 = (bf16[4,96,768]{2,1,0:T(8,128)(2,1)}, bf16[4,96,768]{2,1,0:T(8,128)(2,1)S(1)}, u32[]{:S(2)}, u32[]{:S(2)}) collective-permute-start(bf16[4,96,768]{2,1,0:T(8,128)(2,1)} %pad_maximum_fusion.3.refs_0_), channel_id=1, source_target_pairs={{0,8},{8,0},{16,24},{24,16},{1,9},{9,1},{17,25},{25,17},{2,10},{10... | collective-permute-start | bytes 1769480 | tf_op jit(solution)/shard_map/ppermute | solution.py:514
  91.4 41.3 %all-to-all-start = ((bf16[8,4,32,768]{3,2,1,0:T(8,128)(2,1)}), bf16[8,4,32,768]{3,2,1,0:T(8,128)(2,1)S(1)}, u32[]{:S(2)}, u32[]{:S(2)}) async-start(bf16[8,4,32,768]{3,2,1,0:T(8,128)(2,1)} %get-tuple-element.83), calls=%async_computation | async-start | bytes 3145728 | tf_op jit(solution)/shard_map/all_to_all | solution.py:589
  133.8 28.5 %all-to-all-start.1 = ((bf16[8,4,32,768]{3,2,1,0:T(8,128)(2,1)}), bf16[8,4,32,768]{3,2,1,0:T(8,128)(2,1)}, u32[]{:S(2)}, u32[]{:S(2)}) async-start(bf16[8,4,32,768]{3,2,1,0:T(8,128)(2,1)} %bitcast.201), calls=%async_computation.1 | async-start | bytes 3145728 | tf_op jit(solution)/shard_map/all_to_all | solution.py:589
  138.1 160.2 %reduce-scatter.3.cloned.1.call-start = ((), (), s32[]{:S(2)}) async-start(), calls=%async_computation.6 | async-start | bytes 5308416 | tf_op jit(solution)/shard_map/reduce_scatter | solution.py:696
  138.4 3.0 collective-permute-start.13
  138.8 2.7 collective-permute-start.14
  139.0 3.5 collective-permute-start.15
  139.3 4.0 collective-permute-start.16
  217.3 43.7 %collective-permute-start.17 = (bf16[4,4,96,768]{3,2,1,0:T(8,128)(2,1)}, bf16[4,4,96,768]{3,2,1,0:T(8,128)(2,1)}, u32[]{:S(2)}, u32[]{:S(2)}) collective-permute-start(bf16[4,4,96,768]{3,2,1,0:T(8,128)(2,1)} %slice_bitcast_fusion.1), channel_id=1, source_target_pairs={{0,1},{1,0},{2,3},{3,2},{4,5},{5,4},{6,7},{7,6},{8,9},{9,8},{10,11... | collective-permute-start | bytes 7077896 | tf_op jit(solution)/shard_map/ppermute | solution.py:504
  257.0 41.3 %all-to-all-start.2 = ((bf16[8,4,32,768]{3,2,1,0:T(8,128)(2,1)}), bf16[8,4,32,768]{3,2,1,0:T(8,128)(2,1)S(1)}, u32[]{:S(2)}, u32[]{:S(2)}) async-start(bf16[8,4,32,768]{3,2,1,0:T(8,128)(2,1)} %bitcast.225), calls=%async_computation.3 | async-start | bytes 3145728 | tf_op jit(solution)/shard_map/all_to_all | solution.py:589
  260.9 133.0 %reduce-scatter.5.cloned.1.call-start = ((), (), s32[]{:S(2)}) async-start(), calls=%async_computation.7 | async-start | bytes 5308416 | tf_op jit(solution)/shard_map/reduce_scatter | solution.py:696
  264.1 33.0 %collective-permute-start.19 = (bf16[2,2,96,768]{3,2,1,0:T(8,128)(2,1)S(1)}, bf16[2,2,96,768]{3,2,1,0:T(8,128)(2,1)S(1)}, u32[]{:S(2)}, u32[]{:S(2)}) collective-permute-start(bf16[2,2,96,768]{3,2,1,0:T(8,128)(2,1)S(1)} %slice.194), channel_id=1, source_target_pairs={{0,4},{1,5},{2,6},{3,7},{4,0},{5,1},{6,2},{7,3},{8,12},{9,13},{10,... | collective-permute-start | bytes 1769480 | tf_op jit(solution)/shard_map/ppermute | solution.py:504
  266.3 31.8 %collective-permute-start.18 = (bf16[2,2,96,768]{3,2,1,0:T(8,128)(2,1)S(1)}, bf16[2,2,96,768]{3,2,1,0:T(8,128)(2,1)S(1)}, u32[]{:S(2)}, u32[]{:S(2)}) collective-permute-start(bf16[2,2,96,768]{3,2,1,0:T(8,128)(2,1)S(1)} %slice_bitcast_fusion.5), channel_id=1, source_target_pairs={{0,2},{1,3},{2,0},{3,1},{4,6},{5,7},{6,4},{7,5},{8,10},{9,11},{10,... | collective-permute-start | bytes 1769480 | tf_op jit(solution)/shard_map/ppermute | solution.py:504
  299.6 73.0 %collective-permute-start.27 = (f32[2,97]{1,0:T(2,128)S(1)}, f32[2,97]{1,0:T(2,128)S(1)}, u32[]{:S(2)}, u32[]{:S(2)}) collective-permute-start(f32[2,97]{1,0:T(2,128)S(1)} %pad_maximum_fusion.8), channel_id=1, source_target_pairs={{0,24},{8,16},{16,8},{24,0},{1,25},{9,17},{17,9},{25,1},{2,26},{10... | collective-permute-start | bytes 2336 | tf_op jit(solution)/shard_map/ppermute | solution.py:514
  303.0 69.6 %collective-permute-start.26 = (f32[2,97]{1,0:T(2,128)S(1)}, f32[2,97]{1,0:T(2,128)S(1)}, u32[]{:S(2)}, u32[]{:S(2)}) collective-permute-start(f32[2,97]{1,0:T(2,128)S(1)} %pad_maximum_fusion.8), channel_id=1, source_target_pairs={{0,16},{8,24},{16,0},{24,8},{1,17},{9,25},{17,1},{25,9},{2,18},{10... | collective-permute-start | bytes 2336 | tf_op jit(solution)/shard_map/ppermute | solution.py:514
  303.0 3.6 collective-permute-start.25
  306.6 62.7 %all-to-all-start.3 = ((bf16[8,4,32,768]{3,2,1,0:T(8,128)(2,1)}), bf16[8,4,32,768]{3,2,1,0:T(8,128)(2,1)S(1)}, u32[]{:S(2)}, u32[]{:S(2)}) async-start(bf16[8,4,32,768]{3,2,1,0:T(8,128)(2,1)} %bitcast.223), calls=%async_computation.4 | async-start | bytes 3145728 | tf_op jit(solution)/shard_map/all_to_all | solution.py:589
  310.2 179.3 %all-reduce.3.cloned.1.call-start = ((), (), s32[]{:S(2)}) async-start(), calls=%async_computation.8 | async-start | bytes 2359296 | tf_op jit(solution)/shard_map/psum | solution.py:789
  312.0 47.1 %collective-permute-start.21 = (bf16[2,96,768]{2,1,0:T(8,128)(2,1)}, bf16[2,96,768]{2,1,0:T(8,128)(2,1)}, u32[]{:S(2)}, u32[]{:S(2)}) collective-permute-start(bf16[2,96,768]{2,1,0:T(8,128)(2,1)} %slice_bitcast_fusion.12), channel_id=1, source_target_pairs={{0,2},{1,3},{2,0},{3,1},{4,6},{5,7},{6,4},{7,5},{8,10},{9,11},{10,... | collective-permute-start | bytes 884744 | tf_op jit(solution)/shard_map/ppermute | solution.py:504
  314.6 46.3 %collective-permute-start.20 = (bf16[2,96,768]{2,1,0:T(8,128)(2,1)}, bf16[2,96,768]{2,1,0:T(8,128)(2,1)S(1)}, u32[]{:S(2)}, u32[]{:S(2)}) collective-permute-start(bf16[2,96,768]{2,1,0:T(8,128)(2,1)} %slice_bitcast_fusion.13), channel_id=1, source_target_pairs={{0,4},{1,5},{2,6},{3,7},{4,0},{5,1},{6,2},{7,3},{8,12},{9,13},{10,... | collective-permute-start | bytes 884744 | tf_op jit(solution)/shard_map/ppermute | solution.py:504
  316.9 46.6 %collective-permute-start.24 = (bf16[96,768]{1,0:T(8,128)(2,1)}, bf16[96,768]{1,0:T(8,128)(2,1)}, u32[]{:S(2)}, u32[]{:S(2)}) collective-permute-start(bf16[96,768]{1,0:T(8,128)(2,1)} %get-tuple-element.142), channel_id=1, source_target_pairs={{0,24},{8,16},{16,8},{24,0},{1,25},{9,17},{17,9},{25,1},{2,26},{10... | collective-permute-start | bytes 442376 | tf_op jit(solution)/shard_map/ppermute | solution.py:514
  359.2 9.4 %collective-permute-start.23 = (bf16[96,768]{1,0:T(8,128)(2,1)}, bf16[96,768]{1,0:T(8,128)(2,1)S(1)}, u32[]{:S(2)}, u32[]{:S(2)}) collective-permute-start(bf16[96,768]{1,0:T(8,128)(2,1)} %get-tuple-element.143), channel_id=1, source_target_pairs={{0,16},{8,24},{16,0},{24,8},{1,17},{9,25},{17,1},{25,9},{2,18},{10... | collective-permute-start | bytes 442376 | tf_op jit(solution)/shard_map/ppermute | solution.py:514
  361.0 8.3 %collective-permute-start.22 = (bf16[96,768]{1,0:T(8,128)(2,1)S(1)}, bf16[96,768]{1,0:T(8,128)(2,1)}, u32[]{:S(2)}, u32[]{:S(2)}) collective-permute-start(bf16[96,768]{1,0:T(8,128)(2,1)S(1)} %get-tuple-element.144), channel_id=1, source_target_pairs={{0,8},{8,0},{16,24},{24,16},{1,9},{9,1},{17,25},{25,17},{2,10},{10... | collective-permute-start | bytes 442376 | tf_op jit(solution)/shard_map/ppermute | solution.py:514
  372.6 17.5 %collective-permute-start.31 = (bf16[4,4,96,768]{3,2,1,0:T(8,128)(2,1)}, bf16[4,4,96,768]{3,2,1,0:T(8,128)(2,1)}, u32[]{:S(2)}, u32[]{:S(2)}) collective-permute-start(bf16[4,4,96,768]{3,2,1,0:T(8,128)(2,1)} %slice_bitcast_fusion), channel_id=1, source_target_pairs={{0,1},{1,0},{2,3},{3,2},{4,5},{5,4},{6,7},{7,6},{8,9},{9,8},{10,11... | collective-permute-start | bytes 7077896 | tf_op jit(solution)/shard_map/ppermute | solution.py:504
  373.0 6.1 %collective-permute-start.28 = (f32[138,128]{1,0:T(8,128)S(1)}, f32[138,128]{1,0:T(8,128)S(1)}, u32[]{:S(2)}, u32[]{:S(2)}) collective-permute-start(f32[138,128]{1,0:T(8,128)S(1)} %maximum_bitcast_fusion.1), channel_id=1, source_target_pairs={{0,1},{1,0},{2,3},{3,2},{4,5},{5,4},{6,7},{7,6},{8,9},{9,8},{10,11... | collective-permute-start | bytes 211976 | tf_op jit(solution)/shard_map/ppermute | solution.py:504
  374.6 9.5 %collective-permute-start.47 = (bf16[96,768]{1,0:T(8,128)(2,1)S(1)}, bf16[96,768]{1,0:T(8,128)(2,1)S(1)}, u32[]{:S(2)}, u32[]{:S(2)}) collective-permute-start(bf16[96,768]{1,0:T(8,128)(2,1)S(1)} %add_convert_fusion.2), channel_id=1, source_target_pairs={{0,8},{8,0},{16,24},{24,16},{1,9},{9,1},{17,25},{25,17},{2,10},{10... | collective-permute-start | bytes 442376 | tf_op jit(solution)/shard_map/ppermute | solution.py:514
  374.7 14.1 %collective-permute-start.46 = (bf16[96,768]{1,0:T(8,128)(2,1)S(1)}, bf16[96,768]{1,0:T(8,128)(2,1)S(1)}, u32[]{:S(2)}, u32[]{:S(2)}) collective-permute-start(bf16[96,768]{1,0:T(8,128)(2,1)S(1)} %add_convert_fusion.2), channel_id=1, source_target_pairs={{0,16},{8,24},{16,0},{24,8},{1,17},{9,25},{17,1},{25,9},{2,18},{10... | collective-permute-start | bytes 442376 | tf_op jit(solution)/shard_map/ppermute | solution.py:514
  377.2 11.6 %collective-permute-start.45 = (bf16[96,768]{1,0:T(8,128)(2,1)S(1)}, bf16[96,768]{1,0:T(8,128)(2,1)S(1)}, u32[]{:S(2)}, u32[]{:S(2)}) collective-permute-start(bf16[96,768]{1,0:T(8,128)(2,1)S(1)} %add_convert_fusion.2), channel_id=1, source_target_pairs={{0,24},{8,16},{16,8},{24,0},{1,25},{9,17},{17,9},{25,1},{2,26},{10... | collective-permute-start | bytes 442376 | tf_op jit(solution)/shard_map/ppermute | solution.py:514
  379.1 4.4 collective-permute-start.29
  379.7 10.4 %slice-start = ((s8[4718592]{0:T(1024)(128)(4,1)}), s8[4194304]{0:T(1024)(128)(4,1)S(1)}, s32[]{:S(2)}) async-start(s8[4718592]{0:T(1024)(128)(4,1)} %bitcast.210), calls=%async_computation.10 | async-start | bytes 8388608
  380.0 10.1 %slice-start.1 = ((s8[4718592]{0:T(1024)(128)(4,1)}), s8[524288]{0:T(1024)(128)(4,1)S(1)}, s32[]{:S(2)}) async-start(s8[4718592]{0:T(1024)(128)(4,1)} %bitcast.210), calls=%async_computation.11 | async-start | bytes 1048576
  383.5 6.6 %collective-permute-start.30 = (f32[138,128]{1,0:T(8,128)S(1)}, f32[138,128]{1,0:T(8,128)S(1)}, u32[]{:S(2)}, u32[]{:S(2)}) collective-permute-start(f32[138,128]{1,0:T(8,128)S(1)} %fusion.44), channel_id=1, source_target_pairs={{0,4},{1,5},{2,6},{3,7},{4,0},{5,1},{6,2},{7,3},{8,12},{9,13},{10,... | collective-permute-start | bytes 211976 | tf_op jit(solution)/shard_map/ppermute | solution.py:504
  395.0 12.9 %collective-permute-start.34 = (bf16[2,2,96,768]{3,2,1,0:T(8,128)(2,1)S(1)}, bf16[2,2,96,768]{3,2,1,0:T(8,128)(2,1)S(1)}, u32[]{:S(2)}, u32[]{:S(2)}) collective-permute-start(bf16[2,2,96,768]{3,2,1,0:T(8,128)(2,1)S(1)} %slice.164), channel_id=1, source_target_pairs={{0,4},{1,5},{2,6},{3,7},{4,0},{5,1},{6,2},{7,3},{8,12},{9,13},{10,... | collective-permute-start | bytes 1769480 | tf_op jit(solution)/shard_map/ppermute | solution.py:504
  397.1 14.6 %collective-permute-start.32 = (bf16[2,2,96,768]{3,2,1,0:T(8,128)(2,1)S(1)}, bf16[2,2,96,768]{3,2,1,0:T(8,128)(2,1)S(1)}, u32[]{:S(2)}, u32[]{:S(2)}) collective-permute-start(bf16[2,2,96,768]{3,2,1,0:T(8,128)(2,1)S(1)} %slice_bitcast_fusion.3), channel_id=1, source_target_pairs={{0,2},{1,3},{2,0},{3,1},{4,6},{5,7},{6,4},{7,5},{8,10},{9,11},{10,... | collective-permute-start | bytes 1769480 | tf_op jit(solution)/shard_map/ppermute | solution.py:504
  409.2 7.3 %collective-permute-start.35 = (bf16[2,96,768]{2,1,0:T(8,128)(2,1)S(1)}, bf16[2,96,768]{2,1,0:T(8,128)(2,1)S(1)}, u32[]{:S(2)}, u32[]{:S(2)}) collective-permute-start(bf16[2,96,768]{2,1,0:T(8,128)(2,1)S(1)} %slice_bitcast_fusion.8), channel_id=1, source_target_pairs={{0,2},{1,3},{2,0},{3,1},{4,6},{5,7},{6,4},{7,5},{8,10},{9,11},{10,... | collective-permute-start | bytes 884744 | tf_op jit(solution)/shard_map/ppermute | solution.py:504
  412.7 6.9 %collective-permute-start.33 = (bf16[2,96,768]{2,1,0:T(8,128)(2,1)}, bf16[2,96,768]{2,1,0:T(8,128)(2,1)S(1)}, u32[]{:S(2)}, u32[]{:S(2)}) collective-permute-start(bf16[2,96,768]{2,1,0:T(8,128)(2,1)} %slice_bitcast_fusion.10), channel_id=1, source_target_pairs={{0,4},{1,5},{2,6},{3,7},{4,0},{5,1},{6,2},{7,3},{8,12},{9,13},{10,... | collective-permute-start | bytes 884744 | tf_op jit(solution)/shard_map/ppermute | solution.py:504
  419.7 13.5 %collective-permute-start.38 = (f32[1,112,128]{2,1,0:T(8,128)S(1)}, f32[1,112,128]{2,1,0:T(8,128)S(1)}, u32[]{:S(2)}, u32[]{:S(2)}) collective-permute-start(f32[1,112,128]{2,1,0:T(8,128)S(1)} %fusion.14), channel_id=1, source_target_pairs={{0,24},{8,16},{16,8},{24,0},{1,25},{9,17},{17,9},{25,1},{2,26},{10... | collective-permute-start | bytes 172040 | tf_op jit(solution)/shard_map/ppermute | solution.py:514
  422.4 10.8 %collective-permute-start.37 = (f32[1,112,128]{2,1,0:T(8,128)S(1)}, f32[1,112,128]{2,1,0:T(8,128)S(1)}, u32[]{:S(2)}, u32[]{:S(2)}) collective-permute-start(f32[1,112,128]{2,1,0:T(8,128)S(1)} %fusion.14), channel_id=1, source_target_pairs={{0,16},{8,24},{16,0},{24,8},{1,17},{9,25},{17,1},{25,9},{2,18},{10... | collective-permute-start | bytes 172040 | tf_op jit(solution)/shard_map/ppermute | solution.py:514
  423.8 7.2 %collective-permute-start.36 = (f32[1,112,128]{2,1,0:T(8,128)S(1)}, f32[1,112,128]{2,1,0:T(8,128)S(1)}, u32[]{:S(2)}, u32[]{:S(2)}) collective-permute-start(f32[1,112,128]{2,1,0:T(8,128)S(1)} %fusion.14), channel_id=1, source_target_pairs={{0,8},{8,0},{16,24},{24,16},{1,9},{9,1},{17,25},{25,17},{2,10},{10... | collective-permute-start | bytes 172040 | tf_op jit(solution)/shard_map/ppermute | solution.py:514
  424.3 18.6 %collective-permute-start.39 = (bf16[96,768]{1,0:T(8,128)(2,1)S(1)}, bf16[96,768]{1,0:T(8,128)(2,1)S(1)}, u32[]{:S(2)}, u32[]{:S(2)}) collective-permute-start(bf16[96,768]{1,0:T(8,128)(2,1)S(1)} %get-tuple-element.139), channel_id=1, source_target_pairs={{0,8},{8,0},{16,24},{24,16},{1,9},{9,1},{17,25},{25,17},{2,10},{10... | collective-permute-start | bytes 442376 | tf_op jit(solution)/shard_map/ppermute | solution.py:514
  426.0 19.2 %collective-permute-start.41 = (bf16[96,768]{1,0:T(8,128)(2,1)S(1)}, bf16[96,768]{1,0:T(8,128)(2,1)S(1)}, u32[]{:S(2)}, u32[]{:S(2)}) collective-permute-start(bf16[96,768]{1,0:T(8,128)(2,1)S(1)} %get-tuple-element.140), channel_id=1, source_target_pairs={{0,24},{8,16},{16,8},{24,0},{1,25},{9,17},{17,9},{25,1},{2,26},{10... | collective-permute-start | bytes 442376 | tf_op jit(solution)/shard_map/ppermute | solution.py:514
  431.0 26.8 %collective-permute-start.40 = (bf16[96,768]{1,0:T(8,128)(2,1)S(1)}, bf16[96,768]{1,0:T(8,128)(2,1)S(1)}, u32[]{:S(2)}, u32[]{:S(2)}) collective-permute-start(bf16[96,768]{1,0:T(8,128)(2,1)S(1)} %get-tuple-element.141), channel_id=1, source_target_pairs={{0,16},{8,24},{16,0},{24,8},{1,17},{9,25},{17,1},{25,9},{2,18},{10... | collective-permute-start | bytes 442376 | tf_op jit(solution)/shard_map/ppermute | solution.py:514
  457.8 36.5 %collective-permute-start.44 = (bf16[96,768]{1,0:T(8,128)(2,1)S(1)}, bf16[96,768]{1,0:T(8,128)(2,1)S(1)}, u32[]{:S(2)}, u32[]{:S(2)}) collective-permute-start(bf16[96,768]{1,0:T(8,128)(2,1)S(1)} %fusion.11), channel_id=1, source_target_pairs={{0,8},{8,0},{16,24},{24,16},{1,9},{9,1},{17,25},{25,17},{2,10},{10... | collective-permute-start | bytes 442376 | tf_op jit(solution)/shard_map/ppermute | solution.py:514
  457.9 36.5 %collective-permute-start.43 = (bf16[96,768]{1,0:T(8,128)(2,1)S(1)}, bf16[96,768]{1,0:T(8,128)(2,1)S(1)}, u32[]{:S(2)}, u32[]{:S(2)}) collective-permute-start(bf16[96,768]{1,0:T(8,128)(2,1)S(1)} %fusion.11), channel_id=1, source_target_pairs={{0,16},{8,24},{16,0},{24,8},{1,17},{9,25},{17,1},{25,9},{2,18},{10... | collective-permute-start | bytes 442376 | tf_op jit(solution)/shard_map/ppermute | solution.py:514
  460.5 33.9 %collective-permute-start.42 = (bf16[96,768]{1,0:T(8,128)(2,1)S(1)}, bf16[96,768]{1,0:T(8,128)(2,1)S(1)}, u32[]{:S(2)}, u32[]{:S(2)}) collective-permute-start(bf16[96,768]{1,0:T(8,128)(2,1)S(1)} %fusion.11), channel_id=1, source_target_pairs={{0,24},{8,16},{16,8},{24,0},{1,25},{9,17},{17,9},{25,1},{2,26},{10... | collective-permute-start | bytes 442376 | tf_op jit(solution)/shard_map/ppermute | solution.py:514
  (28 other events, 81.6 us)
Sparse Core Ops, SparseCore 0:
  57.9 75.2 all-gather.2
  214.1 58.2 reduce-scatter.2
  298.5 66.6 reduce-scatter.4
  414.8 74.6 all-reduce.2

commit v6 on v4

--- a/solution.py
+++ b/solution.py
@@ -736,11 +736,11 @@
         3 * mixer_flops, "time_backward",
     )
     grad_space = exchange(going.reshape(own_shape))
+    up_share = lax.psum(up_share, "grp")
     time_grads, up_share, grad_space, result, *down_far = lax.optimization_barrier(
         (time_grads, up_share, grad_space, result, *down_far)
     )
     time_share = shard_total(time_grads)
-    up_parts = parts_of(up_share)
     down_share = far_finish(down_far)
     arrived = exchange(result.reshape(own_shape))
     grad_rows, space_mods, space_grads = run(
@@ -752,14 +752,16 @@
         weight_scratch + back_scratch(frame_count) + [dma(())],
         3 * mixer_flops, "space_backward",
     )
-    space_grads, space_mods, arrived, down_share, *up_parts = lax.optimization_barrier(
-        (space_grads, space_mods, arrived, down_share, *up_parts)
+    space_grads, space_mods, arrived, down_share = lax.optimization_barrier(
+        (space_grads, space_mods, arrived, down_share)
     )
     space_near = near_total(space_grads)
-    up_share = spread_parts(up_parts, up_share)
+    up_share = up_share.astype(F32)
     frames_out = to_rows(arrived)
     space_near, time_share = lax.optimization_barrier((space_near, time_share))
-    space_share = far_finish(far_start(space_near))
+    space_far = far_start(space_near)
+    space_far, space_mods = lax.optimization_barrier((space_far, space_mods))
+    space_share = far_finish(space_far)
     pair = total(jnp.stack([down_share, time_share], axis=1))
     down_share, time_share = pair[:, 0], pair[:, 1]
 

time: 494 us -> 501 us (1.014)
  waiting for transfers between devices: 140 us -> 153 us
  starting transfers between devices: 77 us -> 69.4 us
    psum x0 -> x1, waiting for transfers between devices: none -> 16.5 us  [body(): up_share = lax.psum(up_share, 'grp')]
    ppermute x24 -> x18, starting transfers between devices: 39.9 us -> 28.7 us  [swap_group(): return lax.ppermute(values, 'grp', pairs)]
    ppermute x24 -> x18, waiting for transfers between devices: 56.3 us -> 47.4 us  [swap_group(): return lax.ppermute(values, 'grp', pairs)]
  transfers between devices with their start and end apart: 58 -> 53, of which waited for: 19 -> 23; matrix products, arithmetic and copies ran while one was open for 11% -> 11% of each run, Pallas kernels for 24% -> 24%
where the time goes in v6:
time: 501 us; the launch traced here: 494 us
  Pallas kernels  162 us (32%)
  waiting for transfers between devices  153 us (31%)
  starting transfers between devices  69.4 us (14%)
  local copies, waits for them, and re-layouts  36.9 us (7%)
  other arithmetic  28 us (6%)
  blocking collectives  26.2 us (5%)
  between operations  15 us (3%)
    pallas_call x5, Pallas kernels, run(): pl.pallas_call(kernel, grid_spec=pltpu.PrefetchScalarGridSpec(num_scalar_...  162 us
    ppermute x27, waiting for transfers between devices, swap(): return lax.ppermute(values, 'shard', pairs)  58.3 us
    ppermute x18, waiting for transfers between devices, swap_group(): return lax.ppermute(values, 'grp', pairs)  47.4 us
    all_to_all x4, waiting for transfers between devices, exchange(): lax.all_to_all(parts, 'shard', split_axis=0, concat_axis=0, tiled=True)  29.3 us
    ppermute x18, starting transfers between devices, swap_group(): return lax.ppermute(values, 'grp', pairs)  28.7 us
    all_gather x1, blocking collectives, body(): lax.all_gather(small.reshape(1, -1, 128), 'shard', axis=0, tiled=True)  26.2 us
    ppermute x27, starting transfers between devices, swap(): return lax.ppermute(values, 'shard', pairs)  24.2 us
    psum x1, waiting for transfers between devices, body(): up_share = lax.psum(up_share, 'grp')  16.5 us
  transfers between devices with their start and end apart: 53, of which 23 were waited for; matrix products, arithmetic and copies ran while one was open for 11% of the time, Pallas kernels for 24%

profile of v6, /device:TPU:0, one launch (start us, length us, event | category | flops | bytes accessed | tf_op | source)
XLA Modules:
  0.0 493.8 jit_solution(3178446436294314528)
XLA Ops:
  8.5 1.8 pad_maximum_fusion.3.refs_0_
  10.3 3.9 collective-permute-start.5
  20.0 26.2 %all_gather.6 = f32[8,138,128]{2,1,0:T(8,128)S(1)} all-gather(f32[1,138,128]{2,1,0:T(8,128)S(1)} %maximum_bitcast_fusion), channel_id=1, replica_groups=mesh['grp'=4,'shard'=8] {'shard'}, dimensions={0}, use_global_device_ids=true | all-gather | bytes 635904 | tf_op jit(solution)/shard_map/all_gather | solution.py:540
  53.1 18.8 %space_forward.1 = (bf16[8,4,32,768]{3,2,1,0:T(8,128)(2,1)}, bf16[4,256,2304]{2,1,0:T(8,128)(2,1)}, bf16[4,256,768]{2,1,0:T(8,128)(2,1)}, f32[4,16,256]{2,1,0:T(8,128)}, bf16[4,256,768]{2,1,0:T(8,128)(2,1)}) custom-call(s32[5]{0:T(128)} %pad_add_fusion.where, f32[4,256,768]{2,1,0:T(8,128)} %frames_ref.3, f32[2,9,768]{2,1,0:T(8,128)} %reshape.321.mods_ref, ...), custom_call_target="tpu_custom_call" | custom-call | flops 6442450944 | bytes 17422336 | tf_op jit(solution)/shard_map/space_forward/pallas_call | solution.py:431
  72.0 3.6 all-to-all-start
  76.9 2.8 collective-permute-start.12
  80.4 2.2 multiply_convert_fusion
  82.6 1.2 copy.133
  83.9 29.2 %all-to-all-done = bf16[8,4,32,768]{3,2,1,0:T(8,128)(2,1)S(1)} async-done(((bf16[8,4,32,768]{3,2,1,0:T(8,128)(2,1)}), bf16[8,4,32,768]{3,2,1,0:T(8,128)(2,1)S(1)}, u32[]{:S(2)}, u32[]{:S(2)}) %all-to-all-start) | async-done | bytes 1572896 | tf_op jit(solution)/shard_map/all_to_all | solution.py:566
  114.3 4.4 all-to-all-start.1
  119.3 15.8 %collective-permute-done.12.refs_6_ = bf16[4,96,768]{2,1,0:T(8,128)(2,1)} collective-permute-done((bf16[4,96,768]{2,1,0:T(8,128)(2,1)S(1)}, bf16[4,96,768]{2,1,0:T(8,128)(2,1)}, u32[]{:S(2)}, u32[]{:S(2)}) %collective-permute-start.12) | collective-permute-done | bytes 589856 | tf_op jit(solution)/shard_map/ppermute | solution.py:485
  135.1 6.7 %collective-permute-done.10.refs_4_ = bf16[4,96,768]{2,1,0:T(8,128)(2,1)} collective-permute-done((bf16[4,96,768]{2,1,0:T(8,128)(2,1)S(1)}, bf16[4,96,768]{2,1,0:T(8,128)(2,1)}, u32[]{:S(2)}, u32[]{:S(2)}) %collective-permute-start.10) | collective-permute-done | bytes 589856 | tf_op jit(solution)/shard_map/ppermute | solution.py:485
  141.8 5.0 %collective-permute-done.8.refs_2_ = bf16[4,96,768]{2,1,0:T(8,128)(2,1)} collective-permute-done((bf16[4,96,768]{2,1,0:T(8,128)(2,1)S(1)}, bf16[4,96,768]{2,1,0:T(8,128)(2,1)}, u32[]{:S(2)}, u32[]{:S(2)}) %collective-permute-start.8) | collective-permute-done | bytes 589856 | tf_op jit(solution)/shard_map/ppermute | solution.py:485
  147.5 1.3 slice.188
  151.1 19.0 %time_forward.1 = (bf16[4,256,768]{2,1,0:T(8,128)(2,1)}, f32[4,256,768]{2,1,0:T(8,128)}, bf16[4,256,2304]{2,1,0:T(8,128)(2,1)}, bf16[4,256,768]{2,1,0:T(8,128)(2...) custom-call(s32[33]{0:T(128)} %pad_add_fusion.1.inverse, bf16[32,32,768]{2,1,0:T(8,128)(2,1)} %bitcast.227, ...), custom_call_target="tpu_custom_call" | custom-call | flops 6442450944 | bytes 18995200 | tf_op jit(solution)/shard_map/time_forward/pallas_call | solution.py:431
  170.2 43.8 %feed.1 = (bf16[32,32,768]{2,1,0:T(8,128)(2,1)}, f32[4,256,768]{2,1,0:T(8,128)}, f32[2,3,768]{2,1,0:T(4,128)}, f32[1,3072]{1,0:T(1,128)}, f32[1,768]{1,0:T(1,128...) custom-call(s32[33]{0:T(128)} %pad_add_fusion.1.inverse, ...), custom_call_target="tpu_custom_call" | custom-call | flops 28991029248 | bytes 28416000 | tf_op jit(solution)/shard_map/feed/pallas_call | solution.py:431
  214.1 3.2 slice_bitcast_fusion.1
  217.8 39.9 %time_backward.1 = (bf16[32,32,768]{2,1,0:T(8,128)(2,1)}, f32[2,3,768]{2,1,0:T(4,128)}, bf16[8,4,96,768]{3,2,1,0:T(8,128)(2,1)}) custom-call(s32[33]{0:T(128)} %pad_add_fusion.1.inverse, f32[4,256,768]{2,1,0:T(8,128)} %get-tuple-element.65.grad_ref, bf16[4,256,768]{2,1,0:T(8,128)(2,1)} %get-tuple-element.66.resid_ref, f32[2,9,768]{2,1,0:T(8,128)} %reshape.321.mods_ref, ...), custom_call_target="tpu_custom_call" | custom-call | flops 19327352832 | bytes 23732224 | tf_op jit(solution)/shard_map/time_backward/pallas_call | solution.py:431
  257.7 4.3 all-to-all-start.2
  262.1 3.1 fusion.1
  265.2 2.0 collective-permute-start.16
  268.1 1.5 collective-permute-start.15
  270.9 26.0 %collective-permute-done.16 = bf16[2,2,96,768]{3,2,1,0:T(8,128)(2,1)} collective-permute-done((bf16[2,2,96,768]{3,2,1,0:T(8,128)(2,1)S(1)}, bf16[2,2,96,768]{3,2,1,0:T(8,128)(2,1)}, u32[]{:S(2)}, u32[]{:S(2)}) %collective-permute-start.16) | collective-permute-done | bytes 589856 | tf_op jit(solution)/shard_map/ppermute | solution.py:485
  296.9 1.4 add_convert_fusion.1
  298.3 2.0 fusion.3
  300.3 16.5 %all-reduce.3.cloned.1.call-done = bf16[4,96,768]{2,1,0:T(8,128)(2,1)} async-done(((bf16[4,96,768]{2,1,0:T(8,128)(2,1)}), bf16[4,96,768]{2,1,0:T(8,128)(2,1)}) %all-reduce.3.cloned.1.call-update) | async-done | bytes 589840 | tf_op jit(solution)/shard_map/psum | solution.py:739
  316.8 3.9 all-to-all-start.3
  321.4 2.0 collective-permute-start.18
  323.4 1.7 slice_bitcast_fusion.11
  325.1 1.5 collective-permute-start.17
  326.6 40.1 %space_backward.1 = (f32[4,256,768]{2,1,0:T(8,128)}, f32[2,3,768]{2,1,0:T(4,128)}, bf16[2,4,4,96,768]{4,3,2,1,0:T(8,128)(2,1)}) custom-call(s32[5]{0:T(128)} %pad_add_fusion.where, bf16[8,4,32,768]{3,2,1,0:T(8,128)(2,1)} %all-to-all-done.2.grad_ref, f32[4,256,768]{2,1,0:T(8,128)} %frames_ref.3, f32[2,9,768]{2,1,0:T(8,128)} %reshape.321.mods_ref, ...), custom_call_target="tpu_custom_call" | custom-call | flops 19327352832 | bytes 25305088 | tf_op jit(solution)/shard_map/space_backward/pallas_call | solution.py:431
  368.8 3.2 slice_bitcast_fusion
  372.3 1.9 collective-permute-start.21
  375.1 1.6 collective-permute-start.19
  376.7 1.9 collective-permute-done.19
  381.7 4.5 fusion
  387.4 1.4 slice.156
  389.8 1.7 collective-permute-start.39
  391.5 1.7 collective-permute-start.41
  393.7 2.0 copy.106
  395.7 5.3 %collective-permute-done.39 = bf16[192,768]{1,0:T(8,128)(2,1)S(1)} collective-permute-done((bf16[192,768]{1,0:T(8,128)(2,1)S(1)}, bf16[192,768]{1,0:T(8,128)(2,1)S(1)}, u32[]{:S(2)}, u32[]{:S(2)}) %collective-permute-start.39) | collective-permute-done | bytes 294944 | tf_op jit(solution)/shard_map/ppermute | solution.py:495
  401.1 6.5 %collective-permute-done.41 = bf16[192,768]{1,0:T(8,128)(2,1)S(1)} collective-permute-done((bf16[192,768]{1,0:T(8,128)(2,1)S(1)}, bf16[192,768]{1,0:T(8,128)(2,1)S(1)}, u32[]{:S(2)}, u32[]{:S(2)}) %collective-permute-start.41) | collective-permute-done | bytes 294944 | tf_op jit(solution)/shard_map/ppermute | solution.py:495
  407.5 10.2 %collective-permute-done.40 = bf16[192,768]{1,0:T(8,128)(2,1)S(1)} collective-permute-done((bf16[192,768]{1,0:T(8,128)(2,1)S(1)}, bf16[192,768]{1,0:T(8,128)(2,1)S(1)}, u32[]{:S(2)}, u32[]{:S(2)}) %collective-permute-start.40) | collective-permute-done | bytes 294944 | tf_op jit(solution)/shard_map/ppermute | solution.py:495
  418.0 2.4 collective-permute-start.43
  420.5 1.9 collective-permute-start.42
  424.6 1.8 collective-permute-start.29
  426.5 3.8 collective-permute-done.44
  430.2 1.7 collective-permute-start.28
  432.0 9.1 %collective-permute-done.43 = bf16[192,768]{1,0:T(8,128)(2,1)S(1)} collective-permute-done((bf16[192,768]{1,0:T(8,128)(2,1)S(1)}, bf16[192,768]{1,0:T(8,128)(2,1)S(1)}, u32[]{:S(2)}, u32[]{:S(2)}) %collective-permute-start.43) | collective-permute-done | bytes 294944 | tf_op jit(solution)/shard_map/ppermute | solution.py:495
  443.0 1.5 collective-permute-start.26
  444.6 2.9 collective-permute-done.26
  447.4 1.5 collective-permute-start.27
  452.3 2.1 collective-permute-start.32
  454.3 3.7 collective-permute-start.31
  458.1 2.1 collective-permute-start.33
  460.2 1.8 collective-permute-start.35
  462.2 2.2 collective-permute-start.34
  464.4 1.3 collective-permute-done.31
  466.0 2.1 fusion.23
  469.7 2.8 collective-permute-done.34
  472.6 2.4 collective-permute-start.37
  475.0 2.0 collective-permute-start.36
  478.3 1.9 collective-permute-done.38
  480.1 4.3 collective-permute-done.37
  (250 shorter events, 46.7 us)
Async XLA Ops:
  7.2 9.2 %copy-start = (bf16[96,6912]{1,0:T(8,128)(2,1)S(1)}, bf16[96,6912]{1,0:T(8,128)(2,1)}, u32[]{:S(2)}) copy-start(bf16[96,6912]{1,0:T(8,128)(2,1)} %param.20) | copy-start | bytes 3981316
  7.2 8.1 %copy-start.26 = (bf16[864]{0:T(1024)(128)(2,1)S(1)}, bf16[864]{0:T(1024)(128)(2,1)}, u32[]{:S(2)}) copy-start(bf16[864]{0:T(1024)(128)(2,1)} %param.21) | copy-start | bytes 5188
  7.2 8.3 %copy-start.12 = (bf16[1000,96]{0,1:T(8,128)(2,1)S(1)}, bf16[1000,96]{0,1:T(8,128)(2,1)}, u32[]{:S(2)}) copy-start(bf16[1000,96]{0,1:T(8,128)(2,1)} %param.19) | copy-start | bytes 576004
  7.2 162.9 %all-gather.3.cloned.1.call-start = ((), (), s32[]{:S(2)}) async-start(), calls=%async_computation.9 | async-start | bytes 10616832 | tf_op jit(solution)/shard_map/all_gather | solution.py:488
  8.4 8.3 %copy-start.32 = (bf16[96]{0:T(256)(128)(2,1)S(1)}, bf16[96]{0:T(256)(128)(2,1)}, u32[]{:S(2)}) copy-start(bf16[96]{0:T(256)(128)(2,1)} %param.29) | copy-start | bytes 580
  8.4 8.3 %copy-start.27 = (bf16[384]{0:T(512)(128)(2,1)S(1)}, bf16[384]{0:T(512)(128)(2,1)}, u32[]{:S(2)}) copy-start(bf16[384]{0:T(512)(128)(2,1)} %param.27) | copy-start | bytes 2308
  8.4 9.7 %copy-start.10 = (bf16[96,2304]{1,0:T(8,128)(2,1)S(1)}, bf16[96,2304]{1,0:T(8,128)(2,1)}, u32[]{:S(2)}) copy-start(bf16[96,2304]{1,0:T(8,128)(2,1)} %param.24) | copy-start | bytes 1327108
  10.3 36.6 %collective-permute-start.5 = (bf16[4,96,768]{2,1,0:T(8,128)(2,1)}, bf16[4,96,768]{2,1,0:T(8,128)(2,1)}, u32[]{:S(2)}, u32[]{:S(2)}) collective-permute-start(bf16[4,96,768]{2,1,0:T(8,128)(2,1)} %pad_maximum_fusion.3.refs_0_), channel_id=1, source_target_pairs={{0,6},{1,7},{2,4},{3,5},{4,2},{5,3},{6,0},{7,1},{8,14},{9,15},{10,... | collective-permute-start | bytes 1769480 | tf_op jit(solution)/shard_map/ppermute | solution.py:485
  14.2 32.7 %collective-permute-start.3 = (bf16[4,96,768]{2,1,0:T(8,128)(2,1)}, bf16[4,96,768]{2,1,0:T(8,128)(2,1)}, u32[]{:S(2)}, u32[]{:S(2)}) collective-permute-start(bf16[4,96,768]{2,1,0:T(8,128)(2,1)} %pad_maximum_fusion.3.refs_0_), channel_id=1, source_target_pairs={{0,4},{1,5},{2,6},{3,7},{4,0},{5,1},{6,2},{7,3},{8,12},{9,13},{10,... | collective-permute-start | bytes 1769480 | tf_op jit(solution)/shard_map/ppermute | solution.py:485
  14.7 32.2 %collective-permute-start = (bf16[4,96,768]{2,1,0:T(8,128)(2,1)}, bf16[4,96,768]{2,1,0:T(8,128)(2,1)}, u32[]{:S(2)}, u32[]{:S(2)}) collective-permute-start(bf16[4,96,768]{2,1,0:T(8,128)(2,1)} %pad_maximum_fusion.3.refs_0_), channel_id=1, source_target_pairs={{0,2},{1,3},{2,0},{3,1},{4,6},{5,7},{6,4},{7,5},{8,10},{9,11},{10,... | collective-permute-start | bytes 1769480 | tf_op jit(solution)/shard_map/ppermute | solution.py:485
  18.7 27.5 %copy-start.13 = (bf16[96,768]{1,0:T(8,128)(2,1)S(1)}, bf16[96,768]{1,0:T(8,128)(2,1)}, u32[]{:S(2)}) copy-start(bf16[96,768]{1,0:T(8,128)(2,1)} %param.25) | copy-start | bytes 442372
  46.3 72.6 %copy-start.8 = (bf16[4,96,768]{2,1,0:T(8,128)(2,1)}, bf16[4,96,768]{2,1,0:T(8,128)(2,1)S(1)}, u32[]{:S(2)}) copy-start(bf16[4,96,768]{2,1,0:T(8,128)(2,1)S(1)} %pad_maximum_fusion.4.refs_0_) | copy-start | bytes 1769476
  48.2 3.1 collective-permute-start.1
  48.6 2.8 collective-permute-start.6
  48.7 3.5 collective-permute-start.4
  49.1 4.0 collective-permute-start.2
  50.6 21.3 %copy-start.11 = (f32[138,128]{1,0:T(8,128)}, f32[138,128]{1,0:T(8,128)S(1)}, u32[]{:S(2)}) copy-start(f32[138,128]{1,0:T(8,128)S(1)} %reduce_sum.37) | copy-start | bytes 211972
  72.0 41.1 %all-to-all-start = ((bf16[8,4,32,768]{3,2,1,0:T(8,128)(2,1)}), bf16[8,4,32,768]{3,2,1,0:T(8,128)(2,1)S(1)}, u32[]{:S(2)}, u32[]{:S(2)}) async-start(bf16[8,4,32,768]{3,2,1,0:T(8,128)(2,1)} %get-tuple-element.61), calls=%async_computation | async-start | bytes 3145728 | tf_op jit(solution)/shard_map/all_to_all | solution.py:566
  76.9 58.1 %collective-permute-start.12 = (bf16[4,96,768]{2,1,0:T(8,128)(2,1)S(1)}, bf16[4,96,768]{2,1,0:T(8,128)(2,1)}, u32[]{:S(2)}, u32[]{:S(2)}) collective-permute-start(bf16[4,96,768]{2,1,0:T(8,128)(2,1)S(1)} %pad_maximum_fusion.4.refs_0_), channel_id=1, source_target_pairs={{0,6},{1,7},{2,4},{3,5},{4,2},{5,3},{6,0},{7,1},{8,14},{9,15},{10,... | collective-permute-start | bytes 1769480 | tf_op jit(solution)/shard_map/ppermute | solution.py:485
  79.8 62.0 %collective-permute-start.10 = (bf16[4,96,768]{2,1,0:T(8,128)(2,1)S(1)}, bf16[4,96,768]{2,1,0:T(8,128)(2,1)}, u32[]{:S(2)}, u32[]{:S(2)}) collective-permute-start(bf16[4,96,768]{2,1,0:T(8,128)(2,1)S(1)} %pad_maximum_fusion.4.refs_0_), channel_id=1, source_target_pairs={{0,4},{1,5},{2,6},{3,7},{4,0},{5,1},{6,2},{7,3},{8,12},{9,13},{10,... | collective-permute-start | bytes 1769480 | tf_op jit(solution)/shard_map/ppermute | solution.py:485
  80.3 66.5 %collective-permute-start.8 = (bf16[4,96,768]{2,1,0:T(8,128)(2,1)S(1)}, bf16[4,96,768]{2,1,0:T(8,128)(2,1)}, u32[]{:S(2)}, u32[]{:S(2)}) collective-permute-start(bf16[4,96,768]{2,1,0:T(8,128)(2,1)S(1)} %pad_maximum_fusion.4.refs_0_), channel_id=1, source_target_pairs={{0,2},{1,3},{2,0},{3,1},{4,6},{5,7},{6,4},{7,5},{8,10},{9,11},{10,... | collective-permute-start | bytes 1769480 | tf_op jit(solution)/shard_map/ppermute | solution.py:485
  114.3 55.9 %all-to-all-start.1 = ((bf16[8,4,32,768]{3,2,1,0:T(8,128)(2,1)}), bf16[8,4,32,768]{3,2,1,0:T(8,128)(2,1)}, u32[]{:S(2)}, u32[]{:S(2)}) async-start(bf16[8,4,32,768]{3,2,1,0:T(8,128)(2,1)} %bitcast.200), calls=%async_computation.1 | async-start | bytes 3145728 | tf_op jit(solution)/shard_map/all_to_all | solution.py:566
  118.6 152.1 %reduce-scatter.3.cloned.1.call-start = ((), (), s32[]{:S(2)}) async-start(), calls=%async_computation.6 | async-start | bytes 5308416 | tf_op jit(solution)/shard_map/reduce_scatter | solution.py:670
  118.9 31.2 %collective-permute-start.7 = (bf16[4,96,768]{2,1,0:T(8,128)(2,1)S(1)}, bf16[4,96,768]{2,1,0:T(8,128)(2,1)S(1)}, u32[]{:S(2)}, u32[]{:S(2)}) collective-permute-start(bf16[4,96,768]{2,1,0:T(8,128)(2,1)S(1)} %pad_maximum_fusion.4.refs_0_), channel_id=1, source_target_pairs={{0,1},{1,0},{2,3},{3,2},{4,5},{5,4},{6,7},{7,6},{8,9},{9,8},{10,11... | collective-permute-start | bytes 1769480 | tf_op jit(solution)/shard_map/ppermute | solution.py:485
  135.1 15.0 %collective-permute-start.13 = (bf16[4,96,768]{2,1,0:T(8,128)(2,1)}, bf16[4,96,768]{2,1,0:T(8,128)(2,1)S(1)}, u32[]{:S(2)}, u32[]{:S(2)}) collective-permute-start(bf16[4,96,768]{2,1,0:T(8,128)(2,1)} %collective-permute-done.12.refs_6_), channel_id=1, source_target_pairs={{0,1},{1,0},{2,3},{3,2},{4,5},{5,4},{6,7},{7,6},{8,9},{9,8},{10,11... | collective-permute-start | bytes 1769480 | tf_op jit(solution)/shard_map/ppermute | solution.py:485
  141.8 8.3 %collective-permute-start.11 = (bf16[4,96,768]{2,1,0:T(8,128)(2,1)}, bf16[4,96,768]{2,1,0:T(8,128)(2,1)}, u32[]{:S(2)}, u32[]{:S(2)}) collective-permute-start(bf16[4,96,768]{2,1,0:T(8,128)(2,1)} %collective-permute-done.10.refs_4_), channel_id=1, source_target_pairs={{0,1},{1,0},{2,3},{3,2},{4,5},{5,4},{6,7},{7,6},{8,9},{9,8},{10,11... | collective-permute-start | bytes 1769480 | tf_op jit(solution)/shard_map/ppermute | solution.py:485
  146.8 3.3 collective-permute-start.9
  217.3 44.8 %collective-permute-start.14 = (bf16[4,4,96,768]{3,2,1,0:T(8,128)(2,1)}, bf16[4,4,96,768]{3,2,1,0:T(8,128)(2,1)}, u32[]{:S(2)}, u32[]{:S(2)}) collective-permute-start(bf16[4,4,96,768]{3,2,1,0:T(8,128)(2,1)} %slice_bitcast_fusion.1), channel_id=1, source_target_pairs={{0,1},{1,0},{2,3},{3,2},{4,5},{5,4},{6,7},{7,6},{8,9},{9,8},{10,11... | collective-permute-start | bytes 7077896 | tf_op jit(solution)/shard_map/ppermute | solution.py:485
  257.7 42.6 %all-to-all-start.2 = ((bf16[8,4,32,768]{3,2,1,0:T(8,128)(2,1)}), bf16[8,4,32,768]{3,2,1,0:T(8,128)(2,1)}, u32[]{:S(2)}, u32[]{:S(2)}) async-start(bf16[8,4,32,768]{3,2,1,0:T(8,128)(2,1)} %bitcast.228), calls=%async_computation.3 | async-start | bytes 3145728 | tf_op jit(solution)/shard_map/all_to_all | solution.py:566
  262.0 54.7 %all-reduce.3.cloned.1.call-start = ((), (), s32[]{:S(2)}) async-start(), calls=%async_computation.7 | async-start | bytes 1179648 | tf_op jit(solution)/shard_map/psum | solution.py:739
  265.2 31.6 %collective-permute-start.16 = (bf16[2,2,96,768]{3,2,1,0:T(8,128)(2,1)S(1)}, bf16[2,2,96,768]{3,2,1,0:T(8,128)(2,1)}, u32[]{:S(2)}, u32[]{:S(2)}) collective-permute-start(bf16[2,2,96,768]{3,2,1,0:T(8,128)(2,1)S(1)} %slice.194), channel_id=1, source_target_pairs={{0,4},{1,5},{2,6},{3,7},{4,0},{5,1},{6,2},{7,3},{8,12},{9,13},{10,... | collective-permute-start | bytes 1769480 | tf_op jit(solution)/shard_map/ppermute | solution.py:485
  268.1 30.1 %collective-permute-start.15 = (bf16[2,2,96,768]{3,2,1,0:T(8,128)(2,1)}, bf16[2,2,96,768]{3,2,1,0:T(8,128)(2,1)}, u32[]{:S(2)}, u32[]{:S(2)}) collective-permute-start(bf16[2,2,96,768]{3,2,1,0:T(8,128)(2,1)} %slice_bitcast_fusion.5), channel_id=1, source_target_pairs={{0,2},{1,3},{2,0},{3,1},{4,6},{5,7},{6,4},{7,5},{8,10},{9,11},{10,... | collective-permute-start | bytes 1769480 | tf_op jit(solution)/shard_map/ppermute | solution.py:485
  270.8 115.4 %reduce-scatter.5.cloned.1.call-start = ((), (), s32[]{:S(2)}) async-start(), calls=%async_computation.8 | async-start | bytes 5308416 | tf_op jit(solution)/shard_map/reduce_scatter | solution.py:670
  316.8 52.0 %all-to-all-start.3 = ((bf16[8,4,32,768]{3,2,1,0:T(8,128)(2,1)}), bf16[8,4,32,768]{3,2,1,0:T(8,128)(2,1)S(1)}, u32[]{:S(2)}, u32[]{:S(2)}) async-start(bf16[8,4,32,768]{3,2,1,0:T(8,128)(2,1)} %bitcast.226), calls=%async_computation.4 | async-start | bytes 3145728 | tf_op jit(solution)/shard_map/all_to_all | solution.py:566
  321.4 45.2 %collective-permute-start.18 = (bf16[2,96,768]{2,1,0:T(8,128)(2,1)}, bf16[2,96,768]{2,1,0:T(8,128)(2,1)}, u32[]{:S(2)}, u32[]{:S(2)}) collective-permute-start(bf16[2,96,768]{2,1,0:T(8,128)(2,1)} %slice_bitcast_fusion.10), channel_id=1, source_target_pairs={{0,2},{1,3},{2,0},{3,1},{4,6},{5,7},{6,4},{7,5},{8,10},{9,11},{10,... | collective-permute-start | bytes 884744 | tf_op jit(solution)/shard_map/ppermute | solution.py:485
  325.1 42.6 %collective-permute-start.17 = (bf16[2,96,768]{2,1,0:T(8,128)(2,1)}, bf16[2,96,768]{2,1,0:T(8,128)(2,1)S(1)}, u32[]{:S(2)}, u32[]{:S(2)}) collective-permute-start(bf16[2,96,768]{2,1,0:T(8,128)(2,1)} %slice_bitcast_fusion.11), channel_id=1, source_target_pairs={{0,4},{1,5},{2,6},{3,7},{4,0},{5,1},{6,2},{7,3},{8,12},{9,13},{10,... | collective-permute-start | bytes 884744 | tf_op jit(solution)/shard_map/ppermute | solution.py:485
  368.8 10.6 %copy-start.21 = (f32[1,768]{1,0:T(1,128)S(1)}, f32[1,768]{1,0:T(1,128)}, u32[]{:S(2)}) copy-start(f32[1,768]{1,0:T(1,128)} %get-tuple-element.97) | copy-start | bytes 9220
  372.1 9.7 %collective-permute-start.22 = (bf16[4,4,96,768]{3,2,1,0:T(8,128)(2,1)}, bf16[4,4,96,768]{3,2,1,0:T(8,128)(2,1)}, u32[]{:S(2)}, u32[]{:S(2)}) collective-permute-start(bf16[4,4,96,768]{3,2,1,0:T(8,128)(2,1)} %slice_bitcast_fusion), channel_id=1, source_target_pairs={{0,1},{1,0},{2,3},{3,2},{4,5},{5,4},{6,7},{7,6},{8,9},{9,8},{10,11... | collective-permute-start | bytes 7077896 | tf_op jit(solution)/shard_map/ppermute | solution.py:485
  372.3 6.4 %collective-permute-start.21 = (f32[2,97]{1,0:T(2,128)S(1)}, f32[2,97]{1,0:T(2,128)S(1)}, u32[]{:S(2)}, u32[]{:S(2)}) collective-permute-start(f32[2,97]{1,0:T(2,128)S(1)} %pad_maximum_fusion.8), channel_id=1, source_target_pairs={{0,24},{8,16},{16,8},{24,0},{1,25},{9,17},{17,9},{25,1},{2,26},{10... | collective-permute-start | bytes 2336 | tf_op jit(solution)/shard_map/ppermute | solution.py:495
  374.2 4.5 collective-permute-start.20
  375.1 3.6 collective-permute-start.19
  388.9 33.5 %collective-permute-start.24 = (bf16[2,2,96,768]{3,2,1,0:T(8,128)(2,1)S(1)}, bf16[2,2,96,768]{3,2,1,0:T(8,128)(2,1)S(1)}, u32[]{:S(2)}, u32[]{:S(2)}) collective-permute-start(bf16[2,2,96,768]{3,2,1,0:T(8,128)(2,1)S(1)} %slice.160), channel_id=1, source_target_pairs={{0,4},{1,5},{2,6},{3,7},{4,0},{5,1},{6,2},{7,3},{8,12},{9,13},{10,... | collective-permute-start | bytes 1769480 | tf_op jit(solution)/shard_map/ppermute | solution.py:485
  389.6 34.0 %collective-permute-start.23 = (bf16[2,2,96,768]{3,2,1,0:T(8,128)(2,1)S(1)}, bf16[2,2,96,768]{3,2,1,0:T(8,128)(2,1)S(1)}, u32[]{:S(2)}, u32[]{:S(2)}) collective-permute-start(bf16[2,2,96,768]{3,2,1,0:T(8,128)(2,1)S(1)} %slice_bitcast_fusion.3), channel_id=1, source_target_pairs={{0,2},{1,3},{2,0},{3,1},{4,6},{5,7},{6,4},{7,5},{8,10},{9,11},{10,... | collective-permute-start | bytes 1769480 | tf_op jit(solution)/shard_map/ppermute | solution.py:485
  389.8 11.3 %collective-permute-start.39 = (bf16[192,768]{1,0:T(8,128)(2,1)S(1)}, bf16[192,768]{1,0:T(8,128)(2,1)S(1)}, u32[]{:S(2)}, u32[]{:S(2)}) collective-permute-start(bf16[192,768]{1,0:T(8,128)(2,1)S(1)} %get-tuple-element.109), channel_id=1, source_target_pairs={{0,8},{8,0},{16,24},{24,16},{1,9},{9,1},{17,25},{25,17},{2,10},{10... | collective-permute-start | bytes 884744 | tf_op jit(solution)/shard_map/ppermute | solution.py:495
  391.5 16.0 %collective-permute-start.41 = (bf16[192,768]{1,0:T(8,128)(2,1)S(1)}, bf16[192,768]{1,0:T(8,128)(2,1)S(1)}, u32[]{:S(2)}, u32[]{:S(2)}) collective-permute-start(bf16[192,768]{1,0:T(8,128)(2,1)S(1)} %get-tuple-element.110), channel_id=1, source_target_pairs={{0,24},{8,16},{16,8},{24,0},{1,25},{9,17},{17,9},{25,1},{2,26},{10... | collective-permute-start | bytes 884744 | tf_op jit(solution)/shard_map/ppermute | solution.py:495
  393.3 24.5 %collective-permute-start.40 = (bf16[192,768]{1,0:T(8,128)(2,1)S(1)}, bf16[192,768]{1,0:T(8,128)(2,1)S(1)}, u32[]{:S(2)}, u32[]{:S(2)}) collective-permute-start(bf16[192,768]{1,0:T(8,128)(2,1)S(1)} %get-tuple-element.111), channel_id=1, source_target_pairs={{0,16},{8,24},{16,0},{24,8},{1,17},{9,25},{17,1},{25,9},{2,18},{10... | collective-permute-start | bytes 884744 | tf_op jit(solution)/shard_map/ppermute | solution.py:495
  418.0 12.3 %collective-permute-start.44 = (bf16[192,768]{1,0:T(8,128)(2,1)S(1)}, bf16[192,768]{1,0:T(8,128)(2,1)S(1)}, u32[]{:S(2)}, u32[]{:S(2)}) collective-permute-start(bf16[192,768]{1,0:T(8,128)(2,1)S(1)} %fusion.6), channel_id=1, source_target_pairs={{0,8},{8,0},{16,24},{24,16},{1,9},{9,1},{17,25},{25,17},{2,10},{10... | collective-permute-start | bytes 884744 | tf_op jit(solution)/shard_map/ppermute | solution.py:495
  418.0 23.1 %collective-permute-start.43 = (bf16[192,768]{1,0:T(8,128)(2,1)S(1)}, bf16[192,768]{1,0:T(8,128)(2,1)S(1)}, u32[]{:S(2)}, u32[]{:S(2)}) collective-permute-start(bf16[192,768]{1,0:T(8,128)(2,1)S(1)} %fusion.6), channel_id=1, source_target_pairs={{0,16},{8,24},{16,0},{24,8},{1,17},{9,25},{17,1},{25,9},{2,18},{10... | collective-permute-start | bytes 884744 | tf_op jit(solution)/shard_map/ppermute | solution.py:495
  420.5 20.6 %collective-permute-start.42 = (bf16[192,768]{1,0:T(8,128)(2,1)S(1)}, bf16[192,768]{1,0:T(8,128)(2,1)}, u32[]{:S(2)}, u32[]{:S(2)}) collective-permute-start(bf16[192,768]{1,0:T(8,128)(2,1)S(1)} %fusion.6), channel_id=1, source_target_pairs={{0,24},{8,16},{16,8},{24,0},{1,25},{9,17},{17,9},{25,1},{2,26},{10... | collective-permute-start | bytes 884744 | tf_op jit(solution)/shard_map/ppermute | solution.py:495
  424.6 17.9 %collective-permute-start.25 = (f32[138,128]{1,0:T(8,128)S(1)}, f32[138,128]{1,0:T(8,128)S(1)}, u32[]{:S(2)}, u32[]{:S(2)}) collective-permute-start(f32[138,128]{1,0:T(8,128)S(1)} %maximum_bitcast_fusion.1), channel_id=1, source_target_pairs={{0,1},{1,0},{2,3},{3,2},{4,5},{5,4},{6,7},{7,6},{8,9},{9,8},{10,11... | collective-permute-start | bytes 211976 | tf_op jit(solution)/shard_map/ppermute | solution.py:485
  424.6 27.4 %collective-permute-start.29 = (bf16[2,96,768]{2,1,0:T(8,128)(2,1)S(1)}, bf16[2,96,768]{2,1,0:T(8,128)(2,1)S(1)}, u32[]{:S(2)}, u32[]{:S(2)}) collective-permute-start(bf16[2,96,768]{2,1,0:T(8,128)(2,1)S(1)} %slice_bitcast_fusion.8), channel_id=1, source_target_pairs={{0,2},{1,3},{2,0},{3,1},{4,6},{5,7},{6,4},{7,5},{8,10},{9,11},{10,... | collective-permute-start | bytes 884744 | tf_op jit(solution)/shard_map/ppermute | solution.py:485
  430.2 21.9 %collective-permute-start.28 = (bf16[2,96,768]{2,1,0:T(8,128)(2,1)S(1)}, bf16[2,96,768]{2,1,0:T(8,128)(2,1)S(1)}, u32[]{:S(2)}, u32[]{:S(2)}) collective-permute-start(bf16[2,96,768]{2,1,0:T(8,128)(2,1)S(1)} %slice_bitcast_fusion.9), channel_id=1, source_target_pairs={{0,4},{1,5},{2,6},{3,7},{4,0},{5,1},{6,2},{7,3},{8,12},{9,13},{10,... | collective-permute-start | bytes 884744 | tf_op jit(solution)/shard_map/ppermute | solution.py:485
  443.0 4.4 collective-permute-start.26
  447.4 4.4 collective-permute-start.27
  452.3 13.4 %collective-permute-start.32 = (f32[1,112,128]{2,1,0:T(8,128)S(1)}, f32[1,112,128]{2,1,0:T(8,128)S(1)}, u32[]{:S(2)}, u32[]{:S(2)}) collective-permute-start(f32[1,112,128]{2,1,0:T(8,128)S(1)} %fusion.16), channel_id=1, source_target_pairs={{0,24},{8,16},{16,8},{24,0},{1,25},{9,17},{17,9},{25,1},{2,26},{10... | collective-permute-start | bytes 172040 | tf_op jit(solution)/shard_map/ppermute | solution.py:495
  454.3 11.4 %collective-permute-start.31 = (f32[1,112,128]{2,1,0:T(8,128)S(1)}, f32[1,112,128]{2,1,0:T(8,128)S(1)}, u32[]{:S(2)}, u32[]{:S(2)}) collective-permute-start(f32[1,112,128]{2,1,0:T(8,128)S(1)} %fusion.16), channel_id=1, source_target_pairs={{0,16},{8,24},{16,0},{24,8},{1,17},{9,25},{17,1},{25,9},{2,18},{10... | collective-permute-start | bytes 172040 | tf_op jit(solution)/shard_map/ppermute | solution.py:495
  458.0 4.2 collective-permute-start.30
  458.1 11.6 %collective-permute-start.33 = (bf16[96,768]{1,0:T(8,128)(2,1)S(1)}, bf16[96,768]{1,0:T(8,128)(2,1)S(1)}, u32[]{:S(2)}, u32[]{:S(2)}) collective-permute-start(bf16[96,768]{1,0:T(8,128)(2,1)S(1)} %get-tuple-element.116), channel_id=1, source_target_pairs={{0,8},{8,0},{16,24},{24,16},{1,9},{9,1},{17,25},{25,17},{2,10},{10... | collective-permute-start | bytes 442376 | tf_op jit(solution)/shard_map/ppermute | solution.py:495
  460.2 9.5 %collective-permute-start.35 = (bf16[96,768]{1,0:T(8,128)(2,1)S(1)}, bf16[96,768]{1,0:T(8,128)(2,1)S(1)}, u32[]{:S(2)}, u32[]{:S(2)}) collective-permute-start(bf16[96,768]{1,0:T(8,128)(2,1)S(1)} %get-tuple-element.117), channel_id=1, source_target_pairs={{0,24},{8,16},{16,8},{24,0},{1,25},{9,17},{17,9},{25,1},{2,26},{10... | collective-permute-start | bytes 442376 | tf_op jit(solution)/shard_map/ppermute | solution.py:495
  462.2 10.3 %collective-permute-start.34 = (bf16[96,768]{1,0:T(8,128)(2,1)S(1)}, bf16[96,768]{1,0:T(8,128)(2,1)S(1)}, u32[]{:S(2)}, u32[]{:S(2)}) collective-permute-start(bf16[96,768]{1,0:T(8,128)(2,1)S(1)} %get-tuple-element.118), channel_id=1, source_target_pairs={{0,16},{8,24},{16,0},{24,8},{1,17},{9,25},{17,1},{25,9},{2,18},{10... | collective-permute-start | bytes 442376 | tf_op jit(solution)/shard_map/ppermute | solution.py:495
  468.1 8.9 %copy-start.22 = (s32[8]{0:T(128)S(1)}, s32[8]{0:T(128)}, u32[]{:S(2)}) copy-start(s32[8]{0:T(128)} %convert_reduce_fusion.1) | copy-start | bytes 100
  472.6 7.6 %collective-permute-start.38 = (bf16[96,768]{1,0:T(8,128)(2,1)S(1)}, bf16[96,768]{1,0:T(8,128)(2,1)S(1)}, u32[]{:S(2)}, u32[]{:S(2)}) collective-permute-start(bf16[96,768]{1,0:T(8,128)(2,1)S(1)} %fusion.14), channel_id=1, source_target_pairs={{0,8},{8,0},{16,24},{24,16},{1,9},{9,1},{17,25},{25,17},{2,10},{10... | collective-permute-start | bytes 442376 | tf_op jit(solution)/shard_map/ppermute | solution.py:495
  472.6 11.8 %collective-permute-start.37 = (bf16[96,768]{1,0:T(8,128)(2,1)S(1)}, bf16[96,768]{1,0:T(8,128)(2,1)S(1)}, u32[]{:S(2)}, u32[]{:S(2)}) collective-permute-start(bf16[96,768]{1,0:T(8,128)(2,1)S(1)} %fusion.14), channel_id=1, source_target_pairs={{0,16},{8,24},{16,0},{24,8},{1,17},{9,25},{17,1},{25,9},{2,18},{10... | collective-permute-start | bytes 442376 | tf_op jit(solution)/shard_map/ppermute | solution.py:495
  475.0 9.4 %collective-permute-start.36 = (bf16[96,768]{1,0:T(8,128)(2,1)S(1)}, bf16[96,768]{1,0:T(8,128)(2,1)S(1)}, u32[]{:S(2)}, u32[]{:S(2)}) collective-permute-start(bf16[96,768]{1,0:T(8,128)(2,1)S(1)} %fusion.14), channel_id=1, source_target_pairs={{0,24},{8,16},{16,8},{24,0},{1,25},{9,17},{17,9},{25,1},{2,26},{10... | collective-permute-start | bytes 442376 | tf_op jit(solution)/shard_map/ppermute | solution.py:495
  (23 other events, 74.4 us)
Sparse Core Ops, SparseCore 0:
  48.3 109.5 all-gather.2
  214.2 56.5 reduce-scatter.2
  273.1 43.5 all-reduce.2
  320.0 54.6 reduce-scatter.4

commit v7 on v4

--- a/solution.py
+++ b/solution.py
@@ -145,15 +145,6 @@
     return grad_in, (grad_shift, grad_scale, grad_gate)
 
 
-def by_distance(me, grad, out, block, shards):
-    rows = grad.shape[0] // shards
-    for shard in range(shards):
-        distance = jnp.bitwise_xor(me, shard)
-        out[jnp.bitwise_and(distance, 1), lax.shift_right_logical(distance, 1), block] = grad[
-            shard * rows : (shard + 1) * rows
-        ]
-
-
 def fetch_weights(packed, places, sem):
     copies = []
     for shard in range(packed.shape[0]):
@@ -230,7 +221,6 @@
         mods_out[...] = jnp.zeros_like(mods_out)
 
     clip = where[step]
-    me = where[pl.num_programs(0)]
     own = pl.ds(pl.multiple_of(step * ROWS, ROWS), ROWS)
     grad_out = grad_ref[...].reshape(ROWS, width).astype(F32)
     grad_in, grads = mixer_backward(
@@ -245,7 +235,7 @@
     @pl.when(step == pl.num_programs(0) - 1)
     def _():
         def put(block, grad):
-            by_distance(me, grad, grads_out, block, shards)
+            grads_out[:, block] = grad.reshape(shards, width // shards, width)
 
         mixer_weight_grads(entry, packed_grad, mixed[...], branch_grad, put, width)
 
@@ -576,7 +566,6 @@
     mods_out = shaped((clips, 3, width), F32)
     mods_out_spec = whole((clips, 3, width))
     grads_shape = (shards, 4, rows, width)
-    split_shape = (2, shards // 2, 4, rows, width)
     weight_scratch = [
         pltpu.VMEM((width, 3 * width), BF),
         pltpu.VMEM((width, width), BF),
@@ -747,21 +736,19 @@
         partial(space_backward_kernel, shards), frame_count, where,
         [grad_space, frames_in, modul] + space_kept + space_w,
         [own_spec, per_step(frames_in.shape), mods_spec] + space_keep_specs + [ANY] * shards,
-        [shaped(frames_in.shape, F32), mods_out, shaped(split_shape, BF)],
-        [per_step(frames_in.shape), mods_out_spec, whole(split_shape)],
+        [shaped(frames_in.shape, F32), mods_out, shaped(grads_shape, BF)],
+        [per_step(frames_in.shape), mods_out_spec, whole(grads_shape)],
         weight_scratch + back_scratch(frame_count) + [dma(())],
         3 * mixer_flops, "space_backward",
     )
     space_grads, space_mods, arrived, down_share, *up_parts = lax.optimization_barrier(
         (space_grads, space_mods, arrived, down_share, *up_parts)
     )
-    space_near = near_total(space_grads)
+    space_share = shard_total(space_grads)
     up_share = spread_parts(up_parts, up_share)
     frames_out = to_rows(arrived)
-    space_near, time_share = lax.optimization_barrier((space_near, time_share))
-    space_share = far_finish(far_start(space_near))
-    pair = total(jnp.stack([down_share, time_share], axis=1))
-    down_share, time_share = pair[:, 0], pair[:, 1]
+    pair = jnp.stack([down_share, time_share], axis=1)
+    pair_parts = parts_of(pair)
 
     mod_part = jnp.concatenate([space_mods, time_mods, mlp_mods], axis=1)
     small_grads = jnp.concatenate(
@@ -782,7 +769,9 @@
     )
     small_size = small_grads.shape[0]
     small_grads = jnp.pad(small_grads, (0, -small_size % 1024)).reshape(1, -1, 128)
-    small_grads, space_share = lax.optimization_barrier((small_grads, space_share))
+    small_grads, pair_parts = lax.optimization_barrier((small_grads, pair_parts))
+    pair = spread_parts(pair_parts, pair)
+    down_share, time_share = pair[:, 0], pair[:, 1]
     space_share = total(space_share)
     every_small = every(small_grads).reshape(groups, -1)
     every_modul = every_small[:, :mod_size].reshape(groups * clips, 9 * width).astype(BF)

time: 494 us -> 499 us (1.010)
  starting transfers between devices: 77 us -> 85.4 us
    reduce_scatter x2 -> x3, starting transfers between devices: 0.26 us -> 11.7 us  [shard_total(): return lax.psum_scatter(packed, 'shard', scatter_dimension=0, tiled=True)[0]]
    ppermute x27 -> x22, waiting for transfers between devices: 54.7 us -> 48.5 us  [swap(): return lax.ppermute(values, 'shard', pairs)]
    ppermute x24, waiting for transfers between devices: 56.3 us -> 61.7 us  [swap_group(): return lax.ppermute(values, 'grp', pairs)]
    ppermute x27 -> x22, starting transfers between devices: 21.5 us -> 18.1 us  [swap(): return lax.ppermute(values, 'shard', pairs)]
  transfers between devices with their start and end apart: 58 -> 54, of which waited for: 19 -> 20; matrix products, arithmetic and copies ran while one was open for 11% -> 11% of each run, Pallas kernels for 24% -> 24%
where the time goes in v7:
time: 499 us; the launch traced here: 491 us
  Pallas kernels  160 us (32%)
  waiting for transfers between devices  139 us (28%)
  starting transfers between devices  85.4 us (17%)
  local copies, waits for them, and re-layouts  36.4 us (7%)
  blocking collectives  26.2 us (5%)
  other arithmetic  24.3 us (5%)
  between operations  15 us (3%)
    pallas_call x5, Pallas kernels, run(): pl.pallas_call(kernel, grid_spec=pltpu.PrefetchScalarGridSpec(num_scalar_...  160 us
    ppermute x24, waiting for transfers between devices, swap_group(): return lax.ppermute(values, 'grp', pairs)  61.7 us
    ppermute x22, waiting for transfers between devices, swap(): return lax.ppermute(values, 'shard', pairs)  48.5 us
    ppermute x24, starting transfers between devices, swap_group(): return lax.ppermute(values, 'grp', pairs)  40.4 us
    all_to_all x4, waiting for transfers between devices, exchange(): lax.all_to_all(parts, 'shard', split_axis=0, concat_axis=0, tiled=True)  29.3 us
    all_gather x1, blocking collectives, body(): lax.all_gather(small.reshape(1, -1, 128), 'shard', axis=0, tiled=True)  26.2 us
    ppermute x22, starting transfers between devices, swap(): return lax.ppermute(values, 'shard', pairs)  18.1 us
    all_to_all x4, starting transfers between devices, exchange(): lax.all_to_all(parts, 'shard', split_axis=0, concat_axis=0, tiled=True)  15.2 us
  transfers between devices with their start and end apart: 54, of which 20 were waited for; matrix products, arithmetic and copies ran while one was open for 11% of the time, Pallas kernels for 24%

profile of v7, /device:TPU:0, one launch (start us, length us, event | category | flops | bytes accessed | tf_op | source)
XLA Modules:
  0.0 491.4 jit_solution(17111806795923539309)
XLA Ops:
  7.3 1.1 copy.124
  8.5 1.8 pad_maximum_fusion.3.refs_0_
  10.3 3.9 collective-permute-start.5
  20.0 26.2 %all_gather.6 = f32[8,138,128]{2,1,0:T(8,128)S(1)} all-gather(f32[1,138,128]{2,1,0:T(8,128)S(1)} %maximum_bitcast_fusion), channel_id=1, replica_groups=mesh['grp'=4,'shard'=8] {'shard'}, dimensions={0}, use_global_device_ids=true | all-gather | bytes 635904 | tf_op jit(solution)/shard_map/all_gather | solution.py:530
  46.9 1.2 copy.96
  53.1 18.8 %space_forward.1 = (bf16[8,4,32,768]{3,2,1,0:T(8,128)(2,1)}, bf16[4,256,2304]{2,1,0:T(8,128)(2,1)}, bf16[4,256,768]{2,1,0:T(8,128)(2,1)}, f32[4,16,256]{2,1,0:T(8,128)}, bf16[4,256,768]{2,1,0:T(8,128)(2,1)}) custom-call(s32[5]{0:T(128)} %pad_add_fusion.where, f32[4,256,768]{2,1,0:T(8,128)} %frames_ref.3, f32[2,9,768]{2,1,0:T(8,128)} %reshape.314.mods_ref, ...), custom_call_target="tpu_custom_call" | custom-call | flops 6442450944 | bytes 17422336 | tf_op jit(solution)/shard_map/space_forward/pallas_call | solution.py:421
  72.0 3.6 all-to-all-start
  76.9 2.8 collective-permute-start.12
  80.4 2.2 multiply_convert_fusion
  82.6 1.2 copy.122
  83.9 29.2 %all-to-all-done = bf16[8,4,32,768]{3,2,1,0:T(8,128)(2,1)S(1)} async-done(((bf16[8,4,32,768]{3,2,1,0:T(8,128)(2,1)}), bf16[8,4,32,768]{3,2,1,0:T(8,128)(2,1)S(1)}, u32[]{:S(2)}, u32[]{:S(2)}) %all-to-all-start) | async-done | bytes 1572896 | tf_op jit(solution)/shard_map/all_to_all | solution.py:556
  114.3 4.4 all-to-all-start.1
  118.6 11.6 %reduce-scatter.4.cloned.1.call-start = ((), (), s32[]{:S(2)}) async-start(), calls=%async_computation.7 | async-start | bytes 5308416 | tf_op jit(solution)/shard_map/reduce_scatter | solution.py:659
  130.4 4.7 collective-permute-done.12.refs_6_
  135.1 6.7 %collective-permute-done.10.refs_4_ = bf16[4,96,768]{2,1,0:T(8,128)(2,1)} collective-permute-done((bf16[4,96,768]{2,1,0:T(8,128)(2,1)S(1)}, bf16[4,96,768]{2,1,0:T(8,128)(2,1)}, u32[]{:S(2)}, u32[]{:S(2)}) %collective-permute-start.10) | collective-permute-done | bytes 589856 | tf_op jit(solution)/shard_map/ppermute | solution.py:475
  141.8 5.0 %collective-permute-done.8.refs_2_ = bf16[4,96,768]{2,1,0:T(8,128)(2,1)} collective-permute-done((bf16[4,96,768]{2,1,0:T(8,128)(2,1)S(1)}, bf16[4,96,768]{2,1,0:T(8,128)(2,1)}, u32[]{:S(2)}, u32[]{:S(2)}) %collective-permute-start.8) | collective-permute-done | bytes 589856 | tf_op jit(solution)/shard_map/ppermute | solution.py:475
  147.5 1.3 slice.139
  151.1 19.0 %time_forward.1 = (bf16[4,256,768]{2,1,0:T(8,128)(2,1)}, f32[4,256,768]{2,1,0:T(8,128)}, bf16[4,256,2304]{2,1,0:T(8,128)(2,1)}, bf16[4,256,768]{2,1,0:T(8,128)(2...) custom-call(s32[33]{0:T(128)} %pad_add_fusion.1.inverse, bf16[32,32,768]{2,1,0:T(8,128)(2,1)} %bitcast.206, ...), custom_call_target="tpu_custom_call" | custom-call | flops 6442450944 | bytes 18995200 | tf_op jit(solution)/shard_map/time_forward/pallas_call | solution.py:421
  170.1 43.9 %feed.1 = (bf16[32,32,768]{2,1,0:T(8,128)(2,1)}, f32[4,256,768]{2,1,0:T(8,128)}, f32[2,3,768]{2,1,0:T(4,128)}, f32[1,3072]{1,0:T(1,128)}, f32[1,768]{1,0:T(1,128...) custom-call(s32[33]{0:T(128)} %pad_add_fusion.1.inverse, ...), custom_call_target="tpu_custom_call" | custom-call | flops 28991029248 | bytes 28416000 | tf_op jit(solution)/shard_map/feed/pallas_call | solution.py:421
  214.0 3.2 slice_bitcast_fusion
  217.7 39.7 %time_backward.1 = (bf16[32,32,768]{2,1,0:T(8,128)(2,1)}, f32[2,3,768]{2,1,0:T(4,128)}, bf16[8,4,96,768]{3,2,1,0:T(8,128)(2,1)}) custom-call(s32[33]{0:T(128)} %pad_add_fusion.1.inverse, f32[4,256,768]{2,1,0:T(8,128)} %get-tuple-element.67.grad_ref, bf16[4,256,768]{2,1,0:T(8,128)(2,1)} %get-tuple-element.68.resid_ref, f32[2,9,768]{2,1,0:T(8,128)} %reshape.314.mods_ref, ...), custom_call_target="tpu_custom_call" | custom-call | flops 19327352832 | bytes 23732224 | tf_op jit(solution)/shard_map/time_backward/pallas_call | solution.py:421
  257.5 3.6 all-to-all-start.2
  261.1 3.1 fusion
  264.3 2.0 collective-permute-start.16
  266.3 1.6 collective-permute-start.15
  267.9 28.9 %collective-permute-done.16 = bf16[2,2,96,768]{3,2,1,0:T(8,128)(2,1)S(1)} collective-permute-done((bf16[2,2,96,768]{3,2,1,0:T(8,128)(2,1)S(1)}, bf16[2,2,96,768]{3,2,1,0:T(8,128)(2,1)S(1)}, u32[]{:S(2)}, u32[]{:S(2)}) %collective-permute-start.16) | collective-permute-done | bytes 589856 | tf_op jit(solution)/shard_map/ppermute | solution.py:475
  299.1 3.6 all-to-all-start.3
  303.5 1.9 collective-permute-start.18
  305.4 1.7 slice_bitcast_fusion.6
  307.1 1.5 collective-permute-start.17
  309.4 3.3 collective-permute-start.21
  313.8 39.0 %space_backward.1 = (f32[4,256,768]{2,1,0:T(8,128)}, f32[2,3,768]{2,1,0:T(4,128)}, bf16[8,4,96,768]{3,2,1,0:T(8,128)(2,1)}) custom-call(s32[5]{0:T(128)} %pad_add_fusion.where, bf16[8,4,32,768]{3,2,1,0:T(8,128)(2,1)} %copy-done.4, f32[4,256,768]{2,1,0:T(8,128)} %frames_ref.3, f32[2,9,768]{2,1,0:T(8,128)} %reshape.314.mods_ref, ...), custom_call_target="tpu_custom_call" | custom-call | flops 19327352832 | bytes 25305088 | tf_op jit(solution)/shard_map/space_backward/pallas_call | solution.py:421
  355.9 3.3 collective-permute-start.24
  360.3 2.5 collective-permute-done.22
  364.5 1.4 pad_maximum_fusion.7
  367.5 1.2 add_convert_fusion.2
  369.1 1.9 collective-permute-start.44
  370.9 2.3 collective-permute-start.43
  375.1 2.0 copy.99
  377.1 1.2 collective-permute-done.26
  379.2 3.9 collective-permute-done.44
  384.5 1.2 pad_maximum_fusion.1
  385.8 3.4 collective-permute-start.30
  389.3 1.4 collective-permute-start.29
  391.3 6.4 %collective-permute-done.30 = bf16[192,768]{1,0:T(8,128)(2,1)S(1)} collective-permute-done((bf16[192,768]{1,0:T(8,128)(2,1)S(1)}, bf16[192,768]{1,0:T(8,128)(2,1)S(1)}, u32[]{:S(2)}, u32[]{:S(2)}) %collective-permute-start.30) | collective-permute-done | bytes 294944 | tf_op jit(solution)/shard_map/ppermute | solution.py:485
  397.7 17.4 %collective-permute-done.29 = bf16[192,768]{1,0:T(8,128)(2,1)S(1)} collective-permute-done((bf16[192,768]{1,0:T(8,128)(2,1)S(1)}, bf16[192,768]{1,0:T(8,128)(2,1)S(1)}, u32[]{:S(2)}, u32[]{:S(2)}) %collective-permute-start.29) | collective-permute-done | bytes 294944 | tf_op jit(solution)/shard_map/ppermute | solution.py:485
  415.2 2.1 collective-permute-start.33
  417.3 2.2 collective-permute-start.31
  419.8 2.7 collective-permute-start.41
  422.5 6.7 %collective-permute-done.31 = f32[1,112,128]{2,1,0:T(8,128)S(1)} collective-permute-done((f32[1,112,128]{2,1,0:T(8,128)S(1)}, f32[1,112,128]{2,1,0:T(8,128)S(1)}, u32[]{:S(2)}, u32[]{:S(2)}) %collective-permute-start.31) | collective-permute-done | bytes 57376 | tf_op jit(solution)/shard_map/ppermute | solution.py:485
  429.2 2.3 collective-permute-start.40
  432.3 1.3 fusion.4
  434.8 2.1 fusion.16
  436.8 6.4 %collective-permute-done.41 = bf16[192,768]{1,0:T(8,128)(2,1)S(1)} collective-permute-done((bf16[192,768]{1,0:T(8,128)(2,1)S(1)}, bf16[192,768]{1,0:T(8,128)(2,1)S(1)}, u32[]{:S(2)}, u32[]{:S(2)}) %collective-permute-start.41) | collective-permute-done | bytes 294944 | tf_op jit(solution)/shard_map/ppermute | solution.py:485
  444.6 1.6 convert.18
  447.3 5.9 %collective-permute-start.34 = (bf16[96,768]{1,0:T(8,128)(2,1)S(1)}, bf16[96,768]{1,0:T(8,128)(2,1)S(1)}, u32[]{:S(2)}, u32[]{:S(2)}) collective-permute-start(bf16[96,768]{1,0:T(8,128)(2,1)S(1)} %get-tuple-element.125), channel_id=1, source_target_pairs={{0,8},{8,0},{16,24},{24,16},{1,9},{9,1},{17,25},{25,17},{2,10},{10... | collective-permute-start | bytes 442376 | tf_op jit(solution)/shard_map/ppermute | solution.py:485
  453.2 2.1 collective-permute-start.36
  455.3 1.2 slice_bitcast_fusion.1
  457.5 5.3 %collective-permute-done.36 = bf16[96,768]{1,0:T(8,128)(2,1)S(1)} collective-permute-done((bf16[96,768]{1,0:T(8,128)(2,1)S(1)}, bf16[96,768]{1,0:T(8,128)(2,1)S(1)}, u32[]{:S(2)}, u32[]{:S(2)}) %collective-permute-start.36) | collective-permute-done | bytes 147488 | tf_op jit(solution)/shard_map/ppermute | solution.py:485
  462.9 4.5 collective-permute-done.35
  468.4 2.7 collective-permute-start.38
  471.1 1.7 collective-permute-start.37
  472.8 1.7 slice_bitcast_fusion.4
  475.4 6.6 %collective-permute-done.38 = bf16[96,768]{1,0:T(8,128)(2,1)S(1)} collective-permute-done((bf16[96,768]{1,0:T(8,128)(2,1)S(1)}, bf16[96,768]{1,0:T(8,128)(2,1)S(1)}, u32[]{:S(2)}, u32[]{:S(2)}) %collective-permute-start.38) | collective-permute-done | bytes 147488 | tf_op jit(solution)/shard_map/ppermute | solution.py:485
  (240 shorter events, 45.6 us)
Async XLA Ops:
  7.2 9.1 %copy-start = (bf16[96,6912]{1,0:T(8,128)(2,1)S(1)}, bf16[96,6912]{1,0:T(8,128)(2,1)}, u32[]{:S(2)}) copy-start(bf16[96,6912]{1,0:T(8,128)(2,1)} %param.20) | copy-start | bytes 3981316
  7.2 162.9 %all-gather.3.cloned.1.call-start = ((), (), s32[]{:S(2)}) async-start(), calls=%async_computation.10 | async-start | bytes 10616832 | tf_op jit(solution)/shard_map/all_gather | solution.py:478
  8.4 9.7 %copy-start.10 = (bf16[96,2304]{1,0:T(8,128)(2,1)S(1)}, bf16[96,2304]{1,0:T(8,128)(2,1)}, u32[]{:S(2)}) copy-start(bf16[96,2304]{1,0:T(8,128)(2,1)} %param.24) | copy-start | bytes 1327108
  10.3 36.6 %collective-permute-start.5 = (bf16[4,96,768]{2,1,0:T(8,128)(2,1)}, bf16[4,96,768]{2,1,0:T(8,128)(2,1)}, u32[]{:S(2)}, u32[]{:S(2)}) collective-permute-start(bf16[4,96,768]{2,1,0:T(8,128)(2,1)} %pad_maximum_fusion.3.refs_0_), channel_id=1, source_target_pairs={{0,6},{1,7},{2,4},{3,5},{4,2},{5,3},{6,0},{7,1},{8,14},{9,15},{10,... | collective-permute-start | bytes 1769480 | tf_op jit(solution)/shard_map/ppermute | solution.py:475
  14.2 32.7 %collective-permute-start.3 = (bf16[4,96,768]{2,1,0:T(8,128)(2,1)}, bf16[4,96,768]{2,1,0:T(8,128)(2,1)}, u32[]{:S(2)}, u32[]{:S(2)}) collective-permute-start(bf16[4,96,768]{2,1,0:T(8,128)(2,1)} %pad_maximum_fusion.3.refs_0_), channel_id=1, source_target_pairs={{0,4},{1,5},{2,6},{3,7},{4,0},{5,1},{6,2},{7,3},{8,12},{9,13},{10,... | collective-permute-start | bytes 1769480 | tf_op jit(solution)/shard_map/ppermute | solution.py:475
  14.7 32.2 %collective-permute-start = (bf16[4,96,768]{2,1,0:T(8,128)(2,1)}, bf16[4,96,768]{2,1,0:T(8,128)(2,1)}, u32[]{:S(2)}, u32[]{:S(2)}) collective-permute-start(bf16[4,96,768]{2,1,0:T(8,128)(2,1)} %pad_maximum_fusion.3.refs_0_), channel_id=1, source_target_pairs={{0,2},{1,3},{2,0},{3,1},{4,6},{5,7},{6,4},{7,5},{8,10},{9,11},{10,... | collective-permute-start | bytes 1769480 | tf_op jit(solution)/shard_map/ppermute | solution.py:475
  18.7 27.6 %copy-start.13 = (bf16[96,768]{1,0:T(8,128)(2,1)S(1)}, bf16[96,768]{1,0:T(8,128)(2,1)}, u32[]{:S(2)}) copy-start(bf16[96,768]{1,0:T(8,128)(2,1)} %param.25) | copy-start | bytes 442372
  46.3 84.0 %copy-start.8 = (bf16[4,96,768]{2,1,0:T(8,128)(2,1)}, bf16[4,96,768]{2,1,0:T(8,128)(2,1)S(1)}, u32[]{:S(2)}) copy-start(bf16[4,96,768]{2,1,0:T(8,128)(2,1)S(1)} %pad_maximum_fusion.4.refs_0_) | copy-start | bytes 1769476
  48.2 3.1 collective-permute-start.1
  48.6 2.8 collective-permute-start.6
  48.7 3.5 collective-permute-start.4
  49.1 4.0 collective-permute-start.2
  50.6 21.4 %copy-start.11 = (f32[138,128]{1,0:T(8,128)}, f32[138,128]{1,0:T(8,128)S(1)}, u32[]{:S(2)}) copy-start(f32[138,128]{1,0:T(8,128)S(1)} %reduce_sum.37) | copy-start | bytes 211972
  72.0 41.1 %all-to-all-start = ((bf16[8,4,32,768]{3,2,1,0:T(8,128)(2,1)}), bf16[8,4,32,768]{3,2,1,0:T(8,128)(2,1)S(1)}, u32[]{:S(2)}, u32[]{:S(2)}) async-start(bf16[8,4,32,768]{3,2,1,0:T(8,128)(2,1)} %get-tuple-element.63), calls=%async_computation | async-start | bytes 3145728 | tf_op jit(solution)/shard_map/all_to_all | solution.py:556
  76.9 58.1 %collective-permute-start.12 = (bf16[4,96,768]{2,1,0:T(8,128)(2,1)S(1)}, bf16[4,96,768]{2,1,0:T(8,128)(2,1)}, u32[]{:S(2)}, u32[]{:S(2)}) collective-permute-start(bf16[4,96,768]{2,1,0:T(8,128)(2,1)S(1)} %pad_maximum_fusion.4.refs_0_), channel_id=1, source_target_pairs={{0,6},{1,7},{2,4},{3,5},{4,2},{5,3},{6,0},{7,1},{8,14},{9,15},{10,... | collective-permute-start | bytes 1769480 | tf_op jit(solution)/shard_map/ppermute | solution.py:475
  79.8 62.0 %collective-permute-start.10 = (bf16[4,96,768]{2,1,0:T(8,128)(2,1)S(1)}, bf16[4,96,768]{2,1,0:T(8,128)(2,1)}, u32[]{:S(2)}, u32[]{:S(2)}) collective-permute-start(bf16[4,96,768]{2,1,0:T(8,128)(2,1)S(1)} %pad_maximum_fusion.4.refs_0_), channel_id=1, source_target_pairs={{0,4},{1,5},{2,6},{3,7},{4,0},{5,1},{6,2},{7,3},{8,12},{9,13},{10,... | collective-permute-start | bytes 1769480 | tf_op jit(solution)/shard_map/ppermute | solution.py:475
  80.3 66.5 %collective-permute-start.8 = (bf16[4,96,768]{2,1,0:T(8,128)(2,1)S(1)}, bf16[4,96,768]{2,1,0:T(8,128)(2,1)}, u32[]{:S(2)}, u32[]{:S(2)}) collective-permute-start(bf16[4,96,768]{2,1,0:T(8,128)(2,1)S(1)} %pad_maximum_fusion.4.refs_0_), channel_id=1, source_target_pairs={{0,2},{1,3},{2,0},{3,1},{4,6},{5,7},{6,4},{7,5},{8,10},{9,11},{10,... | collective-permute-start | bytes 1769480 | tf_op jit(solution)/shard_map/ppermute | solution.py:475
  114.3 55.8 %all-to-all-start.1 = ((bf16[8,4,32,768]{3,2,1,0:T(8,128)(2,1)}), bf16[8,4,32,768]{3,2,1,0:T(8,128)(2,1)}, u32[]{:S(2)}, u32[]{:S(2)}) async-start(bf16[8,4,32,768]{3,2,1,0:T(8,128)(2,1)} %bitcast.181), calls=%async_computation.1 | async-start | bytes 3145728 | tf_op jit(solution)/shard_map/all_to_all | solution.py:556
  118.6 179.3 %reduce-scatter.4.cloned.1.call-start = ((), (), s32[]{:S(2)}) async-start(), calls=%async_computation.7 | async-start | bytes 5308416 | tf_op jit(solution)/shard_map/reduce_scatter | solution.py:659
  130.3 19.8 %collective-permute-start.7 = (bf16[4,96,768]{2,1,0:T(8,128)(2,1)S(1)}, bf16[4,96,768]{2,1,0:T(8,128)(2,1)S(1)}, u32[]{:S(2)}, u32[]{:S(2)}) collective-permute-start(bf16[4,96,768]{2,1,0:T(8,128)(2,1)S(1)} %pad_maximum_fusion.4.refs_0_), channel_id=1, source_target_pairs={{0,1},{1,0},{2,3},{3,2},{4,5},{5,4},{6,7},{7,6},{8,9},{9,8},{10,11... | collective-permute-start | bytes 1769480 | tf_op jit(solution)/shard_map/ppermute | solution.py:475
  135.1 15.0 %collective-permute-start.13 = (bf16[4,96,768]{2,1,0:T(8,128)(2,1)}, bf16[4,96,768]{2,1,0:T(8,128)(2,1)S(1)}, u32[]{:S(2)}, u32[]{:S(2)}) collective-permute-start(bf16[4,96,768]{2,1,0:T(8,128)(2,1)} %collective-permute-done.12.refs_6_), channel_id=1, source_target_pairs={{0,1},{1,0},{2,3},{3,2},{4,5},{5,4},{6,7},{7,6},{8,9},{9,8},{10,11... | collective-permute-start | bytes 1769480 | tf_op jit(solution)/shard_map/ppermute | solution.py:475
  141.8 8.3 %collective-permute-start.11 = (bf16[4,96,768]{2,1,0:T(8,128)(2,1)}, bf16[4,96,768]{2,1,0:T(8,128)(2,1)}, u32[]{:S(2)}, u32[]{:S(2)}) collective-permute-start(bf16[4,96,768]{2,1,0:T(8,128)(2,1)} %collective-permute-done.10.refs_4_), channel_id=1, source_target_pairs={{0,1},{1,0},{2,3},{3,2},{4,5},{5,4},{6,7},{7,6},{8,9},{9,8},{10,11... | collective-permute-start | bytes 1769480 | tf_op jit(solution)/shard_map/ppermute | solution.py:475
  146.8 3.3 collective-permute-start.9
  217.2 43.9 %collective-permute-start.14 = (bf16[4,4,96,768]{3,2,1,0:T(8,128)(2,1)}, bf16[4,4,96,768]{3,2,1,0:T(8,128)(2,1)}, u32[]{:S(2)}, u32[]{:S(2)}) collective-permute-start(bf16[4,4,96,768]{3,2,1,0:T(8,128)(2,1)} %slice_bitcast_fusion), channel_id=1, source_target_pairs={{0,1},{1,0},{2,3},{3,2},{4,5},{5,4},{6,7},{7,6},{8,9},{9,8},{10,11... | collective-permute-start | bytes 7077896 | tf_op jit(solution)/shard_map/ppermute | solution.py:475
  257.5 40.5 %all-to-all-start.2 = ((bf16[8,4,32,768]{3,2,1,0:T(8,128)(2,1)}), bf16[8,4,32,768]{3,2,1,0:T(8,128)(2,1)S(1)}, u32[]{:S(2)}, u32[]{:S(2)}) async-start(bf16[8,4,32,768]{3,2,1,0:T(8,128)(2,1)} %bitcast.207), calls=%async_computation.3 | async-start | bytes 3145728 | tf_op jit(solution)/shard_map/all_to_all | solution.py:556
  261.1 123.4 %reduce-scatter.6.cloned.1.call-start = ((), (), s32[]{:S(2)}) async-start(), calls=%async_computation.8 | async-start | bytes 5308416 | tf_op jit(solution)/shard_map/reduce_scatter | solution.py:659
  264.3 32.6 %collective-permute-start.16 = (bf16[2,2,96,768]{3,2,1,0:T(8,128)(2,1)S(1)}, bf16[2,2,96,768]{3,2,1,0:T(8,128)(2,1)S(1)}, u32[]{:S(2)}, u32[]{:S(2)}) collective-permute-start(bf16[2,2,96,768]{3,2,1,0:T(8,128)(2,1)S(1)} %slice.145), channel_id=1, source_target_pairs={{0,4},{1,5},{2,6},{3,7},{4,0},{5,1},{6,2},{7,3},{8,12},{9,13},{10,... | collective-permute-start | bytes 1769480 | tf_op jit(solution)/shard_map/ppermute | solution.py:475
  266.3 30.7 %collective-permute-start.15 = (bf16[2,2,96,768]{3,2,1,0:T(8,128)(2,1)S(1)}, bf16[2,2,96,768]{3,2,1,0:T(8,128)(2,1)S(1)}, u32[]{:S(2)}, u32[]{:S(2)}) collective-permute-start(bf16[2,2,96,768]{3,2,1,0:T(8,128)(2,1)S(1)} %slice_bitcast_fusion.2), channel_id=1, source_target_pairs={{0,2},{1,3},{2,0},{3,1},{4,6},{5,7},{6,4},{7,5},{8,10},{9,11},{10,... | collective-permute-start | bytes 1769480 | tf_op jit(solution)/shard_map/ppermute | solution.py:475
  299.1 55.9 %all-to-all-start.3 = ((bf16[8,4,32,768]{3,2,1,0:T(8,128)(2,1)}), bf16[8,4,32,768]{3,2,1,0:T(8,128)(2,1)S(1)}, u32[]{:S(2)}, u32[]{:S(2)}) async-start(bf16[8,4,32,768]{3,2,1,0:T(8,128)(2,1)} %bitcast.205), calls=%async_computation.4 | async-start | bytes 3145728 | tf_op jit(solution)/shard_map/all_to_all | solution.py:556
  302.7 143.5 %reduce-scatter.8.cloned.1.call-start = ((), (), s32[]{:S(2)}) async-start(), calls=%async_computation.9 | async-start | bytes 5308416 | tf_op jit(solution)/shard_map/reduce_scatter | solution.py:659
  303.5 49.3 %collective-permute-start.18 = (bf16[2,96,768]{2,1,0:T(8,128)(2,1)}, bf16[2,96,768]{2,1,0:T(8,128)(2,1)}, u32[]{:S(2)}, u32[]{:S(2)}) collective-permute-start(bf16[2,96,768]{2,1,0:T(8,128)(2,1)} %slice_bitcast_fusion.5), channel_id=1, source_target_pairs={{0,2},{1,3},{2,0},{3,1},{4,6},{5,7},{6,4},{7,5},{8,10},{9,11},{10,... | collective-permute-start | bytes 884744 | tf_op jit(solution)/shard_map/ppermute | solution.py:475
  307.1 46.8 %collective-permute-start.17 = (bf16[2,96,768]{2,1,0:T(8,128)(2,1)}, bf16[2,96,768]{2,1,0:T(8,128)(2,1)S(1)}, u32[]{:S(2)}, u32[]{:S(2)}) collective-permute-start(bf16[2,96,768]{2,1,0:T(8,128)(2,1)} %slice_bitcast_fusion.6), channel_id=1, source_target_pairs={{0,4},{1,5},{2,6},{3,7},{4,0},{5,1},{6,2},{7,3},{8,12},{9,13},{10,... | collective-permute-start | bytes 884744 | tf_op jit(solution)/shard_map/ppermute | solution.py:475
  309.4 45.6 %collective-permute-start.21 = (bf16[96,768]{1,0:T(8,128)(2,1)}, bf16[96,768]{1,0:T(8,128)(2,1)}, u32[]{:S(2)}, u32[]{:S(2)}) collective-permute-start(bf16[96,768]{1,0:T(8,128)(2,1)} %get-tuple-element.128), channel_id=1, source_target_pairs={{0,24},{8,16},{16,8},{24,0},{1,25},{9,17},{17,9},{25,1},{2,26},{10... | collective-permute-start | bytes 442376 | tf_op jit(solution)/shard_map/ppermute | solution.py:485
  312.7 42.3 %collective-permute-start.20 = (bf16[96,768]{1,0:T(8,128)(2,1)}, bf16[96,768]{1,0:T(8,128)(2,1)}, u32[]{:S(2)}, u32[]{:S(2)}) collective-permute-start(bf16[96,768]{1,0:T(8,128)(2,1)} %get-tuple-element.129), channel_id=1, source_target_pairs={{0,16},{8,24},{16,0},{24,8},{1,17},{9,25},{17,1},{25,9},{2,18},{10... | collective-permute-start | bytes 442376 | tf_op jit(solution)/shard_map/ppermute | solution.py:485
  312.7 42.3 %collective-permute-start.19 = (bf16[96,768]{1,0:T(8,128)(2,1)S(1)}, bf16[96,768]{1,0:T(8,128)(2,1)}, u32[]{:S(2)}, u32[]{:S(2)}) collective-permute-start(bf16[96,768]{1,0:T(8,128)(2,1)S(1)} %get-tuple-element.130), channel_id=1, source_target_pairs={{0,8},{8,0},{16,24},{24,16},{1,9},{9,1},{17,25},{25,17},{2,10},{10... | collective-permute-start | bytes 442376 | tf_op jit(solution)/shard_map/ppermute | solution.py:485
  355.0 9.4 %copy-start.20 = (f32[1,768]{1,0:T(1,128)S(1)}, f32[1,768]{1,0:T(1,128)}, u32[]{:S(2)}) copy-start(f32[1,768]{1,0:T(1,128)} %get-tuple-element.96) | copy-start | bytes 9220
  355.0 9.4 %copy-start.15 = (f32[2,3,768]{2,1,0:T(4,128)S(1)}, f32[2,3,768]{2,1,0:T(4,128)}, u32[]{:S(2)}) copy-start(f32[2,3,768]{2,1,0:T(4,128)} %get-tuple-element.94) | copy-start | bytes 55300
  355.0 9.4 %copy-start.16 = (f32[2,3,768]{2,1,0:T(4,128)S(1)}, f32[2,3,768]{2,1,0:T(4,128)}, u32[]{:S(2)}) copy-start(f32[2,3,768]{2,1,0:T(4,128)} %get-tuple-element.93) | copy-start | bytes 55300
  355.9 7.8 %collective-permute-start.24 = (f32[2,97]{1,0:T(2,128)S(1)}, f32[2,97]{1,0:T(2,128)S(1)}, u32[]{:S(2)}, u32[]{:S(2)}) collective-permute-start(f32[2,97]{1,0:T(2,128)S(1)} %pad_maximum_fusion.8), channel_id=1, source_target_pairs={{0,24},{8,16},{16,8},{24,0},{1,25},{9,17},{17,9},{25,1},{2,26},{10... | collective-permute-start | bytes 2336 | tf_op jit(solution)/shard_map/ppermute | solution.py:485
  359.3 4.5 collective-permute-start.23
  359.3 3.6 collective-permute-start.22
  367.5 5.7 %collective-permute-start.25 = (f32[138,128]{1,0:T(8,128)S(1)}, f32[138,128]{1,0:T(8,128)S(1)}, u32[]{:S(2)}, u32[]{:S(2)}) collective-permute-start(f32[138,128]{1,0:T(8,128)S(1)} %maximum_bitcast_fusion.1), channel_id=1, source_target_pairs={{0,1},{1,0},{2,3},{3,2},{4,5},{5,4},{6,7},{7,6},{8,9},{9,8},{10,11... | collective-permute-start | bytes 211976 | tf_op jit(solution)/shard_map/ppermute | solution.py:475
  368.8 10.4 %collective-permute-start.45 = (bf16[96,768]{1,0:T(8,128)(2,1)S(1)}, bf16[96,768]{1,0:T(8,128)(2,1)S(1)}, u32[]{:S(2)}, u32[]{:S(2)}) collective-permute-start(bf16[96,768]{1,0:T(8,128)(2,1)S(1)} %add_convert_fusion.2), channel_id=1, source_target_pairs={{0,8},{8,0},{16,24},{24,16},{1,9},{9,1},{17,25},{25,17},{2,10},{10... | collective-permute-start | bytes 442376 | tf_op jit(solution)/shard_map/ppermute | solution.py:485
  369.1 14.0 %collective-permute-start.44 = (bf16[96,768]{1,0:T(8,128)(2,1)S(1)}, bf16[96,768]{1,0:T(8,128)(2,1)S(1)}, u32[]{:S(2)}, u32[]{:S(2)}) collective-permute-start(bf16[96,768]{1,0:T(8,128)(2,1)S(1)} %add_convert_fusion.2), channel_id=1, source_target_pairs={{0,16},{8,24},{16,0},{24,8},{1,17},{9,25},{17,1},{25,9},{2,18},{10... | collective-permute-start | bytes 442376 | tf_op jit(solution)/shard_map/ppermute | solution.py:485
  370.9 12.1 %collective-permute-start.43 = (bf16[96,768]{1,0:T(8,128)(2,1)S(1)}, bf16[96,768]{1,0:T(8,128)(2,1)S(1)}, u32[]{:S(2)}, u32[]{:S(2)}) collective-permute-start(bf16[96,768]{1,0:T(8,128)(2,1)S(1)} %add_convert_fusion.2), channel_id=1, source_target_pairs={{0,24},{8,16},{16,8},{24,0},{1,25},{9,17},{17,9},{25,1},{2,26},{10... | collective-permute-start | bytes 442376 | tf_op jit(solution)/shard_map/ppermute | solution.py:485
  373.9 4.4 collective-permute-start.26
  378.4 6.0 %collective-permute-start.27 = (f32[138,128]{1,0:T(8,128)S(1)}, f32[138,128]{1,0:T(8,128)S(1)}, u32[]{:S(2)}, u32[]{:S(2)}) collective-permute-start(f32[138,128]{1,0:T(8,128)S(1)} %fusion.39), channel_id=1, source_target_pairs={{0,4},{1,5},{2,6},{3,7},{4,0},{5,1},{6,2},{7,3},{8,12},{9,13},{10,... | collective-permute-start | bytes 211976 | tf_op jit(solution)/shard_map/ppermute | solution.py:475
  385.8 11.9 %collective-permute-start.30 = (bf16[192,768]{1,0:T(8,128)(2,1)S(1)}, bf16[192,768]{1,0:T(8,128)(2,1)S(1)}, u32[]{:S(2)}, u32[]{:S(2)}) collective-permute-start(bf16[192,768]{1,0:T(8,128)(2,1)S(1)} %get-tuple-element.113), channel_id=1, source_target_pairs={{0,24},{8,16},{16,8},{24,0},{1,25},{9,17},{17,9},{25,1},{2,26},{10... | collective-permute-start | bytes 884744 | tf_op jit(solution)/shard_map/ppermute | solution.py:485
  389.3 25.9 %collective-permute-start.29 = (bf16[192,768]{1,0:T(8,128)(2,1)S(1)}, bf16[192,768]{1,0:T(8,128)(2,1)S(1)}, u32[]{:S(2)}, u32[]{:S(2)}) collective-permute-start(bf16[192,768]{1,0:T(8,128)(2,1)S(1)} %get-tuple-element.114), channel_id=1, source_target_pairs={{0,16},{8,24},{16,0},{24,8},{1,17},{9,25},{17,1},{25,9},{2,18},{10... | collective-permute-start | bytes 884744 | tf_op jit(solution)/shard_map/ppermute | solution.py:485
  390.6 24.5 %collective-permute-start.28 = (bf16[192,768]{1,0:T(8,128)(2,1)S(1)}, bf16[192,768]{1,0:T(8,128)(2,1)S(1)}, u32[]{:S(2)}, u32[]{:S(2)}) collective-permute-start(bf16[192,768]{1,0:T(8,128)(2,1)S(1)} %get-tuple-element.115), channel_id=1, source_target_pairs={{0,8},{8,0},{16,24},{24,16},{1,9},{9,1},{17,25},{25,17},{2,10},{10... | collective-permute-start | bytes 884744 | tf_op jit(solution)/shard_map/ppermute | solution.py:485
  415.2 16.4 %collective-permute-start.33 = (f32[1,112,128]{2,1,0:T(8,128)S(1)}, f32[1,112,128]{2,1,0:T(8,128)S(1)}, u32[]{:S(2)}, u32[]{:S(2)}) collective-permute-start(f32[1,112,128]{2,1,0:T(8,128)S(1)} %fusion.9), channel_id=1, source_target_pairs={{0,24},{8,16},{16,8},{24,0},{1,25},{9,17},{17,9},{25,1},{2,26},{10... | collective-permute-start | bytes 172040 | tf_op jit(solution)/shard_map/ppermute | solution.py:485
  417.3 14.2 %collective-permute-start.32 = (f32[1,112,128]{2,1,0:T(8,128)S(1)}, f32[1,112,128]{2,1,0:T(8,128)S(1)}, u32[]{:S(2)}, u32[]{:S(2)}) collective-permute-start(f32[1,112,128]{2,1,0:T(8,128)S(1)} %fusion.9), channel_id=1, source_target_pairs={{0,16},{8,24},{16,0},{24,8},{1,17},{9,25},{17,1},{25,9},{2,18},{10... | collective-permute-start | bytes 172040 | tf_op jit(solution)/shard_map/ppermute | solution.py:485
  417.3 11.9 %collective-permute-start.31 = (f32[1,112,128]{2,1,0:T(8,128)S(1)}, f32[1,112,128]{2,1,0:T(8,128)S(1)}, u32[]{:S(2)}, u32[]{:S(2)}) collective-permute-start(f32[1,112,128]{2,1,0:T(8,128)S(1)} %fusion.9), channel_id=1, source_target_pairs={{0,8},{8,0},{16,24},{24,16},{1,9},{9,1},{17,25},{25,17},{2,10},{10... | collective-permute-start | bytes 172040 | tf_op jit(solution)/shard_map/ppermute | solution.py:485
  419.7 12.6 %copy-start.21 = (s32[8]{0:T(128)S(1)}, s32[8]{0:T(128)}, u32[]{:S(2)}) copy-start(s32[8]{0:T(128)} %convert_reduce_fusion.1) | copy-start | bytes 100
  419.7 17.1 %collective-permute-start.42 = (bf16[192,768]{1,0:T(8,128)(2,1)S(1)}, bf16[192,768]{1,0:T(8,128)(2,1)S(1)}, u32[]{:S(2)}, u32[]{:S(2)}) collective-permute-start(bf16[192,768]{1,0:T(8,128)(2,1)S(1)} %add_convert_fusion.1), channel_id=1, source_target_pairs={{0,8},{8,0},{16,24},{24,16},{1,9},{9,1},{17,25},{25,17},{2,10},{10... | collective-permute-start | bytes 884744 | tf_op jit(solution)/shard_map/ppermute | solution.py:485
  419.8 23.5 %collective-permute-start.41 = (bf16[192,768]{1,0:T(8,128)(2,1)S(1)}, bf16[192,768]{1,0:T(8,128)(2,1)S(1)}, u32[]{:S(2)}, u32[]{:S(2)}) collective-permute-start(bf16[192,768]{1,0:T(8,128)(2,1)S(1)} %add_convert_fusion.1), channel_id=1, source_target_pairs={{0,16},{8,24},{16,0},{24,8},{1,17},{9,25},{17,1},{25,9},{2,18},{10... | collective-permute-start | bytes 884744 | tf_op jit(solution)/shard_map/ppermute | solution.py:485
  429.2 14.0 %collective-permute-start.40 = (bf16[192,768]{1,0:T(8,128)(2,1)S(1)}, bf16[192,768]{1,0:T(8,128)(2,1)S(1)}, u32[]{:S(2)}, u32[]{:S(2)}) collective-permute-start(bf16[192,768]{1,0:T(8,128)(2,1)S(1)} %add_convert_fusion.1), channel_id=1, source_target_pairs={{0,24},{8,16},{16,8},{24,0},{1,25},{9,17},{17,9},{25,1},{2,26},{10... | collective-permute-start | bytes 884744 | tf_op jit(solution)/shard_map/ppermute | solution.py:485
  433.6 9.9 %copy-start.24 = (f32[480]{0:T(512)}, f32[480]{0:T(512)S(1)}, u32[]{:S(2)}) copy-start(f32[480]{0:T(512)S(1)} %slice_reduce_fusion) | copy-start | bytes 5764
  447.3 10.2 %collective-permute-start.34 = (bf16[96,768]{1,0:T(8,128)(2,1)S(1)}, bf16[96,768]{1,0:T(8,128)(2,1)S(1)}, u32[]{:S(2)}, u32[]{:S(2)}) collective-permute-start(bf16[96,768]{1,0:T(8,128)(2,1)S(1)} %get-tuple-element.125), channel_id=1, source_target_pairs={{0,8},{8,0},{16,24},{24,16},{1,9},{9,1},{17,25},{25,17},{2,10},{10... | collective-permute-start | bytes 442376 | tf_op jit(solution)/shard_map/ppermute | solution.py:485
  453.2 9.7 %collective-permute-start.36 = (bf16[96,768]{1,0:T(8,128)(2,1)S(1)}, bf16[96,768]{1,0:T(8,128)(2,1)S(1)}, u32[]{:S(2)}, u32[]{:S(2)}) collective-permute-start(bf16[96,768]{1,0:T(8,128)(2,1)S(1)} %get-tuple-element.126), channel_id=1, source_target_pairs={{0,24},{8,16},{16,8},{24,0},{1,25},{9,17},{17,9},{25,1},{2,26},{10... | collective-permute-start | bytes 442376 | tf_op jit(solution)/shard_map/ppermute | solution.py:485
  455.3 12.0 %collective-permute-start.35 = (bf16[96,768]{1,0:T(8,128)(2,1)S(1)}, bf16[96,768]{1,0:T(8,128)(2,1)S(1)}, u32[]{:S(2)}, u32[]{:S(2)}) collective-permute-start(bf16[96,768]{1,0:T(8,128)(2,1)S(1)} %get-tuple-element.127), channel_id=1, source_target_pairs={{0,16},{8,24},{16,0},{24,8},{1,17},{9,25},{17,1},{25,9},{2,18},{10... | collective-permute-start | bytes 442376 | tf_op jit(solution)/shard_map/ppermute | solution.py:485
  468.3 7.1 %collective-permute-start.39 = (bf16[96,768]{1,0:T(8,128)(2,1)S(1)}, bf16[96,768]{1,0:T(8,128)(2,1)S(1)}, u32[]{:S(2)}, u32[]{:S(2)}) collective-permute-start(bf16[96,768]{1,0:T(8,128)(2,1)S(1)} %fusion.7), channel_id=1, source_target_pairs={{0,8},{8,0},{16,24},{24,16},{1,9},{9,1},{17,25},{25,17},{2,10},{10... | collective-permute-start | bytes 442376 | tf_op jit(solution)/shard_map/ppermute | solution.py:485
  468.4 13.6 %collective-permute-start.38 = (bf16[96,768]{1,0:T(8,128)(2,1)S(1)}, bf16[96,768]{1,0:T(8,128)(2,1)S(1)}, u32[]{:S(2)}, u32[]{:S(2)}) collective-permute-start(bf16[96,768]{1,0:T(8,128)(2,1)S(1)} %fusion.7), channel_id=1, source_target_pairs={{0,16},{8,24},{16,0},{24,8},{1,17},{9,25},{17,1},{25,9},{2,18},{10... | collective-permute-start | bytes 442376 | tf_op jit(solution)/shard_map/ppermute | solution.py:485
  471.1 10.9 %collective-permute-start.37 = (bf16[96,768]{1,0:T(8,128)(2,1)S(1)}, bf16[96,768]{1,0:T(8,128)(2,1)S(1)}, u32[]{:S(2)}, u32[]{:S(2)}) collective-permute-start(bf16[96,768]{1,0:T(8,128)(2,1)S(1)} %fusion.7), channel_id=1, source_target_pairs={{0,24},{8,16},{16,8},{24,0},{1,25},{9,17},{17,9},{25,1},{2,26},{10... | collective-permute-start | bytes 442376 | tf_op jit(solution)/shard_map/ppermute | solution.py:485
  (22 other events, 84.0 us)
Sparse Core Ops, SparseCore 0:
  48.3 109.5 all-gather.2
  214.1 57.6 reduce-scatter.3
  298.1 60.0 reduce-scatter.5
  361.5 53.7 reduce-scatter.7

commit v8 on v7

--- a/solution.py
+++ b/solution.py
@@ -604,6 +604,7 @@
     own_ids = jnp.concatenate([embed, timesteps.astype(F32)[:, None]], axis=1)
     own_ids, _ = lax.optimization_barrier((own_ids, after_space))
     every_ids = every(own_ids).reshape(-1, own_ids.shape[1])
+    received, every_ids = lax.optimization_barrier((received, every_ids))
 
     cols_spec = whole((group_frames, columns, width))
     cols_shape = shaped((group_frames, columns, width), BF)
@@ -741,14 +742,18 @@
         weight_scratch + back_scratch(frame_count) + [dma(())],
         3 * mixer_flops, "space_backward",
     )
-    space_grads, space_mods, arrived, down_share, *up_parts = lax.optimization_barrier(
-        (space_grads, space_mods, arrived, down_share, *up_parts)
+    space_grads, space_mods, arrived, down_share, time_share, *up_parts = lax.optimization_barrier(
+        (space_grads, space_mods, arrived, down_share, time_share, *up_parts)
     )
     space_share = shard_total(space_grads)
+    pair = jnp.stack([down_share, time_share], axis=1)
+    pair_parts, up_parts, space_mods, arrived = lax.optimization_barrier(
+        (parts_of(pair), up_parts, space_mods, arrived)
+    )
+    pair = spread_parts(pair_parts, pair)
+    down_share, time_share = pair[:, 0], pair[:, 1]
     up_share = spread_parts(up_parts, up_share)
     frames_out = to_rows(arrived)
-    pair = jnp.stack([down_share, time_share], axis=1)
-    pair_parts = parts_of(pair)
 
     mod_part = jnp.concatenate([space_mods, time_mods, mlp_mods], axis=1)
     small_grads = jnp.concatenate(
@@ -769,9 +774,6 @@
     )
     small_size = small_grads.shape[0]
     small_grads = jnp.pad(small_grads, (0, -small_size % 1024)).reshape(1, -1, 128)
-    small_grads, pair_parts = lax.optimization_barrier((small_grads, pair_parts))
-    pair = spread_parts(pair_parts, pair)
-    down_share, time_share = pair[:, 0], pair[:, 1]
     space_share = total(space_share)
     every_small = every(small_grads).reshape(groups, -1)
     every_modul = every_small[:, :mod_size].reshape(groups * clips, 9 * width).astype(BF)

time: 499 us -> 496 us (level)
  waiting for transfers between devices: 139 us -> 134 us
    reduce_scatter x3, waiting for transfers between devices: 0.02 us -> 7.7 us  [shard_total(): return lax.psum_scatter(packed, 'shard', scatter_dimension=0, tiled=True)[0]]
    all_to_all x4, waiting for transfers between devices: 29.3 us -> 23.7 us  [exchange(): lax.all_to_all(parts, 'shard', split_axis=0, concat_axis=0, tiled=True)]
  transfers between devices with their start and end apart: 54 -> 54, of which waited for: 20 -> 21; matrix products, arithmetic and copies ran while one was open for 11% -> 11% of each run, Pallas kernels for 24% -> 24%
where the time goes in v8:
time: 496 us; the launch traced here: 489 us
  Pallas kernels  161 us (32%)
  waiting for transfers between devices  134 us (27%)
  starting transfers between devices  87.9 us (18%)
  local copies, waits for them, and re-layouts  33.1 us (7%)
  blocking collectives  28.2 us (6%)
  other arithmetic  25.3 us (5%)
  between operations  15 us (3%)
    pallas_call x5, Pallas kernels, run(): pl.pallas_call(kernel, grid_spec=pltpu.PrefetchScalarGridSpec(num_scalar_...  161 us
    ppermute x24, waiting for transfers between devices, swap_group(): return lax.ppermute(values, 'grp', pairs)  56.8 us
    ppermute x22, waiting for transfers between devices, swap(): return lax.ppermute(values, 'shard', pairs)  46 us
    ppermute x24, starting transfers between devices, swap_group(): return lax.ppermute(values, 'grp', pairs)  42 us
    all_gather x1, blocking collectives, body(): lax.all_gather(small.reshape(1, -1, 128), 'shard', axis=0, tiled=True)  28.2 us
    all_to_all x4, waiting for transfers between devices, exchange(): lax.all_to_all(parts, 'shard', split_axis=0, concat_axis=0, tiled=True)  23.7 us
    ppermute x22, starting transfers between devices, swap(): return lax.ppermute(values, 'shard', pairs)  18.2 us
    all_to_all x4, starting transfers between devices, exchange(): lax.all_to_all(parts, 'shard', split_axis=0, concat_axis=0, tiled=True)  15.9 us
  transfers between devices with their start and end apart: 54, of which 21 were waited for; matrix products, arithmetic and copies ran while one was open for 11% of the time, Pallas kernels for 24%

profile of v8, /device:TPU:0, one launch (start us, length us, event | category | flops | bytes accessed | tf_op | source)
XLA Modules:
  0.0 488.8 jit_solution(12433958725931802282)
XLA Ops:
  8.5 1.8 pad_maximum_fusion.3.refs_0_
  10.3 3.0 collective-permute-start
  13.3 1.5 collective-permute-start.3
  18.9 28.2 %all_gather.6 = f32[8,138,128]{2,1,0:T(8,128)S(1)} all-gather(f32[1,138,128]{2,1,0:T(8,128)S(1)} %maximum_bitcast_fusion), channel_id=1, replica_groups=mesh['grp'=4,'shard'=8] {'shard'}, dimensions={0}, use_global_device_ids=true | all-gather | bytes 635904 | tf_op jit(solution)/shard_map/all_gather | solution.py:530
  54.0 18.8 %space_forward.1 = (bf16[8,4,32,768]{3,2,1,0:T(8,128)(2,1)}, bf16[4,256,2304]{2,1,0:T(8,128)(2,1)}, bf16[4,256,768]{2,1,0:T(8,128)(2,1)}, f32[4,16,256]{2,1,0:T(8,128)}, bf16[4,256,768]{2,1,0:T(8,128)(2,1)}) custom-call(s32[5]{0:T(128)} %pad_add_fusion.where, f32[4,256,768]{2,1,0:T(8,128)} %frames_ref.3, f32[2,9,768]{2,1,0:T(8,128)} %reshape.315.mods_ref, ...), custom_call_target="tpu_custom_call" | custom-call | flops 6442450944 | bytes 17422336 | tf_op jit(solution)/shard_map/space_forward/pallas_call | solution.py:421
  72.9 4.4 all-to-all-start
  78.9 2.9 multiply_convert_fusion
  81.8 1.9 collective-permute-start.11
  83.7 1.5 collective-permute-start.13
  86.0 1.3 copy.121
  87.4 1.3 slice.139
  90.0 1.9 collective-permute-start.7
  91.9 23.7 %all-to-all-done = bf16[8,4,32,768]{3,2,1,0:T(8,128)(2,1)} async-done(((bf16[8,4,32,768]{3,2,1,0:T(8,128)(2,1)}), bf16[8,4,32,768]{3,2,1,0:T(8,128)(2,1)}, u32[]{:S(2)}, u32[]{:S(2)}) %all-to-all-start) | async-done | bytes 1572896 | tf_op jit(solution)/shard_map/all_to_all | solution.py:556
  115.6 3.6 all-to-all-start.1
  119.1 11.7 %reduce-scatter.4.cloned.1.call-start = ((), (), s32[]{:S(2)}) async-start(), calls=%async_computation.7 | async-start | bytes 5308416 | tf_op jit(solution)/shard_map/reduce_scatter | solution.py:660
  130.8 4.9 %collective-permute-done.11.refs_2_ = bf16[4,96,768]{2,1,0:T(8,128)(2,1)} collective-permute-done((bf16[4,96,768]{2,1,0:T(8,128)(2,1)S(1)}, bf16[4,96,768]{2,1,0:T(8,128)(2,1)}, u32[]{:S(2)}, u32[]{:S(2)}) %collective-permute-start.11) | collective-permute-done | bytes 589856 | tf_op jit(solution)/shard_map/ppermute | solution.py:475
  135.8 2.5 collective-permute-start.8
  138.3 11.1 %collective-permute-done.15.refs_6_ = bf16[4,96,768]{2,1,0:T(8,128)(2,1)} collective-permute-done((bf16[4,96,768]{2,1,0:T(8,128)(2,1)S(1)}, bf16[4,96,768]{2,1,0:T(8,128)(2,1)}, u32[]{:S(2)}, u32[]{:S(2)}) %collective-permute-start.15) | collective-permute-done | bytes 589856 | tf_op jit(solution)/shard_map/ppermute | solution.py:475
  149.9 3.4 collective-permute-start.9
  153.4 1.9 collective-permute-done.9
  155.3 19.0 %time_forward.1 = (bf16[4,256,768]{2,1,0:T(8,128)(2,1)}, f32[4,256,768]{2,1,0:T(8,128)}, bf16[4,256,2304]{2,1,0:T(8,128)(2,1)}, bf16[4,256,768]{2,1,0:T(8,128)(2...) custom-call(s32[33]{0:T(128)} %pad_add_fusion.1.inverse, bf16[32,32,768]{2,1,0:T(8,128)(2,1)} %bitcast.7.source, ...), custom_call_target="tpu_custom_call" | custom-call | flops 6442450944 | bytes 18995200 | tf_op jit(solution)/shard_map/time_forward/pallas_call | solution.py:421
  175.4 43.8 %feed.1 = (bf16[32,32,768]{2,1,0:T(8,128)(2,1)}, f32[4,256,768]{2,1,0:T(8,128)}, f32[2,3,768]{2,1,0:T(4,128)}, f32[1,3072]{1,0:T(1,128)}, f32[1,768]{1,0:T(1,128...) custom-call(s32[33]{0:T(128)} %pad_add_fusion.1.inverse, ...), custom_call_target="tpu_custom_call" | custom-call | flops 28991029248 | bytes 28416000 | tf_op jit(solution)/shard_map/feed/pallas_call | solution.py:421
  219.3 3.2 slice_bitcast_fusion
  222.5 39.9 %time_backward.1 = (bf16[32,32,768]{2,1,0:T(8,128)(2,1)}, f32[2,3,768]{2,1,0:T(4,128)}, bf16[8,4,96,768]{3,2,1,0:T(8,128)(2,1)}) custom-call(s32[33]{0:T(128)} %pad_add_fusion.1.inverse, f32[4,256,768]{2,1,0:T(8,128)} %get-tuple-element.77.grad_ref, bf16[4,256,768]{2,1,0:T(8,128)(2,1)} %get-tuple-element.78.resid_ref, f32[2,9,768]{2,1,0:T(8,128)} %reshape.315.mods_ref, ...), custom_call_target="tpu_custom_call" | custom-call | flops 19327352832 | bytes 23732224 | tf_op jit(solution)/shard_map/time_backward/pallas_call | solution.py:421
  262.5 4.3 all-to-all-start.2
  266.9 3.1 fusion
  270.1 1.9 collective-permute-start.19
  272.1 1.5 collective-permute-start.18
  273.7 27.2 %collective-permute-done.19 = bf16[2,2,96,768]{3,2,1,0:T(8,128)(2,1)S(1)} collective-permute-done((bf16[2,2,96,768]{3,2,1,0:T(8,128)(2,1)S(1)}, bf16[2,2,96,768]{3,2,1,0:T(8,128)(2,1)S(1)}, u32[]{:S(2)}, u32[]{:S(2)}) %collective-permute-start.19) | collective-permute-done | bytes 589856 | tf_op jit(solution)/shard_map/ppermute | solution.py:475
  302.7 1.4 collective-permute-start.20
  306.3 1.5 collective-permute-start.22
  307.8 2.4 collective-permute-start.23
  310.7 3.6 all-to-all-start.3
  314.4 39.1 %space_backward.1 = (f32[4,256,768]{2,1,0:T(8,128)}, f32[2,3,768]{2,1,0:T(4,128)}, bf16[8,4,96,768]{3,2,1,0:T(8,128)(2,1)}) custom-call(s32[5]{0:T(128)} %pad_add_fusion.where, bf16[8,4,32,768]{3,2,1,0:T(8,128)(2,1)} %all-to-all-done.2.grad_ref, f32[4,256,768]{2,1,0:T(8,128)} %frames_ref.3, f32[2,9,768]{2,1,0:T(8,128)} %reshape.315.mods_ref, ...), custom_call_target="tpu_custom_call" | custom-call | flops 19327352832 | bytes 25305088 | tf_op jit(solution)/shard_map/space_backward/pallas_call | solution.py:421
  355.8 7.7 %reduce-scatter.6.cloned.1.call-done = bf16[1,4,96,768]{3,2,1,0:T(8,128)(2,1)} async-done(((bf16[8,4,96,768]{3,2,1,0:T(8,128)(2,1)}), bf16[1,4,96,768]{3,2,1,0:T(8,128)(2,1)}) %reduce-scatter.6.cloned.1.call-update) | async-done | bytes 589840 | tf_op jit(solution)/shard_map/reduce_scatter | solution.py:660
  365.8 1.5 collective-permute-start.25
  367.3 2.4 collective-permute-start.26
  370.9 9.2 %collective-permute-done.25 = bf16[192,768]{1,0:T(8,128)(2,1)} collective-permute-done((bf16[192,768]{1,0:T(8,128)(2,1)}, bf16[192,768]{1,0:T(8,128)(2,1)}, u32[]{:S(2)}, u32[]{:S(2)}) %collective-permute-start.25) | collective-permute-done | bytes 294944 | tf_op jit(solution)/shard_map/ppermute | solution.py:485
  380.1 10.9 %collective-permute-done.26 = bf16[192,768]{1,0:T(8,128)(2,1)} collective-permute-done((bf16[192,768]{1,0:T(8,128)(2,1)}, bf16[192,768]{1,0:T(8,128)(2,1)}, u32[]{:S(2)}, u32[]{:S(2)}) %collective-permute-start.26) | collective-permute-done | bytes 294944 | tf_op jit(solution)/shard_map/ppermute | solution.py:485
  391.0 1.8 add_convert_fusion.2
  392.8 2.4 collective-permute-start.43
  395.2 6.0 %collective-permute-start.44 = (bf16[96,768]{1,0:T(8,128)(2,1)}, bf16[96,768]{1,0:T(8,128)(2,1)}, u32[]{:S(2)}, u32[]{:S(2)}) collective-permute-start(bf16[96,768]{1,0:T(8,128)(2,1)} %add_convert_fusion.2), channel_id=1, source_target_pairs={{0,16},{8,24},{16,0},{24,8},{1,17},{9,25},{17,1},{25,9},{2,18},{10... | collective-permute-start | bytes 442376 | tf_op jit(solution)/shard_map/ppermute | solution.py:485
  401.4 1.3 add_convert_fusion.1
  402.7 2.4 collective-permute-start.40
  405.8 1.5 collective-permute-start.29
  407.8 2.0 copy.101
  412.4 12.4 %collective-permute-done.44 = bf16[96,768]{1,0:T(8,128)(2,1)} collective-permute-done((bf16[96,768]{1,0:T(8,128)(2,1)}, bf16[96,768]{1,0:T(8,128)(2,1)}, u32[]{:S(2)}, u32[]{:S(2)}) %collective-permute-start.44) | collective-permute-done | bytes 147488 | tf_op jit(solution)/shard_map/ppermute | solution.py:485
  424.8 1.5 collective-permute-start.30
  429.4 2.0 collective-permute-start.32
  431.4 4.5 collective-permute-done.31
  435.9 1.6 collective-permute-start.33
  437.5 1.3 collective-permute-done.32
  438.8 3.1 collective-permute-done.33
  442.6 1.3 fusion.4
  445.1 2.1 fusion.16
  448.3 1.6 convert.18
  452.3 2.1 collective-permute-start.35
  454.4 2.2 collective-permute-start.36
  459.3 3.9 collective-permute-done.35
  464.3 1.7 collective-permute-start.37
  466.0 2.0 collective-permute-start.38
  468.7 1.7 slice_bitcast_fusion.4
  470.4 1.6 collective-permute-done.37
  472.0 7.4 %collective-permute-done.38 = bf16[96,768]{1,0:T(8,128)(2,1)S(1)} collective-permute-done((bf16[96,768]{1,0:T(8,128)(2,1)S(1)}, bf16[96,768]{1,0:T(8,128)(2,1)S(1)}, u32[]{:S(2)}, u32[]{:S(2)}) %collective-permute-start.38) | collective-permute-done | bytes 147488 | tf_op jit(solution)/shard_map/ppermute | solution.py:485
  (244 shorter events, 47.2 us)
Async XLA Ops:
  7.2 167.1 %all-gather.3.cloned.1.call-start = ((), (), s32[]{:S(2)}) async-start(), calls=%async_computation.10 | async-start | bytes 10616832 | tf_op jit(solution)/shard_map/all_gather | solution.py:478
  8.4 9.2 %copy-start.7 = (bf16[96,3072]{1,0:T(8,128)(2,1)S(1)}, bf16[96,3072]{1,0:T(8,128)(2,1)}, u32[]{:S(2)}) copy-start(bf16[96,3072]{1,0:T(8,128)(2,1)} %param.26) | copy-start | bytes 1769476
  10.3 37.5 %collective-permute-start = (bf16[4,96,768]{2,1,0:T(8,128)(2,1)}, bf16[4,96,768]{2,1,0:T(8,128)(2,1)}, u32[]{:S(2)}, u32[]{:S(2)}) collective-permute-start(bf16[4,96,768]{2,1,0:T(8,128)(2,1)} %pad_maximum_fusion.3.refs_0_), channel_id=1, source_target_pairs={{0,2},{1,3},{2,0},{3,1},{4,6},{5,7},{6,4},{7,5},{8,10},{9,11},{10,... | collective-permute-start | bytes 1769480 | tf_op jit(solution)/shard_map/ppermute | solution.py:475
  13.3 34.5 %collective-permute-start.3 = (bf16[4,96,768]{2,1,0:T(8,128)(2,1)}, bf16[4,96,768]{2,1,0:T(8,128)(2,1)}, u32[]{:S(2)}, u32[]{:S(2)}) collective-permute-start(bf16[4,96,768]{2,1,0:T(8,128)(2,1)} %pad_maximum_fusion.3.refs_0_), channel_id=1, source_target_pairs={{0,4},{1,5},{2,6},{3,7},{4,0},{5,1},{6,2},{7,3},{8,12},{9,13},{10,... | collective-permute-start | bytes 1769480 | tf_op jit(solution)/shard_map/ppermute | solution.py:475
  14.8 33.0 %collective-permute-start.5 = (bf16[4,96,768]{2,1,0:T(8,128)(2,1)}, bf16[4,96,768]{2,1,0:T(8,128)(2,1)}, u32[]{:S(2)}, u32[]{:S(2)}) collective-permute-start(bf16[4,96,768]{2,1,0:T(8,128)(2,1)} %pad_maximum_fusion.3.refs_0_), channel_id=1, source_target_pairs={{0,6},{1,7},{2,4},{3,5},{4,2},{5,3},{6,0},{7,1},{8,14},{9,15},{10,... | collective-permute-start | bytes 1769480 | tf_op jit(solution)/shard_map/ppermute | solution.py:475
  18.1 29.0 %copy-start.15 = (bf16[96,768]{1,0:T(8,128)(2,1)S(1)}, bf16[96,768]{1,0:T(8,128)(2,1)}, u32[]{:S(2)}) copy-start(bf16[96,768]{1,0:T(8,128)(2,1)} %param.25) | copy-start | bytes 442372
  47.2 40.2 %copy-start.9 = (bf16[4,96,768]{2,1,0:T(8,128)(2,1)}, bf16[4,96,768]{2,1,0:T(8,128)(2,1)S(1)}, u32[]{:S(2)}) copy-start(bf16[4,96,768]{2,1,0:T(8,128)(2,1)S(1)} %pad_maximum_fusion.4.refs_0_) | copy-start | bytes 1769476
  49.1 3.1 collective-permute-start.1
  49.5 2.8 collective-permute-start.2
  49.7 3.5 collective-permute-start.4
  50.0 4.0 collective-permute-start.6
  51.5 21.4 %copy-start.12 = (f32[138,128]{1,0:T(8,128)}, f32[138,128]{1,0:T(8,128)S(1)}, u32[]{:S(2)}) copy-start(f32[138,128]{1,0:T(8,128)S(1)} %reduce_sum.37) | copy-start | bytes 211972
  72.9 42.6 %all-to-all-start = ((bf16[8,4,32,768]{3,2,1,0:T(8,128)(2,1)}), bf16[8,4,32,768]{3,2,1,0:T(8,128)(2,1)}, u32[]{:S(2)}, u32[]{:S(2)}) async-start(bf16[8,4,32,768]{3,2,1,0:T(8,128)(2,1)} %get-tuple-element.71), calls=%async_computation | async-start | bytes 3145728 | tf_op jit(solution)/shard_map/all_to_all | solution.py:556
  81.8 54.0 %collective-permute-start.11 = (bf16[4,96,768]{2,1,0:T(8,128)(2,1)S(1)}, bf16[4,96,768]{2,1,0:T(8,128)(2,1)}, u32[]{:S(2)}, u32[]{:S(2)}) collective-permute-start(bf16[4,96,768]{2,1,0:T(8,128)(2,1)S(1)} %pad_maximum_fusion.4.refs_0_), channel_id=1, source_target_pairs={{0,2},{1,3},{2,0},{3,1},{4,6},{5,7},{6,4},{7,5},{8,10},{9,11},{10,... | collective-permute-start | bytes 1769480 | tf_op jit(solution)/shard_map/ppermute | solution.py:475
  83.7 54.5 %collective-permute-start.13 = (bf16[4,96,768]{2,1,0:T(8,128)(2,1)S(1)}, bf16[4,96,768]{2,1,0:T(8,128)(2,1)}, u32[]{:S(2)}, u32[]{:S(2)}) collective-permute-start(bf16[4,96,768]{2,1,0:T(8,128)(2,1)S(1)} %pad_maximum_fusion.4.refs_0_), channel_id=1, source_target_pairs={{0,4},{1,5},{2,6},{3,7},{4,0},{5,1},{6,2},{7,3},{8,12},{9,13},{10,... | collective-permute-start | bytes 1769480 | tf_op jit(solution)/shard_map/ppermute | solution.py:475
  85.2 64.2 %collective-permute-start.15 = (bf16[4,96,768]{2,1,0:T(8,128)(2,1)S(1)}, bf16[4,96,768]{2,1,0:T(8,128)(2,1)}, u32[]{:S(2)}, u32[]{:S(2)}) collective-permute-start(bf16[4,96,768]{2,1,0:T(8,128)(2,1)S(1)} %pad_maximum_fusion.4.refs_0_), channel_id=1, source_target_pairs={{0,6},{1,7},{2,4},{3,5},{4,2},{5,3},{6,0},{7,1},{8,14},{9,15},{10,... | collective-permute-start | bytes 1769480 | tf_op jit(solution)/shard_map/ppermute | solution.py:475
  87.4 67.9 %collective-permute-start.10 = (bf16[4,96,768]{2,1,0:T(8,128)(2,1)S(1)}, bf16[4,96,768]{2,1,0:T(8,128)(2,1)}, u32[]{:S(2)}, u32[]{:S(2)}) collective-permute-start(bf16[4,96,768]{2,1,0:T(8,128)(2,1)S(1)} %pad_maximum_fusion.4.refs_0_), channel_id=1, source_target_pairs={{0,1},{1,0},{2,3},{3,2},{4,5},{5,4},{6,7},{7,6},{8,9},{9,8},{10,11... | collective-permute-start | bytes 1769480 | tf_op jit(solution)/shard_map/ppermute | solution.py:475
  90.0 59.4 %collective-permute-start.7 = (f32[2,97]{1,0:T(2,128)S(1)}, f32[2,97]{1,0:T(2,128)S(1)}, u32[]{:S(2)}, u32[]{:S(2)}) collective-permute-start(f32[2,97]{1,0:T(2,128)S(1)} %pad_maximum_fusion.8), channel_id=1, source_target_pairs={{0,8},{8,0},{16,24},{24,16},{1,9},{9,1},{17,25},{25,17},{2,10},{10... | collective-permute-start | bytes 2336 | tf_op jit(solution)/shard_map/ppermute | solution.py:485
  115.6 58.7 %all-to-all-start.1 = ((bf16[8,4,32,768]{3,2,1,0:T(8,128)(2,1)}), bf16[8,4,32,768]{3,2,1,0:T(8,128)(2,1)S(1)}, u32[]{:S(2)}, u32[]{:S(2)}) async-start(bf16[8,4,32,768]{3,2,1,0:T(8,128)(2,1)} %bitcast.180), calls=%async_computation.1 | async-start | bytes 3145728 | tf_op jit(solution)/shard_map/all_to_all | solution.py:556
  119.1 182.1 %reduce-scatter.4.cloned.1.call-start = ((), (), s32[]{:S(2)}) async-start(), calls=%async_computation.7 | async-start | bytes 5308416 | tf_op jit(solution)/shard_map/reduce_scatter | solution.py:660
  135.8 14.1 %collective-permute-start.8 = (f32[2,97]{1,0:T(2,128)S(1)}, f32[2,97]{1,0:T(2,128)S(1)}, u32[]{:S(2)}, u32[]{:S(2)}) collective-permute-start(f32[2,97]{1,0:T(2,128)S(1)} %pad_maximum_fusion.8), channel_id=1, source_target_pairs={{0,16},{8,24},{16,0},{24,8},{1,17},{9,25},{17,1},{25,9},{2,18},{10... | collective-permute-start | bytes 2336 | tf_op jit(solution)/shard_map/ppermute | solution.py:485
  138.2 17.0 %collective-permute-start.12 = (bf16[4,96,768]{2,1,0:T(8,128)(2,1)}, bf16[4,96,768]{2,1,0:T(8,128)(2,1)}, u32[]{:S(2)}, u32[]{:S(2)}) collective-permute-start(bf16[4,96,768]{2,1,0:T(8,128)(2,1)} %collective-permute-done.11.refs_2_), channel_id=1, source_target_pairs={{0,1},{1,0},{2,3},{3,2},{4,5},{5,4},{6,7},{7,6},{8,9},{9,8},{10,11... | collective-permute-start | bytes 1769480 | tf_op jit(solution)/shard_map/ppermute | solution.py:475
  149.4 5.9 %collective-permute-start.14 = (bf16[4,96,768]{2,1,0:T(8,128)(2,1)}, bf16[4,96,768]{2,1,0:T(8,128)(2,1)}, u32[]{:S(2)}, u32[]{:S(2)}) collective-permute-start(bf16[4,96,768]{2,1,0:T(8,128)(2,1)} %collective-permute-done.13.refs_4_), channel_id=1, source_target_pairs={{0,1},{1,0},{2,3},{3,2},{4,5},{5,4},{6,7},{7,6},{8,9},{9,8},{10,11... | collective-permute-start | bytes 1769480 | tf_op jit(solution)/shard_map/ppermute | solution.py:475
  149.4 5.9 %collective-permute-start.16 = (bf16[4,96,768]{2,1,0:T(8,128)(2,1)}, bf16[4,96,768]{2,1,0:T(8,128)(2,1)}, u32[]{:S(2)}, u32[]{:S(2)}) collective-permute-start(bf16[4,96,768]{2,1,0:T(8,128)(2,1)} %collective-permute-done.15.refs_6_), channel_id=1, source_target_pairs={{0,1},{1,0},{2,3},{3,2},{4,5},{5,4},{6,7},{7,6},{8,9},{9,8},{10,11... | collective-permute-start | bytes 1769480 | tf_op jit(solution)/shard_map/ppermute | solution.py:475
  149.9 5.4 %collective-permute-start.9 = (f32[2,97]{1,0:T(2,128)S(1)}, f32[2,97]{1,0:T(2,128)S(1)}, u32[]{:S(2)}, u32[]{:S(2)}) collective-permute-start(f32[2,97]{1,0:T(2,128)S(1)} %pad_maximum_fusion.8), channel_id=1, source_target_pairs={{0,24},{8,16},{16,8},{24,0},{1,25},{9,17},{17,9},{25,1},{2,26},{10... | collective-permute-start | bytes 2336 | tf_op jit(solution)/shard_map/ppermute | solution.py:485
  222.5 44.3 %collective-permute-start.17 = (bf16[4,4,96,768]{3,2,1,0:T(8,128)(2,1)}, bf16[4,4,96,768]{3,2,1,0:T(8,128)(2,1)}, u32[]{:S(2)}, u32[]{:S(2)}) collective-permute-start(bf16[4,4,96,768]{3,2,1,0:T(8,128)(2,1)} %slice_bitcast_fusion), channel_id=1, source_target_pairs={{0,1},{1,0},{2,3},{3,2},{4,5},{5,4},{6,7},{7,6},{8,9},{9,8},{10,11... | collective-permute-start | bytes 7077896 | tf_op jit(solution)/shard_map/ppermute | solution.py:475
  262.5 38.7 %all-to-all-start.2 = ((bf16[8,4,32,768]{3,2,1,0:T(8,128)(2,1)}), bf16[8,4,32,768]{3,2,1,0:T(8,128)(2,1)}, u32[]{:S(2)}, u32[]{:S(2)}) async-start(bf16[8,4,32,768]{3,2,1,0:T(8,128)(2,1)} %bitcast.206), calls=%async_computation.3 | async-start | bytes 3145728 | tf_op jit(solution)/shard_map/all_to_all | solution.py:556
  266.8 96.7 %reduce-scatter.6.cloned.1.call-start = ((), (), s32[]{:S(2)}) async-start(), calls=%async_computation.8 | async-start | bytes 5308416 | tf_op jit(solution)/shard_map/reduce_scatter | solution.py:660
  270.1 30.8 %collective-permute-start.19 = (bf16[2,2,96,768]{3,2,1,0:T(8,128)(2,1)S(1)}, bf16[2,2,96,768]{3,2,1,0:T(8,128)(2,1)S(1)}, u32[]{:S(2)}, u32[]{:S(2)}) collective-permute-start(bf16[2,2,96,768]{3,2,1,0:T(8,128)(2,1)S(1)} %slice.145), channel_id=1, source_target_pairs={{0,4},{1,5},{2,6},{3,7},{4,0},{5,1},{6,2},{7,3},{8,12},{9,13},{10,... | collective-permute-start | bytes 1769480 | tf_op jit(solution)/shard_map/ppermute | solution.py:475
  272.1 28.9 %collective-permute-start.18 = (bf16[2,2,96,768]{3,2,1,0:T(8,128)(2,1)S(1)}, bf16[2,2,96,768]{3,2,1,0:T(8,128)(2,1)S(1)}, u32[]{:S(2)}, u32[]{:S(2)}) collective-permute-start(bf16[2,2,96,768]{3,2,1,0:T(8,128)(2,1)S(1)} %slice_bitcast_fusion.2), channel_id=1, source_target_pairs={{0,2},{1,3},{2,0},{3,1},{4,6},{5,7},{6,4},{7,5},{8,10},{9,11},{10,... | collective-permute-start | bytes 1769480 | tf_op jit(solution)/shard_map/ppermute | solution.py:475
  302.7 50.7 %collective-permute-start.20 = (bf16[2,96,768]{2,1,0:T(8,128)(2,1)}, bf16[2,96,768]{2,1,0:T(8,128)(2,1)}, u32[]{:S(2)}, u32[]{:S(2)}) collective-permute-start(bf16[2,96,768]{2,1,0:T(8,128)(2,1)} %slice_bitcast_fusion.6), channel_id=1, source_target_pairs={{0,4},{1,5},{2,6},{3,7},{4,0},{5,1},{6,2},{7,3},{8,12},{9,13},{10,... | collective-permute-start | bytes 884744 | tf_op jit(solution)/shard_map/ppermute | solution.py:475
  304.9 49.8 %collective-permute-start.21 = (bf16[2,96,768]{2,1,0:T(8,128)(2,1)}, bf16[2,96,768]{2,1,0:T(8,128)(2,1)}, u32[]{:S(2)}, u32[]{:S(2)}) collective-permute-start(bf16[2,96,768]{2,1,0:T(8,128)(2,1)} %slice_bitcast_fusion.5), channel_id=1, source_target_pairs={{0,2},{1,3},{2,0},{3,1},{4,6},{5,7},{6,4},{7,5},{8,10},{9,11},{10,... | collective-permute-start | bytes 884744 | tf_op jit(solution)/shard_map/ppermute | solution.py:475
  306.3 49.5 %collective-permute-start.22 = (bf16[96,768]{1,0:T(8,128)(2,1)}, bf16[96,768]{1,0:T(8,128)(2,1)}, u32[]{:S(2)}, u32[]{:S(2)}) collective-permute-start(bf16[96,768]{1,0:T(8,128)(2,1)} %get-tuple-element.146), channel_id=1, source_target_pairs={{0,8},{8,0},{16,24},{24,16},{1,9},{9,1},{17,25},{25,17},{2,10},{10... | collective-permute-start | bytes 442376 | tf_op jit(solution)/shard_map/ppermute | solution.py:485
  307.8 48.0 %collective-permute-start.23 = (bf16[96,768]{1,0:T(8,128)(2,1)}, bf16[96,768]{1,0:T(8,128)(2,1)}, u32[]{:S(2)}, u32[]{:S(2)}) collective-permute-start(bf16[96,768]{1,0:T(8,128)(2,1)} %get-tuple-element.145), channel_id=1, source_target_pairs={{0,16},{8,24},{16,0},{24,8},{1,17},{9,25},{17,1},{25,9},{2,18},{10... | collective-permute-start | bytes 442376 | tf_op jit(solution)/shard_map/ppermute | solution.py:485
  310.2 45.6 %collective-permute-start.24 = (bf16[96,768]{1,0:T(8,128)(2,1)}, bf16[96,768]{1,0:T(8,128)(2,1)}, u32[]{:S(2)}, u32[]{:S(2)}) collective-permute-start(bf16[96,768]{1,0:T(8,128)(2,1)} %get-tuple-element.144), channel_id=1, source_target_pairs={{0,24},{8,16},{16,8},{24,0},{1,25},{9,17},{17,9},{25,1},{2,26},{10... | collective-permute-start | bytes 442376 | tf_op jit(solution)/shard_map/ppermute | solution.py:485
  310.7 45.1 %all-to-all-start.3 = ((bf16[8,4,32,768]{3,2,1,0:T(8,128)(2,1)}), bf16[8,4,32,768]{3,2,1,0:T(8,128)(2,1)S(1)}, u32[]{:S(2)}, u32[]{:S(2)}) async-start(bf16[8,4,32,768]{3,2,1,0:T(8,128)(2,1)} %bitcast.204), calls=%async_computation.4 | async-start | bytes 3145728 | tf_op jit(solution)/shard_map/all_to_all | solution.py:556
  314.3 136.8 %reduce-scatter.8.cloned.1.call-start = ((), (), s32[]{:S(2)}) async-start(), calls=%async_computation.9 | async-start | bytes 5308416 | tf_op jit(solution)/shard_map/reduce_scatter | solution.py:660
  364.8 26.2 %copy-start.6 = (bf16[96,768]{1,0:T(8,128)(2,1)S(1)}, bf16[96,768]{1,0:T(8,128)(2,1)}, u32[]{:S(2)}) copy-start(bf16[96,768]{1,0:T(8,128)(2,1)} %get-tuple-element.121) | copy-start | bytes 442372
  364.8 36.4 %copy-start.18 = (f32[2,3,768]{2,1,0:T(4,128)S(1)}, f32[2,3,768]{2,1,0:T(4,128)}, u32[]{:S(2)}) copy-start(f32[2,3,768]{2,1,0:T(4,128)} %get-tuple-element.113) | copy-start | bytes 55300
  364.8 36.4 %copy-start.19 = (f32[2,3,768]{2,1,0:T(4,128)S(1)}, f32[2,3,768]{2,1,0:T(4,128)}, u32[]{:S(2)}) copy-start(f32[2,3,768]{2,1,0:T(4,128)} %get-tuple-element.112) | copy-start | bytes 55300
  364.8 36.4 %copy-start.20 = (f32[2,3,768]{2,1,0:T(4,128)S(1)}, f32[2,3,768]{2,1,0:T(4,128)}, u32[]{:S(2)}) copy-start(f32[2,3,768]{2,1,0:T(4,128)} %get-tuple-element.111) | copy-start | bytes 55300
  364.8 36.4 %copy-start.16 = (f32[1,3072]{1,0:T(1,128)S(1)}, f32[1,3072]{1,0:T(1,128)}, u32[]{:S(2)}) copy-start(f32[1,3072]{1,0:T(1,128)} %get-tuple-element.114) | copy-start | bytes 36868
  365.8 14.3 %collective-permute-start.25 = (bf16[192,768]{1,0:T(8,128)(2,1)}, bf16[192,768]{1,0:T(8,128)(2,1)}, u32[]{:S(2)}, u32[]{:S(2)}) collective-permute-start(bf16[192,768]{1,0:T(8,128)(2,1)} %get-tuple-element.131), channel_id=1, source_target_pairs={{0,8},{8,0},{16,24},{24,16},{1,9},{9,1},{17,25},{25,17},{2,10},{10... | collective-permute-start | bytes 884744 | tf_op jit(solution)/shard_map/ppermute | solution.py:485
  367.3 23.7 %collective-permute-start.26 = (bf16[192,768]{1,0:T(8,128)(2,1)}, bf16[192,768]{1,0:T(8,128)(2,1)}, u32[]{:S(2)}, u32[]{:S(2)}) collective-permute-start(bf16[192,768]{1,0:T(8,128)(2,1)} %get-tuple-element.130), channel_id=1, source_target_pairs={{0,16},{8,24},{16,0},{24,8},{1,17},{9,25},{17,1},{25,9},{2,18},{10... | collective-permute-start | bytes 884744 | tf_op jit(solution)/shard_map/ppermute | solution.py:485
  369.7 21.3 %collective-permute-start.27 = (bf16[192,768]{1,0:T(8,128)(2,1)}, bf16[192,768]{1,0:T(8,128)(2,1)}, u32[]{:S(2)}, u32[]{:S(2)}) collective-permute-start(bf16[192,768]{1,0:T(8,128)(2,1)} %get-tuple-element.129), channel_id=1, source_target_pairs={{0,24},{8,16},{16,8},{24,0},{1,25},{9,17},{17,9},{25,1},{2,26},{10... | collective-permute-start | bytes 884744 | tf_op jit(solution)/shard_map/ppermute | solution.py:485
  392.8 18.6 %collective-permute-start.43 = (bf16[96,768]{1,0:T(8,128)(2,1)}, bf16[96,768]{1,0:T(8,128)(2,1)}, u32[]{:S(2)}, u32[]{:S(2)}) collective-permute-start(bf16[96,768]{1,0:T(8,128)(2,1)} %add_convert_fusion.2), channel_id=1, source_target_pairs={{0,24},{8,16},{16,8},{24,0},{1,25},{9,17},{17,9},{25,1},{2,26},{10... | collective-permute-start | bytes 442376 | tf_op jit(solution)/shard_map/ppermute | solution.py:485
  395.2 29.5 %collective-permute-start.44 = (bf16[96,768]{1,0:T(8,128)(2,1)}, bf16[96,768]{1,0:T(8,128)(2,1)}, u32[]{:S(2)}, u32[]{:S(2)}) collective-permute-start(bf16[96,768]{1,0:T(8,128)(2,1)} %add_convert_fusion.2), channel_id=1, source_target_pairs={{0,16},{8,24},{16,0},{24,8},{1,17},{9,25},{17,1},{25,9},{2,18},{10... | collective-permute-start | bytes 442376 | tf_op jit(solution)/shard_map/ppermute | solution.py:485
  401.2 25.0 %collective-permute-start.45 = (bf16[96,768]{1,0:T(8,128)(2,1)}, bf16[96,768]{1,0:T(8,128)(2,1)}, u32[]{:S(2)}, u32[]{:S(2)}) collective-permute-start(bf16[96,768]{1,0:T(8,128)(2,1)} %add_convert_fusion.2), channel_id=1, source_target_pairs={{0,8},{8,0},{16,24},{24,16},{1,9},{9,1},{17,25},{25,17},{2,10},{10... | collective-permute-start | bytes 442376 | tf_op jit(solution)/shard_map/ppermute | solution.py:485
  401.3 3.8 collective-permute-start.28
  402.7 44.5 %collective-permute-start.40 = (bf16[192,768]{1,0:T(8,128)(2,1)S(1)}, bf16[192,768]{1,0:T(8,128)(2,1)}, u32[]{:S(2)}, u32[]{:S(2)}) collective-permute-start(bf16[192,768]{1,0:T(8,128)(2,1)S(1)} %add_convert_fusion.1), channel_id=1, source_target_pairs={{0,24},{8,16},{16,8},{24,0},{1,25},{9,17},{17,9},{25,1},{2,26},{10... | collective-permute-start | bytes 884744 | tf_op jit(solution)/shard_map/ppermute | solution.py:485
  405.8 4.5 collective-permute-start.29
  410.3 36.9 %collective-permute-start.41 = (bf16[192,768]{1,0:T(8,128)(2,1)S(1)}, bf16[192,768]{1,0:T(8,128)(2,1)S(1)}, u32[]{:S(2)}, u32[]{:S(2)}) collective-permute-start(bf16[192,768]{1,0:T(8,128)(2,1)S(1)} %add_convert_fusion.1), channel_id=1, source_target_pairs={{0,16},{8,24},{16,0},{24,8},{1,17},{9,25},{17,1},{25,9},{2,18},{10... | collective-permute-start | bytes 884744 | tf_op jit(solution)/shard_map/ppermute | solution.py:485
  411.4 35.8 %collective-permute-start.42 = (bf16[192,768]{1,0:T(8,128)(2,1)S(1)}, bf16[192,768]{1,0:T(8,128)(2,1)S(1)}, u32[]{:S(2)}, u32[]{:S(2)}) collective-permute-start(bf16[192,768]{1,0:T(8,128)(2,1)S(1)} %add_convert_fusion.1), channel_id=1, source_target_pairs={{0,8},{8,0},{16,24},{24,16},{1,9},{9,1},{17,25},{25,17},{2,10},{10... | collective-permute-start | bytes 884744 | tf_op jit(solution)/shard_map/ppermute | solution.py:485
  424.8 4.4 collective-permute-start.30
  429.3 13.3 %copy-start.24 = (s32[8]{0:T(128)S(1)}, s32[8]{0:T(128)}, u32[]{:S(2)}) copy-start(s32[8]{0:T(128)} %convert_reduce_fusion.1) | copy-start | bytes 100
  429.3 6.6 %collective-permute-start.31 = (f32[1,112,128]{2,1,0:T(8,128)S(1)}, f32[1,112,128]{2,1,0:T(8,128)S(1)}, u32[]{:S(2)}, u32[]{:S(2)}) collective-permute-start(f32[1,112,128]{2,1,0:T(8,128)S(1)} %fusion.9), channel_id=1, source_target_pairs={{0,8},{8,0},{16,24},{24,16},{1,9},{9,1},{17,25},{25,17},{2,10},{10... | collective-permute-start | bytes 172040 | tf_op jit(solution)/shard_map/ppermute | solution.py:485
  429.4 9.4 %collective-permute-start.32 = (f32[1,112,128]{2,1,0:T(8,128)S(1)}, f32[1,112,128]{2,1,0:T(8,128)S(1)}, u32[]{:S(2)}, u32[]{:S(2)}) collective-permute-start(f32[1,112,128]{2,1,0:T(8,128)S(1)} %fusion.9), channel_id=1, source_target_pairs={{0,16},{8,24},{16,0},{24,8},{1,17},{9,25},{17,1},{25,9},{2,18},{10... | collective-permute-start | bytes 172040 | tf_op jit(solution)/shard_map/ppermute | solution.py:485
  435.9 6.0 %collective-permute-start.33 = (f32[1,112,128]{2,1,0:T(8,128)S(1)}, f32[1,112,128]{2,1,0:T(8,128)S(1)}, u32[]{:S(2)}, u32[]{:S(2)}) collective-permute-start(f32[1,112,128]{2,1,0:T(8,128)S(1)} %fusion.9), channel_id=1, source_target_pairs={{0,24},{8,16},{16,8},{24,0},{1,25},{9,17},{17,9},{25,1},{2,26},{10... | collective-permute-start | bytes 172040 | tf_op jit(solution)/shard_map/ppermute | solution.py:485
  452.2 7.2 %collective-permute-start.34 = (bf16[96,768]{1,0:T(8,128)(2,1)S(1)}, bf16[96,768]{1,0:T(8,128)(2,1)S(1)}, u32[]{:S(2)}, u32[]{:S(2)}) collective-permute-start(bf16[96,768]{1,0:T(8,128)(2,1)S(1)} %get-tuple-element.141), channel_id=1, source_target_pairs={{0,8},{8,0},{16,24},{24,16},{1,9},{9,1},{17,25},{25,17},{2,10},{10... | collective-permute-start | bytes 442376 | tf_op jit(solution)/shard_map/ppermute | solution.py:485
  452.3 11.0 %collective-permute-start.35 = (bf16[96,768]{1,0:T(8,128)(2,1)S(1)}, bf16[96,768]{1,0:T(8,128)(2,1)S(1)}, u32[]{:S(2)}, u32[]{:S(2)}) collective-permute-start(bf16[96,768]{1,0:T(8,128)(2,1)S(1)} %get-tuple-element.143), channel_id=1, source_target_pairs={{0,16},{8,24},{16,0},{24,8},{1,17},{9,25},{17,1},{25,9},{2,18},{10... | collective-permute-start | bytes 442376 | tf_op jit(solution)/shard_map/ppermute | solution.py:485
  454.4 8.9 %collective-permute-start.36 = (bf16[96,768]{1,0:T(8,128)(2,1)S(1)}, bf16[96,768]{1,0:T(8,128)(2,1)S(1)}, u32[]{:S(2)}, u32[]{:S(2)}) collective-permute-start(bf16[96,768]{1,0:T(8,128)(2,1)S(1)} %get-tuple-element.142), channel_id=1, source_target_pairs={{0,24},{8,16},{16,8},{24,0},{1,25},{9,17},{17,9},{25,1},{2,26},{10... | collective-permute-start | bytes 442376 | tf_op jit(solution)/shard_map/ppermute | solution.py:485
  464.3 7.7 %collective-permute-start.37 = (bf16[96,768]{1,0:T(8,128)(2,1)S(1)}, bf16[96,768]{1,0:T(8,128)(2,1)S(1)}, u32[]{:S(2)}, u32[]{:S(2)}) collective-permute-start(bf16[96,768]{1,0:T(8,128)(2,1)S(1)} %fusion.7), channel_id=1, source_target_pairs={{0,24},{8,16},{16,8},{24,0},{1,25},{9,17},{17,9},{25,1},{2,26},{10... | collective-permute-start | bytes 442376 | tf_op jit(solution)/shard_map/ppermute | solution.py:485
  466.0 13.4 %collective-permute-start.38 = (bf16[96,768]{1,0:T(8,128)(2,1)S(1)}, bf16[96,768]{1,0:T(8,128)(2,1)S(1)}, u32[]{:S(2)}, u32[]{:S(2)}) collective-permute-start(bf16[96,768]{1,0:T(8,128)(2,1)S(1)} %fusion.7), channel_id=1, source_target_pairs={{0,16},{8,24},{16,0},{24,8},{1,17},{9,25},{17,1},{25,9},{2,18},{10... | collective-permute-start | bytes 442376 | tf_op jit(solution)/shard_map/ppermute | solution.py:485
  467.9 11.5 %collective-permute-start.39 = (bf16[96,768]{1,0:T(8,128)(2,1)S(1)}, bf16[96,768]{1,0:T(8,128)(2,1)S(1)}, u32[]{:S(2)}, u32[]{:S(2)}) collective-permute-start(bf16[96,768]{1,0:T(8,128)(2,1)S(1)} %fusion.7), channel_id=1, source_target_pairs={{0,8},{8,0},{16,24},{24,16},{1,9},{9,1},{17,25},{25,17},{2,10},{10... | collective-permute-start | bytes 442376 | tf_op jit(solution)/shard_map/ppermute | solution.py:485
  (24 other events, 111.3 us)
Sparse Core Ops, SparseCore 0:
  49.2 105.5 all-gather.2
  219.4 54.6 reduce-scatter.3
  301.4 62.0 reduce-scatter.5
  366.8 54.5 reduce-scatter.7
